TPU v7x, 32 devices: a whole 2x2x4 slice. The times are simulated.
32 devices in a mesh: fsdp: 4 (over y, x), ctx: 4 (over z), tp: 2 (over core).
Axes of the slice: x: 2, y: 2, z: 4, core: 2. Of those that a mesh axis runs over, the one named last changes fastest.
Arguments:
- tokens: bfloat16 [8, 1568, 1024], P('fsdp', 'ctx'), may hold values from -6 to 6
- clip_mask: int32 [8], P('fsdp'), may hold values 0 or 1
- cotangent: bfloat16 [8, 1568, 1024], P('fsdp', 'ctx'), may hold values from -6 to 6
- first_gain: float32 [1024], replicated, may hold values from 0.1 to 1.9
- first_shift: float32 [1024], replicated, may hold values from -1.75 to 1.75
- joint_weight: bfloat16 [1024, 3, 1024], P('fsdp', None, 'tp'), may hold values from -0.1875 to 0.1875
- joint_bias: float32 [2, 1024], P(None, 'tp'), may hold values from -0.625 to 0.625
- mixer_weight: bfloat16 [1024, 1024], P('fsdp', 'tp'), may hold values from -2 to 2
- mixer_bias: float32 [1024], replicated, may hold values from -1.75 to 1.75
- second_gain: float32 [1024], replicated, may hold values from 0.1 to 1.9
- second_shift: float32 [1024], replicated, may hold values from -1.75 to 1.75
- expand_weight: bfloat16 [1024, 4096], P('fsdp', 'tp'), may hold values from -0.1875 to 0.1875
- expand_bias: float32 [4096], P('tp'), may hold values from -1.75 to 1.75
- reduce_weight: bfloat16 [1024, 4096], P('fsdp', 'tp'), may hold values from -0.09375 to 0.09375
- reduce_bias: float32 [1024], replicated, may hold values from -1.75 to 1.75
Outputs:
- result: bfloat16 [8, 1568, 1024], P('fsdp', 'ctx')
- tokens_grad: float32 [8, 1568, 1024], P('fsdp', 'ctx')
- grad_first_gain: float32 [1024], P('fsdp')
- grad_first_shift: float32 [1024], P('fsdp')
- grad_joint_weight: float32 [1024, 3, 1024], P('fsdp', None, 'tp')
- grad_joint_bias: float32 [2, 1024], P(None, ('tp', 'fsdp'))
- grad_mixer_weight: float32 [1024, 1024], P('fsdp', 'tp')
- grad_mixer_bias: float32 [1024], P('fsdp')
- grad_second_gain: float32 [1024], P('fsdp')
- grad_second_shift: float32 [1024], P('fsdp')
- grad_expand_weight: float32 [1024, 4096], P('fsdp', 'tp')
- grad_expand_bias: float32 [4096], P(('tp', 'fsdp'))
- grad_reduce_weight: float32 [1024, 4096], P('fsdp', 'tp')
- grad_reduce_bias: float32 [1024], P('fsdp')
Inputs may be any that keep to these rules, and one draw needn't show every extreme that they name: `clip_mask`: 1 marks a real clip, 0 a padding clip.
All inputs are finite; a program needn't handle non-finite values. No bound on the sum of `clip_mask` on one device may be relied on, other than what follows from the above.
Results may differ from a plain program's by a relative error of at most 0.02.
Values may be sent and summed in bfloat16 or wider, within the bound.
No kernel may reach another device: no remote copies, remote signals or barrier semaphores. Data moves between devices by JAX's collectives and lax.ppermute only.
A program may use at most 192 MiB of HBM per device.

v0:
```python
import jax
import jax.numpy as jnp
from jax import lax
from jax.experimental import pallas as pl
from jax.experimental.pallas import tpu as pltpu
from jax.sharding import PartitionSpec as P

HEAD_DIM = 64
EPSILON = 1e-06
LOW = jnp.bfloat16
FULL = jnp.float32

ROW_BY_ROW = (((1,), (1,)), ((), ()))
PLAIN = (((1,), (0,)), ((), ()))
COLUMN_BY_COLUMN = (((0,), (0,)), ((), ()))


def product(left, right, dims):
    return lax.dot_general(left, right, dims, preferred_element_type=FULL)


def normalize(value_rows):
    center = value_rows - jnp.mean(value_rows, axis=-1, keepdims=True)
    inverse = lax.rsqrt(jnp.mean(center * center, axis=-1, keepdims=True) + EPSILON)
    return (center * inverse, inverse)


def norm_back(upstream, gain, scaled, inverse):
    weighted = upstream * gain
    return inverse * (
        weighted
        - jnp.mean(weighted, axis=-1, keepdims=True)
        - scaled * jnp.mean(weighted * scaled, axis=-1, keepdims=True)
    )


def row_chunk(count, most):
    for chunk in range(most, 0, -16):
        if count % chunk == 0:
            return chunk
    raise ValueError("rows")


def first_norm_kernel(tokens_ref, gain_ref, shift_ref, out_ref):
    scaled, _ = normalize(tokens_ref[...].astype(FULL))
    out_ref[...] = (scaled * gain_ref[...] + shift_ref[...]).astype(LOW)


def second_norm_kernel(tokens_ref, one_ref, two_ref, bias_ref, gain_ref, shift_ref, out_ref):
    mixed = one_ref[...].astype(FULL) + two_ref[...].astype(FULL) + bias_ref[...]
    scaled, _ = normalize(tokens_ref[...].astype(FULL) + mixed)
    out_ref[...] = (scaled * gain_ref[...] + shift_ref[...]).astype(LOW)


def add_sums(ref, rows):
    sums = jnp.concatenate([jnp.sum(row, axis=0, keepdims=True) for row in rows], axis=0)

    @pl.when(pl.program_id(0) == 0)
    def _():
        ref[: len(rows)] = sums

    @pl.when(pl.program_id(0) > 0)
    def _():
        ref[: len(rows)] += sums


def second_norm_back_kernel(
    tokens_ref, one_ref, two_ref, bias_ref, gain_ref, left_ref, right_ref, outer_ref,
    slope_ref, back_ref, sums_ref,
):
    mixed = one_ref[...].astype(FULL) + two_ref[...].astype(FULL) + bias_ref[...]
    scaled, inverse = normalize(tokens_ref[...].astype(FULL) + mixed)
    upstream = left_ref[...].astype(FULL) + right_ref[...].astype(FULL)
    back = norm_back(upstream, gain_ref[...], scaled, inverse)
    slope = (outer_ref[...].astype(FULL) + back).astype(LOW)
    slope_ref[...] = slope
    back_ref[...] = back
    add_sums(sums_ref, [upstream * scaled, upstream, slope.astype(FULL)])


def first_norm_back_kernel(
    tokens_ref, upstream_ref, gain_ref, outer_ref, back_ref, out_ref, sums_ref
):
    scaled, inverse = normalize(tokens_ref[...].astype(FULL))
    upstream = upstream_ref[...].astype(FULL)
    back = norm_back(upstream, gain_ref[...], scaled, inverse)
    out_ref[...] = outer_ref[...].astype(FULL) + back_ref[...] + back
    add_sums(sums_ref, [upstream * scaled, upstream])


def by_rows(kernel, name, out_types, sums, *values):
    count, width = values[0].shape
    chunk = row_chunk(count, 112)
    part = pl.BlockSpec((chunk, width), lambda i: (i, 0))
    in_specs = [
        part if value.shape[0] == count else pl.BlockSpec((1, width), lambda i: (0, 0))
        for value in values
    ]
    out_specs = [part for _ in out_types]
    out_shape = [jax.ShapeDtypeStruct((count, width), kind) for kind in out_types]
    if sums:
        out_specs.append(pl.BlockSpec((8, width), lambda i: (0, 0)))
        out_shape.append(jax.ShapeDtypeStruct((8, width), FULL))
    return pl.pallas_call(
        kernel,
        grid=(count // chunk,),
        in_specs=in_specs,
        out_specs=out_specs,
        out_shape=out_shape,
        compiler_params=pltpu.CompilerParams(vmem_limit_bytes=16 << 20),
        name=name,
    )(*values)


def joint_kernel(mine_ref, other_ref, weight_ref, bias_ref, out_ref):
    half = mine_ref.shape[1]
    out = product(mine_ref[...], weight_ref[:half], PLAIN)
    out += product(other_ref[...], weight_ref[half:], PLAIN)
    out_ref[...] = (out + bias_ref[...]).astype(LOW)


def joint_projection(mine, other, weight, bias):
    count, half = mine.shape
    columns = weight.shape[1]
    chunk = row_chunk(count, 784)
    part = pl.BlockSpec((chunk, half), lambda i: (i, 0))
    return pl.pallas_call(
        joint_kernel,
        grid=(count // chunk,),
        in_specs=[
            part,
            part,
            pl.BlockSpec(weight.shape, lambda i: (0, 0)),
            pl.BlockSpec((1, columns), lambda i: (0, 0)),
        ],
        out_specs=pl.BlockSpec((chunk, columns), lambda i: (i, 0)),
        out_shape=jax.ShapeDtypeStruct((count, columns), LOW),
        compiler_params=pltpu.CompilerParams(vmem_limit_bytes=40 << 20),
        name="joint_projection",
    )(mine, other, weight, bias)


def rows_kernel(left_ref, right_ref, out_ref):
    out_ref[...] = product(left_ref[...], right_ref[...], ROW_BY_ROW).astype(LOW)


def rows_product(left, right, name):
    count, depth = left.shape
    columns = right.shape[0]
    chunk = row_chunk(count, 400)
    return pl.pallas_call(
        rows_kernel,
        grid=(count // chunk,),
        in_specs=[
            pl.BlockSpec((chunk, depth), lambda i: (i, 0)),
            pl.BlockSpec((columns, depth), lambda i: (0, 0)),
        ],
        out_specs=pl.BlockSpec((chunk, columns), lambda i: (i, 0)),
        out_shape=jax.ShapeDtypeStruct((count, columns), LOW),
        compiler_params=pltpu.CompilerParams(vmem_limit_bytes=48 << 20),
        name=name,
    )(left, right)


def grad_kernel(distances, place_ref, *refs):
    lefts, (right_ref, out_ref) = refs[:-2], refs[-2:]
    left = lefts[0][...]
    if len(lefts) == 2:
        slot = place_ref[0] ^ distance_at(distances, pl.program_id(0))
        left = jnp.where((slot >> 1) == 0, left, lefts[1][...])
    out_ref[0] = product(left, right_ref[...], COLUMN_BY_COLUMN).astype(LOW)


def distance_at(distances, step):
    if len(distances) == 1:
        return distances[0]
    return distances[0] + step * (distances[1] - distances[0])


def grad_products(lefts, right, place, distances, name):
    tokens_here, columns = right.shape
    quarter = sum(left.shape[1] for left in lefts) // 4
    blocks = lefts[0].shape[1] // quarter

    def left_at(i, place):
        return (0, (place[0] ^ distance_at(distances, i)) & (blocks - 1))

    return pl.pallas_call(
        lambda *refs: grad_kernel(distances, *refs),
        grid_spec=pltpu.PrefetchScalarGridSpec(
            num_scalar_prefetch=1,
            grid=(len(distances),),
            in_specs=[pl.BlockSpec((tokens_here, quarter), left_at) for _ in lefts]
            + [pl.BlockSpec((tokens_here, columns), lambda i, place: (0, 0))],
            out_specs=pl.BlockSpec((1, quarter, columns), lambda i, place: (i, 0, 0)),
        ),
        out_shape=jax.ShapeDtypeStruct((len(distances), quarter, columns), LOW),
        compiler_params=pltpu.CompilerParams(vmem_limit_bytes=48 << 20),
        name=name,
    )(place.astype(jnp.int32).reshape(1), *lefts, right)


def attention_forward_kernel(q_ref, k_ref, v_ref, o_ref, lse_ref):
    count, width = q_ref.shape
    rows = row_chunk(count, 256)
    lane = lax.broadcasted_iota(jnp.int32, (rows, width), 1)
    k = k_ref[...]
    v = v_ref[...]
    units = [(start, head) for start in range(0, count, rows) for head in range(width // HEAD_DIM)]

    def scores_of(unit):
        start, head = unit
        q = q_ref[start : start + rows] * jnp.asarray(HEAD_DIM ** (-0.5), LOW)
        return product(jnp.where((lane // HEAD_DIM) == head, q, jnp.zeros_like(q)), k, ROW_BY_ROW)

    logs = []
    ahead = scores_of(units[0])
    for step, (start, head) in enumerate(units):
        scores = ahead
        if step + 1 < len(units):
            ahead = scores_of(units[step + 1])
        top = jnp.max(scores, axis=-1, keepdims=True)
        weights = jnp.exp(scores - top)
        total = jnp.sum(weights, axis=-1, keepdims=True)
        part = product(weights.astype(LOW), v, PLAIN) / total
        if head == 0:
            out = part
            logs.append(jnp.zeros((rows, width), FULL))
        else:
            out = jnp.where((lane // HEAD_DIM) == head, part, out)
            o_ref[start : start + rows] = out.astype(LOW)
        logs[-1] = jnp.where(lane == head, top + jnp.log(total), logs[-1])
    lse_ref[...] = jnp.concatenate(logs, axis=0).T[: lse_ref.shape[0]]


def attention_forward(joint, pair):
    count, columns = joint.shape
    width = 2 * HEAD_DIM
    kind = columns // (3 * width)
    return pl.pallas_call(
        attention_forward_kernel,
        grid=(1,),
        in_specs=[
            pl.BlockSpec((count, width), lambda i: (0, pair)),
            pl.BlockSpec((count, width), lambda i: (0, kind + pair)),
            pl.BlockSpec((count, width), lambda i: (0, 2 * kind + pair)),
        ],
        out_specs=[
            pl.BlockSpec((count, width), lambda i: (0, 0)),
            pl.BlockSpec((8, count), lambda i: (0, 0)),
        ],
        out_shape=[
            jax.ShapeDtypeStruct((count, width), LOW),
            jax.ShapeDtypeStruct((8, count), FULL),
        ],
        compiler_params=pltpu.CompilerParams(vmem_limit_bytes=48 << 20),
        name="attention_forward",
    )(joint, joint, joint)


def attention_backward_kernel(
    q_ref, k_ref, v_ref, da_ref, o_ref, lse_ref, dq_ref, dk_ref, dv_ref,
    q_heads, da_heads, delta_ref, dq_total,
):
    count, width = q_ref.shape
    rows = row_chunk(count, 256)
    heads = width // HEAD_DIM
    scale = jnp.asarray(HEAD_DIM ** (-0.5), LOW)

    lane = lax.broadcasted_iota(jnp.int32, (count, width), 1)
    delta = jnp.zeros((count, width), FULL)
    q = q_ref[...] * scale
    da = da_ref[...]
    both_rows = da.astype(FULL) * o_ref[...].astype(FULL)
    for head in range(heads):
        mask = (lane // HEAD_DIM) == head
        q_heads[head] = jnp.where(mask, q, jnp.zeros_like(q))
        da_heads[head] = jnp.where(mask, da, jnp.zeros_like(da))
        row = jnp.sum(jnp.where(mask, both_rows, 0.0), axis=-1, keepdims=True)
        delta = jnp.where(lane == head, row, delta)
    delta_ref[...] = delta.T[:8]
    dq_total[...] = jnp.zeros_like(dq_total)

    lane = lax.broadcasted_iota(jnp.int32, (rows, width), 1)
    for start in range(0, count, rows):
        k = k_ref[start : start + rows]
        v = v_ref[start : start + rows]
        scaled_k = k * scale
        dk = dv = None
        for head in range(heads):
            q = q_heads[head]
            da = da_heads[head]
            probs = jnp.exp(product(k, q, ROW_BY_ROW) - lse_ref[head : head + 1, :])
            slope = probs * (product(v, da, ROW_BY_ROW) - delta_ref[head : head + 1, :])
            slope = slope.astype(LOW)
            dv_part = product(probs.astype(LOW), da, PLAIN)
            dk_part = product(slope, q, PLAIN)
            dv = dv_part if dv is None else dv + dv_part
            dk = dk_part if dk is None else dk + dk_part
            one_k = jnp.where((lane // HEAD_DIM) == head, scaled_k, jnp.zeros_like(k))
            dq_total[...] += product(slope, one_k, COLUMN_BY_COLUMN)
        dk_ref[start : start + rows] = dk.astype(LOW)
        dv_ref[start : start + rows] = dv.astype(LOW)
    dq_ref[...] = dq_total[...].astype(LOW)


def attention_backward(joint, da, out, lse, pair):
    count, columns = joint.shape
    width = 2 * HEAD_DIM
    kind = columns // (3 * width)
    alone = pl.BlockSpec((count, width), lambda i: (0, 0))
    grad = jax.ShapeDtypeStruct((count, width), LOW)
    return pl.pallas_call(
        attention_backward_kernel,
        grid=(1,),
        in_specs=[
            pl.BlockSpec((count, width), lambda i: (0, pair)),
            pl.BlockSpec((count, width), lambda i: (0, kind + pair)),
            pl.BlockSpec((count, width), lambda i: (0, 2 * kind + pair)),
            alone,
            alone,
            pl.BlockSpec((8, count), lambda i: (0, 0)),
        ],
        out_specs=[alone, alone, alone],
        out_shape=[grad, grad, grad],
        scratch_shapes=[
            pltpu.VMEM((2, count, width), LOW),
            pltpu.VMEM((2, count, width), LOW),
            pltpu.VMEM((8, count), FULL),
            pltpu.VMEM((count, width), FULL),
        ],
        compiler_params=pltpu.CompilerParams(vmem_limit_bytes=48 << 20),
        name="attention_backward",
    )(joint, joint, joint, da, out, lse)


def put_together(place_ref, whole_ref, piece_refs):
    for piece, piece_ref in enumerate(piece_refs):
        rows = piece_ref.shape[0]
        start = pl.multiple_of(place_ref[piece], rows)
        whole_ref[pl.ds(start, rows), :] = piece_ref[...]


def feed_forward_kernel(pieces, place_ref, normed_ref, slope_ref, bias_ref, *refs):
    active_ref, expand_slope_ref, back_ref, bias_grad_ref = refs[2 * pieces : 2 * pieces + 4]
    total, expand_ref, reduce_ref = refs[2 * pieces + 4 :]
    put_together(place_ref, expand_ref, refs[:pieces])
    put_together(place_ref, reduce_ref, refs[pieces : 2 * pieces])
    step = pl.program_id(0)
    count = normed_ref.shape[0]
    half = count // 2
    bias_grad = None
    for rows in (slice(0, half), slice(half, count)):
        hidden = product(normed_ref[rows], expand_ref[...], PLAIN) + bias_ref[...]
        upstream = product(slope_ref[rows], reduce_ref[...], PLAIN)
        share = 0.5 * (1.0 + lax.erf(hidden * (0.5**0.5)))
        active_ref[rows] = (hidden * share).astype(LOW)
        density = jnp.exp(-0.5 * hidden * hidden) * 0.3989422804014327
        slope = (upstream * (share + hidden * density)).astype(LOW)
        expand_slope_ref[rows] = slope
        part = jnp.sum(slope.astype(FULL), axis=0, keepdims=True)
        bias_grad = part if bias_grad is None else bias_grad + part
        back = product(slope, expand_ref[...], ROW_BY_ROW)

        @pl.when(step == 0)
        def _():
            total[rows] = back

        @pl.when(step > 0)
        def _():
            total[rows] += back

    bias_grad_ref[...] = bias_grad

    @pl.when(step == pl.num_programs(0) - 1)
    def _():
        back_ref[...] = total[...].astype(LOW)


def feed_forward(normed, slope, bias, expand, reduce, place):
    count, width = normed.shape
    hidden = bias.shape[1]
    block = 512 if hidden % 512 == 0 else hidden
    whole = pl.BlockSpec((count, width), lambda i, place: (0, 0))
    out = pl.BlockSpec((count, block), lambda i, place: (0, i))
    row = pl.BlockSpec((1, block), lambda i, place: (0, i))
    return pl.pallas_call(
        lambda *refs: feed_forward_kernel(len(reduce), *refs),
        grid_spec=pltpu.PrefetchScalarGridSpec(
            num_scalar_prefetch=1,
            grid=(hidden // block,),
            in_specs=[whole, whole, row]
            + [
                pl.BlockSpec((piece.shape[0], block), lambda i, place: (0, i))
                for piece in [*expand, *reduce]
            ],
            out_specs=[out, out, whole, row],
            scratch_shapes=[
                pltpu.VMEM((count, width), FULL),
                pltpu.VMEM((width, block), LOW),
                pltpu.VMEM((width, block), LOW),
            ],
        ),
        out_shape=[
            jax.ShapeDtypeStruct((count, hidden), LOW),
            jax.ShapeDtypeStruct((count, hidden), LOW),
            jax.ShapeDtypeStruct((count, width), LOW),
            jax.ShapeDtypeStruct((1, hidden), FULL),
        ],
        compiler_params=pltpu.CompilerParams(vmem_limit_bytes=44 << 20),
        name="feed_forward",
    )(place, normed, slope, bias, *expand, *reduce)


def reduce_kernel(place_ref, active_ref, *refs):
    out_ref, total, reduce_ref = refs[-3:]
    put_together(place_ref, reduce_ref, refs[:-3])
    part = product(active_ref[...], reduce_ref[...], ROW_BY_ROW)

    @pl.when(pl.program_id(0) == 0)
    def _():
        total[...] = part

    @pl.when(pl.program_id(0) > 0)
    def _():
        total[...] += part

    @pl.when(pl.program_id(0) == pl.num_programs(0) - 1)
    def _():
        out_ref[...] = total[...].astype(LOW)


def reduce_output(active, reduce, place):
    count, hidden = active.shape
    width = sum(piece.shape[0] for piece in reduce)
    block = 512 if hidden % 512 == 0 else hidden
    return pl.pallas_call(
        reduce_kernel,
        grid_spec=pltpu.PrefetchScalarGridSpec(
            num_scalar_prefetch=1,
            grid=(hidden // block,),
            in_specs=[pl.BlockSpec((count, block), lambda i, place: (0, i))]
            + [
                pl.BlockSpec((piece.shape[0], block), lambda i, place: (0, i)) for piece in reduce
            ],
            out_specs=pl.BlockSpec((count, width), lambda i, place: (0, 0)),
            scratch_shapes=[pltpu.VMEM((count, width), FULL), pltpu.VMEM((width, block), LOW)],
        ),
        out_shape=jax.ShapeDtypeStruct((count, width), LOW),
        compiler_params=pltpu.CompilerParams(vmem_limit_bytes=32 << 20),
        name="reduce_output",
    )(place, active, *reduce)


def swap(value, axis, distance):
    size = lax.axis_size(axis)
    return lax.ppermute(value, axis, [(i, i ^ distance) for i in range(size)])


def fence(*values):
    return lax.optimization_barrier(values)


def gather_near(rows_here):
    if lax.axis_size("fsdp") != 4:
        return (lax.all_gather(rows_here, "fsdp", axis=0, tiled=True),)
    return (rows_here, swap(rows_here, "fsdp", 1), swap(rows_here, "fsdp", 2))


def gather_far(held):
    if len(held) == 1:
        return held
    rows_here, near, side = held
    half = rows_here.shape[0] // 2
    return held + (swap(side[:half], "fsdp", 1), swap(near[half:], "fsdp", 2))


def place_near(held):
    if len(held) == 1:
        return held[0]
    rows_here, near, side = held[:3]
    me = lax.axis_index("fsdp")
    count, width = rows_here.shape
    out = jnp.zeros((4 * count, width), rows_here.dtype)
    out = lax.dynamic_update_slice(out, rows_here, (me * count, 0))
    out = lax.dynamic_update_slice(out, near, ((me ^ 1) * count, 0))
    return lax.dynamic_update_slice(out, side, ((me ^ 2) * count, 0))


def place_far(out, held):
    if len(held) == 1:
        return out
    far_top, far_low = held[3:]
    half = far_top.shape[0]
    start = (lax.axis_index("fsdp") ^ 3) * 2 * half
    out = lax.dynamic_update_slice(out, far_top, (start, 0))
    return lax.dynamic_update_slice(out, far_low, (start + half, 0))


def far_halves(far):
    half = far.shape[0] // 2
    return (swap(far[:half], "fsdp", 1), swap(far[half:], "fsdp", 2))


def add_far(near, side, far):
    half = near.shape[0] // 2
    near = jnp.concatenate([near[:half], both((near[half:], far[1])).astype(LOW)], axis=0)
    side = jnp.concatenate([both((side[:half], far[0])).astype(LOW), side[half:]], axis=0)
    return (near, side)


def near_rows_out(pair):
    return (swap(pair[0], "fsdp", 1), swap(pair[1], "fsdp", 2))


def halves(value, bit):
    half = value.shape[0] // 2
    keep = lax.dynamic_slice_in_dim(value, bit * half, half, 0)
    send = lax.dynamic_slice_in_dim(value, (1 - bit) * half, half, 0)
    return keep, send.astype(LOW)


def split_rows(value, bit, distance):
    keep, send = halves(value, bit)
    return keep, swap(send, "ctx", distance)


def both(pair):
    return pair[0].astype(FULL) + pair[1].astype(FULL)


def join_rows(value, bit, distance):
    other = swap(value, "ctx", distance)
    return jnp.where(
        bit == 0,
        jnp.concatenate([value, other], axis=0),
        jnp.concatenate([other, value], axis=0),
    )


def pairwise(pieces):
    return (pieces[0] + pieces[1]) + (pieces[2] + pieces[3])


def swapped_if(bit, pair):
    return [jnp.where(bit == 0, pair[0], pair[1]), jnp.where(bit == 0, pair[1], pair[0])]


def per_device(
    tokens,
    clip_mask,
    cotangent,
    first_gain,
    first_shift,
    joint_weight,
    joint_bias,
    mixer_weight,
    mixer_bias,
    second_gain,
    second_shift,
    expand_weight,
    expand_bias,
    reduce_weight,
    reduce_bias,
):
    clips_here, rows_here, width = tokens.shape
    if lax.axis_size("ctx") != 4 or lax.axis_size("tp") != 2 or clips_here != 2:
        raise ValueError("mesh")
    shard = lax.axis_index("fsdp")
    block = lax.axis_index("ctx")
    core = lax.axis_index("tp")
    clip_at = block >> 1
    part_at = block & 1
    width_half = width // 2
    quarter = width_half // 2
    features = joint_weight.shape[2]
    part_width = features // 2
    pair_width = 2 * HEAD_DIM
    tokens_here = clips_here * rows_here

    flat_tokens = tokens.reshape(tokens_here, width)
    (first_normed,) = by_rows(
        first_norm_kernel, "first_norm", [LOW], False,
        flat_tokens, first_gain[None], first_shift[None],
    )
    first_normed = first_normed.reshape(clips_here, rows_here, width)
    mine = lax.dynamic_slice_in_dim(first_normed, core * width_half, width_half, 2)
    other_side = lax.dynamic_slice_in_dim(first_normed, (1 - core) * width_half, width_half, 2)
    own_clip = lax.dynamic_index_in_dim(mine, clip_at, 0, False)
    own_other = lax.dynamic_index_in_dim(other_side, clip_at, 0, False)
    other_clip = lax.dynamic_index_in_dim(mine, 1 - clip_at, 0, False)
    joint_part = lax.dynamic_slice_in_dim(joint_weight, part_at * part_width, part_width, 2)
    both_parts = jnp.concatenate([joint_part[:, kind] for kind in range(3)] + [mixer_weight], axis=1)

    own_clip, left, right, both_parts = fence(
        own_clip, other_clip[:, :quarter], other_clip[:, quarter:], both_parts
    )
    near_rows = swap(own_clip, "ctx", 1)
    across_left = swap(left, "ctx", 2)
    far_right = swap(right, "ctx", 3)
    held = gather_near(both_parts)

    near_rows, across_left, far_right, held, expand_weight = fence(
        near_rows, across_left, far_right, held, expand_weight
    )
    passed = swap(jnp.concatenate([across_left, far_right], axis=1), "ctx", 1)
    held = gather_far(held)
    expand_held = gather_near(expand_weight)

    passed, held = fence(passed, held)
    cross_rows = jnp.concatenate(
        [
            near_rows,
            jnp.concatenate([across_left, passed[:, quarter:]], axis=1),
            jnp.concatenate([passed[:, :quarter], far_right], axis=1),
        ],
        axis=0,
    )
    cross_other = swap(cross_rows, "tp", 1)
    both_full = place_far(place_near(held), held)
    joint_columns = 3 * part_width
    joint_full = jnp.concatenate(
        [
            lax.dynamic_slice(both_full, (start * width_half, 0), (width_half, joint_columns))
            for start in (core, 1 - core)
        ],
        axis=0,
    )

    cross_other, joint_full, both_full, reduce_weight = fence(
        cross_other, joint_full, both_full, reduce_weight
    )
    mixer_full = both_full[:, joint_columns:]
    reduce_held = gather_near(reduce_weight)
    normed_mine = jnp.concatenate([own_clip, cross_rows], axis=0)
    normed_other = jnp.concatenate([own_other, cross_other], axis=0)
    bias_part = lax.dynamic_slice_in_dim(joint_bias, part_at * part_width, part_width, 1)
    bias_row = jnp.concatenate([bias_part[0], jnp.zeros_like(bias_part[0]), bias_part[1]])
    joint_out = joint_projection(normed_mine, normed_other, joint_full, bias_row[None])
    out_first, log_first = attention_forward(joint_out, 0)

    out_first, joint_out, mixer_full, expand_held = fence(
        out_first, joint_out, mixer_full, expand_held
    )
    first_blocks = out_first.reshape(4, rows_here, pair_width)
    arrived_first = [swap(first_blocks[d], "ctx", d) for d in (1, 2, 3)]
    out_second, log_second = attention_forward(joint_out, 1)

    out_second, arrived_first, reduce_held, expand_held = fence(
        out_second, arrived_first, reduce_held, expand_held
    )
    second_blocks = out_second.reshape(4, rows_here, pair_width)
    arrived_second = [swap(second_blocks[d], "ctx", d) for d in (1, 2, 3)]
    expand_held = gather_far(expand_held)

    arrived_second, expand_held, reduce_held, log_first, log_second = fence(
        arrived_second, expand_held, reduce_held, log_first, log_second
    )
    reduce_held = gather_far(reduce_held)
    arrived = [jnp.concatenate([first_blocks[0], second_blocks[0]], axis=1)] + [
        jnp.concatenate([one, two], axis=1) for one, two in zip(arrived_first, arrived_second)
    ]
    own_joined = jnp.concatenate(swapped_if(part_at, arrived[:2]), axis=1)
    other_joined = jnp.concatenate(swapped_if(part_at, arrived[2:]), axis=1)
    mixed_in = jnp.concatenate(swapped_if(clip_at, [own_joined, other_joined]), axis=0)
    mixer_part = product(mixed_in, mixer_full, ROW_BY_ROW).astype(LOW)
    mixer_swapped = swap(mixer_part, "tp", 1)
    mixer_row = mixer_bias[None]
    (second_normed,) = by_rows(
        second_norm_kernel, "second_norm", [LOW], False,
        flat_tokens, mixer_part, mixer_swapped, mixer_row, second_gain[None], second_shift[None],
    )
    valid = clip_mask.astype(FULL)[:, None, None]
    reduce_slope = (cotangent.astype(FULL) * valid).astype(LOW).reshape(tokens_here, width)
    reduce_bias_grad = jnp.sum(reduce_slope.astype(FULL), axis=0)

    second_normed, reduce_slope, reduce_held = fence(second_normed, reduce_slope, reduce_held)
    four = lax.axis_size("fsdp") == 4
    start = jnp.zeros((), jnp.int32)
    if four:
        rows = width // 4
        pieces_at = jnp.stack([shard, shard ^ 1, shard ^ 2, shard ^ 3, shard ^ 3]) * rows
        pieces_at = pieces_at.astype(jnp.int32) + jnp.array([0, 0, 0, 0, rows // 2], jnp.int32)
    else:
        pieces_at = start.reshape(1)
    activated, expand_slope, second_part, expand_bias_grad = feed_forward(
        second_normed, reduce_slope, expand_bias[None], expand_held, reduce_held, pieces_at
    )
    expand_bias_grad = expand_bias_grad[0]

    second_swapped = swap(second_part, "tp", 1)
    place, order = (shard, (3, 2, 1, 0)) if four else (start, (0, 1, 2, 3))
    expand_parts = grad_products([second_normed], expand_slope, place, order, "expand_grad")
    second_swapped, expand_parts = fence(second_swapped, expand_parts)
    expand_far = far_halves(expand_parts[0]) if four else ()
    mixer_slope, first_sum_back, second_sums = by_rows(
        second_norm_back_kernel, "second_norm_back", [LOW, FULL], True,
        flat_tokens, mixer_part, mixer_swapped, mixer_row, second_gain[None],
        second_part, second_swapped, reduce_slope,
    )
    attended_slope = product(mixer_slope, mixer_full, PLAIN).astype(LOW)

    leaving = []
    for pair in range(2):
        for distance in range(4):
            to = block ^ distance
            corner = ((to >> 1) * rows_here, (to & 1) * part_width + pair * pair_width)
            leaving.append(lax.dynamic_slice(attended_slope, corner, (rows_here, pair_width)))
    leaving, mixer_slope, mixed_in, activated, expand_far = fence(
        leaving, mixer_slope, mixed_in, activated, expand_far
    )
    slope_first = [leaving[0]] + [swap(leaving[d], "ctx", d) for d in (1, 2, 3)]
    expand_near = add_far(expand_parts[2], expand_parts[1], expand_far) if four else ()
    reduce_parts = grad_products([reduce_slope], activated, place, order, "reduce_grad")
    mixer_parts = grad_products([mixer_slope], mixed_in, place, order, "mixer_grad")
    wide = jnp.concatenate([reduce_parts, mixer_parts], axis=2)

    slope_first, leaving, wide, expand_near = fence(slope_first, leaving, wide, expand_near)
    half = width // 8
    slope_second = [leaving[4]] + [swap(leaving[4 + d], "ctx", d) for d in (1, 2, 3)]
    if four:
        expand_near = near_rows_out(expand_near)
    grad_first = attention_backward(
        joint_out, jnp.concatenate(slope_first, axis=0), out_first, log_first, 0
    )

    grad_first, slope_second, expand_near, wide = fence(
        grad_first, slope_second, expand_near, wide
    )
    if four:
        expand_sum = expand_parts[3].astype(FULL) + both(expand_near)
    else:
        expand_sum = lax.psum_scatter(
            expand_parts.reshape(width, -1), "fsdp", scatter_dimension=0, tiled=True
        ).astype(FULL)
    expand_keep, expand_send = halves(expand_sum, part_at)
    expand_send, slope_second = fence(expand_send, slope_second)
    expand_rows = (expand_keep, swap(expand_send, "ctx", 1))
    wide_far = far_halves(wide[0]) if four else ()
    grad_second = attention_backward(
        joint_out, jnp.concatenate(slope_second, axis=0), out_second, log_second, 1
    )

    grad_second, expand_rows, wide_far = fence(grad_second, expand_rows, wide_far)
    expand_rows = split_rows(both(expand_rows), clip_at, 2)
    if four:
        wide_near = near_rows_out(add_far(wide[2], wide[1], wide_far))
    joint_slope = jnp.concatenate(
        [grad[kind] for kind in range(3) for grad in (grad_first, grad_second)], axis=1
    )
    first_there = product(joint_slope, joint_full[width_half:], ROW_BY_ROW).astype(LOW)
    first_here = rows_product(joint_slope, joint_full[:width_half], "first_slope")
    first_half = both((first_here, swap(first_there, "tp", 1))).astype(LOW)

    first_half, joint_slope, expand_rows = fence(first_half, joint_slope, expand_rows)
    expand_rows = both(expand_rows).astype(LOW)
    pieces = first_half.reshape(4, rows_here, width_half)
    passing = jnp.concatenate([pieces[1], pieces[3][:, :quarter], pieces[2][:, quarter:]], axis=1)
    passing = swap(passing, "ctx", 1)
    place = (shard if four else start) ^ (2 * core)
    joint_parts = grad_products([normed_mine, normed_other], joint_slope, place, order, "joint_grad")
    slope_sums = jnp.sum(joint_slope.astype(FULL), axis=0)
    bias_sums = jnp.stack([slope_sums[:part_width], slope_sums[2 * part_width :]])
    joint_bias_grad = lax.dynamic_update_slice(
        jnp.zeros((2, features), FULL), bias_sums, (0, part_at * part_width)
    )

    expand_rows = join_rows(expand_rows, clip_at, 2)

    if not four:
        wide_near = lax.psum_scatter(
            wide.reshape(width, -1), "fsdp", scatter_dimension=0, tiled=True
        )
    passing, joint_parts, expand_rows = fence(passing, joint_parts, expand_rows)
    own_half = both((pieces[0], passing[:, :width_half])).astype(LOW)
    to_left = both((pieces[2][:, :quarter], passing[:, width_half : width_half + quarter]))
    to_right = both((pieces[3][:, quarter:], passing[:, width_half + quarter :]))
    to_left, to_right, own_half, joint_parts, activated = fence(
        to_left.astype(LOW), to_right.astype(LOW), own_half, joint_parts, activated
    )
    other_half = jnp.concatenate(
        [swap(to_left, "ctx", 2), swap(to_right, "ctx", 3)], axis=1
    )
    joint_leaves, wide_near = fence(joint_parts[0], wide_near)
    joint_far = far_halves(joint_leaves) if four else ()
    reduce_part = reduce_output(activated, reduce_held, pieces_at)

    other_half, joint_far, wide_near, reduce_part, expand_rows = fence(
        other_half, joint_far, wide_near, reduce_part, expand_rows
    )
    reduce_swapped = swap(reduce_part, "tp", 1)
    wide_sum = wide[3].astype(FULL) + both(wide_near) if four else wide_near.astype(FULL)
    wide_rows = split_rows(wide_sum, part_at, 1)
    slope_half = jnp.concatenate(
        swapped_if(clip_at, [own_half, other_half]), axis=0
    )
    slope_other = swap(slope_half, "tp", 1)
    first_slope = jnp.concatenate(swapped_if(core, [slope_half, slope_other]), axis=1)
    tokens_grad, first_sums = by_rows(
        first_norm_back_kernel, "first_norm_back", [FULL], True,
        flat_tokens, first_slope, first_gain[None],
        cotangent.reshape(tokens_here, width), first_sum_back,
    )
    if four:
        joint_near = near_rows_out(add_far(joint_parts[2], joint_parts[1], joint_far))
    else:
        joint_near = lax.psum_scatter(
            joint_parts.reshape(width, -1), "fsdp", scatter_dimension=0, tiled=True
        )

    first_sums, tokens_grad, joint_near, wide_rows, reduce_swapped = fence(
        first_sums, tokens_grad, joint_near, wide_rows, reduce_swapped
    )
    vectors = [
        first_sums[0],
        first_sums[1],
        joint_bias_grad[0],
        joint_bias_grad[1],
        second_sums[2],
        second_sums[0],
        second_sums[1],
        expand_bias_grad,
        reduce_bias_grad,
    ]
    packed = jnp.concatenate(vectors).reshape(-1, 128)
    packed_pieces = [packed] + [swap(packed, "ctx", d) for d in (1, 2, 3)]
    joint_sum = joint_parts[3].astype(FULL) + both(joint_near) if four else joint_near
    joint_sum = joint_sum.astype(LOW)
    joint_sum = (joint_sum, swap(joint_sum, "ctx", 2))
    wide_rows = split_rows(both(wide_rows), clip_at, 2)
    reduce_out = both((reduce_part, reduce_swapped)) + reduce_bias
    mixer_out = both((mixer_part, mixer_swapped)) + mixer_bias
    branches = (mixer_out + reduce_out).reshape(clips_here, rows_here, width)
    result = (tokens.astype(FULL) + valid * branches).astype(LOW)

    packed_pieces, joint_sum, wide_rows, result = fence(
        packed_pieces, joint_sum, wide_rows, result
    )
    packed = pairwise(packed_pieces)
    if four:
        packed = pairwise([packed] + [swap(packed, "fsdp", d) for d in (1, 2, 3)])
    else:
        packed = lax.psum(packed, "fsdp")
    joint_sum = both(joint_sum).astype(LOW)
    joint_parts = swapped_if(part_at, [joint_sum, swap(joint_sum, "ctx", 1)])
    joint_grad = jnp.concatenate(
        [piece.reshape(-1, 3, part_width) for piece in joint_parts], axis=2
    ).astype(FULL)
    wide_rows = join_rows(both(wide_rows).astype(LOW), clip_at, 2)
    wide_rows = join_rows(wide_rows, part_at, 1).astype(FULL)
    reduce_grad = wide_rows[:, : activated.shape[1]]
    mixer_grad = wide_rows[:, activated.shape[1] :]
    expand_grad = join_rows(expand_rows, part_at, 1).astype(FULL)
    packed = packed.reshape(-1)
    shares = []
    start = 0
    for vector in vectors:
        share = vector.shape[0] // lax.axis_size("fsdp")
        shares.append(lax.dynamic_slice_in_dim(packed, start + shard * share, share, 0))
        start += vector.shape[0]

    shape = (clips_here, rows_here, width)
    return (
        result,
        tokens_grad.reshape(shape),
        shares[0],
        shares[1],
        joint_grad,
        jnp.stack([shares[2], shares[3]]),
        mixer_grad,
        shares[4],
        shares[5],
        shares[6],
        expand_grad,
        shares[7],
        reduce_grad,
        shares[8],
    )


def solution(mesh):
    return jax.shard_map(
        per_device,
        mesh=mesh,
        in_specs=(
            P("fsdp", "ctx", None),
            P("fsdp"),
            P("fsdp", "ctx", None),
            P(),
            P(),
            P("fsdp", None, "tp"),
            P(None, "tp"),
            P("fsdp", "tp"),
            P(),
            P(),
            P(),
            P("fsdp", "tp"),
            P("tp"),
            P("fsdp", "tp"),
            P(),
        ),
        out_specs=(
            P("fsdp", "ctx", None),
            P("fsdp", "ctx", None),
            P("fsdp"),
            P("fsdp"),
            P("fsdp", None, "tp"),
            P(None, ("tp", "fsdp")),
            P("fsdp", "tp"),
            P("fsdp"),
            P("fsdp"),
            P("fsdp"),
            P("fsdp", "tp"),
            P(("tp", "fsdp")),
            P("fsdp", "tp"),
            P("fsdp"),
        ),
        check_vma=False,
    )
```

profile of v0, /device:TPU:0, one launch (start us, length us, event | category | flops | bytes accessed | tf_op | source)
XLA Modules:
  0.0 417.8 jit_solution(7599404667437677842)
XLA Ops:
  7.8 3.0 collective-permute-start.3
  16.7 11.3 %collective-permute-done.1 = bf16[392,256]{1,0:T(8,128)(2,1)S(1)} collective-permute-done((bf16[392,256]{1,0:T(8,128)(2,1)S(1)}, bf16[392,256]{1,0:T(8,128)(2,1)S(1)}, u32[]{:S(2)}, u32[]{:S(2)}) %collective-permute-start.1) | collective-permute-done | bytes 200736 | tf_op jit(solution)/shard_map/ppermute | solution.py:457
  28.0 5.5 %collective-permute-done.2 = bf16[392,256]{1,0:T(8,128)(2,1)S(1)} collective-permute-done((bf16[392,256]{1,0:T(8,128)(2,1)S(1)}, bf16[392,256]{1,0:T(8,128)(2,1)S(1)}, u32[]{:S(2)}, u32[]{:S(2)}) %collective-permute-start.2) | collective-permute-done | bytes 200736 | tf_op jit(solution)/shard_map/ppermute | solution.py:457
  40.6 6.2 %collective-permute-done.6 = bf16[128,1280]{1,0:T(8,128)(2,1)} collective-permute-done((bf16[128,1280]{1,0:T(8,128)(2,1)}, bf16[128,1280]{1,0:T(8,128)(2,1)}, u32[]{:S(2)}, u32[]{:S(2)}) %collective-permute-start.6) | collective-permute-done | bytes 327712 | tf_op jit(solution)/shard_map/ppermute | solution.py:457
  56.5 3.1 joint_projection.1.q_ref.k_ref.v_ref
  60.8 7.2 %attention_forward.2 = (bf16[1568,128]{1,0:T(8,128)(2,1)S(1)}, f32[8,1568]{1,0:T(8,128)S(1)}) custom-call(bf16[1568,768]{1,0:T(8,128)(2,1)S(1)} %joint_projection.1.q_ref.k_ref.v_ref, bf16[1568,768]{1,0:T(8,128)(2,1)S(1)} %joint_projection.1.q_ref.k_ref.v_ref, bf16[1568,768]{1,0:T(8,128)(2,1)S(1)} %joint_projection.1.q_ref.k_ref.v_ref), custom_call_target="tpu_custom_call" | custom-call | tf_op jit(solution)/shard_map/attention_forward/pallas_call | solution.py:240
  75.6 7.7 %attention_forward.3 = (bf16[1568,128]{1,0:T(8,128)(2,1)S(1)}, f32[8,1568]{1,0:T(8,128)S(1)}) custom-call(bf16[1568,768]{1,0:T(8,128)(2,1)S(1)} %joint_projection.1.q_ref.k_ref.v_ref, bf16[1568,768]{1,0:T(8,128)(2,1)S(1)} %joint_projection.1.q_ref.k_ref.v_ref, bf16[1568,768]{1,0:T(8,128)(2,1)S(1)} %joint_projection.1.q_ref.k_ref.v_ref), custom_call_target="tpu_custom_call" | custom-call | tf_op jit(solution)/shard_map/attention_forward/pallas_call | solution.py:240
  83.4 4.9 %collective-permute-done.14.refs_10_.refs_1_ = bf16[256,2048]{1,0:T(8,128)(2,1)S(1)} collective-permute-done((bf16[256,2048]{1,0:T(8,128)(2,1)S(1)}, bf16[256,2048]{1,0:T(8,128)(2,1)S(1)}, u32[]{:S(2)}, u32[]{:S(2)}) %collective-permute-start.14) | collective-permute-done | bytes 1048608 | tf_op jit(solution)/shard_map/ppermute | solution.py:457
  100.7 2.8 collective-permute-done.17
  111.7 5.6 %second_norm.1.refs_1_ = bf16[784,1024]{1,0:T(8,128)(2,1)S(1)} custom-call(bf16[784,1024]{1,0:T(8,128)(2,1)S(1)} %bitcast.104, bf16[784,1024]{1,0:T(8,128)(2,1)} %convolution_convert_fusion.1.one_ref, bf16[784,1024]{1,0:T(8,128)(2,1)} %collective-permute-done.21.two_ref, f32[1,1024]{1,0:T(1,128)S(1)} %bitcast.112, f32[1,1024]{1,0:T(1,128)S(1)} %bitcast.116, ...), custom_call_target="tpu_custom_call" | custom-call | tf_op jit(solution)/shard_map/second_norm/pallas_call | solution.py:104
  118.4 3.5 collective-permute-done.22.refs_12_.refs_3_
  122.3 18.2 %feed_forward.1 = (bf16[784,2048]{1,0:T(8,128)(2,1)}, bf16[784,2048]{1,0:T(8,128)(2,1)}, bf16[784,1024]{1,0:T(8,128)(2,1)}, f32[1,2048]{1,0:T(1,128)S(1)}) custom-call(s32[5]{0:T(128)S(1)} %multiply_add_fusion.refs_0_.place_ref, bf16[784,1024]{1,0:T(8,128)(2,1)} %copy-done.6, bf16[784,1024]{1,0:T(8,128)(2,1)} %bitcast.107, f32[1,2048]{1,0:T(1,128)S(1)} %bitcast.118, ...), custom_call_target="tpu_custom_call" | custom-call | tf_op jit(solution)/shard_map/feed_forward/pallas_call | solution.py:387
  143.9 6.4 %expand_grad.1 = bf16[4,256,2048]{2,1,0:T(8,128)(2,1)} custom-call(s32[1]{0:T(128)} %bitcast.14.refs_0_, bf16[784,1024]{1,0:T(8,128)(2,1)S(1)} %copy-done.7, bf16[784,2048]{1,0:T(8,128)(2,1)S(1)} %copy-done.23), custom_call_target="tpu_custom_call" | custom-call | tf_op jit(solution)/shard_map/expand_grad/pallas_call | solution.py:188
  150.4 2.9 slice_bitcast_fusion.4
  157.2 7.3 %second_norm_back.1 = (bf16[784,1024]{1,0:T(8,128)(2,1)S(1)}, f32[784,1024]{1,0:T(8,128)S(1)}, f32[8,1024]{1,0:T(8,128)S(1)}) custom-call(bf16[784,1024]{1,0:T(8,128)(2,1)S(1)} %bitcast.105, bf16[784,1024]{1,0:T(8,128)(2,1)} %convolution_convert_fusion.1.one_ref, bf16[784,1024]{1,0:T(8,128)(2,1)} %collective-permute-done.21.two_ref, ...), custom_call_target="tpu_custom_call" | custom-call | tf_op jit(solution)/shard_map/second_norm_back/pallas_call | solution.py:104
  168.9 6.4 %reduce_grad.1 = bf16[4,256,2048]{2,1,0:T(8,128)(2,1)} custom-call(s32[1]{0:T(128)} %bitcast.14.refs_0_, bf16[784,1024]{1,0:T(8,128)(2,1)S(1)} %bitcast.109, bf16[784,2048]{1,0:T(8,128)(2,1)S(1)} %copy-done.12), custom_call_target="tpu_custom_call" | custom-call | tf_op jit(solution)/shard_map/reduce_grad/pallas_call | solution.py:188
  185.0 2.7 pad_maximum_fusion
  198.7 15.7 %attention_backward.2 = (bf16[1568,128]{1,0:T(8,128)(2,1)S(1)}, bf16[1568,128]{1,0:T(8,128)(2,1)S(1)}, bf16[1568,128]{1,0:T(8,128)(2,1)S(1)}) custom-call(bf16[1568,768]{1,0:T(8,128)(2,1)S(1)} %joint_projection.1.q_ref.k_ref.v_ref, bf16[1568,768]{1,0:T(8,128)(2,1)S(1)} %joint_projection.1.q_ref.k_ref.v_ref, ...), custom_call_target="tpu_custom_call" | custom-call | tf_op jit(solution)/shard_map/attention_backward/pallas_call | solution.py:313
  221.5 15.9 %attention_backward.3 = (bf16[1568,128]{1,0:T(8,128)(2,1)S(1)}, bf16[1568,128]{1,0:T(8,128)(2,1)S(1)}, bf16[1568,128]{1,0:T(8,128)(2,1)S(1)}) custom-call(bf16[1568,768]{1,0:T(8,128)(2,1)S(1)} %joint_projection.1.q_ref.k_ref.v_ref, bf16[1568,768]{1,0:T(8,128)(2,1)S(1)} %joint_projection.1.q_ref.k_ref.v_ref, ...), custom_call_target="tpu_custom_call" | custom-call | tf_op jit(solution)/shard_map/attention_backward/pallas_call | solution.py:313
  246.8 3.1 first_slope.1
  261.8 5.9 %joint_grad.1 = bf16[4,256,768]{2,1,0:T(8,128)(2,1)S(1)} custom-call(s32[1]{0:T(128)} %bitcast.30.refs_0_, bf16[1568,512]{1,0:T(8,128)(2,1)S(1)} %copy-done.9, bf16[1568,512]{1,0:T(8,128)(2,1)S(1)} %copy-done.11, bf16[1568,768]{1,0:T(8,128)(2,1)} %copy-done.5), custom_call_target="tpu_custom_call" | custom-call | tf_op jit(solution)/shard_map/joint_grad/pallas_call | solution.py:188
  267.7 4.7 %collective-permute-done.41 = bf16[64,2048]{1,0:T(8,128)(2,1)S(1)} collective-permute-done((bf16[64,2048]{1,0:T(8,128)(2,1)S(1)}, bf16[64,2048]{1,0:T(8,128)(2,1)S(1)}, u32[]{:S(2)}, u32[]{:S(2)}) %collective-permute-start.41) | collective-permute-done | bytes 262176 | tf_op jit(solution)/shard_map/ppermute | solution.py:457
  272.6 12.2 %collective-permute-done.40 = bf16[392,1024]{1,0:T(8,128)(2,1)} collective-permute-done((bf16[392,1024]{1,0:T(8,128)(2,1)}, bf16[392,1024]{1,0:T(8,128)(2,1)}, u32[]{:S(2)}, u32[]{:S(2)}) %collective-permute-start.40) | collective-permute-done | bytes 802848 | tf_op jit(solution)/shard_map/ppermute | solution.py:457
  291.5 7.5 %reduce_output.1 = bf16[784,1024]{1,0:T(8,128)(2,1)S(1)} custom-call(s32[5]{0:T(128)S(1)} %multiply_add_fusion.refs_0_.place_ref, bf16[784,2048]{1,0:T(8,128)(2,1)S(1)} %copy-done.13, bf16[256,2048]{1,0:T(8,128)(2,1)S(1)} %copy-done.20, bf16[256,2048]{1,0:T(8,128)(2,1)S(1)} %collective-permute-done.14.refs_10_.refs_1_, ...), custom_call_target="tpu_custom_call" | custom-call | tf_op jit(solution)/shard_map/reduce_output/pallas_call | solution.py:437
  299.0 4.4 %collective-permute-done.42 = bf16[392,256]{1,0:T(8,128)(2,1)S(1)} collective-permute-done((bf16[392,256]{1,0:T(8,128)(2,1)S(1)}, bf16[392,256]{1,0:T(8,128)(2,1)S(1)}, u32[]{:S(2)}, u32[]{:S(2)}) %collective-permute-start.42) | collective-permute-done | bytes 200736 | tf_op jit(solution)/shard_map/ppermute | solution.py:457
  303.4 4.8 %collective-permute-start.64 = (bf16[128,2048]{1,0:T(8,128)(2,1)S(1)}, bf16[128,2048]{1,0:T(8,128)(2,1)S(1)}, u32[]{:S(2)}, u32[]{:S(2)}) collective-permute-start(bf16[128,2048]{1,0:T(8,128)(2,1)S(1)} %maximum_select_fusion.3), channel_id=1, source_target_pairs={{0,2},{2,0},{4,6},{6,4},{1,3},{3,1},{5,7},{7,5},{8,10},{10,8},{12,... | collective-permute-start | bytes 1572872 | tf_op jit(solution)/shard_map/ppermute | solution.py:457
  313.3 7.7 %collective-permute-done.64 = bf16[128,2048]{1,0:T(8,128)(2,1)S(1)} collective-permute-done((bf16[128,2048]{1,0:T(8,128)(2,1)S(1)}, bf16[128,2048]{1,0:T(8,128)(2,1)S(1)}, u32[]{:S(2)}, u32[]{:S(2)}) %collective-permute-start.64) | collective-permute-done | bytes 524320 | tf_op jit(solution)/shard_map/ppermute | solution.py:457
  326.7 5.0 %first_norm_back.1 = (f32[784,1024]{1,0:T(8,128)}, f32[8,1024]{1,0:T(8,128)S(1)}) custom-call(bf16[784,1024]{1,0:T(8,128)(2,1)S(1)} %bitcast.106, bf16[784,1024]{1,0:T(8,128)(2,1)S(1)} %pad_maximum_fusion.2.upstream_ref, f32[1,1024]{1,0:T(1,128)S(1)} %bitcast.115, bf16[784,1024]{1,0:T(8,128)(2,1)S(1)} %bitcast.110, f32[784,1024]{1,0:T(8,128)S(1)} %copy-done.22), custom_call_target="tpu_custom_call" | custom-call | tf_op jit(solution)/shard_map/first_norm_back/pallas_call | solution.py:104
  339.0 3.1 add_add_fusion
  347.4 29.7 %collective-permute-done.57 = bf16[64,2560]{1,0:T(8,128)(2,1)S(1)} collective-permute-done((bf16[64,2560]{1,0:T(8,128)(2,1)S(1)}, bf16[64,2560]{1,0:T(8,128)(2,1)S(1)}, u32[]{:S(2)}, u32[]{:S(2)}) %collective-permute-start.57) | collective-permute-done | bytes 327712 | tf_op jit(solution)/shard_map/ppermute | solution.py:457
  384.7 12.1 %collective-permute-done.62 = bf16[64,2560]{1,0:T(8,128)(2,1)S(1)} collective-permute-done((bf16[64,2560]{1,0:T(8,128)(2,1)S(1)}, bf16[64,2560]{1,0:T(8,128)(2,1)S(1)}, u32[]{:S(2)}, u32[]{:S(2)}) %collective-permute-start.62) | collective-permute-done | bytes 327712 | tf_op jit(solution)/shard_map/ppermute | solution.py:457
  401.1 12.6 %collective-permute-done.63 = bf16[128,2560]{1,0:T(8,128)(2,1)} collective-permute-done((bf16[128,2560]{1,0:T(8,128)(2,1)S(1)}, bf16[128,2560]{1,0:T(8,128)(2,1)}, u32[]{:S(2)}, u32[]{:S(2)}) %collective-permute-start.63) | collective-permute-done | bytes 655392 | tf_op jit(solution)/shard_map/ppermute | solution.py:457
  (398 shorter events, 166.1 us)
Async XLA Ops:
  7.8 25.7 %collective-permute-start.3 = (bf16[256,1280]{1,0:T(8,128)(2,1)S(1)}, bf16[256,1280]{1,0:T(8,128)(2,1)S(1)}, u32[]{:S(2)}, u32[]{:S(2)}) collective-permute-start(bf16[256,1280]{1,0:T(8,128)(2,1)S(1)} %pad_maximum_fusion.11), channel_id=1, source_target_pairs={{0,8},{8,0},{16,24},{24,16},{1,9},{9,1},{17,25},{25,17},{2,10},{10... | collective-permute-start | bytes 1966088 | tf_op jit(solution)/shard_map/ppermute | solution.py:457
  10.8 22.7 %collective-permute-start.4 = (bf16[256,1280]{1,0:T(8,128)(2,1)S(1)}, bf16[256,1280]{1,0:T(8,128)(2,1)S(1)}, u32[]{:S(2)}, u32[]{:S(2)}) collective-permute-start(bf16[256,1280]{1,0:T(8,128)(2,1)S(1)} %pad_maximum_fusion.11), channel_id=1, source_target_pairs={{0,16},{8,24},{16,0},{24,8},{1,17},{9,25},{17,1},{25,9},{2,18},{10... | collective-permute-start | bytes 1966088 | tf_op jit(solution)/shard_map/ppermute | solution.py:457
  12.3 21.2 %collective-permute-start = (bf16[392,512]{1,0:T(8,128)(2,1)S(1)}, bf16[392,512]{1,0:T(8,128)(2,1)S(1)}, u32[]{:S(2)}, u32[]{:S(2)}) collective-permute-start(bf16[392,512]{1,0:T(8,128)(2,1)S(1)} %get-tuple-element.176), channel_id=1, source_target_pairs={{0,2},{2,0},{4,6},{6,4},{1,3},{3,1},{5,7},{7,5},{8,10},{10,8},{12,... | collective-permute-start | bytes 1204232 | tf_op jit(solution)/shard_map/ppermute | solution.py:457
  16.5 17.0 %collective-permute-start.2 = (bf16[392,256]{1,0:T(8,128)(2,1)S(1)}, bf16[392,256]{1,0:T(8,128)(2,1)S(1)}, u32[]{:S(2)}, u32[]{:S(2)}) collective-permute-start(bf16[392,256]{1,0:T(8,128)(2,1)S(1)} %get-tuple-element.178), channel_id=1, source_target_pairs={{0,6},{2,4},{4,2},{6,0},{1,7},{3,5},{5,3},{7,1},{8,14},{10,12},{12... | collective-permute-start | bytes 602120 | tf_op jit(solution)/shard_map/ppermute | solution.py:457
  37.6 32.8 %collective-permute-start.10 = (bf16[256,2048]{1,0:T(8,128)(2,1)}, bf16[256,2048]{1,0:T(8,128)(2,1)S(1)}, u32[]{:S(2)}, u32[]{:S(2)}) collective-permute-start(bf16[256,2048]{1,0:T(8,128)(2,1)} %refs_4_), channel_id=1, source_target_pairs={{0,16},{8,24},{16,0},{24,8},{1,17},{9,25},{17,1},{25,9},{2,18},{10... | collective-permute-start | bytes 3145736 | tf_op jit(solution)/shard_map/ppermute | solution.py:457
  39.1 31.3 %collective-permute-start.9 = (bf16[256,2048]{1,0:T(8,128)(2,1)}, bf16[256,2048]{1,0:T(8,128)(2,1)S(1)}, u32[]{:S(2)}, u32[]{:S(2)}) collective-permute-start(bf16[256,2048]{1,0:T(8,128)(2,1)} %refs_4_), channel_id=1, source_target_pairs={{0,8},{8,0},{16,24},{24,16},{1,9},{9,1},{17,25},{25,17},{2,10},{10... | collective-permute-start | bytes 3145736 | tf_op jit(solution)/shard_map/ppermute | solution.py:457
  53.1 35.2 %collective-permute-start.14 = (bf16[256,2048]{1,0:T(8,128)(2,1)S(1)}, bf16[256,2048]{1,0:T(8,128)(2,1)S(1)}, u32[]{:S(2)}, u32[]{:S(2)}) collective-permute-start(bf16[256,2048]{1,0:T(8,128)(2,1)S(1)} %copy-done.18), channel_id=1, source_target_pairs={{0,8},{8,0},{16,24},{24,16},{1,9},{9,1},{17,25},{25,17},{2,10},{10... | collective-permute-start | bytes 3145736 | tf_op jit(solution)/shard_map/ppermute | solution.py:457
  54.6 34.8 %collective-permute-start.15 = (bf16[256,2048]{1,0:T(8,128)(2,1)S(1)}, bf16[256,2048]{1,0:T(8,128)(2,1)}, u32[]{:S(2)}, u32[]{:S(2)}) collective-permute-start(bf16[256,2048]{1,0:T(8,128)(2,1)S(1)} %copy-done.18), channel_id=1, source_target_pairs={{0,16},{8,24},{16,0},{24,8},{1,17},{9,25},{17,1},{25,9},{2,18},{10... | collective-permute-start | bytes 3145736 | tf_op jit(solution)/shard_map/ppermute | solution.py:457
  153.2 14.9 %collective-permute-start.25 = (bf16[128,2048]{1,0:T(8,128)(2,1)S(1)}, bf16[128,2048]{1,0:T(8,128)(2,1)}, u32[]{:S(2)}, u32[]{:S(2)}) collective-permute-start(bf16[128,2048]{1,0:T(8,128)(2,1)S(1)} %get-tuple-element.365), channel_id=1, source_target_pairs={{0,8},{8,0},{16,24},{24,16},{1,9},{9,1},{17,25},{25,17},{2,10},{10... | collective-permute-start | bytes 1572872 | tf_op jit(solution)/shard_map/ppermute | solution.py:457
  188.8 25.7 %collective-permute-start.33 = (bf16[256,2048]{1,0:T(8,128)(2,1)}, bf16[256,2048]{1,0:T(8,128)(2,1)}, u32[]{:S(2)}, u32[]{:S(2)}) collective-permute-start(bf16[256,2048]{1,0:T(8,128)(2,1)} %pad_maximum_fusion.6), channel_id=1, source_target_pairs={{0,8},{8,0},{16,24},{24,16},{1,9},{9,1},{17,25},{25,17},{2,10},{10... | collective-permute-start | bytes 3145736 | tf_op jit(solution)/shard_map/ppermute | solution.py:457
  189.4 25.1 %collective-permute-start.34 = (bf16[256,2048]{1,0:T(8,128)(2,1)}, bf16[256,2048]{1,0:T(8,128)(2,1)}, u32[]{:S(2)}, u32[]{:S(2)}) collective-permute-start(bf16[256,2048]{1,0:T(8,128)(2,1)} %pad_maximum_fusion.7), channel_id=1, source_target_pairs={{0,16},{8,24},{16,0},{24,8},{1,17},{9,25},{17,1},{25,9},{2,18},{10... | collective-permute-start | bytes 3145736 | tf_op jit(solution)/shard_map/ppermute | solution.py:457
  193.0 21.4 %collective-permute-start.30 = (bf16[392,128]{1,0:T(8,128)(2,1)}, bf16[392,128]{1,0:T(8,128)(2,1)S(1)}, u32[]{:S(2)}, u32[]{:S(2)}) collective-permute-start(bf16[392,128]{1,0:T(8,128)(2,1)} %get-tuple-element.263), channel_id=1, source_target_pairs={{0,2},{2,0},{4,6},{6,4},{1,3},{3,1},{5,7},{7,5},{8,10},{10,8},{12,... | collective-permute-start | bytes 301064 | tf_op jit(solution)/shard_map/ppermute | solution.py:457
  193.8 20.6 %collective-permute-start.31 = (bf16[392,128]{1,0:T(8,128)(2,1)}, bf16[392,128]{1,0:T(8,128)(2,1)S(1)}, u32[]{:S(2)}, u32[]{:S(2)}) collective-permute-start(bf16[392,128]{1,0:T(8,128)(2,1)} %get-tuple-element.264), channel_id=1, source_target_pairs={{0,4},{2,6},{4,0},{6,2},{1,5},{3,7},{5,1},{7,3},{8,12},{10,14},{12... | collective-permute-start | bytes 301064 | tf_op jit(solution)/shard_map/ppermute | solution.py:457
  195.4 19.0 %collective-permute-start.32 = (bf16[392,128]{1,0:T(8,128)(2,1)}, bf16[392,128]{1,0:T(8,128)(2,1)S(1)}, u32[]{:S(2)}, u32[]{:S(2)}) collective-permute-start(bf16[392,128]{1,0:T(8,128)(2,1)} %get-tuple-element.265), channel_id=1, source_target_pairs={{0,6},{2,4},{4,2},{6,0},{1,7},{3,5},{5,3},{7,1},{8,14},{10,12},{12... | collective-permute-start | bytes 301064 | tf_op jit(solution)/shard_map/ppermute | solution.py:457
  217.9 21.0 %collective-permute-start.35 = (bf16[128,2048]{1,0:T(8,128)(2,1)}, bf16[128,2048]{1,0:T(8,128)(2,1)S(1)}, u32[]{:S(2)}, u32[]{:S(2)}) collective-permute-start(bf16[128,2048]{1,0:T(8,128)(2,1)} %dynamic-slice_convert_fusion.1), channel_id=1, source_target_pairs={{0,2},{2,0},{4,6},{6,4},{1,3},{3,1},{5,7},{7,5},{8,10},{10,8},{12,... | collective-permute-start | bytes 1572872 | tf_op jit(solution)/shard_map/ppermute | solution.py:457
  219.2 19.6 %collective-permute-start.36 = (bf16[128,2560]{1,0:T(8,128)(2,1)}, bf16[128,2560]{1,0:T(8,128)(2,1)}, u32[]{:S(2)}, u32[]{:S(2)}) collective-permute-start(bf16[128,2560]{1,0:T(8,128)(2,1)} %get-tuple-element.359), channel_id=1, source_target_pairs={{0,8},{8,0},{16,24},{24,16},{1,9},{9,1},{17,25},{25,17},{2,10},{10... | collective-permute-start | bytes 1966088 | tf_op jit(solution)/shard_map/ppermute | solution.py:457
  220.7 18.2 %collective-permute-start.37 = (bf16[128,2560]{1,0:T(8,128)(2,1)S(1)}, bf16[128,2560]{1,0:T(8,128)(2,1)}, u32[]{:S(2)}, u32[]{:S(2)}) collective-permute-start(bf16[128,2560]{1,0:T(8,128)(2,1)S(1)} %get-tuple-element.358), channel_id=1, source_target_pairs={{0,16},{8,24},{16,0},{24,8},{1,17},{9,25},{17,1},{25,9},{2,18},{10... | collective-permute-start | bytes 1966088 | tf_op jit(solution)/shard_map/ppermute | solution.py:457
  241.6 15.0 %collective-permute-start.39 = (bf16[64,2048]{1,0:T(8,128)(2,1)}, bf16[64,2048]{1,0:T(8,128)(2,1)}, u32[]{:S(2)}, u32[]{:S(2)}) collective-permute-start(bf16[64,2048]{1,0:T(8,128)(2,1)} %dynamic-slice_convert_fusion.3), channel_id=1, source_target_pairs={{0,4},{2,6},{4,0},{6,2},{1,5},{3,7},{5,1},{7,3},{8,12},{10,14},{12... | collective-permute-start | bytes 786440 | tf_op jit(solution)/shard_map/ppermute | solution.py:457
  252.8 34.3 %collective-permute-start.45 = (bf16[256,2560]{1,0:T(8,128)(2,1)}, bf16[256,2560]{1,0:T(8,128)(2,1)}, u32[]{:S(2)}, u32[]{:S(2)}) collective-permute-start(bf16[256,2560]{1,0:T(8,128)(2,1)} %pad_maximum_fusion.5), channel_id=1, source_target_pairs={{0,16},{8,24},{16,0},{24,8},{1,17},{9,25},{17,1},{25,9},{2,18},{10... | collective-permute-start | bytes 3932168 | tf_op jit(solution)/shard_map/ppermute | solution.py:457
  255.4 31.7 %collective-permute-start.44 = (bf16[256,2560]{1,0:T(8,128)(2,1)}, bf16[256,2560]{1,0:T(8,128)(2,1)}, u32[]{:S(2)}, u32[]{:S(2)}) collective-permute-start(bf16[256,2560]{1,0:T(8,128)(2,1)} %pad_maximum_fusion.4), channel_id=1, source_target_pairs={{0,8},{8,0},{16,24},{24,16},{1,9},{9,1},{17,25},{25,17},{2,10},{10... | collective-permute-start | bytes 3932168 | tf_op jit(solution)/shard_map/ppermute | solution.py:457
  257.7 14.8 %collective-permute-start.41 = (bf16[64,2048]{1,0:T(8,128)(2,1)S(1)}, bf16[64,2048]{1,0:T(8,128)(2,1)S(1)}, u32[]{:S(2)}, u32[]{:S(2)}) collective-permute-start(bf16[64,2048]{1,0:T(8,128)(2,1)S(1)} %add_convert_fusion.5), channel_id=1, source_target_pairs={{0,4},{2,6},{4,0},{6,2},{1,5},{3,7},{5,1},{7,3},{8,12},{10,14},{12... | collective-permute-start | bytes 786440 | tf_op jit(solution)/shard_map/ppermute | solution.py:457
  259.7 25.2 %collective-permute-start.40 = (bf16[392,1024]{1,0:T(8,128)(2,1)}, bf16[392,1024]{1,0:T(8,128)(2,1)}, u32[]{:S(2)}, u32[]{:S(2)}) collective-permute-start(bf16[392,1024]{1,0:T(8,128)(2,1)} %pad_maximum_fusion.9), channel_id=1, source_target_pairs={{0,2},{2,0},{4,6},{6,4},{1,3},{3,1},{5,7},{7,5},{8,10},{10,8},{12,... | collective-permute-start | bytes 2408456 | tf_op jit(solution)/shard_map/ppermute | solution.py:457
  287.2 16.2 %collective-permute-start.46 = (bf16[128,768]{1,0:T(8,128)(2,1)S(1)}, bf16[128,768]{1,0:T(8,128)(2,1)S(1)}, u32[]{:S(2)}, u32[]{:S(2)}) collective-permute-start(bf16[128,768]{1,0:T(8,128)(2,1)S(1)} %get-tuple-element.415), channel_id=1, source_target_pairs={{0,8},{8,0},{16,24},{24,16},{1,9},{9,1},{17,25},{25,17},{2,10},{10... | collective-permute-start | bytes 589832 | tf_op jit(solution)/shard_map/ppermute | solution.py:457
  303.4 17.6 %collective-permute-start.64 = (bf16[128,2048]{1,0:T(8,128)(2,1)S(1)}, bf16[128,2048]{1,0:T(8,128)(2,1)S(1)}, u32[]{:S(2)}, u32[]{:S(2)}) collective-permute-start(bf16[128,2048]{1,0:T(8,128)(2,1)S(1)} %maximum_select_fusion.3), channel_id=1, source_target_pairs={{0,2},{2,0},{4,6},{6,4},{1,3},{3,1},{5,7},{7,5},{8,10},{10,8},{12,... | collective-permute-start | bytes 1572872 | tf_op jit(solution)/shard_map/ppermute | solution.py:457
  310.6 23.8 %collective-permute-start.51 = (bf16[128,2560]{1,0:T(8,128)(2,1)S(1)}, bf16[128,2560]{1,0:T(8,128)(2,1)S(1)}, u32[]{:S(2)}, u32[]{:S(2)}) collective-permute-start(bf16[128,2560]{1,0:T(8,128)(2,1)S(1)} %dynamic-slice_convert_fusion), channel_id=1, source_target_pairs={{0,2},{2,0},{4,6},{6,4},{1,3},{3,1},{5,7},{7,5},{8,10},{10,8},{12,... | collective-permute-start | bytes 1966088 | tf_op jit(solution)/shard_map/ppermute | solution.py:457
  310.7 23.8 %collective-permute-start.52 = (bf16[784,1024]{1,0:T(8,128)(2,1)S(1)}, bf16[784,1024]{1,0:T(8,128)(2,1)S(1)}, u32[]{:S(2)}, u32[]{:S(2)}) collective-permute-start(bf16[784,1024]{1,0:T(8,128)(2,1)S(1)} %reduce_output.1), channel_id=1, source_target_pairs={{0,1},{1,0},{2,3},{3,2},{4,5},{5,4},{6,7},{7,6},{8,9},{9,8},{10,11... | collective-permute-start | bytes 4816904 | tf_op jit(solution)/shard_map/ppermute | solution.py:457
  311.6 20.2 %collective-permute-start.50 = (bf16[256,768]{1,0:T(8,128)(2,1)S(1)}, bf16[256,768]{1,0:T(8,128)(2,1)S(1)}, u32[]{:S(2)}, u32[]{:S(2)}) collective-permute-start(bf16[256,768]{1,0:T(8,128)(2,1)S(1)} %pad_maximum_fusion.19), channel_id=1, source_target_pairs={{0,16},{8,24},{16,0},{24,8},{1,17},{9,25},{17,1},{25,9},{2,18},{10... | collective-permute-start | bytes 1179656 | tf_op jit(solution)/shard_map/ppermute | solution.py:457
  344.1 33.1 %collective-permute-start.56 = (bf16[256,768]{1,0:T(8,128)(2,1)S(1)}, bf16[256,768]{1,0:T(8,128)(2,1)S(1)}, u32[]{:S(2)}, u32[]{:S(2)}) collective-permute-start(bf16[256,768]{1,0:T(8,128)(2,1)S(1)} %fusion.6), channel_id=1, source_target_pairs={{0,4},{2,6},{4,0},{6,2},{1,5},{3,7},{5,1},{7,3},{8,12},{10,14},{12... | collective-permute-start | bytes 1179656 | tf_op jit(solution)/shard_map/ppermute | solution.py:457
  345.5 31.6 %collective-permute-start.57 = (bf16[64,2560]{1,0:T(8,128)(2,1)S(1)}, bf16[64,2560]{1,0:T(8,128)(2,1)S(1)}, u32[]{:S(2)}, u32[]{:S(2)}) collective-permute-start(bf16[64,2560]{1,0:T(8,128)(2,1)S(1)} %dynamic-slice_convert_fusion.2), channel_id=1, source_target_pairs={{0,4},{2,6},{4,0},{6,2},{1,5},{3,7},{5,1},{7,3},{8,12},{10,14},{12... | collective-permute-start | bytes 983048 | tf_op jit(solution)/shard_map/ppermute | solution.py:457
  380.8 16.0 %collective-permute-start.62 = (bf16[64,2560]{1,0:T(8,128)(2,1)S(1)}, bf16[64,2560]{1,0:T(8,128)(2,1)S(1)}, u32[]{:S(2)}, u32[]{:S(2)}) collective-permute-start(bf16[64,2560]{1,0:T(8,128)(2,1)S(1)} %add_convert_fusion.4), channel_id=1, source_target_pairs={{0,4},{2,6},{4,0},{6,2},{1,5},{3,7},{5,1},{7,3},{8,12},{10,14},{12... | collective-permute-start | bytes 983048 | tf_op jit(solution)/shard_map/ppermute | solution.py:457
  381.0 18.0 %collective-permute-start.61 = (bf16[256,768]{1,0:T(8,128)(2,1)S(1)}, bf16[256,768]{1,0:T(8,128)(2,1)S(1)}, u32[]{:S(2)}, u32[]{:S(2)}) collective-permute-start(bf16[256,768]{1,0:T(8,128)(2,1)S(1)} %add_convert_fusion.3), channel_id=1, source_target_pairs={{0,2},{2,0},{4,6},{6,4},{1,3},{3,1},{5,7},{7,5},{8,10},{10,8},{12,... | collective-permute-start | bytes 1179656 | tf_op jit(solution)/shard_map/ppermute | solution.py:457
  396.9 16.8 %collective-permute-start.63 = (bf16[128,2560]{1,0:T(8,128)(2,1)S(1)}, bf16[128,2560]{1,0:T(8,128)(2,1)}, u32[]{:S(2)}, u32[]{:S(2)}) collective-permute-start(bf16[128,2560]{1,0:T(8,128)(2,1)S(1)} %maximum_select_fusion.2), channel_id=1, source_target_pairs={{0,2},{2,0},{4,6},{6,4},{1,3},{3,1},{5,7},{7,5},{8,10},{10,8},{12,... | collective-permute-start | bytes 1966088 | tf_op jit(solution)/shard_map/ppermute | solution.py:457
  (108 other events, 856.9 us)
where the time goes:
time: 423 us; the launch traced here: 418 us
  waiting for transfers between devices  126 us (30%)
  Pallas kernels  119 us (28%)
  starting transfers between devices  78 us (18%)
  local copies, waits for them, and re-layouts  48.3 us (11%)
  other arithmetic  37.7 us (9%)
  matrix products  5.8 us (1%)
    ppermute x65, waiting for transfers between devices, swap(): return lax.ppermute(value, axis, [(i, i ^ distance) for i in range(size)])  126 us
    ppermute x65, starting transfers between devices, swap(): return lax.ppermute(value, axis, [(i, i ^ distance) for i in range(size)])  78 us
    pallas_call x2, Pallas kernels, attention_backward(): pl.pallas_call(attention_backward_kernel, grid=(1,), in_specs=[pl.BlockSp...  31.6 us
    pallas_call x4, Pallas kernels, grad_products(): pl.pallas_call(lambda *refs: grad_kernel(distances, *refs), grid_spec=plt...  21 us
    unnamed x166, local copies, waits for them, and re-layouts  20.8 us
    pallas_call x4, Pallas kernels, by_rows(): pl.pallas_call(kernel, grid=(count // chunk,), in_specs=in_specs, out_spe...  19.8 us
    pallas_call x1, Pallas kernels, feed_forward(): pl.pallas_call(lambda *refs: feed_forward_kernel(len(reduce), *refs), gri...  18.2 us
    pallas_call x2, Pallas kernels, attention_forward(): pl.pallas_call(attention_forward_kernel, grid=(1,), in_specs=[pl.BlockSpe...  14.9 us
  transfers between devices with their start and end apart: 65, of which 20 were waited for; matrix products, arithmetic and copies ran while one was open for 13% of the time, Pallas kernels for 22%

commit v1 on v0

--- a/solution.py
+++ b/solution.py
@@ -467,12 +467,19 @@
     return (rows_here, swap(rows_here, "fsdp", 1), swap(rows_here, "fsdp", 2))
 
 
+def far_of(held):
+    if len(held) == 1:
+        return ()
+    half = held[0].shape[0] // 2
+    return (held[2][:half], held[1][half:])
+
+
+def send_far(leaves):
+    return (swap(leaves[0], "fsdp", 1), swap(leaves[1], "fsdp", 2)) if leaves else ()
+
+
 def gather_far(held):
-    if len(held) == 1:
-        return held
-    rows_here, near, side = held
-    half = rows_here.shape[0] // 2
-    return held + (swap(side[:half], "fsdp", 1), swap(near[half:], "fsdp", 2))
+    return held + send_far(far_of(held))
 
 
 def place_near(held):
@@ -706,45 +713,60 @@
             to = block ^ distance
             corner = ((to >> 1) * rows_here, (to & 1) * part_width + pair * pair_width)
             leaving.append(lax.dynamic_slice(attended_slope, corner, (rows_here, pair_width)))
-    leaving, mixer_slope, mixed_in, activated, expand_far = fence(
-        leaving, mixer_slope, mixed_in, activated, expand_far
+    expand_near = add_far(expand_parts[2], expand_parts[1], expand_far) if four else ()
+    leaving, mixer_slope, mixed_in, activated, expand_near = fence(
+        leaving, mixer_slope, mixed_in, activated, expand_near
     )
     slope_first = [leaving[0]] + [swap(leaving[d], "ctx", d) for d in (1, 2, 3)]
-    expand_near = add_far(expand_parts[2], expand_parts[1], expand_far) if four else ()
+    if four:
+        expand_near = near_rows_out(expand_near)
     reduce_parts = grad_products([reduce_slope], activated, place, order, "reduce_grad")
     mixer_parts = grad_products([mixer_slope], mixed_in, place, order, "mixer_grad")
     wide = jnp.concatenate([reduce_parts, mixer_parts], axis=2)
-
-    slope_first, leaving, wide, expand_near = fence(slope_first, leaving, wide, expand_near)
-    half = width // 8
+    if four:
+        half = width // 8
+        far_top, far_low = wide[0][:half], wide[0][half:]
+        wide_early = (wide[2][:half], wide[1][half:])
+    else:
+        far_top, far_low, wide_early = (), (), ()
+
+    slope_first, leaving, expand_near, far_top, far_low = fence(
+        slope_first, leaving, expand_near, far_top, far_low
+    )
     slope_second = [leaving[4]] + [swap(leaving[4 + d], "ctx", d) for d in (1, 2, 3)]
-    if four:
-        expand_near = near_rows_out(expand_near)
+    wide_far = (swap(far_top, "fsdp", 1), swap(far_low, "fsdp", 2)) if four else ()
     grad_first = attention_backward(
         joint_out, jnp.concatenate(slope_first, axis=0), out_first, log_first, 0
     )
 
-    grad_first, slope_second, expand_near, wide = fence(
-        grad_first, slope_second, expand_near, wide
-    )
+    grad_first, slope_second, wide_far = fence(grad_first, slope_second, wide_far)
     if four:
         expand_sum = expand_parts[3].astype(FULL) + both(expand_near)
+        wide_late = (
+            both((wide[2][half:], wide_far[1])).astype(LOW),
+            both((wide[1][:half], wide_far[0])).astype(LOW),
+        )
     else:
+        wide_late = ()
         expand_sum = lax.psum_scatter(
             expand_parts.reshape(width, -1), "fsdp", scatter_dimension=0, tiled=True
         ).astype(FULL)
     expand_keep, expand_send = halves(expand_sum, part_at)
-    expand_send, slope_second = fence(expand_send, slope_second)
+    slope_second = jnp.concatenate(slope_second, axis=0)
+    expand_send, slope_second, wide_early, wide_late = fence(
+        expand_send, slope_second, wide_early, wide_late
+    )
+    if four:
+        wide_early = near_rows_out(wide_early)
     expand_rows = (expand_keep, swap(expand_send, "ctx", 1))
-    wide_far = far_halves(wide[0]) if four else ()
-    grad_second = attention_backward(
-        joint_out, jnp.concatenate(slope_second, axis=0), out_second, log_second, 1
-    )
-
-    grad_second, expand_rows, wide_far = fence(grad_second, expand_rows, wide_far)
+    grad_second = attention_backward(joint_out, slope_second, out_second, log_second, 1)
+
+    grad_second, expand_rows, wide_early, wide_late = fence(
+        grad_second, expand_rows, wide_early, wide_late
+    )
+    if four:
+        wide_late = near_rows_out(wide_late)
     expand_rows = split_rows(both(expand_rows), clip_at, 2)
-    if four:
-        wide_near = near_rows_out(add_far(wide[2], wide[1], wide_far))
     joint_slope = jnp.concatenate(
         [grad[kind] for kind in range(3) for grad in (grad_first, grad_second)], axis=1
     )
@@ -752,65 +774,68 @@
     first_here = rows_product(joint_slope, joint_full[:width_half], "first_slope")
     first_half = both((first_here, swap(first_there, "tp", 1))).astype(LOW)
 
-    first_half, joint_slope, expand_rows = fence(first_half, joint_slope, expand_rows)
-    expand_rows = both(expand_rows).astype(LOW)
+    if not four:
+        wide_near = lax.psum_scatter(
+            wide.reshape(width, -1), "fsdp", scatter_dimension=0, tiled=True
+        )
+    first_half, joint_slope, expand_rows, wide_late = fence(
+        first_half, joint_slope, expand_rows, wide_late
+    )
+    expand_rows = join_rows(both(expand_rows).astype(LOW), clip_at, 2)
     pieces = first_half.reshape(4, rows_here, width_half)
     passing = jnp.concatenate([pieces[1], pieces[3][:, :quarter], pieces[2][:, quarter:]], axis=1)
     passing = swap(passing, "ctx", 1)
     place = (shard if four else start) ^ (2 * core)
     joint_parts = grad_products([normed_mine, normed_other], joint_slope, place, order, "joint_grad")
+    if four:
+        near_sum = [both((wide_early[0], wide_late[1])), both((wide_late[0], wide_early[1]))]
+        wide_sum = wide[3].astype(FULL) + jnp.concatenate(near_sum, axis=0)
+    else:
+        wide_sum = wide_near.astype(FULL)
+    wide_keep, wide_send = halves(wide_sum, part_at)
+    joint_parts, wide_send = fence(joint_parts, wide_send)
+    joint_far = far_halves(joint_parts[0]) if four else ()
     slope_sums = jnp.sum(joint_slope.astype(FULL), axis=0)
     bias_sums = jnp.stack([slope_sums[:part_width], slope_sums[2 * part_width :]])
     joint_bias_grad = lax.dynamic_update_slice(
         jnp.zeros((2, features), FULL), bias_sums, (0, part_at * part_width)
     )
 
-    expand_rows = join_rows(expand_rows, clip_at, 2)
-
-    if not four:
-        wide_near = lax.psum_scatter(
-            wide.reshape(width, -1), "fsdp", scatter_dimension=0, tiled=True
-        )
-    passing, joint_parts, expand_rows = fence(passing, joint_parts, expand_rows)
+    passing, joint_far = fence(passing, joint_far)
     own_half = both((pieces[0], passing[:, :width_half])).astype(LOW)
     to_left = both((pieces[2][:, :quarter], passing[:, width_half : width_half + quarter]))
     to_right = both((pieces[3][:, quarter:], passing[:, width_half + quarter :]))
-    to_left, to_right, own_half, joint_parts, activated = fence(
-        to_left.astype(LOW), to_right.astype(LOW), own_half, joint_parts, activated
-    )
-    other_half = jnp.concatenate(
-        [swap(to_left, "ctx", 2), swap(to_right, "ctx", 3)], axis=1
-    )
-    joint_leaves, wide_near = fence(joint_parts[0], wide_near)
-    joint_far = far_halves(joint_leaves) if four else ()
+    joint_near = add_far(joint_parts[2], joint_parts[1], joint_far) if four else ()
+    to_left, to_right, own_half, wide_send, joint_near, activated = fence(
+        to_left.astype(LOW), to_right.astype(LOW), own_half, wide_send, joint_near, activated
+    )
+    other_half = jnp.concatenate([swap(to_left, "ctx", 2), swap(to_right, "ctx", 3)], axis=1)
+    wide_rows = (wide_keep, swap(wide_send, "ctx", 1))
+    if four:
+        joint_near = near_rows_out(joint_near)
+    else:
+        joint_near = lax.psum_scatter(
+            joint_parts.reshape(width, -1), "fsdp", scatter_dimension=0, tiled=True
+        )
     reduce_part = reduce_output(activated, reduce_held, pieces_at)
 
-    other_half, joint_far, wide_near, reduce_part, expand_rows = fence(
-        other_half, joint_far, wide_near, reduce_part, expand_rows
-    )
-    reduce_swapped = swap(reduce_part, "tp", 1)
-    wide_sum = wide[3].astype(FULL) + both(wide_near) if four else wide_near.astype(FULL)
-    wide_rows = split_rows(wide_sum, part_at, 1)
-    slope_half = jnp.concatenate(
-        swapped_if(clip_at, [own_half, other_half]), axis=0
-    )
+    other_half, joint_near, wide_rows, reduce_part, expand_rows = fence(
+        other_half, joint_near, wide_rows, reduce_part, expand_rows
+    )
+    slope_half = jnp.concatenate(swapped_if(clip_at, [own_half, other_half]), axis=0)
     slope_other = swap(slope_half, "tp", 1)
     first_slope = jnp.concatenate(swapped_if(core, [slope_half, slope_other]), axis=1)
+    wide_rows = split_rows(both(wide_rows), clip_at, 2)
+    reduce_swapped = swap(reduce_part, "tp", 1)
+    joint_sum = joint_parts[3].astype(FULL) + both(joint_near) if four else joint_near
+    joint_sum = joint_sum.astype(LOW)
+    joint_sum = (joint_sum, swap(joint_sum, "ctx", 2))
     tokens_grad, first_sums = by_rows(
         first_norm_back_kernel, "first_norm_back", [FULL], True,
         flat_tokens, first_slope, first_gain[None],
         cotangent.reshape(tokens_here, width), first_sum_back,
     )
-    if four:
-        joint_near = near_rows_out(add_far(joint_parts[2], joint_parts[1], joint_far))
-    else:
-        joint_near = lax.psum_scatter(
-            joint_parts.reshape(width, -1), "fsdp", scatter_dimension=0, tiled=True
-        )
-
-    first_sums, tokens_grad, joint_near, wide_rows, reduce_swapped = fence(
-        first_sums, tokens_grad, joint_near, wide_rows, reduce_swapped
-    )
+    first_sums, tokens_grad, reduce_swapped = fence(first_sums, tokens_grad, reduce_swapped)
     vectors = [
         first_sums[0],
         first_sums[1],
@@ -824,10 +849,6 @@
     ]
     packed = jnp.concatenate(vectors).reshape(-1, 128)
     packed_pieces = [packed] + [swap(packed, "ctx", d) for d in (1, 2, 3)]
-    joint_sum = joint_parts[3].astype(FULL) + both(joint_near) if four else joint_near
-    joint_sum = joint_sum.astype(LOW)
-    joint_sum = (joint_sum, swap(joint_sum, "ctx", 2))
-    wide_rows = split_rows(both(wide_rows), clip_at, 2)
     reduce_out = both((reduce_part, reduce_swapped)) + reduce_bias
     mixer_out = both((mixer_part, mixer_swapped)) + mixer_bias
     branches = (mixer_out + reduce_out).reshape(clips_here, rows_here, width)

time: 423 us -> 415 us (0.981)
  waiting for transfers between devices: 126 us -> 120 us
    unnamed x166 -> x202, local copies, waits for them, and re-layouts: 20.8 us -> 27.9 us
    ppermute x65 -> x67, waiting for transfers between devices: 126 us -> 120 us  [swap(): return lax.ppermute(value, axis, [(i, i ^ distance) for i in range(size)])]
    ppermute x65 -> x67, starting transfers between devices: 78 us -> 76.3 us  [swap(): return lax.ppermute(value, axis, [(i, i ^ distance) for i in range(size)])]
  transfers between devices with their start and end apart: 65 -> 67, of which waited for: 20 -> 28; matrix products, arithmetic and copies ran while one was open for 13% -> 12% of each run, Pallas kernels for 22% -> 24%
where the time goes in v1:
time: 415 us; the launch traced here: 410 us
  waiting for transfers between devices  120 us (29%)
  Pallas kernels  119 us (29%)
  starting transfers between devices  76.3 us (18%)
  local copies, waits for them, and re-layouts  52.4 us (13%)
  other arithmetic  34.2 us (8%)
  matrix products  5.78 us (1%)
    ppermute x67, waiting for transfers between devices, swap(): return lax.ppermute(value, axis, [(i, i ^ distance) for i in range(size)])  120 us
    ppermute x67, starting transfers between devices, swap(): return lax.ppermute(value, axis, [(i, i ^ distance) for i in range(size)])  76.3 us
    pallas_call x2, Pallas kernels, attention_backward(): pl.pallas_call(attention_backward_kernel, grid=(1,), in_specs=[pl.BlockSp...  31.5 us
    unnamed x202, local copies, waits for them, and re-layouts  27.9 us
    pallas_call x4, Pallas kernels, grad_products(): pl.pallas_call(lambda *refs: grad_kernel(distances, *refs), grid_spec=plt...  20.9 us
    pallas_call x4, Pallas kernels, by_rows(): pl.pallas_call(kernel, grid=(count // chunk,), in_specs=in_specs, out_spe...  19.8 us
    pallas_call x1, Pallas kernels, feed_forward(): pl.pallas_call(lambda *refs: feed_forward_kernel(len(reduce), *refs), gri...  18.2 us
    pallas_call x2, Pallas kernels, attention_forward(): pl.pallas_call(attention_forward_kernel, grid=(1,), in_specs=[pl.BlockSpe...  14.9 us
  transfers between devices with their start and end apart: 67, of which 28 were waited for; matrix products, arithmetic and copies ran while one was open for 12% of the time, Pallas kernels for 24%

profile of v1, /device:TPU:0, one launch (start us, length us, event | category | flops | bytes accessed | tf_op | source)
XLA Modules:
  0.0 410.5 jit_solution(1367733550651063842)
XLA Ops:
  7.1 3.0 collective-permute-start.3
  16.0 11.3 %collective-permute-done.1 = bf16[392,256]{1,0:T(8,128)(2,1)S(1)} collective-permute-done((bf16[392,256]{1,0:T(8,128)(2,1)S(1)}, bf16[392,256]{1,0:T(8,128)(2,1)S(1)}, u32[]{:S(2)}, u32[]{:S(2)}) %collective-permute-start.1) | collective-permute-done | bytes 200736 | tf_op jit(solution)/shard_map/ppermute | solution.py:457
  27.3 5.5 %collective-permute-done.2 = bf16[392,256]{1,0:T(8,128)(2,1)S(1)} collective-permute-done((bf16[392,256]{1,0:T(8,128)(2,1)S(1)}, bf16[392,256]{1,0:T(8,128)(2,1)S(1)}, u32[]{:S(2)}, u32[]{:S(2)}) %collective-permute-start.2) | collective-permute-done | bytes 200736 | tf_op jit(solution)/shard_map/ppermute | solution.py:457
  39.9 6.2 %collective-permute-done.6 = bf16[128,1280]{1,0:T(8,128)(2,1)} collective-permute-done((bf16[128,1280]{1,0:T(8,128)(2,1)}, bf16[128,1280]{1,0:T(8,128)(2,1)}, u32[]{:S(2)}, u32[]{:S(2)}) %collective-permute-start.6) | collective-permute-done | bytes 327712 | tf_op jit(solution)/shard_map/ppermute | solution.py:457
  56.1 3.1 joint_projection.1.q_ref.k_ref.v_ref
  60.4 7.2 %attention_forward.2 = (bf16[1568,128]{1,0:T(8,128)(2,1)S(1)}, f32[8,1568]{1,0:T(8,128)S(1)}) custom-call(bf16[1568,768]{1,0:T(8,128)(2,1)S(1)} %joint_projection.1.q_ref.k_ref.v_ref, bf16[1568,768]{1,0:T(8,128)(2,1)S(1)} %joint_projection.1.q_ref.k_ref.v_ref, bf16[1568,768]{1,0:T(8,128)(2,1)S(1)} %joint_projection.1.q_ref.k_ref.v_ref), custom_call_target="tpu_custom_call" | custom-call | tf_op jit(solution)/shard_map/attention_forward/pallas_call | solution.py:240
  74.9 7.8 %attention_forward.3 = (bf16[1568,128]{1,0:T(8,128)(2,1)S(1)}, f32[8,1568]{1,0:T(8,128)S(1)}) custom-call(bf16[1568,768]{1,0:T(8,128)(2,1)S(1)} %joint_projection.1.q_ref.k_ref.v_ref, bf16[1568,768]{1,0:T(8,128)(2,1)S(1)} %joint_projection.1.q_ref.k_ref.v_ref, bf16[1568,768]{1,0:T(8,128)(2,1)S(1)} %joint_projection.1.q_ref.k_ref.v_ref), custom_call_target="tpu_custom_call" | custom-call | tf_op jit(solution)/shard_map/attention_forward/pallas_call | solution.py:240
  82.7 4.9 %collective-permute-done.14.refs_10_.refs_1_ = bf16[256,2048]{1,0:T(8,128)(2,1)S(1)} collective-permute-done((bf16[256,2048]{1,0:T(8,128)(2,1)S(1)}, bf16[256,2048]{1,0:T(8,128)(2,1)S(1)}, u32[]{:S(2)}, u32[]{:S(2)}) %collective-permute-start.14) | collective-permute-done | bytes 1048608 | tf_op jit(solution)/shard_map/ppermute | solution.py:457
  99.9 2.9 collective-permute-done.17
  111.8 5.6 %second_norm.1.refs_1_ = bf16[784,1024]{1,0:T(8,128)(2,1)S(1)} custom-call(bf16[784,1024]{1,0:T(8,128)(2,1)S(1)} %bitcast.112, bf16[784,1024]{1,0:T(8,128)(2,1)} %convolution_convert_fusion.1.one_ref, bf16[784,1024]{1,0:T(8,128)(2,1)} %collective-permute-done.21.two_ref, f32[1,1024]{1,0:T(1,128)S(1)} %bitcast.120, f32[1,1024]{1,0:T(1,128)S(1)} %bitcast.124, ...), custom_call_target="tpu_custom_call" | custom-call | tf_op jit(solution)/shard_map/second_norm/pallas_call | solution.py:104
  118.6 3.5 collective-permute-done.22.refs_12_.refs_3_
  122.4 18.2 %feed_forward.1 = (bf16[784,2048]{1,0:T(8,128)(2,1)}, bf16[784,2048]{1,0:T(8,128)(2,1)}, bf16[784,1024]{1,0:T(8,128)(2,1)}, f32[1,2048]{1,0:T(1,128)S(1)}) custom-call(s32[5]{0:T(128)S(1)} %multiply_add_fusion.refs_0_.place_ref, bf16[784,1024]{1,0:T(8,128)(2,1)} %copy-done.8, bf16[784,1024]{1,0:T(8,128)(2,1)} %bitcast.115, f32[1,2048]{1,0:T(1,128)S(1)} %bitcast.126, ...), custom_call_target="tpu_custom_call" | custom-call | tf_op jit(solution)/shard_map/feed_forward/pallas_call | solution.py:387
  144.1 6.4 %expand_grad.1 = bf16[4,256,2048]{2,1,0:T(8,128)(2,1)} custom-call(s32[1]{0:T(128)} %bitcast.14.refs_0_, bf16[784,1024]{1,0:T(8,128)(2,1)S(1)} %copy-done.9, bf16[784,2048]{1,0:T(8,128)(2,1)S(1)} %copy-done.27), custom_call_target="tpu_custom_call" | custom-call | tf_op jit(solution)/shard_map/expand_grad/pallas_call | solution.py:188
  156.4 7.3 %second_norm_back.1 = (bf16[784,1024]{1,0:T(8,128)(2,1)S(1)}, f32[784,1024]{1,0:T(8,128)S(1)}, f32[8,1024]{1,0:T(8,128)S(1)}) custom-call(bf16[784,1024]{1,0:T(8,128)(2,1)S(1)} %bitcast.113, bf16[784,1024]{1,0:T(8,128)(2,1)} %convolution_convert_fusion.1.one_ref, bf16[784,1024]{1,0:T(8,128)(2,1)} %collective-permute-done.21.two_ref, ...), custom_call_target="tpu_custom_call" | custom-call | tf_op jit(solution)/shard_map/second_norm_back/pallas_call | solution.py:104
  177.1 6.4 %reduce_grad.1 = bf16[4,256,2048]{2,1,0:T(8,128)(2,1)} custom-call(s32[1]{0:T(128)} %bitcast.14.refs_0_, bf16[784,1024]{1,0:T(8,128)(2,1)S(1)} %bitcast.117, bf16[784,2048]{1,0:T(8,128)(2,1)S(1)} %copy-done.14), custom_call_target="tpu_custom_call" | custom-call | tf_op jit(solution)/shard_map/reduce_grad/pallas_call | solution.py:188
  190.3 2.8 maximum_bitcast_fusion.2
  207.2 15.7 %attention_backward.2 = (bf16[1568,128]{1,0:T(8,128)(2,1)S(1)}, bf16[1568,128]{1,0:T(8,128)(2,1)S(1)}, bf16[1568,128]{1,0:T(8,128)(2,1)S(1)}) custom-call(bf16[1568,768]{1,0:T(8,128)(2,1)S(1)} %joint_projection.1.q_ref.k_ref.v_ref, bf16[1568,768]{1,0:T(8,128)(2,1)S(1)} %joint_projection.1.q_ref.k_ref.v_ref, ...), custom_call_target="tpu_custom_call" | custom-call | tf_op jit(solution)/shard_map/attention_backward/pallas_call | solution.py:313
  231.3 15.8 %attention_backward.3 = (bf16[1568,128]{1,0:T(8,128)(2,1)S(1)}, bf16[1568,128]{1,0:T(8,128)(2,1)S(1)}, bf16[1568,128]{1,0:T(8,128)(2,1)S(1)}) custom-call(bf16[1568,768]{1,0:T(8,128)(2,1)S(1)} %joint_projection.1.q_ref.k_ref.v_ref, bf16[1568,768]{1,0:T(8,128)(2,1)S(1)} %joint_projection.1.q_ref.k_ref.v_ref, ...), custom_call_target="tpu_custom_call" | custom-call | tf_op jit(solution)/shard_map/attention_backward/pallas_call | solution.py:313
  258.4 3.1 first_slope.1
  263.4 7.5 %collective-permute-done.41 = bf16[64,2048]{1,0:T(8,128)(2,1)S(1)} collective-permute-done((bf16[64,2048]{1,0:T(8,128)(2,1)S(1)}, bf16[64,2048]{1,0:T(8,128)(2,1)S(1)}, u32[]{:S(2)}, u32[]{:S(2)}) %collective-permute-start.41) | collective-permute-done | bytes 262176 | tf_op jit(solution)/shard_map/ppermute | solution.py:457
  270.9 3.2 collective-permute-done.42
  280.5 5.8 %joint_grad.1 = bf16[4,256,768]{2,1,0:T(8,128)(2,1)S(1)} custom-call(s32[1]{0:T(128)} %bitcast.34.refs_0_, bf16[1568,512]{1,0:T(8,128)(2,1)S(1)} %copy-done.11, bf16[1568,512]{1,0:T(8,128)(2,1)S(1)} %copy-done.13, bf16[1568,768]{1,0:T(8,128)(2,1)} %copy-done.6), custom_call_target="tpu_custom_call" | custom-call | tf_op jit(solution)/shard_map/joint_grad/pallas_call | solution.py:188
  293.6 13.1 %collective-permute-done.44 = bf16[392,1024]{1,0:T(8,128)(2,1)S(1)} collective-permute-done((bf16[392,1024]{1,0:T(8,128)(2,1)S(1)}, bf16[392,1024]{1,0:T(8,128)(2,1)S(1)}, u32[]{:S(2)}, u32[]{:S(2)}) %collective-permute-start.44) | collective-permute-done | bytes 802848 | tf_op jit(solution)/shard_map/ppermute | solution.py:457
  315.1 7.5 %reduce_output.1 = bf16[784,1024]{1,0:T(8,128)(2,1)S(1)} custom-call(s32[5]{0:T(128)S(1)} %multiply_add_fusion.refs_0_.place_ref, bf16[784,2048]{1,0:T(8,128)(2,1)S(1)} %copy-done.15, bf16[256,2048]{1,0:T(8,128)(2,1)S(1)} %copy-done.24, bf16[256,2048]{1,0:T(8,128)(2,1)S(1)} %copy-done.19, bf16[256,2048]{1,0:T(8,128)(2,1)} %collective-permute-done.15.refs_11_.refs_2_, ...), custom_call_target="tpu_custom_call" | custom-call | tf_op jit(solution)/shard_map/reduce_output/pallas_call | solution.py:437
  322.6 4.0 collective-permute-done.47
  326.5 5.2 %collective-permute-done.48 = bf16[392,256]{1,0:T(8,128)(2,1)S(1)} collective-permute-done((bf16[392,256]{1,0:T(8,128)(2,1)S(1)}, bf16[392,256]{1,0:T(8,128)(2,1)S(1)}, u32[]{:S(2)}, u32[]{:S(2)}) %collective-permute-start.48) | collective-permute-done | bytes 200736 | tf_op jit(solution)/shard_map/ppermute | solution.py:457
  332.7 3.0 collective-permute-start.59
  336.0 11.8 %collective-permute-done.66 = bf16[128,2048]{1,0:T(8,128)(2,1)S(1)} collective-permute-done((bf16[128,2048]{1,0:T(8,128)(2,1)S(1)}, bf16[128,2048]{1,0:T(8,128)(2,1)S(1)}, u32[]{:S(2)}, u32[]{:S(2)}) %collective-permute-start.66) | collective-permute-done | bytes 524320 | tf_op jit(solution)/shard_map/ppermute | solution.py:457
  352.3 5.0 %first_norm_back.1 = (f32[784,1024]{1,0:T(8,128)}, f32[8,1024]{1,0:T(8,128)S(1)}) custom-call(bf16[784,1024]{1,0:T(8,128)(2,1)S(1)} %bitcast.114, bf16[784,1024]{1,0:T(8,128)(2,1)S(1)} %pad_maximum_fusion.1.upstream_ref, f32[1,1024]{1,0:T(1,128)S(1)} %bitcast.123, bf16[784,1024]{1,0:T(8,128)(2,1)S(1)} %bitcast.118, f32[784,1024]{1,0:T(8,128)S(1)} %copy-done.26), custom_call_target="tpu_custom_call" | custom-call | tf_op jit(solution)/shard_map/first_norm_back/pallas_call | solution.py:104
  361.9 3.4 add_add_fusion
  377.3 12.7 %collective-permute-done.64 = bf16[64,2560]{1,0:T(8,128)(2,1)S(1)} collective-permute-done((bf16[64,2560]{1,0:T(8,128)(2,1)S(1)}, bf16[64,2560]{1,0:T(8,128)(2,1)S(1)}, u32[]{:S(2)}, u32[]{:S(2)}) %collective-permute-start.64) | collective-permute-done | bytes 327712 | tf_op jit(solution)/shard_map/ppermute | solution.py:457
  394.3 12.0 %collective-permute-done.65 = bf16[128,2560]{1,0:T(8,128)(2,1)} collective-permute-done((bf16[128,2560]{1,0:T(8,128)(2,1)S(1)}, bf16[128,2560]{1,0:T(8,128)(2,1)}, u32[]{:S(2)}, u32[]{:S(2)}) %collective-permute-start.65) | collective-permute-done | bytes 655392 | tf_op jit(solution)/shard_map/ppermute | solution.py:457
  (435 shorter events, 177.1 us)
Async XLA Ops:
  7.1 25.7 %collective-permute-start.3 = (bf16[256,1280]{1,0:T(8,128)(2,1)S(1)}, bf16[256,1280]{1,0:T(8,128)(2,1)S(1)}, u32[]{:S(2)}, u32[]{:S(2)}) collective-permute-start(bf16[256,1280]{1,0:T(8,128)(2,1)S(1)} %pad_maximum_fusion.9), channel_id=1, source_target_pairs={{0,8},{8,0},{16,24},{24,16},{1,9},{9,1},{17,25},{25,17},{2,10},{10... | collective-permute-start | bytes 1966088 | tf_op jit(solution)/shard_map/ppermute | solution.py:457
  10.1 22.7 %collective-permute-start.4 = (bf16[256,1280]{1,0:T(8,128)(2,1)S(1)}, bf16[256,1280]{1,0:T(8,128)(2,1)S(1)}, u32[]{:S(2)}, u32[]{:S(2)}) collective-permute-start(bf16[256,1280]{1,0:T(8,128)(2,1)S(1)} %pad_maximum_fusion.9), channel_id=1, source_target_pairs={{0,16},{8,24},{16,0},{24,8},{1,17},{9,25},{17,1},{25,9},{2,18},{10... | collective-permute-start | bytes 1966088 | tf_op jit(solution)/shard_map/ppermute | solution.py:457
  11.6 21.2 %collective-permute-start = (bf16[392,512]{1,0:T(8,128)(2,1)S(1)}, bf16[392,512]{1,0:T(8,128)(2,1)S(1)}, u32[]{:S(2)}, u32[]{:S(2)}) collective-permute-start(bf16[392,512]{1,0:T(8,128)(2,1)S(1)} %get-tuple-element.178), channel_id=1, source_target_pairs={{0,2},{2,0},{4,6},{6,4},{1,3},{3,1},{5,7},{7,5},{8,10},{10,8},{12,... | collective-permute-start | bytes 1204232 | tf_op jit(solution)/shard_map/ppermute | solution.py:457
  15.8 17.0 %collective-permute-start.2 = (bf16[392,256]{1,0:T(8,128)(2,1)S(1)}, bf16[392,256]{1,0:T(8,128)(2,1)S(1)}, u32[]{:S(2)}, u32[]{:S(2)}) collective-permute-start(bf16[392,256]{1,0:T(8,128)(2,1)S(1)} %get-tuple-element.180), channel_id=1, source_target_pairs={{0,6},{2,4},{4,2},{6,0},{1,7},{3,5},{5,3},{7,1},{8,14},{10,12},{12... | collective-permute-start | bytes 602120 | tf_op jit(solution)/shard_map/ppermute | solution.py:457
  36.9 32.8 %collective-permute-start.10 = (bf16[256,2048]{1,0:T(8,128)(2,1)}, bf16[256,2048]{1,0:T(8,128)(2,1)S(1)}, u32[]{:S(2)}, u32[]{:S(2)}) collective-permute-start(bf16[256,2048]{1,0:T(8,128)(2,1)} %refs_4_), channel_id=1, source_target_pairs={{0,16},{8,24},{16,0},{24,8},{1,17},{9,25},{17,1},{25,9},{2,18},{10... | collective-permute-start | bytes 3145736 | tf_op jit(solution)/shard_map/ppermute | solution.py:457
  38.4 31.3 %collective-permute-start.9 = (bf16[256,2048]{1,0:T(8,128)(2,1)}, bf16[256,2048]{1,0:T(8,128)(2,1)S(1)}, u32[]{:S(2)}, u32[]{:S(2)}) collective-permute-start(bf16[256,2048]{1,0:T(8,128)(2,1)} %refs_4_), channel_id=1, source_target_pairs={{0,8},{8,0},{16,24},{24,16},{1,9},{9,1},{17,25},{25,17},{2,10},{10... | collective-permute-start | bytes 3145736 | tf_op jit(solution)/shard_map/ppermute | solution.py:457
  52.6 35.0 %collective-permute-start.14 = (bf16[256,2048]{1,0:T(8,128)(2,1)S(1)}, bf16[256,2048]{1,0:T(8,128)(2,1)S(1)}, u32[]{:S(2)}, u32[]{:S(2)}) collective-permute-start(bf16[256,2048]{1,0:T(8,128)(2,1)S(1)} %copy-done.22), channel_id=1, source_target_pairs={{0,8},{8,0},{16,24},{24,16},{1,9},{9,1},{17,25},{25,17},{2,10},{10... | collective-permute-start | bytes 3145736 | tf_op jit(solution)/shard_map/ppermute | solution.py:457
  54.1 34.6 %collective-permute-start.15 = (bf16[256,2048]{1,0:T(8,128)(2,1)S(1)}, bf16[256,2048]{1,0:T(8,128)(2,1)}, u32[]{:S(2)}, u32[]{:S(2)}) collective-permute-start(bf16[256,2048]{1,0:T(8,128)(2,1)S(1)} %copy-done.22), channel_id=1, source_target_pairs={{0,16},{8,24},{16,0},{24,8},{1,17},{9,25},{17,1},{25,9},{2,18},{10... | collective-permute-start | bytes 3145736 | tf_op jit(solution)/shard_map/ppermute | solution.py:457
  171.7 24.7 %collective-permute-start.30 = (bf16[256,2048]{1,0:T(8,128)(2,1)}, bf16[256,2048]{1,0:T(8,128)(2,1)}, u32[]{:S(2)}, u32[]{:S(2)}) collective-permute-start(bf16[256,2048]{1,0:T(8,128)(2,1)} %pad_maximum_fusion.4), channel_id=1, source_target_pairs={{0,8},{8,0},{16,24},{24,16},{1,9},{9,1},{17,25},{25,17},{2,10},{10... | collective-permute-start | bytes 3145736 | tf_op jit(solution)/shard_map/ppermute | solution.py:457
  173.2 24.4 %collective-permute-start.31 = (bf16[256,2048]{1,0:T(8,128)(2,1)}, bf16[256,2048]{1,0:T(8,128)(2,1)}, u32[]{:S(2)}, u32[]{:S(2)}) collective-permute-start(bf16[256,2048]{1,0:T(8,128)(2,1)} %pad_maximum_fusion.5), channel_id=1, source_target_pairs={{0,16},{8,24},{16,0},{24,8},{1,17},{9,25},{17,1},{25,9},{2,18},{10... | collective-permute-start | bytes 3145736 | tf_op jit(solution)/shard_map/ppermute | solution.py:457
  197.7 25.2 %collective-permute-start.35 = (bf16[128,2560]{1,0:T(8,128)(2,1)S(1)}, bf16[128,2560]{1,0:T(8,128)(2,1)S(1)}, u32[]{:S(2)}, u32[]{:S(2)}) collective-permute-start(bf16[128,2560]{1,0:T(8,128)(2,1)S(1)} %get-tuple-element.268), channel_id=1, source_target_pairs={{0,8},{8,0},{16,24},{24,16},{1,9},{9,1},{17,25},{25,17},{2,10},{10... | collective-permute-start | bytes 1966088 | tf_op jit(solution)/shard_map/ppermute | solution.py:457
  198.2 24.7 %collective-permute-start.36 = (bf16[128,2560]{1,0:T(8,128)(2,1)S(1)}, bf16[128,2560]{1,0:T(8,128)(2,1)S(1)}, u32[]{:S(2)}, u32[]{:S(2)}) collective-permute-start(bf16[128,2560]{1,0:T(8,128)(2,1)S(1)} %get-tuple-element.269), channel_id=1, source_target_pairs={{0,16},{8,24},{16,0},{24,8},{1,17},{9,25},{17,1},{25,9},{2,18},{10... | collective-permute-start | bytes 1966088 | tf_op jit(solution)/shard_map/ppermute | solution.py:457
  198.8 24.1 %collective-permute-start.32 = (bf16[392,128]{1,0:T(8,128)(2,1)S(1)}, bf16[392,128]{1,0:T(8,128)(2,1)S(1)}, u32[]{:S(2)}, u32[]{:S(2)}) collective-permute-start(bf16[392,128]{1,0:T(8,128)(2,1)S(1)} %copy-done.82), channel_id=1, source_target_pairs={{0,2},{2,0},{4,6},{6,4},{1,3},{3,1},{5,7},{7,5},{8,10},{10,8},{12,... | collective-permute-start | bytes 301064 | tf_op jit(solution)/shard_map/ppermute | solution.py:457
  200.4 22.4 %collective-permute-start.33 = (bf16[392,128]{1,0:T(8,128)(2,1)S(1)}, bf16[392,128]{1,0:T(8,128)(2,1)S(1)}, u32[]{:S(2)}, u32[]{:S(2)}) collective-permute-start(bf16[392,128]{1,0:T(8,128)(2,1)S(1)} %copy-done.81), channel_id=1, source_target_pairs={{0,4},{2,6},{4,0},{6,2},{1,5},{3,7},{5,1},{7,3},{8,12},{10,14},{12... | collective-permute-start | bytes 301064 | tf_op jit(solution)/shard_map/ppermute | solution.py:457
  201.1 21.7 %collective-permute-start.34 = (bf16[392,128]{1,0:T(8,128)(2,1)S(1)}, bf16[392,128]{1,0:T(8,128)(2,1)S(1)}, u32[]{:S(2)}, u32[]{:S(2)}) collective-permute-start(bf16[392,128]{1,0:T(8,128)(2,1)S(1)} %copy-done.80), channel_id=1, source_target_pairs={{0,6},{2,4},{4,2},{6,0},{1,7},{3,5},{5,3},{7,1},{8,14},{10,12},{12... | collective-permute-start | bytes 301064 | tf_op jit(solution)/shard_map/ppermute | solution.py:457
  225.2 22.0 %collective-permute-start.38 = (bf16[128,2560]{1,0:T(8,128)(2,1)}, bf16[128,2560]{1,0:T(8,128)(2,1)}, u32[]{:S(2)}, u32[]{:S(2)}) collective-permute-start(bf16[128,2560]{1,0:T(8,128)(2,1)} %get-tuple-element.285), channel_id=1, source_target_pairs={{0,8},{8,0},{16,24},{24,16},{1,9},{9,1},{17,25},{25,17},{2,10},{10... | collective-permute-start | bytes 1966088 | tf_op jit(solution)/shard_map/ppermute | solution.py:457
  226.7 20.5 %collective-permute-start.39 = (bf16[128,2560]{1,0:T(8,128)(2,1)}, bf16[128,2560]{1,0:T(8,128)(2,1)}, u32[]{:S(2)}, u32[]{:S(2)}) collective-permute-start(bf16[128,2560]{1,0:T(8,128)(2,1)} %get-tuple-element.286), channel_id=1, source_target_pairs={{0,16},{8,24},{16,0},{24,8},{1,17},{9,25},{17,1},{25,9},{2,18},{10... | collective-permute-start | bytes 1966088 | tf_op jit(solution)/shard_map/ppermute | solution.py:457
  228.2 19.1 %collective-permute-start.37 = (bf16[128,2048]{1,0:T(8,128)(2,1)}, bf16[128,2048]{1,0:T(8,128)(2,1)}, u32[]{:S(2)}, u32[]{:S(2)}) collective-permute-start(bf16[128,2048]{1,0:T(8,128)(2,1)} %dynamic-slice_convert_fusion.1), channel_id=1, source_target_pairs={{0,2},{2,0},{4,6},{6,4},{1,3},{3,1},{5,7},{7,5},{8,10},{10,8},{12,... | collective-permute-start | bytes 1572872 | tf_op jit(solution)/shard_map/ppermute | solution.py:457
  257.3 16.9 %collective-permute-start.42 = (bf16[128,2560]{1,0:T(8,128)(2,1)S(1)}, bf16[128,2560]{1,0:T(8,128)(2,1)S(1)}, u32[]{:S(2)}, u32[]{:S(2)}) collective-permute-start(bf16[128,2560]{1,0:T(8,128)(2,1)S(1)} %copy-done.75), channel_id=1, source_target_pairs={{0,8},{8,0},{16,24},{24,16},{1,9},{9,1},{17,25},{25,17},{2,10},{10... | collective-permute-start | bytes 1966088 | tf_op jit(solution)/shard_map/ppermute | solution.py:457
  257.8 16.6 %collective-permute-start.43 = (bf16[128,2560]{1,0:T(8,128)(2,1)S(1)}, bf16[128,2560]{1,0:T(8,128)(2,1)S(1)}, u32[]{:S(2)}, u32[]{:S(2)}) collective-permute-start(bf16[128,2560]{1,0:T(8,128)(2,1)S(1)} %copy-done.74), channel_id=1, source_target_pairs={{0,16},{8,24},{16,0},{24,8},{1,17},{9,25},{17,1},{25,9},{2,18},{10... | collective-permute-start | bytes 1966088 | tf_op jit(solution)/shard_map/ppermute | solution.py:457
  274.5 37.0 %collective-permute-start.52 = (bf16[64,2048]{1,0:T(8,128)(2,1)S(1)}, bf16[64,2048]{1,0:T(8,128)(2,1)}, u32[]{:S(2)}, u32[]{:S(2)}) collective-permute-start(bf16[64,2048]{1,0:T(8,128)(2,1)S(1)} %add_convert_fusion.5), channel_id=1, source_target_pairs={{0,4},{2,6},{4,0},{6,2},{1,5},{3,7},{5,1},{7,3},{8,12},{10,14},{12... | collective-permute-start | bytes 786440 | tf_op jit(solution)/shard_map/ppermute | solution.py:457
  288.7 18.1 %collective-permute-start.44 = (bf16[392,1024]{1,0:T(8,128)(2,1)S(1)}, bf16[392,1024]{1,0:T(8,128)(2,1)S(1)}, u32[]{:S(2)}, u32[]{:S(2)}) collective-permute-start(bf16[392,1024]{1,0:T(8,128)(2,1)S(1)} %pad_maximum_fusion.7), channel_id=1, source_target_pairs={{0,2},{2,0},{4,6},{6,4},{1,3},{3,1},{5,7},{7,5},{8,10},{10,8},{12,... | collective-permute-start | bytes 2408456 | tf_op jit(solution)/shard_map/ppermute | solution.py:457
  307.2 24.5 %collective-permute-start.51 = (bf16[128,2560]{1,0:T(8,128)(2,1)S(1)}, bf16[128,2560]{1,0:T(8,128)(2,1)S(1)}, u32[]{:S(2)}, u32[]{:S(2)}) collective-permute-start(bf16[128,2560]{1,0:T(8,128)(2,1)S(1)} %dynamic-slice_convert_fusion), channel_id=1, source_target_pairs={{0,2},{2,0},{4,6},{6,4},{1,3},{3,1},{5,7},{7,5},{8,10},{10,8},{12,... | collective-permute-start | bytes 1966088 | tf_op jit(solution)/shard_map/ppermute | solution.py:457
  308.6 23.1 %collective-permute-start.49 = (bf16[256,768]{1,0:T(8,128)(2,1)S(1)}, bf16[256,768]{1,0:T(8,128)(2,1)S(1)}, u32[]{:S(2)}, u32[]{:S(2)}) collective-permute-start(bf16[256,768]{1,0:T(8,128)(2,1)S(1)} %pad_maximum_fusion.16), channel_id=1, source_target_pairs={{0,8},{8,0},{16,24},{24,16},{1,9},{9,1},{17,25},{25,17},{2,10},{10... | collective-permute-start | bytes 1179656 | tf_op jit(solution)/shard_map/ppermute | solution.py:457
  309.3 22.5 %collective-permute-start.50 = (bf16[256,768]{1,0:T(8,128)(2,1)S(1)}, bf16[256,768]{1,0:T(8,128)(2,1)S(1)}, u32[]{:S(2)}, u32[]{:S(2)}) collective-permute-start(bf16[256,768]{1,0:T(8,128)(2,1)S(1)} %pad_maximum_fusion.17), channel_id=1, source_target_pairs={{0,16},{8,24},{16,0},{24,8},{1,17},{9,25},{17,1},{25,9},{2,18},{10... | collective-permute-start | bytes 1179656 | tf_op jit(solution)/shard_map/ppermute | solution.py:457
  311.5 20.2 %collective-permute-start.48 = (bf16[392,256]{1,0:T(8,128)(2,1)S(1)}, bf16[392,256]{1,0:T(8,128)(2,1)S(1)}, u32[]{:S(2)}, u32[]{:S(2)}) collective-permute-start(bf16[392,256]{1,0:T(8,128)(2,1)S(1)} %get-tuple-element.311), channel_id=1, source_target_pairs={{0,6},{2,4},{4,2},{6,0},{1,7},{3,5},{5,3},{7,1},{8,14},{10,12},{12... | collective-permute-start | bytes 602120 | tf_op jit(solution)/shard_map/ppermute | solution.py:457
  332.0 17.4 %collective-permute-start.53 = (bf16[784,512]{1,0:T(8,128)(2,1)S(1)}, bf16[784,512]{1,0:T(8,128)(2,1)S(1)}, u32[]{:S(2)}, u32[]{:S(2)}) collective-permute-start(bf16[784,512]{1,0:T(8,128)(2,1)S(1)} %pad_maximum_fusion.8), channel_id=1, source_target_pairs={{0,1},{1,0},{2,3},{3,2},{4,5},{5,4},{6,7},{7,6},{8,9},{9,8},{10,11... | collective-permute-start | bytes 2408456 | tf_op jit(solution)/shard_map/ppermute | solution.py:457
  332.0 25.3 %collective-permute-start.54 = (bf16[784,1024]{1,0:T(8,128)(2,1)S(1)}, bf16[784,1024]{1,0:T(8,128)(2,1)S(1)}, u32[]{:S(2)}, u32[]{:S(2)}) collective-permute-start(bf16[784,1024]{1,0:T(8,128)(2,1)S(1)} %reduce_output.1), channel_id=1, source_target_pairs={{0,1},{1,0},{2,3},{3,2},{4,5},{5,4},{6,7},{7,6},{8,9},{9,8},{10,11... | collective-permute-start | bytes 4816904 | tf_op jit(solution)/shard_map/ppermute | solution.py:457
  332.7 34.4 %collective-permute-start.59 = (bf16[64,2560]{1,0:T(8,128)(2,1)S(1)}, bf16[64,2560]{1,0:T(8,128)(2,1)S(1)}, u32[]{:S(2)}, u32[]{:S(2)}) collective-permute-start(bf16[64,2560]{1,0:T(8,128)(2,1)S(1)} %dynamic-slice_convert_fusion.2), channel_id=1, source_target_pairs={{0,4},{2,6},{4,0},{6,2},{1,5},{3,7},{5,1},{7,3},{8,12},{10,14},{12... | collective-permute-start | bytes 983048 | tf_op jit(solution)/shard_map/ppermute | solution.py:457
  335.8 33.9 %collective-permute-start.58 = (bf16[256,768]{1,0:T(8,128)(2,1)S(1)}, bf16[256,768]{1,0:T(8,128)(2,1)S(1)}, u32[]{:S(2)}, u32[]{:S(2)}) collective-permute-start(bf16[256,768]{1,0:T(8,128)(2,1)S(1)} %fusion.7), channel_id=1, source_target_pairs={{0,4},{2,6},{4,0},{6,2},{1,5},{3,7},{5,1},{7,3},{8,12},{10,14},{12... | collective-permute-start | bytes 1179656 | tf_op jit(solution)/shard_map/ppermute | solution.py:457
  375.7 16.4 %collective-permute-start.63 = (bf16[256,768]{1,0:T(8,128)(2,1)S(1)}, bf16[256,768]{1,0:T(8,128)(2,1)S(1)}, u32[]{:S(2)}, u32[]{:S(2)}) collective-permute-start(bf16[256,768]{1,0:T(8,128)(2,1)S(1)} %add_convert_fusion.3), channel_id=1, source_target_pairs={{0,2},{2,0},{4,6},{6,4},{1,3},{3,1},{5,7},{7,5},{8,10},{10,8},{12,... | collective-permute-start | bytes 1179656 | tf_op jit(solution)/shard_map/ppermute | solution.py:457
  390.1 16.2 %collective-permute-start.65 = (bf16[128,2560]{1,0:T(8,128)(2,1)S(1)}, bf16[128,2560]{1,0:T(8,128)(2,1)}, u32[]{:S(2)}, u32[]{:S(2)}) collective-permute-start(bf16[128,2560]{1,0:T(8,128)(2,1)S(1)} %maximum_select_fusion.2), channel_id=1, source_target_pairs={{0,2},{2,0},{4,6},{6,4},{1,3},{3,1},{5,7},{7,5},{8,10},{10,8},{12,... | collective-permute-start | bytes 1966088 | tf_op jit(solution)/shard_map/ppermute | solution.py:457
  (129 other events, 951.1 us)

commit v2 on v1

--- a/solution.py
+++ b/solution.py
@@ -504,6 +504,15 @@
     return lax.dynamic_update_slice(out, far_low, (start + half, 0))
 
 
+def rows_at(matrices, distance):
+    parts = []
+    for matrix in matrices:
+        count = matrix.shape[0] // 4
+        start = (lax.axis_index("fsdp") ^ distance) * count
+        parts.append(lax.dynamic_slice_in_dim(matrix, start, count, 0))
+    return parts[0] if len(parts) == 1 else jnp.concatenate(parts, axis=1)
+
+
 def far_halves(far):
     half = far.shape[0] // 2
     return (swap(far[:half], "fsdp", 1), swap(far[half:], "fsdp", 2))
@@ -697,9 +706,9 @@
 
     second_swapped = swap(second_part, "tp", 1)
     place, order = (shard, (3, 2, 1, 0)) if four else (start, (0, 1, 2, 3))
-    expand_parts = grad_products([second_normed], expand_slope, place, order, "expand_grad")
-    second_swapped, expand_parts = fence(second_swapped, expand_parts)
-    expand_far = far_halves(expand_parts[0]) if four else ()
+    expand_whole = product(second_normed, expand_slope, COLUMN_BY_COLUMN).astype(LOW)
+    second_swapped, expand_whole = fence(second_swapped, expand_whole)
+    expand_far = far_halves(rows_at((expand_whole,), 3)) if four else ()
     mixer_slope, first_sum_back, second_sums = by_rows(
         second_norm_back_kernel, "second_norm_back", [LOW, FULL], True,
         flat_tokens, mixer_part, mixer_swapped, mixer_row, second_gain[None],
@@ -713,20 +722,27 @@
             to = block ^ distance
             corner = ((to >> 1) * rows_here, (to & 1) * part_width + pair * pair_width)
             leaving.append(lax.dynamic_slice(attended_slope, corner, (rows_here, pair_width)))
-    expand_near = add_far(expand_parts[2], expand_parts[1], expand_far) if four else ()
+    if four:
+        expand_near = add_far(
+            rows_at((expand_whole,), 1), rows_at((expand_whole,), 2), expand_far
+        )
+    else:
+        expand_near = ()
     leaving, mixer_slope, mixed_in, activated, expand_near = fence(
         leaving, mixer_slope, mixed_in, activated, expand_near
     )
     slope_first = [leaving[0]] + [swap(leaving[d], "ctx", d) for d in (1, 2, 3)]
     if four:
         expand_near = near_rows_out(expand_near)
-    reduce_parts = grad_products([reduce_slope], activated, place, order, "reduce_grad")
-    mixer_parts = grad_products([mixer_slope], mixed_in, place, order, "mixer_grad")
-    wide = jnp.concatenate([reduce_parts, mixer_parts], axis=2)
+    wide = (
+        product(reduce_slope, activated, COLUMN_BY_COLUMN).astype(LOW),
+        product(mixer_slope, mixed_in, COLUMN_BY_COLUMN).astype(LOW),
+    )
     if four:
         half = width // 8
-        far_top, far_low = wide[0][:half], wide[0][half:]
-        wide_early = (wide[2][:half], wide[1][half:])
+        wide_far, wide_side, wide_next = (rows_at(wide, distance) for distance in (3, 2, 1))
+        far_top, far_low = wide_far[:half], wide_far[half:]
+        wide_early = (wide_next[:half], wide_side[half:])
     else:
         far_top, far_low, wide_early = (), (), ()
 
@@ -741,15 +757,15 @@
 
     grad_first, slope_second, wide_far = fence(grad_first, slope_second, wide_far)
     if four:
-        expand_sum = expand_parts[3].astype(FULL) + both(expand_near)
+        expand_sum = rows_at((expand_whole,), 0).astype(FULL) + both(expand_near)
         wide_late = (
-            both((wide[2][half:], wide_far[1])).astype(LOW),
-            both((wide[1][:half], wide_far[0])).astype(LOW),
+            both((wide_next[half:], wide_far[1])).astype(LOW),
+            both((wide_side[:half], wide_far[0])).astype(LOW),
         )
     else:
         wide_late = ()
         expand_sum = lax.psum_scatter(
-            expand_parts.reshape(width, -1), "fsdp", scatter_dimension=0, tiled=True
+            expand_whole, "fsdp", scatter_dimension=0, tiled=True
         ).astype(FULL)
     expand_keep, expand_send = halves(expand_sum, part_at)
     slope_second = jnp.concatenate(slope_second, axis=0)
@@ -766,76 +782,81 @@
     )
     if four:
         wide_late = near_rows_out(wide_late)
-    expand_rows = split_rows(both(expand_rows), clip_at, 2)
     joint_slope = jnp.concatenate(
         [grad[kind] for kind in range(3) for grad in (grad_first, grad_second)], axis=1
     )
+    expand_keep, expand_send = halves(both(expand_rows), clip_at)
+    joint_slope, expand_send = fence(joint_slope, expand_send)
+    expand_rows = (expand_keep, swap(expand_send, "ctx", 2))
     first_there = product(joint_slope, joint_full[width_half:], ROW_BY_ROW).astype(LOW)
     first_here = rows_product(joint_slope, joint_full[:width_half], "first_slope")
     first_half = both((first_here, swap(first_there, "tp", 1))).astype(LOW)
 
     if not four:
         wide_near = lax.psum_scatter(
-            wide.reshape(width, -1), "fsdp", scatter_dimension=0, tiled=True
+            jnp.concatenate(wide, axis=1), "fsdp", scatter_dimension=0, tiled=True
         )
-    first_half, joint_slope, expand_rows, wide_late = fence(
-        first_half, joint_slope, expand_rows, wide_late
-    )
+    first_half, joint_slope, expand_rows = fence(first_half, joint_slope, expand_rows)
     expand_rows = join_rows(both(expand_rows).astype(LOW), clip_at, 2)
     pieces = first_half.reshape(4, rows_here, width_half)
     passing = jnp.concatenate([pieces[1], pieces[3][:, :quarter], pieces[2][:, quarter:]], axis=1)
     passing = swap(passing, "ctx", 1)
     place = (shard if four else start) ^ (2 * core)
     joint_parts = grad_products([normed_mine, normed_other], joint_slope, place, order, "joint_grad")
-    if four:
-        near_sum = [both((wide_early[0], wide_late[1])), both((wide_late[0], wide_early[1]))]
-        wide_sum = wide[3].astype(FULL) + jnp.concatenate(near_sum, axis=0)
-    else:
-        wide_sum = wide_near.astype(FULL)
-    wide_keep, wide_send = halves(wide_sum, part_at)
-    joint_parts, wide_send = fence(joint_parts, wide_send)
-    joint_far = far_halves(joint_parts[0]) if four else ()
     slope_sums = jnp.sum(joint_slope.astype(FULL), axis=0)
     bias_sums = jnp.stack([slope_sums[:part_width], slope_sums[2 * part_width :]])
     joint_bias_grad = lax.dynamic_update_slice(
         jnp.zeros((2, features), FULL), bias_sums, (0, part_at * part_width)
     )
 
-    passing, joint_far = fence(passing, joint_far)
+    passing, joint_parts, wide_late, expand_rows = fence(
+        passing, joint_parts, wide_late, expand_rows
+    )
+    if four:
+        near_sum = [both((wide_early[0], wide_late[1])), both((wide_late[0], wide_early[1]))]
+        wide_sum = rows_at(wide, 0).astype(FULL) + jnp.concatenate(near_sum, axis=0)
+    else:
+        wide_sum = wide_near.astype(FULL)
+    wide_keep, wide_send = halves(wide_sum, part_at)
     own_half = both((pieces[0], passing[:, :width_half])).astype(LOW)
     to_left = both((pieces[2][:, :quarter], passing[:, width_half : width_half + quarter]))
     to_right = both((pieces[3][:, quarter:], passing[:, width_half + quarter :]))
-    joint_near = add_far(joint_parts[2], joint_parts[1], joint_far) if four else ()
-    to_left, to_right, own_half, wide_send, joint_near, activated = fence(
-        to_left.astype(LOW), to_right.astype(LOW), own_half, wide_send, joint_near, activated
+    to_left, to_right, own_half, wide_send, joint_parts, activated = fence(
+        to_left.astype(LOW), to_right.astype(LOW), own_half, wide_send, joint_parts, activated
     )
     other_half = jnp.concatenate([swap(to_left, "ctx", 2), swap(to_right, "ctx", 3)], axis=1)
     wide_rows = (wide_keep, swap(wide_send, "ctx", 1))
+    joint_far = far_halves(joint_parts[0]) if four else ()
+    reduce_part = reduce_output(activated, reduce_held, pieces_at)
+
+    other_half, joint_far, wide_rows, reduce_part = fence(
+        other_half, joint_far, wide_rows, reduce_part
+    )
+    slope_half = jnp.concatenate(swapped_if(clip_at, [own_half, other_half]), axis=0)
+    slope_other = swap(slope_half, "tp", 1)
+    slope_other, expand_rows = fence(slope_other, expand_rows)
+    expand_grad = join_rows(expand_rows, part_at, 1).astype(FULL)
+    first_slope = jnp.concatenate(swapped_if(core, [slope_half, slope_other]), axis=1)
+    wide_rows = split_rows(both(wide_rows), clip_at, 2)
+    reduce_swapped = swap(reduce_part, "tp", 1)
     if four:
-        joint_near = near_rows_out(joint_near)
+        joint_near = near_rows_out(add_far(joint_parts[2], joint_parts[1], joint_far))
     else:
         joint_near = lax.psum_scatter(
             joint_parts.reshape(width, -1), "fsdp", scatter_dimension=0, tiled=True
         )
-    reduce_part = reduce_output(activated, reduce_held, pieces_at)
-
-    other_half, joint_near, wide_rows, reduce_part, expand_rows = fence(
-        other_half, joint_near, wide_rows, reduce_part, expand_rows
-    )
-    slope_half = jnp.concatenate(swapped_if(clip_at, [own_half, other_half]), axis=0)
-    slope_other = swap(slope_half, "tp", 1)
-    first_slope = jnp.concatenate(swapped_if(core, [slope_half, slope_other]), axis=1)
-    wide_rows = split_rows(both(wide_rows), clip_at, 2)
-    reduce_swapped = swap(reduce_part, "tp", 1)
-    joint_sum = joint_parts[3].astype(FULL) + both(joint_near) if four else joint_near
-    joint_sum = joint_sum.astype(LOW)
-    joint_sum = (joint_sum, swap(joint_sum, "ctx", 2))
     tokens_grad, first_sums = by_rows(
         first_norm_back_kernel, "first_norm_back", [FULL], True,
         flat_tokens, first_slope, first_gain[None],
         cotangent.reshape(tokens_here, width), first_sum_back,
     )
-    first_sums, tokens_grad, reduce_swapped = fence(first_sums, tokens_grad, reduce_swapped)
+    first_sums, tokens_grad, reduce_swapped, joint_near, wide_rows = fence(
+        first_sums, tokens_grad, reduce_swapped, joint_near, wide_rows
+    )
+    joint_sum = joint_parts[3].astype(FULL) + both(joint_near) if four else joint_near
+    joint_sum = joint_sum.astype(LOW)
+    joint_sum = (joint_sum, swap(joint_sum, "ctx", 2))
+    wide_rows = join_rows(both(wide_rows).astype(LOW), clip_at, 2)
     vectors = [
         first_sums[0],
         first_sums[1],
@@ -867,11 +888,9 @@
     joint_grad = jnp.concatenate(
         [piece.reshape(-1, 3, part_width) for piece in joint_parts], axis=2
     ).astype(FULL)
-    wide_rows = join_rows(both(wide_rows).astype(LOW), clip_at, 2)
     wide_rows = join_rows(wide_rows, part_at, 1).astype(FULL)
     reduce_grad = wide_rows[:, : activated.shape[1]]
     mixer_grad = wide_rows[:, activated.shape[1] :]
-    expand_grad = join_rows(expand_rows, part_at, 1).astype(FULL)
     packed = packed.reshape(-1)
     shares = []
     start = 0

time: 415 us -> 424 us (1.022)
  waiting for transfers between devices: 120 us -> 138 us
  Pallas kernels: 119 us -> 104 us
  matrix products: 5.78 us -> 19 us
  local copies, waits for them, and re-layouts: 52.4 us -> 45.8 us
  other arithmetic: 34.2 us -> 28.7 us
  starting transfers between devices: 76.3 us -> 81.3 us
    ppermute x67, waiting for transfers between devices: 120 us -> 138 us  [swap(): return lax.ppermute(value, axis, [(i, i ^ distance) for i in range(size)])]
    pallas_call x4 -> x1, Pallas kernels: 20.9 us -> 5.86 us  [grad_products(): pl.pallas_call(lambda *refs: grad_kernel(distances, *refs), grid_spec=plt...]
    dot_general x3 -> x6, matrix products: 5.78 us -> 19 us  [product(): return lax.dot_general(left, right, dims, preferred_element_type=FULL)]
    unnamed x202 -> x174, local copies, waits for them, and re-layouts: 27.9 us -> 20.2 us
    ppermute x67, starting transfers between devices: 76.3 us -> 81.3 us  [swap(): return lax.ppermute(value, axis, [(i, i ^ distance) for i in range(size)])]
  transfers between devices with their start and end apart: 67 -> 67, of which waited for: 28 -> 25; matrix products, arithmetic and copies ran while one was open for 12% -> 13% of each run, Pallas kernels for 24% -> 20%
where the time goes in v2:
time: 424 us; the launch traced here: 420 us
  waiting for transfers between devices  138 us (33%)
  Pallas kernels  104 us (25%)
  starting transfers between devices  81.3 us (19%)
  local copies, waits for them, and re-layouts  45.8 us (11%)
  other arithmetic  28.7 us (7%)
  matrix products  19 us (4%)
    ppermute x67, waiting for transfers between devices, swap(): return lax.ppermute(value, axis, [(i, i ^ distance) for i in range(size)])  138 us
    ppermute x67, starting transfers between devices, swap(): return lax.ppermute(value, axis, [(i, i ^ distance) for i in range(size)])  81.3 us
    pallas_call x2, Pallas kernels, attention_backward(): pl.pallas_call(attention_backward_kernel, grid=(1,), in_specs=[pl.BlockSp...  31.5 us
    unnamed x174, local copies, waits for them, and re-layouts  20.2 us
    pallas_call x4, Pallas kernels, by_rows(): pl.pallas_call(kernel, grid=(count // chunk,), in_specs=in_specs, out_spe...  19.6 us
    dot_general x6, matrix products, product(): return lax.dot_general(left, right, dims, preferred_element_type=FULL)  19 us
    pallas_call x1, Pallas kernels, feed_forward(): pl.pallas_call(lambda *refs: feed_forward_kernel(len(reduce), *refs), gri...  18.6 us
    pallas_call x2, Pallas kernels, attention_forward(): pl.pallas_call(attention_forward_kernel, grid=(1,), in_specs=[pl.BlockSpe...  14.6 us
  transfers between devices with their start and end apart: 67, of which 25 were waited for; matrix products, arithmetic and copies ran while one was open for 13% of the time, Pallas kernels for 20%

profile of v2, /device:TPU:0, one launch (start us, length us, event | category | flops | bytes accessed | tf_op | source)
XLA Modules:
  0.0 419.5 jit_solution(708657295114094045)
XLA Ops:
  7.8 3.0 collective-permute-start.3
  16.7 11.3 %collective-permute-done.1 = bf16[392,256]{1,0:T(8,128)(2,1)S(1)} collective-permute-done((bf16[392,256]{1,0:T(8,128)(2,1)S(1)}, bf16[392,256]{1,0:T(8,128)(2,1)S(1)}, u32[]{:S(2)}, u32[]{:S(2)}) %collective-permute-start.1) | collective-permute-done | bytes 200736 | tf_op jit(solution)/shard_map/ppermute | solution.py:457
  28.0 5.5 %collective-permute-done.2 = bf16[392,256]{1,0:T(8,128)(2,1)S(1)} collective-permute-done((bf16[392,256]{1,0:T(8,128)(2,1)S(1)}, bf16[392,256]{1,0:T(8,128)(2,1)S(1)}, u32[]{:S(2)}, u32[]{:S(2)}) %collective-permute-start.2) | collective-permute-done | bytes 200736 | tf_op jit(solution)/shard_map/ppermute | solution.py:457
  40.6 6.2 %collective-permute-done.6 = bf16[128,1280]{1,0:T(8,128)(2,1)} collective-permute-done((bf16[128,1280]{1,0:T(8,128)(2,1)}, bf16[128,1280]{1,0:T(8,128)(2,1)}, u32[]{:S(2)}, u32[]{:S(2)}) %collective-permute-start.6) | collective-permute-done | bytes 327712 | tf_op jit(solution)/shard_map/ppermute | solution.py:457
  56.7 3.1 joint_projection.1.q_ref.k_ref.v_ref
  61.0 7.2 %attention_forward.2 = (bf16[1568,128]{1,0:T(8,128)(2,1)S(1)}, f32[8,1568]{1,0:T(8,128)S(1)}) custom-call(bf16[1568,768]{1,0:T(8,128)(2,1)S(1)} %joint_projection.1.q_ref.k_ref.v_ref, bf16[1568,768]{1,0:T(8,128)(2,1)S(1)} %joint_projection.1.q_ref.k_ref.v_ref, bf16[1568,768]{1,0:T(8,128)(2,1)S(1)} %joint_projection.1.q_ref.k_ref.v_ref), custom_call_target="tpu_custom_call" | custom-call | tf_op jit(solution)/shard_map/attention_forward/pallas_call | solution.py:240
  75.5 7.4 %attention_forward.3 = (bf16[1568,128]{1,0:T(8,128)(2,1)S(1)}, f32[8,1568]{1,0:T(8,128)S(1)}) custom-call(bf16[1568,768]{1,0:T(8,128)(2,1)S(1)} %joint_projection.1.q_ref.k_ref.v_ref, bf16[1568,768]{1,0:T(8,128)(2,1)S(1)} %joint_projection.1.q_ref.k_ref.v_ref, bf16[1568,768]{1,0:T(8,128)(2,1)S(1)} %joint_projection.1.q_ref.k_ref.v_ref), custom_call_target="tpu_custom_call" | custom-call | tf_op jit(solution)/shard_map/attention_forward/pallas_call | solution.py:240
  83.0 5.3 %collective-permute-done.14.refs_10_.refs_1_ = bf16[256,2048]{1,0:T(8,128)(2,1)S(1)} collective-permute-done((bf16[256,2048]{1,0:T(8,128)(2,1)S(1)}, bf16[256,2048]{1,0:T(8,128)(2,1)S(1)}, u32[]{:S(2)}, u32[]{:S(2)}) %collective-permute-start.14) | collective-permute-done | bytes 1048608 | tf_op jit(solution)/shard_map/ppermute | solution.py:457
  100.6 2.9 collective-permute-done.17
  112.5 5.6 %second_norm.1.refs_1_ = bf16[784,1024]{1,0:T(8,128)(2,1)S(1)} custom-call(bf16[784,1024]{1,0:T(8,128)(2,1)S(1)} %bitcast.78, bf16[784,1024]{1,0:T(8,128)(2,1)} %convolution_convert_fusion.3.one_ref, bf16[784,1024]{1,0:T(8,128)(2,1)} %collective-permute-done.21.two_ref, f32[1,1024]{1,0:T(1,128)S(1)} %bitcast.86, f32[1,1024]{1,0:T(1,128)S(1)} %bitcast.90, ...), custom_call_target="tpu_custom_call" | custom-call | tf_op jit(solution)/shard_map/second_norm/pallas_call | solution.py:104
  119.3 3.4 collective-permute-done.22.refs_12_.refs_3_
  123.1 18.6 %feed_forward.1 = (bf16[784,2048]{1,0:T(8,128)(2,1)}, bf16[784,2048]{1,0:T(8,128)(2,1)}, bf16[784,1024]{1,0:T(8,128)(2,1)}, f32[1,2048]{1,0:T(1,128)S(1)}) custom-call(s32[5]{0:T(128)S(1)} %multiply_add_fusion.refs_0_.place_ref, bf16[784,1024]{1,0:T(8,128)(2,1)} %copy-done.14, bf16[784,1024]{1,0:T(8,128)(2,1)} %bitcast.81, f32[1,2048]{1,0:T(1,128)S(1)} %bitcast.92, ...), custom_call_target="tpu_custom_call" | custom-call | tf_op jit(solution)/shard_map/feed_forward/pallas_call | solution.py:387
  141.9 7.0 %convolution_convert_fusion.1 = bf16[1024,2048]{1,0:T(8,128)(2,1)S(1)} fusion(bf16[784,1024]{1,0:T(8,128)(2,1)} %copy-done.14, bf16[784,2048]{1,0:T(8,128)(2,1)} %get-tuple-element.241), kind=kOutput, calls=%fused_computation.2 | convolution fusion | flops 3290431488 | bytes 9011200 | tf_op jit(solution)/shard_map/dot_general | solution.py:19
  152.3 7.4 %second_norm_back.1 = (bf16[784,1024]{1,0:T(8,128)(2,1)S(1)}, f32[784,1024]{1,0:T(8,128)S(1)}, f32[8,1024]{1,0:T(8,128)S(1)}) custom-call(bf16[784,1024]{1,0:T(8,128)(2,1)S(1)} %bitcast.79, bf16[784,1024]{1,0:T(8,128)(2,1)} %convolution_convert_fusion.3.one_ref, bf16[784,1024]{1,0:T(8,128)(2,1)} %collective-permute-done.21.two_ref, f32[1,1024]{1,0:T(1,128)S(1)} %bitcast.87, ...), custom_call_target="tpu_custom_call" | custom-call | tf_op jit(solution)/shard_map/second_norm_back/pallas_call | solution.py:104
  173.9 5.0 %convolution_convert_fusion = bf16[1024,2048]{1,0:T(8,128)(2,1)S(1)} fusion(bf16[784,1024]{1,0:T(8,128)(2,1)S(1)} %bitcast.83, bf16[784,2048]{1,0:T(8,128)(2,1)S(1)} %copy-done.20), kind=kOutput, calls=%fused_computation.1 | convolution fusion | flops 3290431488 | bytes 9011200 | tf_op jit(solution)/shard_map/dot_general | solution.py:19
  183.3 10.1 %collective-permute-done.30 = bf16[256,2048]{1,0:T(8,128)(2,1)S(1)} collective-permute-done((bf16[256,2048]{1,0:T(8,128)(2,1)S(1)}, bf16[256,2048]{1,0:T(8,128)(2,1)S(1)}, u32[]{:S(2)}, u32[]{:S(2)}) %collective-permute-start.30) | collective-permute-done | bytes 1048608 | tf_op jit(solution)/shard_map/ppermute | solution.py:457
  204.0 15.7 %attention_backward.2 = (bf16[1568,128]{1,0:T(8,128)(2,1)S(1)}, bf16[1568,128]{1,0:T(8,128)(2,1)S(1)}, bf16[1568,128]{1,0:T(8,128)(2,1)S(1)}) custom-call(bf16[1568,768]{1,0:T(8,128)(2,1)S(1)} %joint_projection.1.q_ref.k_ref.v_ref, bf16[1568,768]{1,0:T(8,128)(2,1)S(1)} %joint_projection.1.q_ref.k_ref.v_ref, ...), custom_call_target="tpu_custom_call" | custom-call | tf_op jit(solution)/shard_map/attention_backward/pallas_call | solution.py:313
  225.2 15.9 %attention_backward.3 = (bf16[1568,128]{1,0:T(8,128)(2,1)S(1)}, bf16[1568,128]{1,0:T(8,128)(2,1)S(1)}, bf16[1568,128]{1,0:T(8,128)(2,1)S(1)}) custom-call(bf16[1568,768]{1,0:T(8,128)(2,1)S(1)} %joint_projection.1.q_ref.k_ref.v_ref, bf16[1568,768]{1,0:T(8,128)(2,1)S(1)} %joint_projection.1.q_ref.k_ref.v_ref, ...), custom_call_target="tpu_custom_call" | custom-call | tf_op jit(solution)/shard_map/attention_backward/pallas_call | solution.py:313
  250.7 3.1 first_slope.1
  261.2 7.9 %collective-permute-done.41 = bf16[64,2048]{1,0:T(8,128)(2,1)S(1)} collective-permute-done((bf16[64,2048]{1,0:T(8,128)(2,1)S(1)}, bf16[64,2048]{1,0:T(8,128)(2,1)S(1)}, u32[]{:S(2)}, u32[]{:S(2)}) %collective-permute-start.41) | collective-permute-done | bytes 262176 | tf_op jit(solution)/shard_map/ppermute | solution.py:457
  272.3 5.9 %joint_grad.1 = bf16[4,256,768]{2,1,0:T(8,128)(2,1)S(1)} custom-call(s32[1]{0:T(128)} %bitcast.21.refs_0_, bf16[1568,512]{1,0:T(8,128)(2,1)S(1)} %copy-done.6, bf16[1568,512]{1,0:T(8,128)(2,1)S(1)} %copy-done.8, bf16[1568,768]{1,0:T(8,128)(2,1)} %copy-done.4), custom_call_target="tpu_custom_call" | custom-call | tf_op jit(solution)/shard_map/joint_grad/pallas_call | solution.py:188
  278.2 14.1 %collective-permute-done.45 = bf16[64,2048]{1,0:T(8,128)(2,1)S(1)} collective-permute-done((bf16[64,2048]{1,0:T(8,128)(2,1)S(1)}, bf16[64,2048]{1,0:T(8,128)(2,1)S(1)}, u32[]{:S(2)}, u32[]{:S(2)}) %collective-permute-start.45) | collective-permute-done | bytes 262176 | tf_op jit(solution)/shard_map/ppermute | solution.py:457
  305.8 7.5 %reduce_output.1 = bf16[784,1024]{1,0:T(8,128)(2,1)S(1)} custom-call(s32[5]{0:T(128)S(1)} %multiply_add_fusion.refs_0_.place_ref, bf16[784,2048]{1,0:T(8,128)(2,1)S(1)} %copy-done.21, bf16[256,2048]{1,0:T(8,128)(2,1)S(1)} %copy-done.17, bf16[256,2048]{1,0:T(8,128)(2,1)S(1)} %collective-permute-done.14.refs_10_.refs_1_, ...), custom_call_target="tpu_custom_call" | custom-call | tf_op jit(solution)/shard_map/reduce_output/pallas_call | solution.py:437
  313.3 4.7 %collective-permute-done.46 = bf16[392,256]{1,0:T(8,128)(2,1)S(1)} collective-permute-done((bf16[392,256]{1,0:T(8,128)(2,1)S(1)}, bf16[392,256]{1,0:T(8,128)(2,1)S(1)}, u32[]{:S(2)}, u32[]{:S(2)}) %collective-permute-start.46) | collective-permute-done | bytes 200736 | tf_op jit(solution)/shard_map/ppermute | solution.py:457
  318.1 6.2 %collective-permute-done.50 = bf16[128,2560]{1,0:T(8,128)(2,1)S(1)} collective-permute-done((bf16[128,2560]{1,0:T(8,128)(2,1)S(1)}, bf16[128,2560]{1,0:T(8,128)(2,1)S(1)}, u32[]{:S(2)}, u32[]{:S(2)}) %collective-permute-start.50) | collective-permute-done | bytes 655392 | tf_op jit(solution)/shard_map/ppermute | solution.py:457
  333.8 4.9 %first_norm_back.1 = (f32[784,1024]{1,0:T(8,128)}, f32[8,1024]{1,0:T(8,128)S(1)}) custom-call(bf16[784,1024]{1,0:T(8,128)(2,1)S(1)} %bitcast.80, bf16[784,1024]{1,0:T(8,128)(2,1)S(1)} %pad_maximum_fusion.1.upstream_ref, f32[1,1024]{1,0:T(1,128)S(1)} %bitcast.89, bf16[784,1024]{1,0:T(8,128)(2,1)S(1)} %bitcast.84, f32[784,1024]{1,0:T(8,128)S(1)} %copy-done.19), custom_call_target="tpu_custom_call" | custom-call | tf_op jit(solution)/shard_map/first_norm_back/pallas_call | solution.py:104
  338.7 9.1 %collective-permute-done.66 = bf16[128,2048]{1,0:T(8,128)(2,1)S(1)} collective-permute-done((bf16[128,2048]{1,0:T(8,128)(2,1)S(1)}, bf16[128,2048]{1,0:T(8,128)(2,1)S(1)}, u32[]{:S(2)}, u32[]{:S(2)}) %collective-permute-start.66) | collective-permute-done | bytes 524320 | tf_op jit(solution)/shard_map/ppermute | solution.py:457
  354.3 3.0 collective-permute-start.60
  357.2 3.5 add_add_fusion
  362.5 24.8 %collective-permute-done.60 = bf16[64,2560]{1,0:T(8,128)(2,1)S(1)} collective-permute-done((bf16[64,2560]{1,0:T(8,128)(2,1)S(1)}, bf16[64,2560]{1,0:T(8,128)(2,1)S(1)}, u32[]{:S(2)}, u32[]{:S(2)}) %collective-permute-start.60) | collective-permute-done | bytes 327712 | tf_op jit(solution)/shard_map/ppermute | solution.py:457
  396.5 6.8 %collective-permute-done.64 = bf16[256,768]{1,0:T(8,128)(2,1)S(1)} collective-permute-done((bf16[256,768]{1,0:T(8,128)(2,1)S(1)}, bf16[256,768]{1,0:T(8,128)(2,1)S(1)}, u32[]{:S(2)}, u32[]{:S(2)}) %collective-permute-start.64) | collective-permute-done | bytes 393248 | tf_op jit(solution)/shard_map/ppermute | solution.py:457
  405.5 9.9 %collective-permute-done.65 = bf16[128,2560]{1,0:T(8,128)(2,1)} collective-permute-done((bf16[128,2560]{1,0:T(8,128)(2,1)S(1)}, bf16[128,2560]{1,0:T(8,128)(2,1)}, u32[]{:S(2)}, u32[]{:S(2)}) %collective-permute-start.65) | collective-permute-done | bytes 655392 | tf_op jit(solution)/shard_map/ppermute | solution.py:457
  (411 shorter events, 165.3 us)
Async XLA Ops:
  7.8 25.7 %collective-permute-start.3 = (bf16[256,1280]{1,0:T(8,128)(2,1)S(1)}, bf16[256,1280]{1,0:T(8,128)(2,1)S(1)}, u32[]{:S(2)}, u32[]{:S(2)}) collective-permute-start(bf16[256,1280]{1,0:T(8,128)(2,1)S(1)} %pad_maximum_fusion.11), channel_id=1, source_target_pairs={{0,8},{8,0},{16,24},{24,16},{1,9},{9,1},{17,25},{25,17},{2,10},{10... | collective-permute-start | bytes 1966088 | tf_op jit(solution)/shard_map/ppermute | solution.py:457
  10.8 22.7 %collective-permute-start.4 = (bf16[256,1280]{1,0:T(8,128)(2,1)S(1)}, bf16[256,1280]{1,0:T(8,128)(2,1)S(1)}, u32[]{:S(2)}, u32[]{:S(2)}) collective-permute-start(bf16[256,1280]{1,0:T(8,128)(2,1)S(1)} %pad_maximum_fusion.11), channel_id=1, source_target_pairs={{0,16},{8,24},{16,0},{24,8},{1,17},{9,25},{17,1},{25,9},{2,18},{10... | collective-permute-start | bytes 1966088 | tf_op jit(solution)/shard_map/ppermute | solution.py:457
  12.3 21.2 %collective-permute-start = (bf16[392,512]{1,0:T(8,128)(2,1)S(1)}, bf16[392,512]{1,0:T(8,128)(2,1)S(1)}, u32[]{:S(2)}, u32[]{:S(2)}) collective-permute-start(bf16[392,512]{1,0:T(8,128)(2,1)S(1)} %get-tuple-element.181), channel_id=1, source_target_pairs={{0,2},{2,0},{4,6},{6,4},{1,3},{3,1},{5,7},{7,5},{8,10},{10,8},{12,... | collective-permute-start | bytes 1204232 | tf_op jit(solution)/shard_map/ppermute | solution.py:457
  37.6 31.7 %collective-permute-start.9 = (bf16[256,2048]{1,0:T(8,128)(2,1)}, bf16[256,2048]{1,0:T(8,128)(2,1)S(1)}, u32[]{:S(2)}, u32[]{:S(2)}) collective-permute-start(bf16[256,2048]{1,0:T(8,128)(2,1)} %refs_4_), channel_id=1, source_target_pairs={{0,8},{8,0},{16,24},{24,16},{1,9},{9,1},{17,25},{25,17},{2,10},{10... | collective-permute-start | bytes 3145736 | tf_op jit(solution)/shard_map/ppermute | solution.py:457
  39.1 31.3 %collective-permute-start.10 = (bf16[256,2048]{1,0:T(8,128)(2,1)}, bf16[256,2048]{1,0:T(8,128)(2,1)S(1)}, u32[]{:S(2)}, u32[]{:S(2)}) collective-permute-start(bf16[256,2048]{1,0:T(8,128)(2,1)} %refs_4_), channel_id=1, source_target_pairs={{0,16},{8,24},{16,0},{24,8},{1,17},{9,25},{17,1},{25,9},{2,18},{10... | collective-permute-start | bytes 3145736 | tf_op jit(solution)/shard_map/ppermute | solution.py:457
  53.3 35.0 %collective-permute-start.14 = (bf16[256,2048]{1,0:T(8,128)(2,1)S(1)}, bf16[256,2048]{1,0:T(8,128)(2,1)S(1)}, u32[]{:S(2)}, u32[]{:S(2)}) collective-permute-start(bf16[256,2048]{1,0:T(8,128)(2,1)S(1)} %copy-done.15), channel_id=1, source_target_pairs={{0,8},{8,0},{16,24},{24,16},{1,9},{9,1},{17,25},{25,17},{2,10},{10... | collective-permute-start | bytes 3145736 | tf_op jit(solution)/shard_map/ppermute | solution.py:457
  54.8 34.6 %collective-permute-start.15 = (bf16[256,2048]{1,0:T(8,128)(2,1)S(1)}, bf16[256,2048]{1,0:T(8,128)(2,1)}, u32[]{:S(2)}, u32[]{:S(2)}) collective-permute-start(bf16[256,2048]{1,0:T(8,128)(2,1)S(1)} %copy-done.15), channel_id=1, source_target_pairs={{0,16},{8,24},{16,0},{24,8},{1,17},{9,25},{17,1},{25,9},{2,18},{10... | collective-permute-start | bytes 3145736 | tf_op jit(solution)/shard_map/ppermute | solution.py:457
  169.8 23.6 %collective-permute-start.30 = (bf16[256,2048]{1,0:T(8,128)(2,1)S(1)}, bf16[256,2048]{1,0:T(8,128)(2,1)S(1)}, u32[]{:S(2)}, u32[]{:S(2)}) collective-permute-start(bf16[256,2048]{1,0:T(8,128)(2,1)S(1)} %pad_maximum_fusion.3), channel_id=1, source_target_pairs={{0,8},{8,0},{16,24},{24,16},{1,9},{9,1},{17,25},{25,17},{2,10},{10... | collective-permute-start | bytes 3145736 | tf_op jit(solution)/shard_map/ppermute | solution.py:457
  170.3 23.4 %collective-permute-start.31 = (bf16[256,2048]{1,0:T(8,128)(2,1)S(1)}, bf16[256,2048]{1,0:T(8,128)(2,1)S(1)}, u32[]{:S(2)}, u32[]{:S(2)}) collective-permute-start(bf16[256,2048]{1,0:T(8,128)(2,1)S(1)} %pad_maximum_fusion.4), channel_id=1, source_target_pairs={{0,16},{8,24},{16,0},{24,8},{1,17},{9,25},{17,1},{25,9},{2,18},{10... | collective-permute-start | bytes 3145736 | tf_op jit(solution)/shard_map/ppermute | solution.py:457
  193.7 26.0 %collective-permute-start.32 = (bf16[392,128]{1,0:T(8,128)(2,1)}, bf16[392,128]{1,0:T(8,128)(2,1)S(1)}, u32[]{:S(2)}, u32[]{:S(2)}) collective-permute-start(bf16[392,128]{1,0:T(8,128)(2,1)} %get-tuple-element.268), channel_id=1, source_target_pairs={{0,2},{2,0},{4,6},{6,4},{1,3},{3,1},{5,7},{7,5},{8,10},{10,8},{12,... | collective-permute-start | bytes 301064 | tf_op jit(solution)/shard_map/ppermute | solution.py:457
  194.4 25.3 %collective-permute-start.33 = (bf16[392,128]{1,0:T(8,128)(2,1)}, bf16[392,128]{1,0:T(8,128)(2,1)S(1)}, u32[]{:S(2)}, u32[]{:S(2)}) collective-permute-start(bf16[392,128]{1,0:T(8,128)(2,1)} %get-tuple-element.269), channel_id=1, source_target_pairs={{0,4},{2,6},{4,0},{6,2},{1,5},{3,7},{5,1},{7,3},{8,12},{10,14},{12... | collective-permute-start | bytes 301064 | tf_op jit(solution)/shard_map/ppermute | solution.py:457
  196.0 23.7 %collective-permute-start.34 = (bf16[392,128]{1,0:T(8,128)(2,1)}, bf16[392,128]{1,0:T(8,128)(2,1)S(1)}, u32[]{:S(2)}, u32[]{:S(2)}) collective-permute-start(bf16[392,128]{1,0:T(8,128)(2,1)} %get-tuple-element.270), channel_id=1, source_target_pairs={{0,6},{2,4},{4,2},{6,0},{1,7},{3,5},{5,3},{7,1},{8,14},{10,12},{12... | collective-permute-start | bytes 301064 | tf_op jit(solution)/shard_map/ppermute | solution.py:457
  198.1 21.7 %collective-permute-start.35 = (bf16[128,2560]{1,0:T(8,128)(2,1)}, bf16[128,2560]{1,0:T(8,128)(2,1)S(1)}, u32[]{:S(2)}, u32[]{:S(2)}) collective-permute-start(bf16[128,2560]{1,0:T(8,128)(2,1)} %get-tuple-element.271), channel_id=1, source_target_pairs={{0,8},{8,0},{16,24},{24,16},{1,9},{9,1},{17,25},{25,17},{2,10},{10... | collective-permute-start | bytes 1966088 | tf_op jit(solution)/shard_map/ppermute | solution.py:457
  199.5 20.2 %collective-permute-start.36 = (bf16[128,2560]{1,0:T(8,128)(2,1)S(1)}, bf16[128,2560]{1,0:T(8,128)(2,1)S(1)}, u32[]{:S(2)}, u32[]{:S(2)}) collective-permute-start(bf16[128,2560]{1,0:T(8,128)(2,1)S(1)} %get-tuple-element.272), channel_id=1, source_target_pairs={{0,16},{8,24},{16,0},{24,8},{1,17},{9,25},{17,1},{25,9},{2,18},{10... | collective-permute-start | bytes 1966088 | tf_op jit(solution)/shard_map/ppermute | solution.py:457
  222.7 18.5 %collective-permute-start.38 = (bf16[128,2560]{1,0:T(8,128)(2,1)}, bf16[128,2560]{1,0:T(8,128)(2,1)}, u32[]{:S(2)}, u32[]{:S(2)}) collective-permute-start(bf16[128,2560]{1,0:T(8,128)(2,1)} %fusion.5), channel_id=1, source_target_pairs={{0,8},{8,0},{16,24},{24,16},{1,9},{9,1},{17,25},{25,17},{2,10},{10... | collective-permute-start | bytes 1966088 | tf_op jit(solution)/shard_map/ppermute | solution.py:457
  256.2 36.2 %collective-permute-start.43 = (bf16[128,2560]{1,0:T(8,128)(2,1)S(1)}, bf16[128,2560]{1,0:T(8,128)(2,1)S(1)}, u32[]{:S(2)}, u32[]{:S(2)}) collective-permute-start(bf16[128,2560]{1,0:T(8,128)(2,1)S(1)} %copy-done.64), channel_id=1, source_target_pairs={{0,8},{8,0},{16,24},{24,16},{1,9},{9,1},{17,25},{25,17},{2,10},{10... | collective-permute-start | bytes 1966088 | tf_op jit(solution)/shard_map/ppermute | solution.py:457
  257.6 34.8 %collective-permute-start.44 = (bf16[128,2560]{1,0:T(8,128)(2,1)S(1)}, bf16[128,2560]{1,0:T(8,128)(2,1)S(1)}, u32[]{:S(2)}, u32[]{:S(2)}) collective-permute-start(bf16[128,2560]{1,0:T(8,128)(2,1)S(1)} %copy-done.65), channel_id=1, source_target_pairs={{0,16},{8,24},{16,0},{24,8},{1,17},{9,25},{17,1},{25,9},{2,18},{10... | collective-permute-start | bytes 1966088 | tf_op jit(solution)/shard_map/ppermute | solution.py:457
  269.3 25.2 %collective-permute-start.42 = (bf16[392,1024]{1,0:T(8,128)(2,1)S(1)}, bf16[392,1024]{1,0:T(8,128)(2,1)S(1)}, u32[]{:S(2)}, u32[]{:S(2)}) collective-permute-start(bf16[392,1024]{1,0:T(8,128)(2,1)S(1)} %pad_maximum_fusion.6), channel_id=1, source_target_pairs={{0,2},{2,0},{4,6},{6,4},{1,3},{3,1},{5,7},{7,5},{8,10},{10,8},{12,... | collective-permute-start | bytes 2408456 | tf_op jit(solution)/shard_map/ppermute | solution.py:457
  269.4 22.9 %collective-permute-start.45 = (bf16[64,2048]{1,0:T(8,128)(2,1)S(1)}, bf16[64,2048]{1,0:T(8,128)(2,1)S(1)}, u32[]{:S(2)}, u32[]{:S(2)}) collective-permute-start(bf16[64,2048]{1,0:T(8,128)(2,1)S(1)} %add_convert_fusion.9), channel_id=1, source_target_pairs={{0,4},{2,6},{4,0},{6,2},{1,5},{3,7},{5,1},{7,3},{8,12},{10,14},{12... | collective-permute-start | bytes 786440 | tf_op jit(solution)/shard_map/ppermute | solution.py:457
  300.0 18.0 %collective-permute-start.46 = (bf16[392,256]{1,0:T(8,128)(2,1)S(1)}, bf16[392,256]{1,0:T(8,128)(2,1)S(1)}, u32[]{:S(2)}, u32[]{:S(2)}) collective-permute-start(bf16[392,256]{1,0:T(8,128)(2,1)S(1)} %get-tuple-element.314), channel_id=1, source_target_pairs={{0,4},{2,6},{4,0},{6,2},{1,5},{3,7},{5,1},{7,3},{8,12},{10,14},{12... | collective-permute-start | bytes 602120 | tf_op jit(solution)/shard_map/ppermute | solution.py:457
  301.0 23.3 %collective-permute-start.50 = (bf16[128,2560]{1,0:T(8,128)(2,1)S(1)}, bf16[128,2560]{1,0:T(8,128)(2,1)S(1)}, u32[]{:S(2)}, u32[]{:S(2)}) collective-permute-start(bf16[128,2560]{1,0:T(8,128)(2,1)S(1)} %dynamic-slice_convert_fusion), channel_id=1, source_target_pairs={{0,2},{2,0},{4,6},{6,4},{1,3},{3,1},{5,7},{7,5},{8,10},{10,8},{12,... | collective-permute-start | bytes 1966088 | tf_op jit(solution)/shard_map/ppermute | solution.py:457
  324.5 24.9 %collective-permute-start.52 = (bf16[784,1024]{1,0:T(8,128)(2,1)S(1)}, bf16[784,1024]{1,0:T(8,128)(2,1)S(1)}, u32[]{:S(2)}, u32[]{:S(2)}) collective-permute-start(bf16[784,1024]{1,0:T(8,128)(2,1)S(1)} %reduce_output.1), channel_id=1, source_target_pairs={{0,1},{1,0},{2,3},{3,2},{4,5},{5,4},{6,7},{7,6},{8,9},{9,8},{10,11... | collective-permute-start | bytes 4816904 | tf_op jit(solution)/shard_map/ppermute | solution.py:457
  325.1 24.2 %collective-permute-start.53 = (bf16[256,768]{1,0:T(8,128)(2,1)S(1)}, bf16[256,768]{1,0:T(8,128)(2,1)S(1)}, u32[]{:S(2)}, u32[]{:S(2)}) collective-permute-start(bf16[256,768]{1,0:T(8,128)(2,1)S(1)} %pad_maximum_fusion.18), channel_id=1, source_target_pairs={{0,8},{8,0},{16,24},{24,16},{1,9},{9,1},{17,25},{25,17},{2,10},{10... | collective-permute-start | bytes 1179656 | tf_op jit(solution)/shard_map/ppermute | solution.py:457
  326.9 20.9 %collective-permute-start.66 = (bf16[128,2048]{1,0:T(8,128)(2,1)S(1)}, bf16[128,2048]{1,0:T(8,128)(2,1)S(1)}, u32[]{:S(2)}, u32[]{:S(2)}) collective-permute-start(bf16[128,2048]{1,0:T(8,128)(2,1)S(1)} %maximum_select_fusion.3), channel_id=1, source_target_pairs={{0,2},{2,0},{4,6},{6,4},{1,3},{3,1},{5,7},{7,5},{8,10},{10,8},{12,... | collective-permute-start | bytes 1572872 | tf_op jit(solution)/shard_map/ppermute | solution.py:457
  327.0 22.4 %collective-permute-start.54 = (bf16[256,768]{1,0:T(8,128)(2,1)S(1)}, bf16[256,768]{1,0:T(8,128)(2,1)S(1)}, u32[]{:S(2)}, u32[]{:S(2)}) collective-permute-start(bf16[256,768]{1,0:T(8,128)(2,1)S(1)} %pad_maximum_fusion.19), channel_id=1, source_target_pairs={{0,16},{8,24},{16,0},{24,8},{1,17},{9,25},{17,1},{25,9},{2,18},{10... | collective-permute-start | bytes 1179656 | tf_op jit(solution)/shard_map/ppermute | solution.py:457
  328.6 20.8 %collective-permute-start.55 = (bf16[64,2560]{1,0:T(8,128)(2,1)S(1)}, bf16[64,2560]{1,0:T(8,128)(2,1)S(1)}, u32[]{:S(2)}, u32[]{:S(2)}) collective-permute-start(bf16[64,2560]{1,0:T(8,128)(2,1)S(1)} %dynamic-slice_convert_fusion.2), channel_id=1, source_target_pairs={{0,4},{2,6},{4,0},{6,2},{1,5},{3,7},{5,1},{7,3},{8,12},{10,14},{12... | collective-permute-start | bytes 983048 | tf_op jit(solution)/shard_map/ppermute | solution.py:457
  349.5 38.0 %collective-permute-start.56 = (f32[72,128]{1,0:T(8,128)S(1)}, f32[72,128]{1,0:T(8,128)S(1)}, u32[]{:S(2)}, u32[]{:S(2)}) collective-permute-start(f32[72,128]{1,0:T(8,128)S(1)} %bitcast.99), channel_id=1, source_target_pairs={{0,2},{2,0},{4,6},{6,4},{1,3},{3,1},{5,7},{7,5},{8,10},{10,8},{12,... | collective-permute-start | bytes 110600 | tf_op jit(solution)/shard_map/ppermute | solution.py:457
  349.6 37.9 %collective-permute-start.57 = (f32[72,128]{1,0:T(8,128)S(1)}, f32[72,128]{1,0:T(8,128)S(1)}, u32[]{:S(2)}, u32[]{:S(2)}) collective-permute-start(f32[72,128]{1,0:T(8,128)S(1)} %bitcast.100), channel_id=1, source_target_pairs={{0,4},{2,6},{4,0},{6,2},{1,5},{3,7},{5,1},{7,3},{8,12},{10,14},{12... | collective-permute-start | bytes 110600 | tf_op jit(solution)/shard_map/ppermute | solution.py:457
  351.9 35.6 %collective-permute-start.58 = (f32[72,128]{1,0:T(8,128)S(1)}, f32[72,128]{1,0:T(8,128)S(1)}, u32[]{:S(2)}, u32[]{:S(2)}) collective-permute-start(f32[72,128]{1,0:T(8,128)S(1)} %bitcast.101), channel_id=1, source_target_pairs={{0,6},{2,4},{4,2},{6,0},{1,7},{3,5},{5,3},{7,1},{8,14},{10,12},{12... | collective-permute-start | bytes 110600 | tf_op jit(solution)/shard_map/ppermute | solution.py:457
  354.1 33.4 %collective-permute-start.59 = (bf16[256,768]{1,0:T(8,128)(2,1)S(1)}, bf16[256,768]{1,0:T(8,128)(2,1)S(1)}, u32[]{:S(2)}, u32[]{:S(2)}) collective-permute-start(bf16[256,768]{1,0:T(8,128)(2,1)S(1)} %fusion.2), channel_id=1, source_target_pairs={{0,4},{2,6},{4,0},{6,2},{1,5},{3,7},{5,1},{7,3},{8,12},{10,14},{12... | collective-permute-start | bytes 1179656 | tf_op jit(solution)/shard_map/ppermute | solution.py:457
  354.3 33.1 %collective-permute-start.60 = (bf16[64,2560]{1,0:T(8,128)(2,1)S(1)}, bf16[64,2560]{1,0:T(8,128)(2,1)S(1)}, u32[]{:S(2)}, u32[]{:S(2)}) collective-permute-start(bf16[64,2560]{1,0:T(8,128)(2,1)S(1)} %add_convert_fusion.8), channel_id=1, source_target_pairs={{0,4},{2,6},{4,0},{6,2},{1,5},{3,7},{5,1},{7,3},{8,12},{10,14},{12... | collective-permute-start | bytes 983048 | tf_op jit(solution)/shard_map/ppermute | solution.py:457
  391.3 24.1 %collective-permute-start.65 = (bf16[128,2560]{1,0:T(8,128)(2,1)S(1)}, bf16[128,2560]{1,0:T(8,128)(2,1)}, u32[]{:S(2)}, u32[]{:S(2)}) collective-permute-start(bf16[128,2560]{1,0:T(8,128)(2,1)S(1)} %maximum_select_fusion.2), channel_id=1, source_target_pairs={{0,2},{2,0},{4,6},{6,4},{1,3},{3,1},{5,7},{7,5},{8,10},{10,8},{12,... | collective-permute-start | bytes 1966088 | tf_op jit(solution)/shard_map/ppermute | solution.py:457
  (114 other events, 808.1 us)

commit v3 on v2

--- a/solution.py
+++ b/solution.py
@@ -317,7 +317,7 @@
             pl.BlockSpec((count, width), lambda i: (0, pair)),
             pl.BlockSpec((count, width), lambda i: (0, kind + pair)),
             pl.BlockSpec((count, width), lambda i: (0, 2 * kind + pair)),
-            alone,
+            pl.BlockSpec((count, width), lambda i: (0, pair)),
             alone,
             pl.BlockSpec((8, count), lambda i: (0, 0)),
         ],
@@ -717,11 +717,10 @@
     attended_slope = product(mixer_slope, mixer_full, PLAIN).astype(LOW)
 
     leaving = []
-    for pair in range(2):
-        for distance in range(4):
-            to = block ^ distance
-            corner = ((to >> 1) * rows_here, (to & 1) * part_width + pair * pair_width)
-            leaving.append(lax.dynamic_slice(attended_slope, corner, (rows_here, pair_width)))
+    for distance in range(4):
+        to = block ^ distance
+        corner = ((to >> 1) * rows_here, (to & 1) * part_width)
+        leaving.append(lax.dynamic_slice(attended_slope, corner, (rows_here, part_width)))
     if four:
         expand_near = add_far(
             rows_at((expand_whole,), 1), rows_at((expand_whole,), 2), expand_far
@@ -731,7 +730,7 @@
     leaving, mixer_slope, mixed_in, activated, expand_near = fence(
         leaving, mixer_slope, mixed_in, activated, expand_near
     )
-    slope_first = [leaving[0]] + [swap(leaving[d], "ctx", d) for d in (1, 2, 3)]
+    slope_blocks = [leaving[0]] + [swap(leaving[d], "ctx", d) for d in (1, 2, 3)]
     if four:
         expand_near = near_rows_out(expand_near)
     wide = (
@@ -746,48 +745,50 @@
     else:
         far_top, far_low, wide_early = (), (), ()
 
-    slope_first, leaving, expand_near, far_top, far_low = fence(
-        slope_first, leaving, expand_near, far_top, far_low
-    )
-    slope_second = [leaving[4]] + [swap(leaving[4 + d], "ctx", d) for d in (1, 2, 3)]
+    slope_blocks, expand_near, far_top, far_low = fence(
+        slope_blocks, expand_near, far_top, far_low
+    )
+    if four:
+        expand_sum = rows_at((expand_whole,), 0).astype(FULL) + both(expand_near)
+    else:
+        expand_sum = lax.psum_scatter(
+            expand_whole, "fsdp", scatter_dimension=0, tiled=True
+        ).astype(FULL)
+    expand_keep, expand_send = halves(expand_sum, part_at)
+    slope_clip = jnp.concatenate(slope_blocks, axis=0)
+    expand_send, slope_clip, far_top, far_low = fence(expand_send, slope_clip, far_top, far_low)
     wide_far = (swap(far_top, "fsdp", 1), swap(far_low, "fsdp", 2)) if four else ()
-    grad_first = attention_backward(
-        joint_out, jnp.concatenate(slope_first, axis=0), out_first, log_first, 0
-    )
-
-    grad_first, slope_second, wide_far = fence(grad_first, slope_second, wide_far)
-    if four:
-        expand_sum = rows_at((expand_whole,), 0).astype(FULL) + both(expand_near)
+    expand_rows = (expand_keep, swap(expand_send, "ctx", 1))
+    grad_first = attention_backward(joint_out, slope_clip, out_first, log_first, 0)
+
+    grad_first, slope_clip, wide_far, expand_rows = fence(
+        grad_first, slope_clip, wide_far, expand_rows
+    )
+    if four:
         wide_late = (
             both((wide_next[half:], wide_far[1])).astype(LOW),
             both((wide_side[:half], wide_far[0])).astype(LOW),
         )
     else:
         wide_late = ()
-        expand_sum = lax.psum_scatter(
-            expand_whole, "fsdp", scatter_dimension=0, tiled=True
-        ).astype(FULL)
-    expand_keep, expand_send = halves(expand_sum, part_at)
-    slope_second = jnp.concatenate(slope_second, axis=0)
-    expand_send, slope_second, wide_early, wide_late = fence(
-        expand_send, slope_second, wide_early, wide_late
+    expand_keep, expand_send = halves(both(expand_rows), clip_at)
+    expand_send, slope_clip, wide_early, wide_late = fence(
+        expand_send, slope_clip, wide_early, wide_late
     )
     if four:
         wide_early = near_rows_out(wide_early)
-    expand_rows = (expand_keep, swap(expand_send, "ctx", 1))
-    grad_second = attention_backward(joint_out, slope_second, out_second, log_second, 1)
+    expand_rows = (expand_keep, swap(expand_send, "ctx", 2))
+    grad_second = attention_backward(joint_out, slope_clip, out_second, log_second, 1)
 
     grad_second, expand_rows, wide_early, wide_late = fence(
         grad_second, expand_rows, wide_early, wide_late
     )
     if four:
         wide_late = near_rows_out(wide_late)
+    expand_rows = join_rows(both(expand_rows).astype(LOW), clip_at, 2)
     joint_slope = jnp.concatenate(
         [grad[kind] for kind in range(3) for grad in (grad_first, grad_second)], axis=1
     )
-    expand_keep, expand_send = halves(both(expand_rows), clip_at)
-    joint_slope, expand_send = fence(joint_slope, expand_send)
-    expand_rows = (expand_keep, swap(expand_send, "ctx", 2))
     first_there = product(joint_slope, joint_full[width_half:], ROW_BY_ROW).astype(LOW)
     first_here = rows_product(joint_slope, joint_full[:width_half], "first_slope")
     first_half = both((first_here, swap(first_there, "tp", 1))).astype(LOW)
@@ -796,8 +797,7 @@
         wide_near = lax.psum_scatter(
             jnp.concatenate(wide, axis=1), "fsdp", scatter_dimension=0, tiled=True
         )
-    first_half, joint_slope, expand_rows = fence(first_half, joint_slope, expand_rows)
-    expand_rows = join_rows(both(expand_rows).astype(LOW), clip_at, 2)
+    first_half, joint_slope = fence(first_half, joint_slope)
     pieces = first_half.reshape(4, rows_here, width_half)
     passing = jnp.concatenate([pieces[1], pieces[3][:, :quarter], pieces[2][:, quarter:]], axis=1)
     passing = swap(passing, "ctx", 1)
@@ -809,8 +809,9 @@
         jnp.zeros((2, features), FULL), bias_sums, (0, part_at * part_width)
     )
 
-    passing, joint_parts, wide_late, expand_rows = fence(
-        passing, joint_parts, wide_late, expand_rows
+    joint_far = far_halves(joint_parts[0]) if four else ()
+    passing, joint_far, wide_late, expand_rows = fence(
+        passing, joint_far, wide_late, expand_rows
     )
     if four:
         near_sum = [both((wide_early[0], wide_late[1])), both((wide_late[0], wide_early[1]))]
@@ -821,16 +822,22 @@
     own_half = both((pieces[0], passing[:, :width_half])).astype(LOW)
     to_left = both((pieces[2][:, :quarter], passing[:, width_half : width_half + quarter]))
     to_right = both((pieces[3][:, quarter:], passing[:, width_half + quarter :]))
-    to_left, to_right, own_half, wide_send, joint_parts, activated = fence(
-        to_left.astype(LOW), to_right.astype(LOW), own_half, wide_send, joint_parts, activated
+    joint_near = add_far(joint_parts[2], joint_parts[1], joint_far) if four else ()
+    to_left, to_right, own_half, wide_send, joint_near, activated = fence(
+        to_left.astype(LOW), to_right.astype(LOW), own_half, wide_send, joint_near, activated
     )
     other_half = jnp.concatenate([swap(to_left, "ctx", 2), swap(to_right, "ctx", 3)], axis=1)
     wide_rows = (wide_keep, swap(wide_send, "ctx", 1))
-    joint_far = far_halves(joint_parts[0]) if four else ()
+    if four:
+        joint_near = near_rows_out(joint_near)
+    else:
+        joint_near = lax.psum_scatter(
+            joint_parts.reshape(width, -1), "fsdp", scatter_dimension=0, tiled=True
+        )
     reduce_part = reduce_output(activated, reduce_held, pieces_at)
 
-    other_half, joint_far, wide_rows, reduce_part = fence(
-        other_half, joint_far, wide_rows, reduce_part
+    other_half, joint_near, wide_rows, reduce_part = fence(
+        other_half, joint_near, wide_rows, reduce_part
     )
     slope_half = jnp.concatenate(swapped_if(clip_at, [own_half, other_half]), axis=0)
     slope_other = swap(slope_half, "tp", 1)
@@ -839,24 +846,15 @@
     first_slope = jnp.concatenate(swapped_if(core, [slope_half, slope_other]), axis=1)
     wide_rows = split_rows(both(wide_rows), clip_at, 2)
     reduce_swapped = swap(reduce_part, "tp", 1)
-    if four:
-        joint_near = near_rows_out(add_far(joint_parts[2], joint_parts[1], joint_far))
-    else:
-        joint_near = lax.psum_scatter(
-            joint_parts.reshape(width, -1), "fsdp", scatter_dimension=0, tiled=True
-        )
+    joint_sum = joint_parts[3].astype(FULL) + both(joint_near) if four else joint_near
+    joint_sum = joint_sum.astype(LOW)
+    joint_sum = (joint_sum, swap(joint_sum, "ctx", 2))
     tokens_grad, first_sums = by_rows(
         first_norm_back_kernel, "first_norm_back", [FULL], True,
         flat_tokens, first_slope, first_gain[None],
         cotangent.reshape(tokens_here, width), first_sum_back,
     )
-    first_sums, tokens_grad, reduce_swapped, joint_near, wide_rows = fence(
-        first_sums, tokens_grad, reduce_swapped, joint_near, wide_rows
-    )
-    joint_sum = joint_parts[3].astype(FULL) + both(joint_near) if four else joint_near
-    joint_sum = joint_sum.astype(LOW)
-    joint_sum = (joint_sum, swap(joint_sum, "ctx", 2))
-    wide_rows = join_rows(both(wide_rows).astype(LOW), clip_at, 2)
+    first_sums, tokens_grad, reduce_swapped = fence(first_sums, tokens_grad, reduce_swapped)
     vectors = [
         first_sums[0],
         first_sums[1],
@@ -888,6 +886,7 @@
     joint_grad = jnp.concatenate(
         [piece.reshape(-1, 3, part_width) for piece in joint_parts], axis=2
     ).astype(FULL)
+    wide_rows = join_rows(both(wide_rows).astype(LOW), clip_at, 2)
     wide_rows = join_rows(wide_rows, part_at, 1).astype(FULL)
     reduce_grad = wide_rows[:, : activated.shape[1]]
     mixer_grad = wide_rows[:, activated.shape[1] :]

time: 424 us -> 394 us (0.929)
  waiting for transfers between devices: 138 us -> 115 us
    ppermute x67 -> x64, waiting for transfers between devices: 138 us -> 115 us  [swap(): return lax.ppermute(value, axis, [(i, i ^ distance) for i in range(size)])]
    ppermute x67 -> x64, starting transfers between devices: 81.3 us -> 77.4 us  [swap(): return lax.ppermute(value, axis, [(i, i ^ distance) for i in range(size)])]
  transfers between devices with their start and end apart: 67 -> 64, of which waited for: 25 -> 29; matrix products, arithmetic and copies ran while one was open for 13% -> 13% of each run, Pallas kernels for 20% -> 22%
where the time goes in v3:
time: 394 us; the launch traced here: 390 us
  waiting for transfers between devices  115 us (29%)
  Pallas kernels  104 us (26%)
  starting transfers between devices  77.4 us (20%)
  local copies, waits for them, and re-layouts  45.5 us (12%)
  other arithmetic  25.6 us (6%)
  matrix products  19.3 us (5%)
    ppermute x64, waiting for transfers between devices, swap(): return lax.ppermute(value, axis, [(i, i ^ distance) for i in range(size)])  115 us
    ppermute x64, starting transfers between devices, swap(): return lax.ppermute(value, axis, [(i, i ^ distance) for i in range(size)])  77.4 us
    pallas_call x2, Pallas kernels, attention_backward(): pl.pallas_call(attention_backward_kernel, grid=(1,), in_specs=[pl.BlockSp...  31.6 us
    unnamed x174, local copies, waits for them, and re-layouts  24.4 us
    pallas_call x4, Pallas kernels, by_rows(): pl.pallas_call(kernel, grid=(count // chunk,), in_specs=in_specs, out_spe...  19.8 us
    dot_general x6, matrix products, product(): return lax.dot_general(left, right, dims, preferred_element_type=FULL)  19.3 us
    pallas_call x1, Pallas kernels, feed_forward(): pl.pallas_call(lambda *refs: feed_forward_kernel(len(reduce), *refs), gri...  18.4 us
    pallas_call x2, Pallas kernels, attention_forward(): pl.pallas_call(attention_forward_kernel, grid=(1,), in_specs=[pl.BlockSpe...  14.9 us
  transfers between devices with their start and end apart: 64, of which 29 were waited for; matrix products, arithmetic and copies ran while one was open for 13% of the time, Pallas kernels for 22%

profile of v3, /device:TPU:0, one launch (start us, length us, event | category | flops | bytes accessed | tf_op | source)
XLA Modules:
  0.0 389.8 jit_solution(17848365701044783093)
XLA Ops:
  7.1 3.0 collective-permute-start.3
  16.0 11.3 %collective-permute-done.1 = bf16[392,256]{1,0:T(8,128)(2,1)S(1)} collective-permute-done((bf16[392,256]{1,0:T(8,128)(2,1)S(1)}, bf16[392,256]{1,0:T(8,128)(2,1)S(1)}, u32[]{:S(2)}, u32[]{:S(2)}) %collective-permute-start.1) | collective-permute-done | bytes 200736 | tf_op jit(solution)/shard_map/ppermute | solution.py:457
  27.3 5.5 %collective-permute-done.2 = bf16[392,256]{1,0:T(8,128)(2,1)S(1)} collective-permute-done((bf16[392,256]{1,0:T(8,128)(2,1)S(1)}, bf16[392,256]{1,0:T(8,128)(2,1)S(1)}, u32[]{:S(2)}, u32[]{:S(2)}) %collective-permute-start.2) | collective-permute-done | bytes 200736 | tf_op jit(solution)/shard_map/ppermute | solution.py:457
  39.9 6.2 %collective-permute-done.6 = bf16[128,1280]{1,0:T(8,128)(2,1)} collective-permute-done((bf16[128,1280]{1,0:T(8,128)(2,1)}, bf16[128,1280]{1,0:T(8,128)(2,1)}, u32[]{:S(2)}, u32[]{:S(2)}) %collective-permute-start.6) | collective-permute-done | bytes 327712 | tf_op jit(solution)/shard_map/ppermute | solution.py:457
  56.0 3.1 joint_projection.1.q_ref.k_ref.v_ref
  60.3 7.2 %attention_forward.2 = (bf16[1568,128]{1,0:T(8,128)(2,1)S(1)}, f32[8,1568]{1,0:T(8,128)S(1)}) custom-call(bf16[1568,768]{1,0:T(8,128)(2,1)S(1)} %joint_projection.1.q_ref.k_ref.v_ref, bf16[1568,768]{1,0:T(8,128)(2,1)S(1)} %joint_projection.1.q_ref.k_ref.v_ref, bf16[1568,768]{1,0:T(8,128)(2,1)S(1)} %joint_projection.1.q_ref.k_ref.v_ref), custom_call_target="tpu_custom_call" | custom-call | tf_op jit(solution)/shard_map/attention_forward/pallas_call | solution.py:240
  74.8 7.7 %attention_forward.3 = (bf16[1568,128]{1,0:T(8,128)(2,1)S(1)}, f32[8,1568]{1,0:T(8,128)S(1)}) custom-call(bf16[1568,768]{1,0:T(8,128)(2,1)S(1)} %joint_projection.1.q_ref.k_ref.v_ref, bf16[1568,768]{1,0:T(8,128)(2,1)S(1)} %joint_projection.1.q_ref.k_ref.v_ref, bf16[1568,768]{1,0:T(8,128)(2,1)S(1)} %joint_projection.1.q_ref.k_ref.v_ref), custom_call_target="tpu_custom_call" | custom-call | tf_op jit(solution)/shard_map/attention_forward/pallas_call | solution.py:240
  82.6 5.0 %collective-permute-done.14.refs_10_.refs_1_ = bf16[256,2048]{1,0:T(8,128)(2,1)S(1)} collective-permute-done((bf16[256,2048]{1,0:T(8,128)(2,1)S(1)}, bf16[256,2048]{1,0:T(8,128)(2,1)S(1)}, u32[]{:S(2)}, u32[]{:S(2)}) %collective-permute-start.14) | collective-permute-done | bytes 1048608 | tf_op jit(solution)/shard_map/ppermute | solution.py:457
  99.9 2.9 collective-permute-done.17
  111.8 5.6 %second_norm.1.refs_1_ = bf16[784,1024]{1,0:T(8,128)(2,1)S(1)} custom-call(bf16[784,1024]{1,0:T(8,128)(2,1)S(1)} %bitcast.84, bf16[784,1024]{1,0:T(8,128)(2,1)} %convolution_convert_fusion.3.one_ref, bf16[784,1024]{1,0:T(8,128)(2,1)} %collective-permute-done.21.two_ref, f32[1,1024]{1,0:T(1,128)S(1)} %bitcast.92, f32[1,1024]{1,0:T(1,128)S(1)} %bitcast.96, ...), custom_call_target="tpu_custom_call" | custom-call | tf_op jit(solution)/shard_map/second_norm/pallas_call | solution.py:104
  118.6 3.5 collective-permute-done.22.refs_12_.refs_3_
  122.4 18.4 %feed_forward.1 = (bf16[784,2048]{1,0:T(8,128)(2,1)}, bf16[784,2048]{1,0:T(8,128)(2,1)}, bf16[784,1024]{1,0:T(8,128)(2,1)}, f32[1,2048]{1,0:T(1,128)S(1)}) custom-call(s32[5]{0:T(128)S(1)} %multiply_add_fusion.refs_0_.place_ref, bf16[784,1024]{1,0:T(8,128)(2,1)} %copy-done.18, bf16[784,1024]{1,0:T(8,128)(2,1)} %bitcast.87, f32[1,2048]{1,0:T(1,128)S(1)} %bitcast.98, ...), custom_call_target="tpu_custom_call" | custom-call | tf_op jit(solution)/shard_map/feed_forward/pallas_call | solution.py:387
  140.9 7.0 %convolution_convert_fusion.1 = bf16[1024,2048]{1,0:T(8,128)(2,1)S(1)} fusion(bf16[784,1024]{1,0:T(8,128)(2,1)} %copy-done.18, bf16[784,2048]{1,0:T(8,128)(2,1)} %get-tuple-element.231), kind=kOutput, calls=%fused_computation.2 | convolution fusion | flops 3290431488 | bytes 9011200 | tf_op jit(solution)/shard_map/dot_general | solution.py:19
  151.4 7.3 %second_norm_back.1 = (bf16[784,1024]{1,0:T(8,128)(2,1)S(1)}, f32[784,1024]{1,0:T(8,128)S(1)}, f32[8,1024]{1,0:T(8,128)S(1)}) custom-call(bf16[784,1024]{1,0:T(8,128)(2,1)S(1)} %bitcast.85, bf16[784,1024]{1,0:T(8,128)(2,1)} %convolution_convert_fusion.3.one_ref, bf16[784,1024]{1,0:T(8,128)(2,1)} %collective-permute-done.21.two_ref, f32[1,1024]{1,0:T(1,128)S(1)} %bitcast.93, ...), custom_call_target="tpu_custom_call" | custom-call | tf_op jit(solution)/shard_map/second_norm_back/pallas_call | solution.py:104
  170.9 5.0 %convolution_convert_fusion = bf16[1024,2048]{1,0:T(8,128)(2,1)S(1)} fusion(bf16[784,1024]{1,0:T(8,128)(2,1)S(1)} %bitcast.89, bf16[784,2048]{1,0:T(8,128)(2,1)S(1)} %copy-done.24), kind=kOutput, calls=%fused_computation.1 | convolution fusion | flops 3290431488 | bytes 9011200 | tf_op jit(solution)/shard_map/dot_general | solution.py:19
  183.3 9.1 %collective-permute-done.30 = bf16[256,2048]{1,0:T(8,128)(2,1)S(1)} collective-permute-done((bf16[256,2048]{1,0:T(8,128)(2,1)S(1)}, bf16[256,2048]{1,0:T(8,128)(2,1)S(1)}, u32[]{:S(2)}, u32[]{:S(2)}) %collective-permute-start.30) | collective-permute-done | bytes 1048608 | tf_op jit(solution)/shard_map/ppermute | solution.py:457
  199.0 15.9 %attention_backward.2 = (bf16[1568,128]{1,0:T(8,128)(2,1)S(1)}, bf16[1568,128]{1,0:T(8,128)(2,1)S(1)}, bf16[1568,128]{1,0:T(8,128)(2,1)S(1)}) custom-call(bf16[1568,768]{1,0:T(8,128)(2,1)S(1)} %joint_projection.1.q_ref.k_ref.v_ref, bf16[1568,768]{1,0:T(8,128)(2,1)S(1)} %joint_projection.1.q_ref.k_ref.v_ref, ...), custom_call_target="tpu_custom_call" | custom-call | tf_op jit(solution)/shard_map/attention_backward/pallas_call | solution.py:313
  224.7 15.7 %attention_backward.3 = (bf16[1568,128]{1,0:T(8,128)(2,1)S(1)}, bf16[1568,128]{1,0:T(8,128)(2,1)S(1)}, bf16[1568,128]{1,0:T(8,128)(2,1)S(1)}) custom-call(bf16[1568,768]{1,0:T(8,128)(2,1)S(1)} %joint_projection.1.q_ref.k_ref.v_ref, bf16[1568,768]{1,0:T(8,128)(2,1)S(1)} %joint_projection.1.q_ref.k_ref.v_ref, ...), custom_call_target="tpu_custom_call" | custom-call | tf_op jit(solution)/shard_map/attention_backward/pallas_call | solution.py:313
  242.9 2.8 convolution_convert_fusion.2
  248.4 2.9 first_slope.1
  254.3 6.6 %collective-permute-done.44 = bf16[64,2048]{1,0:T(8,128)(2,1)S(1)} collective-permute-done((bf16[64,2048]{1,0:T(8,128)(2,1)S(1)}, bf16[64,2048]{1,0:T(8,128)(2,1)S(1)}, u32[]{:S(2)}, u32[]{:S(2)}) %collective-permute-start.44) | collective-permute-done | bytes 262176 | tf_op jit(solution)/shard_map/ppermute | solution.py:457
  264.9 6.0 %joint_grad.1 = bf16[4,256,768]{2,1,0:T(8,128)(2,1)S(1)} custom-call(s32[1]{0:T(128)} %bitcast.21.refs_0_, bf16[1568,512]{1,0:T(8,128)(2,1)S(1)} %copy-done.8, bf16[1568,512]{1,0:T(8,128)(2,1)S(1)} %copy-done.10, bf16[1568,768]{1,0:T(8,128)(2,1)} %copy-done.4), custom_call_target="tpu_custom_call" | custom-call | tf_op jit(solution)/shard_map/joint_grad/pallas_call | solution.py:188
  274.4 3.5 collective-permute-done.40
  279.0 4.1 %collective-permute-done.39 = bf16[392,1024]{1,0:T(8,128)(2,1)S(1)} collective-permute-done((bf16[392,1024]{1,0:T(8,128)(2,1)S(1)}, bf16[392,1024]{1,0:T(8,128)(2,1)S(1)}, u32[]{:S(2)}, u32[]{:S(2)}) %collective-permute-start.39) | collective-permute-done | bytes 802848 | tf_op jit(solution)/shard_map/ppermute | solution.py:457
  293.2 7.5 %reduce_output.1 = bf16[784,1024]{1,0:T(8,128)(2,1)S(1)} custom-call(s32[5]{0:T(128)S(1)} %multiply_add_fusion.refs_0_.place_ref, bf16[784,2048]{1,0:T(8,128)(2,1)S(1)} %copy-done.25, bf16[256,2048]{1,0:T(8,128)(2,1)S(1)} %copy-done.21, bf16[256,2048]{1,0:T(8,128)(2,1)S(1)} %copy-done.15, bf16[256,2048]{1,0:T(8,128)(2,1)} %collective-permute-done.15.refs_11_.refs_2_, ...), custom_call_target="tpu_custom_call" | custom-call | tf_op jit(solution)/shard_map/reduce_output/pallas_call | solution.py:437
  300.8 8.1 %collective-permute-done.46 = bf16[392,256]{1,0:T(8,128)(2,1)S(1)} collective-permute-done((bf16[392,256]{1,0:T(8,128)(2,1)S(1)}, bf16[392,256]{1,0:T(8,128)(2,1)S(1)}, u32[]{:S(2)}, u32[]{:S(2)}) %collective-permute-start.46) | collective-permute-done | bytes 200736 | tf_op jit(solution)/shard_map/ppermute | solution.py:457
  320.7 5.1 %first_norm_back.1 = (f32[784,1024]{1,0:T(8,128)}, f32[8,1024]{1,0:T(8,128)S(1)}) custom-call(bf16[784,1024]{1,0:T(8,128)(2,1)S(1)} %bitcast.86, bf16[784,1024]{1,0:T(8,128)(2,1)S(1)} %pad_maximum_fusion.1.upstream_ref, f32[1,1024]{1,0:T(1,128)S(1)} %bitcast.95, bf16[784,1024]{1,0:T(8,128)(2,1)S(1)} %bitcast.90, f32[784,1024]{1,0:T(8,128)S(1)} %copy-done.23), custom_call_target="tpu_custom_call" | custom-call | tf_op jit(solution)/shard_map/first_norm_back/pallas_call | solution.py:104
  325.8 12.5 %collective-permute-done.63 = bf16[128,2048]{1,0:T(8,128)(2,1)S(1)} collective-permute-done((bf16[128,2048]{1,0:T(8,128)(2,1)S(1)}, bf16[128,2048]{1,0:T(8,128)(2,1)S(1)}, u32[]{:S(2)}, u32[]{:S(2)}) %collective-permute-start.63) | collective-permute-done | bytes 524320 | tf_op jit(solution)/shard_map/ppermute | solution.py:457
  344.4 3.4 add_add_fusion
  358.8 11.2 %collective-permute-done.61 = bf16[64,2560]{1,0:T(8,128)(2,1)S(1)} collective-permute-done((bf16[64,2560]{1,0:T(8,128)(2,1)S(1)}, bf16[64,2560]{1,0:T(8,128)(2,1)S(1)}, u32[]{:S(2)}, u32[]{:S(2)}) %collective-permute-start.61) | collective-permute-done | bytes 327712 | tf_op jit(solution)/shard_map/ppermute | solution.py:457
  370.2 3.3 collective-permute-start.62
  377.5 8.1 %collective-permute-done.62 = bf16[128,2560]{1,0:T(8,128)(2,1)} collective-permute-done((bf16[128,2560]{1,0:T(8,128)(2,1)S(1)}, bf16[128,2560]{1,0:T(8,128)(2,1)}, u32[]{:S(2)}, u32[]{:S(2)}) %collective-permute-start.62) | collective-permute-done | bytes 655392 | tf_op jit(solution)/shard_map/ppermute | solution.py:457
  (404 shorter events, 162.9 us)
Async XLA Ops:
  7.1 25.7 %collective-permute-start.3 = (bf16[256,1280]{1,0:T(8,128)(2,1)S(1)}, bf16[256,1280]{1,0:T(8,128)(2,1)S(1)}, u32[]{:S(2)}, u32[]{:S(2)}) collective-permute-start(bf16[256,1280]{1,0:T(8,128)(2,1)S(1)} %pad_maximum_fusion.12), channel_id=1, source_target_pairs={{0,8},{8,0},{16,24},{24,16},{1,9},{9,1},{17,25},{25,17},{2,10},{10... | collective-permute-start | bytes 1966088 | tf_op jit(solution)/shard_map/ppermute | solution.py:457
  10.1 22.7 %collective-permute-start.4 = (bf16[256,1280]{1,0:T(8,128)(2,1)S(1)}, bf16[256,1280]{1,0:T(8,128)(2,1)S(1)}, u32[]{:S(2)}, u32[]{:S(2)}) collective-permute-start(bf16[256,1280]{1,0:T(8,128)(2,1)S(1)} %pad_maximum_fusion.12), channel_id=1, source_target_pairs={{0,16},{8,24},{16,0},{24,8},{1,17},{9,25},{17,1},{25,9},{2,18},{10... | collective-permute-start | bytes 1966088 | tf_op jit(solution)/shard_map/ppermute | solution.py:457
  11.6 21.2 %collective-permute-start = (bf16[392,512]{1,0:T(8,128)(2,1)S(1)}, bf16[392,512]{1,0:T(8,128)(2,1)S(1)}, u32[]{:S(2)}, u32[]{:S(2)}) collective-permute-start(bf16[392,512]{1,0:T(8,128)(2,1)S(1)} %get-tuple-element.171), channel_id=1, source_target_pairs={{0,2},{2,0},{4,6},{6,4},{1,3},{3,1},{5,7},{7,5},{8,10},{10,8},{12,... | collective-permute-start | bytes 1204232 | tf_op jit(solution)/shard_map/ppermute | solution.py:457
  15.8 17.0 %collective-permute-start.2 = (bf16[392,256]{1,0:T(8,128)(2,1)S(1)}, bf16[392,256]{1,0:T(8,128)(2,1)S(1)}, u32[]{:S(2)}, u32[]{:S(2)}) collective-permute-start(bf16[392,256]{1,0:T(8,128)(2,1)S(1)} %get-tuple-element.173), channel_id=1, source_target_pairs={{0,6},{2,4},{4,2},{6,0},{1,7},{3,5},{5,3},{7,1},{8,14},{10,12},{12... | collective-permute-start | bytes 602120 | tf_op jit(solution)/shard_map/ppermute | solution.py:457
  36.9 31.8 %collective-permute-start.9 = (bf16[256,2048]{1,0:T(8,128)(2,1)}, bf16[256,2048]{1,0:T(8,128)(2,1)S(1)}, u32[]{:S(2)}, u32[]{:S(2)}) collective-permute-start(bf16[256,2048]{1,0:T(8,128)(2,1)} %refs_4_), channel_id=1, source_target_pairs={{0,8},{8,0},{16,24},{24,16},{1,9},{9,1},{17,25},{25,17},{2,10},{10... | collective-permute-start | bytes 3145736 | tf_op jit(solution)/shard_map/ppermute | solution.py:457
  38.4 31.3 %collective-permute-start.10 = (bf16[256,2048]{1,0:T(8,128)(2,1)}, bf16[256,2048]{1,0:T(8,128)(2,1)S(1)}, u32[]{:S(2)}, u32[]{:S(2)}) collective-permute-start(bf16[256,2048]{1,0:T(8,128)(2,1)} %refs_4_), channel_id=1, source_target_pairs={{0,16},{8,24},{16,0},{24,8},{1,17},{9,25},{17,1},{25,9},{2,18},{10... | collective-permute-start | bytes 3145736 | tf_op jit(solution)/shard_map/ppermute | solution.py:457
  52.6 35.0 %collective-permute-start.14 = (bf16[256,2048]{1,0:T(8,128)(2,1)S(1)}, bf16[256,2048]{1,0:T(8,128)(2,1)S(1)}, u32[]{:S(2)}, u32[]{:S(2)}) collective-permute-start(bf16[256,2048]{1,0:T(8,128)(2,1)S(1)} %copy-done.19), channel_id=1, source_target_pairs={{0,8},{8,0},{16,24},{24,16},{1,9},{9,1},{17,25},{25,17},{2,10},{10... | collective-permute-start | bytes 3145736 | tf_op jit(solution)/shard_map/ppermute | solution.py:457
  54.1 34.6 %collective-permute-start.15 = (bf16[256,2048]{1,0:T(8,128)(2,1)S(1)}, bf16[256,2048]{1,0:T(8,128)(2,1)}, u32[]{:S(2)}, u32[]{:S(2)}) collective-permute-start(bf16[256,2048]{1,0:T(8,128)(2,1)S(1)} %copy-done.19), channel_id=1, source_target_pairs={{0,16},{8,24},{16,0},{24,8},{1,17},{9,25},{17,1},{25,9},{2,18},{10... | collective-permute-start | bytes 3145736 | tf_op jit(solution)/shard_map/ppermute | solution.py:457
  164.4 16.1 %collective-permute-start.27 = (bf16[392,256]{1,0:T(8,128)(2,1)S(1)}, bf16[392,256]{1,0:T(8,128)(2,1)S(1)}, u32[]{:S(2)}, u32[]{:S(2)}) collective-permute-start(bf16[392,256]{1,0:T(8,128)(2,1)S(1)} %get-tuple-element.237), channel_id=1, source_target_pairs={{0,2},{2,0},{4,6},{6,4},{1,3},{3,1},{5,7},{7,5},{8,10},{10,8},{12,... | collective-permute-start | bytes 602120 | tf_op jit(solution)/shard_map/ppermute | solution.py:457
  166.1 17.2 %collective-permute-start.28 = (bf16[392,256]{1,0:T(8,128)(2,1)S(1)}, bf16[392,256]{1,0:T(8,128)(2,1)S(1)}, u32[]{:S(2)}, u32[]{:S(2)}) collective-permute-start(bf16[392,256]{1,0:T(8,128)(2,1)S(1)} %get-tuple-element.238), channel_id=1, source_target_pairs={{0,4},{2,6},{4,0},{6,2},{1,5},{3,7},{5,1},{7,3},{8,12},{10,14},{12... | collective-permute-start | bytes 602120 | tf_op jit(solution)/shard_map/ppermute | solution.py:457
  166.8 16.5 %collective-permute-start.29 = (bf16[392,256]{1,0:T(8,128)(2,1)S(1)}, bf16[392,256]{1,0:T(8,128)(2,1)S(1)}, u32[]{:S(2)}, u32[]{:S(2)}) collective-permute-start(bf16[392,256]{1,0:T(8,128)(2,1)S(1)} %get-tuple-element.239), channel_id=1, source_target_pairs={{0,6},{2,4},{4,2},{6,0},{1,7},{3,5},{5,3},{7,1},{8,14},{10,12},{12... | collective-permute-start | bytes 602120 | tf_op jit(solution)/shard_map/ppermute | solution.py:457
  168.8 23.6 %collective-permute-start.30 = (bf16[256,2048]{1,0:T(8,128)(2,1)S(1)}, bf16[256,2048]{1,0:T(8,128)(2,1)S(1)}, u32[]{:S(2)}, u32[]{:S(2)}) collective-permute-start(bf16[256,2048]{1,0:T(8,128)(2,1)S(1)} %pad_maximum_fusion.3), channel_id=1, source_target_pairs={{0,8},{8,0},{16,24},{24,16},{1,9},{9,1},{17,25},{25,17},{2,10},{10... | collective-permute-start | bytes 3145736 | tf_op jit(solution)/shard_map/ppermute | solution.py:457
  169.4 23.4 %collective-permute-start.31 = (bf16[256,2048]{1,0:T(8,128)(2,1)S(1)}, bf16[256,2048]{1,0:T(8,128)(2,1)S(1)}, u32[]{:S(2)}, u32[]{:S(2)}) collective-permute-start(bf16[256,2048]{1,0:T(8,128)(2,1)S(1)} %pad_maximum_fusion.4), channel_id=1, source_target_pairs={{0,16},{8,24},{16,0},{24,8},{1,17},{9,25},{17,1},{25,9},{2,18},{10... | collective-permute-start | bytes 3145736 | tf_op jit(solution)/shard_map/ppermute | solution.py:457
  193.4 21.6 %collective-permute-start.32 = (bf16[128,2560]{1,0:T(8,128)(2,1)}, bf16[128,2560]{1,0:T(8,128)(2,1)S(1)}, u32[]{:S(2)}, u32[]{:S(2)}) collective-permute-start(bf16[128,2560]{1,0:T(8,128)(2,1)} %get-tuple-element.258), channel_id=1, source_target_pairs={{0,8},{8,0},{16,24},{24,16},{1,9},{9,1},{17,25},{25,17},{2,10},{10... | collective-permute-start | bytes 1966088 | tf_op jit(solution)/shard_map/ppermute | solution.py:457
  194.9 20.2 %collective-permute-start.33 = (bf16[128,2560]{1,0:T(8,128)(2,1)S(1)}, bf16[128,2560]{1,0:T(8,128)(2,1)S(1)}, u32[]{:S(2)}, u32[]{:S(2)}) collective-permute-start(bf16[128,2560]{1,0:T(8,128)(2,1)S(1)} %get-tuple-element.259), channel_id=1, source_target_pairs={{0,16},{8,24},{16,0},{24,8},{1,17},{9,25},{17,1},{25,9},{2,18},{10... | collective-permute-start | bytes 1966088 | tf_op jit(solution)/shard_map/ppermute | solution.py:457
  197.3 17.7 %collective-permute-start.34 = (bf16[128,2048]{1,0:T(8,128)(2,1)S(1)}, bf16[128,2048]{1,0:T(8,128)(2,1)S(1)}, u32[]{:S(2)}, u32[]{:S(2)}) collective-permute-start(bf16[128,2048]{1,0:T(8,128)(2,1)S(1)} %dynamic-slice_convert_fusion.1), channel_id=1, source_target_pairs={{0,2},{2,0},{4,6},{6,4},{1,3},{3,1},{5,7},{7,5},{8,10},{10,8},{12,... | collective-permute-start | bytes 1572872 | tf_op jit(solution)/shard_map/ppermute | solution.py:457
  219.9 20.6 %collective-permute-start.36 = (bf16[128,2560]{1,0:T(8,128)(2,1)}, bf16[128,2560]{1,0:T(8,128)(2,1)}, u32[]{:S(2)}, u32[]{:S(2)}) collective-permute-start(bf16[128,2560]{1,0:T(8,128)(2,1)} %fusion.5), channel_id=1, source_target_pairs={{0,8},{8,0},{16,24},{24,16},{1,9},{9,1},{17,25},{25,17},{2,10},{10... | collective-permute-start | bytes 1966088 | tf_op jit(solution)/shard_map/ppermute | solution.py:457
  220.5 20.0 %collective-permute-start.37 = (bf16[128,2560]{1,0:T(8,128)(2,1)}, bf16[128,2560]{1,0:T(8,128)(2,1)}, u32[]{:S(2)}, u32[]{:S(2)}) collective-permute-start(bf16[128,2560]{1,0:T(8,128)(2,1)} %fusion.4), channel_id=1, source_target_pairs={{0,16},{8,24},{16,0},{24,8},{1,17},{9,25},{17,1},{25,9},{2,18},{10... | collective-permute-start | bytes 1966088 | tf_op jit(solution)/shard_map/ppermute | solution.py:457
  221.0 19.5 %collective-permute-start.35 = (bf16[64,2048]{1,0:T(8,128)(2,1)}, bf16[64,2048]{1,0:T(8,128)(2,1)S(1)}, u32[]{:S(2)}, u32[]{:S(2)}) collective-permute-start(bf16[64,2048]{1,0:T(8,128)(2,1)} %dynamic-slice_convert_fusion.3), channel_id=1, source_target_pairs={{0,4},{2,6},{4,0},{6,2},{1,5},{3,7},{5,1},{7,3},{8,12},{10,14},{12... | collective-permute-start | bytes 786440 | tf_op jit(solution)/shard_map/ppermute | solution.py:457
  251.3 23.1 %collective-permute-start.42 = (bf16[128,2560]{1,0:T(8,128)(2,1)S(1)}, bf16[128,2560]{1,0:T(8,128)(2,1)S(1)}, u32[]{:S(2)}, u32[]{:S(2)}) collective-permute-start(bf16[128,2560]{1,0:T(8,128)(2,1)S(1)} %copy-done.68), channel_id=1, source_target_pairs={{0,8},{8,0},{16,24},{24,16},{1,9},{9,1},{17,25},{25,17},{2,10},{10... | collective-permute-start | bytes 1966088 | tf_op jit(solution)/shard_map/ppermute | solution.py:457
  252.8 21.6 %collective-permute-start.43 = (bf16[128,2560]{1,0:T(8,128)(2,1)S(1)}, bf16[128,2560]{1,0:T(8,128)(2,1)S(1)}, u32[]{:S(2)}, u32[]{:S(2)}) collective-permute-start(bf16[128,2560]{1,0:T(8,128)(2,1)S(1)} %copy-done.69), channel_id=1, source_target_pairs={{0,16},{8,24},{16,0},{24,8},{1,17},{9,25},{17,1},{25,9},{2,18},{10... | collective-permute-start | bytes 1966088 | tf_op jit(solution)/shard_map/ppermute | solution.py:457
  263.1 19.9 %collective-permute-start.39 = (bf16[392,1024]{1,0:T(8,128)(2,1)S(1)}, bf16[392,1024]{1,0:T(8,128)(2,1)S(1)}, u32[]{:S(2)}, u32[]{:S(2)}) collective-permute-start(bf16[392,1024]{1,0:T(8,128)(2,1)S(1)} %pad_maximum_fusion.7), channel_id=1, source_target_pairs={{0,2},{2,0},{4,6},{6,4},{1,3},{3,1},{5,7},{7,5},{8,10},{10,8},{12,... | collective-permute-start | bytes 2408456 | tf_op jit(solution)/shard_map/ppermute | solution.py:457
  286.7 24.5 %collective-permute-start.49 = (bf16[128,2560]{1,0:T(8,128)(2,1)S(1)}, bf16[128,2560]{1,0:T(8,128)(2,1)S(1)}, u32[]{:S(2)}, u32[]{:S(2)}) collective-permute-start(bf16[128,2560]{1,0:T(8,128)(2,1)S(1)} %dynamic-slice_convert_fusion), channel_id=1, source_target_pairs={{0,2},{2,0},{4,6},{6,4},{1,3},{3,1},{5,7},{7,5},{8,10},{10,8},{12,... | collective-permute-start | bytes 1966088 | tf_op jit(solution)/shard_map/ppermute | solution.py:457
  287.0 21.9 %collective-permute-start.46 = (bf16[392,256]{1,0:T(8,128)(2,1)S(1)}, bf16[392,256]{1,0:T(8,128)(2,1)S(1)}, u32[]{:S(2)}, u32[]{:S(2)}) collective-permute-start(bf16[392,256]{1,0:T(8,128)(2,1)S(1)} %get-tuple-element.297), channel_id=1, source_target_pairs={{0,6},{2,4},{4,2},{6,0},{1,7},{3,5},{5,3},{7,1},{8,14},{10,12},{12... | collective-permute-start | bytes 602120 | tf_op jit(solution)/shard_map/ppermute | solution.py:457
  289.0 20.4 %collective-permute-start.45 = (bf16[392,256]{1,0:T(8,128)(2,1)S(1)}, bf16[392,256]{1,0:T(8,128)(2,1)S(1)}, u32[]{:S(2)}, u32[]{:S(2)}) collective-permute-start(bf16[392,256]{1,0:T(8,128)(2,1)S(1)} %get-tuple-element.296), channel_id=1, source_target_pairs={{0,4},{2,6},{4,0},{6,2},{1,5},{3,7},{5,1},{7,3},{8,12},{10,14},{12... | collective-permute-start | bytes 602120 | tf_op jit(solution)/shard_map/ppermute | solution.py:457
  290.2 19.1 %collective-permute-start.47 = (bf16[256,768]{1,0:T(8,128)(2,1)S(1)}, bf16[256,768]{1,0:T(8,128)(2,1)S(1)}, u32[]{:S(2)}, u32[]{:S(2)}) collective-permute-start(bf16[256,768]{1,0:T(8,128)(2,1)S(1)} %pad_maximum_fusion.17), channel_id=1, source_target_pairs={{0,8},{8,0},{16,24},{24,16},{1,9},{9,1},{17,25},{25,17},{2,10},{10... | collective-permute-start | bytes 1179656 | tf_op jit(solution)/shard_map/ppermute | solution.py:457
  291.7 17.7 %collective-permute-start.48 = (bf16[256,768]{1,0:T(8,128)(2,1)S(1)}, bf16[256,768]{1,0:T(8,128)(2,1)S(1)}, u32[]{:S(2)}, u32[]{:S(2)}) collective-permute-start(bf16[256,768]{1,0:T(8,128)(2,1)S(1)} %pad_maximum_fusion.18), channel_id=1, source_target_pairs={{0,16},{8,24},{16,0},{24,8},{1,17},{9,25},{17,1},{25,9},{2,18},{10... | collective-permute-start | bytes 1179656 | tf_op jit(solution)/shard_map/ppermute | solution.py:457
  311.4 28.4 %collective-permute-start.51 = (bf16[784,1024]{1,0:T(8,128)(2,1)S(1)}, bf16[784,1024]{1,0:T(8,128)(2,1)S(1)}, u32[]{:S(2)}, u32[]{:S(2)}) collective-permute-start(bf16[784,1024]{1,0:T(8,128)(2,1)S(1)} %reduce_output.1), channel_id=1, source_target_pairs={{0,1},{1,0},{2,3},{3,2},{4,5},{5,4},{6,7},{7,6},{8,9},{9,8},{10,11... | collective-permute-start | bytes 4816904 | tf_op jit(solution)/shard_map/ppermute | solution.py:457
  313.7 24.6 %collective-permute-start.63 = (bf16[128,2048]{1,0:T(8,128)(2,1)S(1)}, bf16[128,2048]{1,0:T(8,128)(2,1)S(1)}, u32[]{:S(2)}, u32[]{:S(2)}) collective-permute-start(bf16[128,2048]{1,0:T(8,128)(2,1)S(1)} %maximum_select_fusion.3), channel_id=1, source_target_pairs={{0,2},{2,0},{4,6},{6,4},{1,3},{3,1},{5,7},{7,5},{8,10},{10,8},{12,... | collective-permute-start | bytes 1572872 | tf_op jit(solution)/shard_map/ppermute | solution.py:457
  314.8 36.7 %collective-permute-start.55 = (bf16[256,768]{1,0:T(8,128)(2,1)S(1)}, bf16[256,768]{1,0:T(8,128)(2,1)S(1)}, u32[]{:S(2)}, u32[]{:S(2)}) collective-permute-start(bf16[256,768]{1,0:T(8,128)(2,1)S(1)} %fusion.2), channel_id=1, source_target_pairs={{0,4},{2,6},{4,0},{6,2},{1,5},{3,7},{5,1},{7,3},{8,12},{10,14},{12... | collective-permute-start | bytes 1179656 | tf_op jit(solution)/shard_map/ppermute | solution.py:457
  316.2 35.3 %collective-permute-start.56 = (bf16[64,2560]{1,0:T(8,128)(2,1)S(1)}, bf16[64,2560]{1,0:T(8,128)(2,1)S(1)}, u32[]{:S(2)}, u32[]{:S(2)}) collective-permute-start(bf16[64,2560]{1,0:T(8,128)(2,1)S(1)} %dynamic-slice_convert_fusion.2), channel_id=1, source_target_pairs={{0,4},{2,6},{4,0},{6,2},{1,5},{3,7},{5,1},{7,3},{8,12},{10,14},{12... | collective-permute-start | bytes 983048 | tf_op jit(solution)/shard_map/ppermute | solution.py:457
  355.6 19.8 %collective-permute-start.60 = (bf16[256,768]{1,0:T(8,128)(2,1)S(1)}, bf16[256,768]{1,0:T(8,128)(2,1)S(1)}, u32[]{:S(2)}, u32[]{:S(2)}) collective-permute-start(bf16[256,768]{1,0:T(8,128)(2,1)S(1)} %add_convert_fusion.7), channel_id=1, source_target_pairs={{0,2},{2,0},{4,6},{6,4},{1,3},{3,1},{5,7},{7,5},{8,10},{10,8},{12,... | collective-permute-start | bytes 1179656 | tf_op jit(solution)/shard_map/ppermute | solution.py:457
  (111 other events, 787.9 us)

commit v4 on v3

--- a/solution.py
+++ b/solution.py
@@ -334,18 +334,35 @@
     )(joint, joint, joint, da, out, lse)
 
 
-def put_together(place_ref, whole_ref, piece_refs):
-    for piece, piece_ref in enumerate(piece_refs):
-        rows = piece_ref.shape[0]
-        start = pl.multiple_of(place_ref[piece], rows)
-        whole_ref[pl.ds(start, rows), :] = piece_ref[...]
-
-
-def feed_forward_kernel(pieces, place_ref, normed_ref, slope_ref, bias_ref, *refs):
-    active_ref, expand_slope_ref, back_ref, bias_grad_ref = refs[2 * pieces : 2 * pieces + 4]
-    total, expand_ref, reduce_ref = refs[2 * pieces + 4 :]
-    put_together(place_ref, expand_ref, refs[:pieces])
-    put_together(place_ref, reduce_ref, refs[pieces : 2 * pieces])
+def put_together(place_ref, whole_ref, pieces, edge=0):
+    for piece, refs in enumerate(pieces):
+        rows = refs[0].shape[0]
+        place = pl.ds(pl.multiple_of(place_ref[piece], rows), rows)
+        if len(refs) == 1:
+            whole_ref[place, :] = refs[0][...]
+            continue
+
+        @pl.when(pl.program_id(0) < edge)
+        def _():
+            whole_ref[place, :] = refs[0][...]
+
+        @pl.when(pl.program_id(0) >= edge)
+        def _():
+            whole_ref[place, :] = refs[1][...]
+
+
+def nested(refs, like):
+    refs = iter(refs)
+    return [tuple(next(refs) for _ in piece) for piece in like]
+
+
+def feed_forward_kernel(
+    expand, reduce, edge, place_ref, normed_ref, slope_ref, bias_ref, *refs
+):
+    active_ref, expand_slope_ref, back_ref, bias_grad_ref, total, expand_ref, reduce_ref = refs[-7:]
+    arrays = sum(len(piece) for piece in expand)
+    put_together(place_ref, expand_ref, nested(refs[:arrays], expand), edge)
+    put_together(place_ref, reduce_ref, nested(refs[arrays:-7], reduce))
     step = pl.program_id(0)
     count = normed_ref.shape[0]
     half = count // 2
@@ -377,23 +394,30 @@
         back_ref[...] = total[...].astype(LOW)
 
 
-def feed_forward(normed, slope, bias, expand, reduce, place):
+def feed_forward(normed, slope, bias, expand, early, reduce, place):
     count, width = normed.shape
     hidden = bias.shape[1]
-    block = 512 if hidden % 512 == 0 else hidden
+    block = 512
+    edge = early // block
     whole = pl.BlockSpec((count, width), lambda i, place: (0, 0))
     out = pl.BlockSpec((count, block), lambda i, place: (0, i))
     row = pl.BlockSpec((1, block), lambda i, place: (0, i))
+    specs = []
+    arrays = []
+    for piece in [*expand, *reduce]:
+        shape = (piece[0].shape[0], block)
+        arrays += piece
+        if len(piece) == 1:
+            specs.append(pl.BlockSpec(shape, lambda i, place: (0, i)))
+        else:
+            specs.append(pl.BlockSpec(shape, lambda i, place: (0, jnp.minimum(i, edge - 1))))
+            specs.append(pl.BlockSpec(shape, lambda i, place: (0, jnp.maximum(i - edge, 0))))
     return pl.pallas_call(
-        lambda *refs: feed_forward_kernel(len(reduce), *refs),
+        lambda *refs: feed_forward_kernel(expand, reduce, edge, *refs),
         grid_spec=pltpu.PrefetchScalarGridSpec(
             num_scalar_prefetch=1,
             grid=(hidden // block,),
-            in_specs=[whole, whole, row]
-            + [
-                pl.BlockSpec((piece.shape[0], block), lambda i, place: (0, i))
-                for piece in [*expand, *reduce]
-            ],
+            in_specs=[whole, whole, row] + specs,
             out_specs=[out, out, whole, row],
             scratch_shapes=[
                 pltpu.VMEM((count, width), FULL),
@@ -409,12 +433,12 @@
         ],
         compiler_params=pltpu.CompilerParams(vmem_limit_bytes=44 << 20),
         name="feed_forward",
-    )(place, normed, slope, bias, *expand, *reduce)
+    )(place, normed, slope, bias, *arrays)
 
 
 def reduce_kernel(place_ref, active_ref, *refs):
     out_ref, total, reduce_ref = refs[-3:]
-    put_together(place_ref, reduce_ref, refs[:-3])
+    put_together(place_ref, reduce_ref, [(ref,) for ref in refs[:-3]])
     part = product(active_ref[...], reduce_ref[...], ROW_BY_ROW)
 
     @pl.when(pl.program_id(0) == 0)
@@ -478,6 +502,17 @@
     return (swap(leaves[0], "fsdp", 1), swap(leaves[1], "fsdp", 2)) if leaves else ()
 
 
+def far_of(held):
+    if len(held) == 1:
+        return ()
+    half = held[0].shape[0] // 2
+    return (held[2][:half], held[1][half:])
+
+
+def send_far(leaves):
+    return (swap(leaves[0], "fsdp", 1), swap(leaves[1], "fsdp", 2)) if leaves else ()
+
+
 def gather_far(held):
     return held + send_far(far_of(held))
 
@@ -502,6 +537,13 @@
     start = (lax.axis_index("fsdp") ^ 3) * 2 * half
     out = lax.dynamic_update_slice(out, far_top, (start, 0))
     return lax.dynamic_update_slice(out, far_low, (start + half, 0))
+
+
+def grad_rows(left, right, distance):
+    count = left.shape[1] // 4
+    start = (lax.axis_index("fsdp") ^ distance) * count
+    piece = lax.dynamic_slice_in_dim(left, start, count, 1)
+    return product(piece, right, COLUMN_BY_COLUMN).astype(LOW)
 
 
 def rows_at(matrices, distance):
@@ -606,22 +648,26 @@
     own_other = lax.dynamic_index_in_dim(other_side, clip_at, 0, False)
     other_clip = lax.dynamic_index_in_dim(mine, 1 - clip_at, 0, False)
     joint_part = lax.dynamic_slice_in_dim(joint_weight, part_at * part_width, part_width, 2)
-    both_parts = jnp.concatenate([joint_part[:, kind] for kind in range(3)] + [mixer_weight], axis=1)
-
-    own_clip, left, right, both_parts = fence(
-        own_clip, other_clip[:, :quarter], other_clip[:, quarter:], both_parts
+    early = expand_weight.shape[1] // 2
+    wide_part = jnp.concatenate(
+        [expand_weight[:, :early]] + [joint_part[:, kind] for kind in range(3)] + [mixer_weight],
+        axis=1,
+    )
+
+    own_clip, left, right, wide_part = fence(
+        own_clip, other_clip[:, :quarter], other_clip[:, quarter:], wide_part
     )
     near_rows = swap(own_clip, "ctx", 1)
     across_left = swap(left, "ctx", 2)
     far_right = swap(right, "ctx", 3)
-    held = gather_near(both_parts)
-
-    near_rows, across_left, far_right, held, expand_weight = fence(
-        near_rows, across_left, far_right, held, expand_weight
+    wide_held = gather_near(wide_part)
+
+    near_rows, across_left, far_right, wide_held, expand_rest = fence(
+        near_rows, across_left, far_right, wide_held, expand_weight[:, early:]
     )
     passed = swap(jnp.concatenate([across_left, far_right], axis=1), "ctx", 1)
-    held = gather_far(held)
-    expand_held = gather_near(expand_weight)
+    held = gather_far(tuple(piece[:, early:] for piece in wide_held))
+    rest_held = gather_near(expand_rest)
 
     passed, held = fence(passed, held)
     cross_rows = jnp.concatenate(
@@ -655,24 +701,31 @@
     joint_out = joint_projection(normed_mine, normed_other, joint_full, bias_row[None])
     out_first, log_first = attention_forward(joint_out, 0)
 
-    out_first, joint_out, mixer_full, expand_held = fence(
-        out_first, joint_out, mixer_full, expand_held
+    out_first, joint_out, mixer_full, rest_held = fence(
+        out_first, joint_out, mixer_full, rest_held
     )
     first_blocks = out_first.reshape(4, rows_here, pair_width)
     arrived_first = [swap(first_blocks[d], "ctx", d) for d in (1, 2, 3)]
     out_second, log_second = attention_forward(joint_out, 1)
 
-    out_second, arrived_first, reduce_held, expand_held = fence(
-        out_second, arrived_first, reduce_held, expand_held
+    far_leaves = far_of(
+        tuple(
+            jnp.concatenate([one[:, :early], two], axis=1)
+            for one, two in zip(wide_held, rest_held)
+        )
+    )
+    out_second, arrived_first, reduce_held, far_leaves = fence(
+        out_second, arrived_first, reduce_held, far_leaves
     )
     second_blocks = out_second.reshape(4, rows_here, pair_width)
     arrived_second = [swap(second_blocks[d], "ctx", d) for d in (1, 2, 3)]
-    expand_held = gather_far(expand_held)
-
-    arrived_second, expand_held, reduce_held, log_first, log_second = fence(
-        arrived_second, expand_held, reduce_held, log_first, log_second
-    )
-    reduce_held = gather_far(reduce_held)
+    expand_far_rows = send_far(far_leaves)
+
+    arrived_second, expand_far_rows, reduce_held, reduce_leaves = fence(
+        arrived_second, expand_far_rows, reduce_held, far_of(reduce_held)
+    )
+    reduce_held = reduce_held + send_far(reduce_leaves)
+    expand_held = list(zip(wide_held, rest_held)) + [(rows,) for rows in expand_far_rows]
     arrived = [jnp.concatenate([first_blocks[0], second_blocks[0]], axis=1)] + [
         jnp.concatenate([one, two], axis=1) for one, two in zip(arrived_first, arrived_second)
     ]
@@ -700,15 +753,25 @@
     else:
         pieces_at = start.reshape(1)
     activated, expand_slope, second_part, expand_bias_grad = feed_forward(
-        second_normed, reduce_slope, expand_bias[None], expand_held, reduce_held, pieces_at
+        second_normed, reduce_slope, expand_bias[None], expand_held, early,
+        [(piece,) for piece in reduce_held], pieces_at,
     )
     expand_bias_grad = expand_bias_grad[0]
 
     second_swapped = swap(second_part, "tp", 1)
     place, order = (shard, (3, 2, 1, 0)) if four else (start, (0, 1, 2, 3))
-    expand_whole = product(second_normed, expand_slope, COLUMN_BY_COLUMN).astype(LOW)
-    second_swapped, expand_whole = fence(second_swapped, expand_whole)
-    expand_far = far_halves(rows_at((expand_whole,), 3)) if four else ()
+    if four:
+        half = width // 8
+        far = grad_rows(second_normed, expand_slope, 3)
+        far_top, far_low, normed_again, expand_slope = fence(
+            far[:half], far[half:], second_normed, expand_slope
+        )
+        expand_far = (swap(far_top, "fsdp", 1), swap(far_low, "fsdp", 2))
+        expand_parts = [grad_rows(normed_again, expand_slope, d) for d in (0, 1, 2)]
+        expand_parts, second_swapped = fence(expand_parts, second_swapped)
+    else:
+        expand_far = ()
+        expand_whole = product(second_normed, expand_slope, COLUMN_BY_COLUMN).astype(LOW)
     mixer_slope, first_sum_back, second_sums = by_rows(
         second_norm_back_kernel, "second_norm_back", [LOW, FULL], True,
         flat_tokens, mixer_part, mixer_swapped, mixer_row, second_gain[None],
@@ -721,12 +784,7 @@
         to = block ^ distance
         corner = ((to >> 1) * rows_here, (to & 1) * part_width)
         leaving.append(lax.dynamic_slice(attended_slope, corner, (rows_here, part_width)))
-    if four:
-        expand_near = add_far(
-            rows_at((expand_whole,), 1), rows_at((expand_whole,), 2), expand_far
-        )
-    else:
-        expand_near = ()
+    expand_near = add_far(expand_parts[1], expand_parts[2], expand_far) if four else ()
     leaving, mixer_slope, mixed_in, activated, expand_near = fence(
         leaving, mixer_slope, mixed_in, activated, expand_near
     )
@@ -738,7 +796,6 @@
         product(mixer_slope, mixed_in, COLUMN_BY_COLUMN).astype(LOW),
     )
     if four:
-        half = width // 8
         wide_far, wide_side, wide_next = (rows_at(wide, distance) for distance in (3, 2, 1))
         far_top, far_low = wide_far[:half], wide_far[half:]
         wide_early = (wide_next[:half], wide_side[half:])
@@ -749,7 +806,7 @@
         slope_blocks, expand_near, far_top, far_low
     )
     if four:
-        expand_sum = rows_at((expand_whole,), 0).astype(FULL) + both(expand_near)
+        expand_sum = expand_parts[0].astype(FULL) + both(expand_near)
     else:
         expand_sum = lax.psum_scatter(
             expand_whole, "fsdp", scatter_dimension=0, tiled=True

time: 394 us -> 394 us (level)
    unnamed x174 -> x208, local copies, waits for them, and re-layouts: 24.4 us -> 25.2 us
    dot_general x6 -> x9, matrix products: 19.3 us -> 19.5 us  [product(): return lax.dot_general(left, right, dims, preferred_element_type=FULL)]
  transfers between devices with their start and end apart: 64 -> 64, of which waited for: 29 -> 28; matrix products, arithmetic and copies ran while one was open for 13% -> 12% of each run, Pallas kernels for 22% -> 22%
where the time goes in v4:
time: 394 us; the launch traced here: 389 us
  waiting for transfers between devices  113 us (29%)
  Pallas kernels  104 us (26%)
  starting transfers between devices  75.7 us (19%)
  local copies, waits for them, and re-layouts  45.8 us (12%)
  other arithmetic  27.4 us (7%)
  matrix products  19.5 us (5%)
    ppermute x64, waiting for transfers between devices, swap(): return lax.ppermute(value, axis, [(i, i ^ distance) for i in range(size)])  113 us
    ppermute x64, starting transfers between devices, swap(): return lax.ppermute(value, axis, [(i, i ^ distance) for i in range(size)])  75.7 us
    pallas_call x2, Pallas kernels, attention_backward(): pl.pallas_call(attention_backward_kernel, grid=(1,), in_specs=[pl.BlockSp...  31.6 us
    unnamed x208, local copies, waits for them, and re-layouts  25.2 us
    dot_general x9, matrix products, product(): return lax.dot_general(left, right, dims, preferred_element_type=FULL)  19.5 us
    pallas_call x4, Pallas kernels, by_rows(): pl.pallas_call(kernel, grid=(count // chunk,), in_specs=in_specs, out_spe...  19.5 us
    pallas_call x1, Pallas kernels, feed_forward(): pl.pallas_call(lambda *refs: feed_forward_kernel(expand, reduce, edge, *r...  18.7 us
    pallas_call x2, Pallas kernels, attention_forward(): pl.pallas_call(attention_forward_kernel, grid=(1,), in_specs=[pl.BlockSpe...  14.9 us
  transfers between devices with their start and end apart: 64, of which 28 were waited for; matrix products, arithmetic and copies ran while one was open for 12% of the time, Pallas kernels for 22%

profile of v4, /device:TPU:0, one launch (start us, length us, event | category | flops | bytes accessed | tf_op | source)
XLA Modules:
  0.0 388.7 jit_solution(20397070609292830)
XLA Ops:
  8.6 3.0 collective-permute-start.3
  17.5 11.6 %collective-permute-done.1 = bf16[392,256]{1,0:T(8,128)(2,1)S(1)} collective-permute-done((bf16[392,256]{1,0:T(8,128)(2,1)}, bf16[392,256]{1,0:T(8,128)(2,1)S(1)}, u32[]{:S(2)}, u32[]{:S(2)}) %collective-permute-start.1) | collective-permute-done | bytes 200736 | tf_op jit(solution)/shard_map/ppermute | solution.py:481
  29.1 5.4 %collective-permute-done.2 = bf16[392,256]{1,0:T(8,128)(2,1)S(1)} collective-permute-done((bf16[392,256]{1,0:T(8,128)(2,1)}, bf16[392,256]{1,0:T(8,128)(2,1)S(1)}, u32[]{:S(2)}, u32[]{:S(2)}) %collective-permute-start.2) | collective-permute-done | bytes 200736 | tf_op jit(solution)/shard_map/ppermute | solution.py:481
  34.6 3.0 collective-permute-done.3.refs_6_
  48.3 4.9 %collective-permute-done.6 = bf16[128,1280]{1,0:T(8,128)(2,1)} collective-permute-done((bf16[128,1280]{1,0:T(8,128)(2,1)}, bf16[128,1280]{1,0:T(8,128)(2,1)}, u32[]{:S(2)}, u32[]{:S(2)}) %collective-permute-start.6) | collective-permute-done | bytes 327712 | tf_op jit(solution)/shard_map/ppermute | solution.py:481
  65.2 3.1 joint_projection.1.q_ref.k_ref.v_ref
  69.5 7.2 %attention_forward.2 = (bf16[1568,128]{1,0:T(8,128)(2,1)S(1)}, f32[8,1568]{1,0:T(8,128)S(1)}) custom-call(bf16[1568,768]{1,0:T(8,128)(2,1)S(1)} %joint_projection.1.q_ref.k_ref.v_ref, bf16[1568,768]{1,0:T(8,128)(2,1)S(1)} %joint_projection.1.q_ref.k_ref.v_ref, bf16[1568,768]{1,0:T(8,128)(2,1)S(1)} %joint_projection.1.q_ref.k_ref.v_ref), custom_call_target="tpu_custom_call" | custom-call | tf_op jit(solution)/shard_map/attention_forward/pallas_call | solution.py:240
  82.1 7.7 %attention_forward.3 = (bf16[1568,128]{1,0:T(8,128)(2,1)S(1)}, f32[8,1568]{1,0:T(8,128)S(1)}) custom-call(bf16[1568,768]{1,0:T(8,128)(2,1)S(1)} %joint_projection.1.q_ref.k_ref.v_ref, bf16[1568,768]{1,0:T(8,128)(2,1)S(1)} %joint_projection.1.q_ref.k_ref.v_ref, bf16[1568,768]{1,0:T(8,128)(2,1)S(1)} %joint_projection.1.q_ref.k_ref.v_ref), custom_call_target="tpu_custom_call" | custom-call | tf_op jit(solution)/shard_map/attention_forward/pallas_call | solution.py:240
  97.3 5.2 %collective-permute-done.17 = bf16[392,128]{1,0:T(8,128)(2,1)S(1)} collective-permute-done((bf16[392,128]{1,0:T(8,128)(2,1)S(1)}, bf16[392,128]{1,0:T(8,128)(2,1)S(1)}, u32[]{:S(2)}, u32[]{:S(2)}) %collective-permute-start.17) | collective-permute-done | bytes 100384 | tf_op jit(solution)/shard_map/ppermute | solution.py:481
  109.0 3.4 convert_reduce_fusion.1
  114.1 6.2 %second_norm.1.refs_1_ = bf16[784,1024]{1,0:T(8,128)(2,1)S(1)} custom-call(bf16[784,1024]{1,0:T(8,128)(2,1)S(1)} %bitcast.92, bf16[784,1024]{1,0:T(8,128)(2,1)} %convolution_convert_fusion.6.one_ref, bf16[784,1024]{1,0:T(8,128)(2,1)} %collective-permute-done.21.two_ref, f32[1,1024]{1,0:T(1,128)S(1)} %bitcast.100, f32[1,1024]{1,0:T(1,128)S(1)} %bitcast.104, ...), custom_call_target="tpu_custom_call" | custom-call | tf_op jit(solution)/shard_map/second_norm/pallas_call | solution.py:104
  123.1 18.7 %feed_forward.1 = (bf16[784,2048]{1,0:T(8,128)(2,1)}, bf16[784,2048]{1,0:T(8,128)(2,1)}, bf16[784,1024]{1,0:T(8,128)(2,1)}, f32[1,2048]{1,0:T(1,128)S(1)}) custom-call(s32[5]{0:T(128)S(1)} %multiply_add_fusion.refs_0_.place_ref, bf16[784,1024]{1,0:T(8,128)(2,1)} %copy-done.19, bf16[784,1024]{1,0:T(8,128)(2,1)} %bitcast.95, f32[1,2048]{1,0:T(1,128)S(1)} %bitcast.106, ...), custom_call_target="tpu_custom_call" | custom-call | tf_op jit(solution)/shard_map/feed_forward/pallas_call | solution.py:415
  141.9 3.3 convolution_convert_fusion.5
  152.6 6.3 %second_norm_back.1 = (bf16[784,1024]{1,0:T(8,128)(2,1)S(1)}, f32[784,1024]{1,0:T(8,128)S(1)}, f32[8,1024]{1,0:T(8,128)S(1)}) custom-call(bf16[784,1024]{1,0:T(8,128)(2,1)S(1)} %bitcast.93, bf16[784,1024]{1,0:T(8,128)(2,1)} %convolution_convert_fusion.6.one_ref, bf16[784,1024]{1,0:T(8,128)(2,1)} %collective-permute-done.21.two_ref, f32[1,1024]{1,0:T(1,128)S(1)} %bitcast.101, ...), custom_call_target="tpu_custom_call" | custom-call | tf_op jit(solution)/shard_map/second_norm_back/pallas_call | solution.py:104
  169.5 5.0 %convolution_convert_fusion = bf16[1024,2048]{1,0:T(8,128)(2,1)S(1)} fusion(bf16[784,1024]{1,0:T(8,128)(2,1)S(1)} %bitcast.97, bf16[784,2048]{1,0:T(8,128)(2,1)S(1)} %copy-done.32), kind=kOutput, calls=%fused_computation.1 | convolution fusion | flops 3290431488 | bytes 9011200 | tf_op jit(solution)/shard_map/dot_general | solution.py:19
  178.3 3.2 collective-permute-done.28
  181.5 9.6 %collective-permute-done.30 = bf16[256,2048]{1,0:T(8,128)(2,1)S(1)} collective-permute-done((bf16[256,2048]{1,0:T(8,128)(2,1)S(1)}, bf16[256,2048]{1,0:T(8,128)(2,1)S(1)}, u32[]{:S(2)}, u32[]{:S(2)}) %collective-permute-start.30) | collective-permute-done | bytes 1048608 | tf_op jit(solution)/shard_map/ppermute | solution.py:481
  197.4 15.9 %attention_backward.2 = (bf16[1568,128]{1,0:T(8,128)(2,1)S(1)}, bf16[1568,128]{1,0:T(8,128)(2,1)S(1)}, bf16[1568,128]{1,0:T(8,128)(2,1)S(1)}) custom-call(bf16[1568,768]{1,0:T(8,128)(2,1)S(1)} %joint_projection.1.q_ref.k_ref.v_ref, bf16[1568,768]{1,0:T(8,128)(2,1)S(1)} %joint_projection.1.q_ref.k_ref.v_ref, ...), custom_call_target="tpu_custom_call" | custom-call | tf_op jit(solution)/shard_map/attention_backward/pallas_call | solution.py:313
  223.8 15.7 %attention_backward.3 = (bf16[1568,128]{1,0:T(8,128)(2,1)S(1)}, bf16[1568,128]{1,0:T(8,128)(2,1)S(1)}, bf16[1568,128]{1,0:T(8,128)(2,1)S(1)}) custom-call(bf16[1568,768]{1,0:T(8,128)(2,1)S(1)} %joint_projection.1.q_ref.k_ref.v_ref, bf16[1568,768]{1,0:T(8,128)(2,1)S(1)} %joint_projection.1.q_ref.k_ref.v_ref, ...), custom_call_target="tpu_custom_call" | custom-call | tf_op jit(solution)/shard_map/attention_backward/pallas_call | solution.py:313
  246.8 2.9 first_slope.1
  251.9 8.3 %collective-permute-done.44 = bf16[64,2048]{1,0:T(8,128)(2,1)S(1)} collective-permute-done((bf16[64,2048]{1,0:T(8,128)(2,1)S(1)}, bf16[64,2048]{1,0:T(8,128)(2,1)S(1)}, u32[]{:S(2)}, u32[]{:S(2)}) %collective-permute-start.44) | collective-permute-done | bytes 262176 | tf_op jit(solution)/shard_map/ppermute | solution.py:481
  264.1 6.0 %joint_grad.1 = bf16[4,256,768]{2,1,0:T(8,128)(2,1)S(1)} custom-call(s32[1]{0:T(128)} %bitcast.21.refs_0_, bf16[1568,512]{1,0:T(8,128)(2,1)S(1)} %copy-done.7, bf16[1568,512]{1,0:T(8,128)(2,1)S(1)} %copy-done.9, bf16[1568,768]{1,0:T(8,128)(2,1)} %copy-done.3), custom_call_target="tpu_custom_call" | custom-call | tf_op jit(solution)/shard_map/joint_grad/pallas_call | solution.py:188
  272.8 4.0 %collective-permute-done.40 = bf16[128,768]{1,0:T(8,128)(2,1)S(1)} collective-permute-done((bf16[128,768]{1,0:T(8,128)(2,1)S(1)}, bf16[128,768]{1,0:T(8,128)(2,1)S(1)}, u32[]{:S(2)}, u32[]{:S(2)}) %collective-permute-start.40) | collective-permute-done | bytes 196640 | tf_op jit(solution)/shard_map/ppermute | solution.py:481
  277.2 4.8 %collective-permute-done.39 = bf16[392,1024]{1,0:T(8,128)(2,1)S(1)} collective-permute-done((bf16[392,1024]{1,0:T(8,128)(2,1)S(1)}, bf16[392,1024]{1,0:T(8,128)(2,1)S(1)}, u32[]{:S(2)}, u32[]{:S(2)}) %collective-permute-start.39) | collective-permute-done | bytes 802848 | tf_op jit(solution)/shard_map/ppermute | solution.py:481
  291.4 7.6 %reduce_output.1 = bf16[784,1024]{1,0:T(8,128)(2,1)S(1)} custom-call(s32[5]{0:T(128)S(1)} %multiply_add_fusion.refs_0_.place_ref, bf16[784,2048]{1,0:T(8,128)(2,1)S(1)} %copy-done.33, bf16[256,2048]{1,0:T(8,128)(2,1)S(1)} %copy-done.29, bf16[256,2048]{1,0:T(8,128)(2,1)S(1)} %copy-done.14, bf16[256,2048]{1,0:T(8,128)(2,1)S(1)} %copy-done.17, ...), custom_call_target="tpu_custom_call" | custom-call | tf_op jit(solution)/shard_map/reduce_output/pallas_call | solution.py:461
  299.1 8.4 %collective-permute-done.46 = bf16[392,256]{1,0:T(8,128)(2,1)S(1)} collective-permute-done((bf16[392,256]{1,0:T(8,128)(2,1)S(1)}, bf16[392,256]{1,0:T(8,128)(2,1)S(1)}, u32[]{:S(2)}, u32[]{:S(2)}) %collective-permute-start.46) | collective-permute-done | bytes 200736 | tf_op jit(solution)/shard_map/ppermute | solution.py:481
  319.4 5.1 %first_norm_back.1 = (f32[784,1024]{1,0:T(8,128)}, f32[8,1024]{1,0:T(8,128)S(1)}) custom-call(bf16[784,1024]{1,0:T(8,128)(2,1)S(1)} %bitcast.94, bf16[784,1024]{1,0:T(8,128)(2,1)S(1)} %pad_maximum_fusion.1.upstream_ref, f32[1,1024]{1,0:T(1,128)S(1)} %bitcast.103, bf16[784,1024]{1,0:T(8,128)(2,1)S(1)} %bitcast.98, f32[784,1024]{1,0:T(8,128)S(1)} %copy-done.31), custom_call_target="tpu_custom_call" | custom-call | tf_op jit(solution)/shard_map/first_norm_back/pallas_call | solution.py:104
  324.5 12.5 %collective-permute-done.63 = bf16[128,2048]{1,0:T(8,128)(2,1)S(1)} collective-permute-done((bf16[128,2048]{1,0:T(8,128)(2,1)S(1)}, bf16[128,2048]{1,0:T(8,128)(2,1)S(1)}, u32[]{:S(2)}, u32[]{:S(2)}) %collective-permute-start.63) | collective-permute-done | bytes 524320 | tf_op jit(solution)/shard_map/ppermute | solution.py:481
  343.1 3.4 add_add_fusion
  357.4 11.5 %collective-permute-done.61 = bf16[64,2560]{1,0:T(8,128)(2,1)S(1)} collective-permute-done((bf16[64,2560]{1,0:T(8,128)(2,1)S(1)}, bf16[64,2560]{1,0:T(8,128)(2,1)S(1)}, u32[]{:S(2)}, u32[]{:S(2)}) %collective-permute-start.61) | collective-permute-done | bytes 327712 | tf_op jit(solution)/shard_map/ppermute | solution.py:481
  369.0 3.1 collective-permute-start.62
  376.2 8.3 %collective-permute-done.62 = bf16[128,2560]{1,0:T(8,128)(2,1)} collective-permute-done((bf16[128,2560]{1,0:T(8,128)(2,1)S(1)}, bf16[128,2560]{1,0:T(8,128)(2,1)}, u32[]{:S(2)}, u32[]{:S(2)}) %collective-permute-start.62) | collective-permute-done | bytes 655392 | tf_op jit(solution)/shard_map/ppermute | solution.py:481
  (452 shorter events, 161.6 us)
Async XLA Ops:
  8.6 29.0 %collective-permute-start.3 = (bf16[256,2304]{1,0:T(8,128)(2,1)S(1)}, bf16[256,2304]{1,0:T(8,128)(2,1)S(1)}, u32[]{:S(2)}, u32[]{:S(2)}) collective-permute-start(bf16[256,2304]{1,0:T(8,128)(2,1)S(1)} %constant_dynamic-update-slice_fusion.refs_4_), channel_id=1, source_target_pairs={{0,8},{8,0},{16,24},{24,16},{1,9},{9,1},{17,25},{25,17},{2,10},{10... | collective-permute-start | bytes 3538952 | tf_op jit(solution)/shard_map/ppermute | solution.py:481
  11.6 27.4 %collective-permute-start.4 = (bf16[256,2304]{1,0:T(8,128)(2,1)S(1)}, bf16[256,2304]{1,0:T(8,128)(2,1)S(1)}, u32[]{:S(2)}, u32[]{:S(2)}) collective-permute-start(bf16[256,2304]{1,0:T(8,128)(2,1)S(1)} %constant_dynamic-update-slice_fusion.refs_4_), channel_id=1, source_target_pairs={{0,16},{8,24},{16,0},{24,8},{1,17},{9,25},{17,1},{25,9},{2,18},{10... | collective-permute-start | bytes 3538952 | tf_op jit(solution)/shard_map/ppermute | solution.py:481
  13.1 21.4 %collective-permute-start = (bf16[392,512]{1,0:T(8,128)(2,1)}, bf16[392,512]{1,0:T(8,128)(2,1)S(1)}, u32[]{:S(2)}, u32[]{:S(2)}) collective-permute-start(bf16[392,512]{1,0:T(8,128)(2,1)} %get-tuple-element.173), channel_id=1, source_target_pairs={{0,2},{2,0},{4,6},{6,4},{1,3},{3,1},{5,7},{7,5},{8,10},{10,8},{12,... | collective-permute-start | bytes 1204232 | tf_op jit(solution)/shard_map/ppermute | solution.py:481
  17.3 17.3 %collective-permute-start.2 = (bf16[392,256]{1,0:T(8,128)(2,1)}, bf16[392,256]{1,0:T(8,128)(2,1)S(1)}, u32[]{:S(2)}, u32[]{:S(2)}) collective-permute-start(bf16[392,256]{1,0:T(8,128)(2,1)} %get-tuple-element.175), channel_id=1, source_target_pairs={{0,6},{2,4},{4,2},{6,0},{1,7},{3,5},{5,3},{7,1},{8,14},{10,12},{12... | collective-permute-start | bytes 602120 | tf_op jit(solution)/shard_map/ppermute | solution.py:481
  46.3 31.1 %collective-permute-start.9 = (bf16[256,1024]{1,0:T(8,128)(2,1)S(1)}, bf16[256,1024]{1,0:T(8,128)(2,1)S(1)}, u32[]{:S(2)}, u32[]{:S(2)}) collective-permute-start(bf16[256,1024]{1,0:T(8,128)(2,1)S(1)} %copy-done.34), channel_id=1, source_target_pairs={{0,8},{8,0},{16,24},{24,16},{1,9},{9,1},{17,25},{25,17},{2,10},{10... | collective-permute-start | bytes 1572872 | tf_op jit(solution)/shard_map/ppermute | solution.py:481
  47.7 29.7 %collective-permute-start.10 = (bf16[256,1024]{1,0:T(8,128)(2,1)S(1)}, bf16[256,1024]{1,0:T(8,128)(2,1)S(1)}, u32[]{:S(2)}, u32[]{:S(2)}) collective-permute-start(bf16[256,1024]{1,0:T(8,128)(2,1)S(1)} %copy-done.34), channel_id=1, source_target_pairs={{0,16},{8,24},{16,0},{24,8},{1,17},{9,25},{17,1},{25,9},{2,18},{10... | collective-permute-start | bytes 1572872 | tf_op jit(solution)/shard_map/ppermute | solution.py:481
  61.0 28.8 %collective-permute-start.14 = (bf16[256,2048]{1,0:T(8,128)(2,1)S(1)}, bf16[256,2048]{1,0:T(8,128)(2,1)S(1)}, u32[]{:S(2)}, u32[]{:S(2)}) collective-permute-start(bf16[256,2048]{1,0:T(8,128)(2,1)S(1)} %copy-done.27), channel_id=1, source_target_pairs={{0,8},{8,0},{16,24},{24,16},{1,9},{9,1},{17,25},{25,17},{2,10},{10... | collective-permute-start | bytes 3145736 | tf_op jit(solution)/shard_map/ppermute | solution.py:481
  62.4 27.4 %collective-permute-start.15 = (bf16[256,2048]{1,0:T(8,128)(2,1)S(1)}, bf16[256,2048]{1,0:T(8,128)(2,1)S(1)}, u32[]{:S(2)}, u32[]{:S(2)}) collective-permute-start(bf16[256,2048]{1,0:T(8,128)(2,1)S(1)} %copy-done.27), channel_id=1, source_target_pairs={{0,16},{8,24},{16,0},{24,8},{1,17},{9,25},{17,1},{25,9},{2,18},{10... | collective-permute-start | bytes 3145736 | tf_op jit(solution)/shard_map/ppermute | solution.py:481
  162.4 15.9 %collective-permute-start.27 = (bf16[392,256]{1,0:T(8,128)(2,1)S(1)}, bf16[392,256]{1,0:T(8,128)(2,1)S(1)}, u32[]{:S(2)}, u32[]{:S(2)}) collective-permute-start(bf16[392,256]{1,0:T(8,128)(2,1)S(1)} %get-tuple-element.241), channel_id=1, source_target_pairs={{0,2},{2,0},{4,6},{6,4},{1,3},{3,1},{5,7},{7,5},{8,10},{10,8},{12,... | collective-permute-start | bytes 602120 | tf_op jit(solution)/shard_map/ppermute | solution.py:481
  164.1 17.4 %collective-permute-start.28 = (bf16[392,256]{1,0:T(8,128)(2,1)S(1)}, bf16[392,256]{1,0:T(8,128)(2,1)S(1)}, u32[]{:S(2)}, u32[]{:S(2)}) collective-permute-start(bf16[392,256]{1,0:T(8,128)(2,1)S(1)} %get-tuple-element.242), channel_id=1, source_target_pairs={{0,4},{2,6},{4,0},{6,2},{1,5},{3,7},{5,1},{7,3},{8,12},{10,14},{12... | collective-permute-start | bytes 602120 | tf_op jit(solution)/shard_map/ppermute | solution.py:481
  165.3 16.2 %collective-permute-start.29 = (bf16[392,256]{1,0:T(8,128)(2,1)S(1)}, bf16[392,256]{1,0:T(8,128)(2,1)S(1)}, u32[]{:S(2)}, u32[]{:S(2)}) collective-permute-start(bf16[392,256]{1,0:T(8,128)(2,1)S(1)} %get-tuple-element.243), channel_id=1, source_target_pairs={{0,6},{2,4},{4,2},{6,0},{1,7},{3,5},{5,3},{7,1},{8,14},{10,12},{12... | collective-permute-start | bytes 602120 | tf_op jit(solution)/shard_map/ppermute | solution.py:481
  166.8 24.2 %collective-permute-start.30 = (bf16[256,2048]{1,0:T(8,128)(2,1)S(1)}, bf16[256,2048]{1,0:T(8,128)(2,1)S(1)}, u32[]{:S(2)}, u32[]{:S(2)}) collective-permute-start(bf16[256,2048]{1,0:T(8,128)(2,1)S(1)} %pad_maximum_fusion.3), channel_id=1, source_target_pairs={{0,8},{8,0},{16,24},{24,16},{1,9},{9,1},{17,25},{25,17},{2,10},{10... | collective-permute-start | bytes 3145736 | tf_op jit(solution)/shard_map/ppermute | solution.py:481
  168.2 24.0 %collective-permute-start.31 = (bf16[256,2048]{1,0:T(8,128)(2,1)S(1)}, bf16[256,2048]{1,0:T(8,128)(2,1)S(1)}, u32[]{:S(2)}, u32[]{:S(2)}) collective-permute-start(bf16[256,2048]{1,0:T(8,128)(2,1)S(1)} %pad_maximum_fusion.4), channel_id=1, source_target_pairs={{0,16},{8,24},{16,0},{24,8},{1,17},{9,25},{17,1},{25,9},{2,18},{10... | collective-permute-start | bytes 3145736 | tf_op jit(solution)/shard_map/ppermute | solution.py:481
  192.8 20.7 %collective-permute-start.32 = (bf16[128,2560]{1,0:T(8,128)(2,1)S(1)}, bf16[128,2560]{1,0:T(8,128)(2,1)S(1)}, u32[]{:S(2)}, u32[]{:S(2)}) collective-permute-start(bf16[128,2560]{1,0:T(8,128)(2,1)S(1)} %get-tuple-element.262), channel_id=1, source_target_pairs={{0,8},{8,0},{16,24},{24,16},{1,9},{9,1},{17,25},{25,17},{2,10},{10... | collective-permute-start | bytes 1966088 | tf_op jit(solution)/shard_map/ppermute | solution.py:481
  193.6 20.0 %collective-permute-start.33 = (bf16[128,2560]{1,0:T(8,128)(2,1)S(1)}, bf16[128,2560]{1,0:T(8,128)(2,1)S(1)}, u32[]{:S(2)}, u32[]{:S(2)}) collective-permute-start(bf16[128,2560]{1,0:T(8,128)(2,1)S(1)} %get-tuple-element.263), channel_id=1, source_target_pairs={{0,16},{8,24},{16,0},{24,8},{1,17},{9,25},{17,1},{25,9},{2,18},{10... | collective-permute-start | bytes 1966088 | tf_op jit(solution)/shard_map/ppermute | solution.py:481
  196.0 17.5 %collective-permute-start.34 = (bf16[128,2048]{1,0:T(8,128)(2,1)S(1)}, bf16[128,2048]{1,0:T(8,128)(2,1)S(1)}, u32[]{:S(2)}, u32[]{:S(2)}) collective-permute-start(bf16[128,2048]{1,0:T(8,128)(2,1)S(1)} %dynamic-slice_convert_fusion.1), channel_id=1, source_target_pairs={{0,2},{2,0},{4,6},{6,4},{1,3},{3,1},{5,7},{7,5},{8,10},{10,8},{12,... | collective-permute-start | bytes 1572872 | tf_op jit(solution)/shard_map/ppermute | solution.py:481
  217.4 22.2 %collective-permute-start.36 = (bf16[128,2560]{1,0:T(8,128)(2,1)}, bf16[128,2560]{1,0:T(8,128)(2,1)}, u32[]{:S(2)}, u32[]{:S(2)}) collective-permute-start(bf16[128,2560]{1,0:T(8,128)(2,1)} %fusion.5), channel_id=1, source_target_pairs={{0,8},{8,0},{16,24},{24,16},{1,9},{9,1},{17,25},{25,17},{2,10},{10... | collective-permute-start | bytes 1966088 | tf_op jit(solution)/shard_map/ppermute | solution.py:481
  218.8 20.8 %collective-permute-start.37 = (bf16[128,2560]{1,0:T(8,128)(2,1)}, bf16[128,2560]{1,0:T(8,128)(2,1)}, u32[]{:S(2)}, u32[]{:S(2)}) collective-permute-start(bf16[128,2560]{1,0:T(8,128)(2,1)} %fusion.4), channel_id=1, source_target_pairs={{0,16},{8,24},{16,0},{24,8},{1,17},{9,25},{17,1},{25,9},{2,18},{10... | collective-permute-start | bytes 1966088 | tf_op jit(solution)/shard_map/ppermute | solution.py:481
  219.4 20.2 %collective-permute-start.35 = (bf16[64,2048]{1,0:T(8,128)(2,1)}, bf16[64,2048]{1,0:T(8,128)(2,1)S(1)}, u32[]{:S(2)}, u32[]{:S(2)}) collective-permute-start(bf16[64,2048]{1,0:T(8,128)(2,1)} %dynamic-slice_convert_fusion.3), channel_id=1, source_target_pairs={{0,4},{2,6},{4,0},{6,2},{1,5},{3,7},{5,1},{7,3},{8,12},{10,14},{12... | collective-permute-start | bytes 786440 | tf_op jit(solution)/shard_map/ppermute | solution.py:481
  249.7 23.1 %collective-permute-start.42 = (bf16[128,2560]{1,0:T(8,128)(2,1)S(1)}, bf16[128,2560]{1,0:T(8,128)(2,1)S(1)}, u32[]{:S(2)}, u32[]{:S(2)}) collective-permute-start(bf16[128,2560]{1,0:T(8,128)(2,1)S(1)} %copy-done.83), channel_id=1, source_target_pairs={{0,8},{8,0},{16,24},{24,16},{1,9},{9,1},{17,25},{25,17},{2,10},{10... | collective-permute-start | bytes 1966088 | tf_op jit(solution)/shard_map/ppermute | solution.py:481
  250.4 22.4 %collective-permute-start.43 = (bf16[128,2560]{1,0:T(8,128)(2,1)S(1)}, bf16[128,2560]{1,0:T(8,128)(2,1)S(1)}, u32[]{:S(2)}, u32[]{:S(2)}) collective-permute-start(bf16[128,2560]{1,0:T(8,128)(2,1)S(1)} %copy-done.84), channel_id=1, source_target_pairs={{0,16},{8,24},{16,0},{24,8},{1,17},{9,25},{17,1},{25,9},{2,18},{10... | collective-permute-start | bytes 1966088 | tf_op jit(solution)/shard_map/ppermute | solution.py:481
  262.4 19.7 %collective-permute-start.39 = (bf16[392,1024]{1,0:T(8,128)(2,1)S(1)}, bf16[392,1024]{1,0:T(8,128)(2,1)S(1)}, u32[]{:S(2)}, u32[]{:S(2)}) collective-permute-start(bf16[392,1024]{1,0:T(8,128)(2,1)S(1)} %pad_maximum_fusion.7), channel_id=1, source_target_pairs={{0,2},{2,0},{4,6},{6,4},{1,3},{3,1},{5,7},{7,5},{8,10},{10,8},{12,... | collective-permute-start | bytes 2408456 | tf_op jit(solution)/shard_map/ppermute | solution.py:481
  285.7 24.2 %collective-permute-start.49 = (bf16[128,2560]{1,0:T(8,128)(2,1)S(1)}, bf16[128,2560]{1,0:T(8,128)(2,1)S(1)}, u32[]{:S(2)}, u32[]{:S(2)}) collective-permute-start(bf16[128,2560]{1,0:T(8,128)(2,1)S(1)} %dynamic-slice_convert_fusion), channel_id=1, source_target_pairs={{0,2},{2,0},{4,6},{6,4},{1,3},{3,1},{5,7},{7,5},{8,10},{10,8},{12,... | collective-permute-start | bytes 1966088 | tf_op jit(solution)/shard_map/ppermute | solution.py:481
  286.1 21.5 %collective-permute-start.46 = (bf16[392,256]{1,0:T(8,128)(2,1)S(1)}, bf16[392,256]{1,0:T(8,128)(2,1)S(1)}, u32[]{:S(2)}, u32[]{:S(2)}) collective-permute-start(bf16[392,256]{1,0:T(8,128)(2,1)S(1)} %get-tuple-element.301), channel_id=1, source_target_pairs={{0,6},{2,4},{4,2},{6,0},{1,7},{3,5},{5,3},{7,1},{8,14},{10,12},{12... | collective-permute-start | bytes 602120 | tf_op jit(solution)/shard_map/ppermute | solution.py:481
  287.6 20.5 %collective-permute-start.45 = (bf16[392,256]{1,0:T(8,128)(2,1)S(1)}, bf16[392,256]{1,0:T(8,128)(2,1)S(1)}, u32[]{:S(2)}, u32[]{:S(2)}) collective-permute-start(bf16[392,256]{1,0:T(8,128)(2,1)S(1)} %get-tuple-element.300), channel_id=1, source_target_pairs={{0,4},{2,6},{4,0},{6,2},{1,5},{3,7},{5,1},{7,3},{8,12},{10,14},{12... | collective-permute-start | bytes 602120 | tf_op jit(solution)/shard_map/ppermute | solution.py:481
  289.3 18.8 %collective-permute-start.47 = (bf16[256,768]{1,0:T(8,128)(2,1)S(1)}, bf16[256,768]{1,0:T(8,128)(2,1)S(1)}, u32[]{:S(2)}, u32[]{:S(2)}) collective-permute-start(bf16[256,768]{1,0:T(8,128)(2,1)S(1)} %pad_maximum_fusion.18), channel_id=1, source_target_pairs={{0,8},{8,0},{16,24},{24,16},{1,9},{9,1},{17,25},{25,17},{2,10},{10... | collective-permute-start | bytes 1179656 | tf_op jit(solution)/shard_map/ppermute | solution.py:481
  289.9 18.2 %collective-permute-start.48 = (bf16[256,768]{1,0:T(8,128)(2,1)S(1)}, bf16[256,768]{1,0:T(8,128)(2,1)S(1)}, u32[]{:S(2)}, u32[]{:S(2)}) collective-permute-start(bf16[256,768]{1,0:T(8,128)(2,1)S(1)} %pad_maximum_fusion.19), channel_id=1, source_target_pairs={{0,16},{8,24},{16,0},{24,8},{1,17},{9,25},{17,1},{25,9},{2,18},{10... | collective-permute-start | bytes 1179656 | tf_op jit(solution)/shard_map/ppermute | solution.py:481
  310.2 28.4 %collective-permute-start.51 = (bf16[784,1024]{1,0:T(8,128)(2,1)S(1)}, bf16[784,1024]{1,0:T(8,128)(2,1)S(1)}, u32[]{:S(2)}, u32[]{:S(2)}) collective-permute-start(bf16[784,1024]{1,0:T(8,128)(2,1)S(1)} %reduce_output.1), channel_id=1, source_target_pairs={{0,1},{1,0},{2,3},{3,2},{4,5},{5,4},{6,7},{7,6},{8,9},{9,8},{10,11... | collective-permute-start | bytes 4816904 | tf_op jit(solution)/shard_map/ppermute | solution.py:481
  312.4 24.5 %collective-permute-start.63 = (bf16[128,2048]{1,0:T(8,128)(2,1)S(1)}, bf16[128,2048]{1,0:T(8,128)(2,1)S(1)}, u32[]{:S(2)}, u32[]{:S(2)}) collective-permute-start(bf16[128,2048]{1,0:T(8,128)(2,1)S(1)} %maximum_select_fusion.3), channel_id=1, source_target_pairs={{0,2},{2,0},{4,6},{6,4},{1,3},{3,1},{5,7},{7,5},{8,10},{10,8},{12,... | collective-permute-start | bytes 1572872 | tf_op jit(solution)/shard_map/ppermute | solution.py:481
  313.5 36.7 %collective-permute-start.55 = (bf16[256,768]{1,0:T(8,128)(2,1)S(1)}, bf16[256,768]{1,0:T(8,128)(2,1)S(1)}, u32[]{:S(2)}, u32[]{:S(2)}) collective-permute-start(bf16[256,768]{1,0:T(8,128)(2,1)S(1)} %fusion.2), channel_id=1, source_target_pairs={{0,4},{2,6},{4,0},{6,2},{1,5},{3,7},{5,1},{7,3},{8,12},{10,14},{12... | collective-permute-start | bytes 1179656 | tf_op jit(solution)/shard_map/ppermute | solution.py:481
  314.9 35.4 %collective-permute-start.56 = (bf16[64,2560]{1,0:T(8,128)(2,1)S(1)}, bf16[64,2560]{1,0:T(8,128)(2,1)S(1)}, u32[]{:S(2)}, u32[]{:S(2)}) collective-permute-start(bf16[64,2560]{1,0:T(8,128)(2,1)S(1)} %dynamic-slice_convert_fusion.2), channel_id=1, source_target_pairs={{0,4},{2,6},{4,0},{6,2},{1,5},{3,7},{5,1},{7,3},{8,12},{10,14},{12... | collective-permute-start | bytes 983048 | tf_op jit(solution)/shard_map/ppermute | solution.py:481
  354.3 19.8 %collective-permute-start.60 = (bf16[256,768]{1,0:T(8,128)(2,1)S(1)}, bf16[256,768]{1,0:T(8,128)(2,1)S(1)}, u32[]{:S(2)}, u32[]{:S(2)}) collective-permute-start(bf16[256,768]{1,0:T(8,128)(2,1)S(1)} %add_convert_fusion.7), channel_id=1, source_target_pairs={{0,2},{2,0},{4,6},{6,4},{1,3},{3,1},{5,7},{7,5},{8,10},{10,8},{12,... | collective-permute-start | bytes 1179656 | tf_op jit(solution)/shard_map/ppermute | solution.py:481
  (130 other events, 905.8 us)

commit v5 on v4

--- a/solution.py
+++ b/solution.py
@@ -662,14 +662,13 @@
     far_right = swap(right, "ctx", 3)
     wide_held = gather_near(wide_part)
 
-    near_rows, across_left, far_right, wide_held, expand_rest = fence(
-        near_rows, across_left, far_right, wide_held, expand_weight[:, early:]
-    )
+    near_rows, across_left, far_right = fence(near_rows, across_left, far_right)
     passed = swap(jnp.concatenate([across_left, far_right], axis=1), "ctx", 1)
+    wide_held, expand_rest = fence(wide_held, expand_weight[:, early:])
     held = gather_far(tuple(piece[:, early:] for piece in wide_held))
     rest_held = gather_near(expand_rest)
 
-    passed, held = fence(passed, held)
+    (passed,) = fence(passed)
     cross_rows = jnp.concatenate(
         [
             near_rows,
@@ -842,7 +841,7 @@
     )
     if four:
         wide_late = near_rows_out(wide_late)
-    expand_rows = join_rows(both(expand_rows).astype(LOW), clip_at, 2)
+    expand_rows = both(expand_rows).astype(LOW)
     joint_slope = jnp.concatenate(
         [grad[kind] for kind in range(3) for grad in (grad_first, grad_second)], axis=1
     )
@@ -854,7 +853,10 @@
         wide_near = lax.psum_scatter(
             jnp.concatenate(wide, axis=1), "fsdp", scatter_dimension=0, tiled=True
         )
-    first_half, joint_slope = fence(first_half, joint_slope)
+    first_half, joint_slope, expand_rows, wide_late = fence(
+        first_half, joint_slope, expand_rows, wide_late
+    )
+    expand_rows = join_rows(expand_rows, clip_at, 2)
     pieces = first_half.reshape(4, rows_here, width_half)
     passing = jnp.concatenate([pieces[1], pieces[3][:, :quarter], pieces[2][:, quarter:]], axis=1)
     passing = swap(passing, "ctx", 1)
@@ -867,9 +869,7 @@
     )
 
     joint_far = far_halves(joint_parts[0]) if four else ()
-    passing, joint_far, wide_late, expand_rows = fence(
-        passing, joint_far, wide_late, expand_rows
-    )
+    passing, joint_far, expand_rows = fence(passing, joint_far, expand_rows)
     if four:
         near_sum = [both((wide_early[0], wide_late[1])), both((wide_late[0], wide_early[1]))]
         wide_sum = rows_at(wide, 0).astype(FULL) + jnp.concatenate(near_sum, axis=0)

time: 394 us -> 405 us (1.028)
  waiting for transfers between devices: 113 us -> 127 us
  local copies, waits for them, and re-layouts: 45.8 us -> 39 us
    ppermute x64, waiting for transfers between devices: 113 us -> 127 us  [swap(): return lax.ppermute(value, axis, [(i, i ^ distance) for i in range(size)])]
    unnamed x208 -> x196, local copies, waits for them, and re-layouts: 25.2 us -> 22.8 us
  transfers between devices with their start and end apart: 64 -> 64, of which waited for: 28 -> 28; matrix products, arithmetic and copies ran while one was open for 12% -> 13% of each run, Pallas kernels for 22% -> 21%
where the time goes in v5:
time: 405 us; the launch traced here: 400 us
  waiting for transfers between devices  127 us (31%)
  Pallas kernels  104 us (26%)
  starting transfers between devices  77.2 us (19%)
  local copies, waits for them, and re-layouts  39 us (10%)
  other arithmetic  30.5 us (8%)
  matrix products  19.5 us (5%)
    ppermute x64, waiting for transfers between devices, swap(): return lax.ppermute(value, axis, [(i, i ^ distance) for i in range(size)])  127 us
    ppermute x64, starting transfers between devices, swap(): return lax.ppermute(value, axis, [(i, i ^ distance) for i in range(size)])  77.2 us
    pallas_call x2, Pallas kernels, attention_backward(): pl.pallas_call(attention_backward_kernel, grid=(1,), in_specs=[pl.BlockSp...  31.6 us
    unnamed x196, local copies, waits for them, and re-layouts  22.8 us
    dot_general x9, matrix products, product(): return lax.dot_general(left, right, dims, preferred_element_type=FULL)  19.5 us
    pallas_call x4, Pallas kernels, by_rows(): pl.pallas_call(kernel, grid=(count // chunk,), in_specs=in_specs, out_spe...  19.5 us
    pallas_call x1, Pallas kernels, feed_forward(): pl.pallas_call(lambda *refs: feed_forward_kernel(expand, reduce, edge, *r...  18.7 us
    pallas_call x2, Pallas kernels, attention_forward(): pl.pallas_call(attention_forward_kernel, grid=(1,), in_specs=[pl.BlockSpe...  14.9 us
  transfers between devices with their start and end apart: 64, of which 28 were waited for; matrix products, arithmetic and copies ran while one was open for 13% of the time, Pallas kernels for 21%

profile of v5, /device:TPU:0, one launch (start us, length us, event | category | flops | bytes accessed | tf_op | source)
XLA Modules:
  0.0 400.4 jit_solution(4021416436466579133)
XLA Ops:
  8.6 3.1 collective-permute-start
  17.5 8.5 %collective-permute-done.1 = bf16[392,256]{1,0:T(8,128)(2,1)S(1)} collective-permute-done((bf16[392,256]{1,0:T(8,128)(2,1)}, bf16[392,256]{1,0:T(8,128)(2,1)S(1)}, u32[]{:S(2)}, u32[]{:S(2)}) %collective-permute-start.1) | collective-permute-done | bytes 200736 | tf_op jit(solution)/shard_map/ppermute | solution.py:481
  26.1 6.0 %collective-permute-done.2 = bf16[392,256]{1,0:T(8,128)(2,1)S(1)} collective-permute-done((bf16[392,256]{1,0:T(8,128)(2,1)}, bf16[392,256]{1,0:T(8,128)(2,1)S(1)}, u32[]{:S(2)}, u32[]{:S(2)}) %collective-permute-start.2) | collective-permute-done | bytes 200736 | tf_op jit(solution)/shard_map/ppermute | solution.py:481
  33.7 9.6 %collective-permute-done.3 = bf16[392,512]{1,0:T(8,128)(2,1)} collective-permute-done((bf16[392,512]{1,0:T(8,128)(2,1)}, bf16[392,512]{1,0:T(8,128)(2,1)}, u32[]{:S(2)}, u32[]{:S(2)}) %collective-permute-start.3) | collective-permute-done | bytes 401440 | tf_op jit(solution)/shard_map/ppermute | solution.py:481
  50.5 16.7 %collective-permute-done.7 = bf16[128,1280]{1,0:T(8,128)(2,1)S(1)} collective-permute-done((bf16[128,1280]{1,0:T(8,128)(2,1)S(1)}, bf16[128,1280]{1,0:T(8,128)(2,1)S(1)}, u32[]{:S(2)}, u32[]{:S(2)}) %collective-permute-start.7) | collective-permute-done | bytes 327712 | tf_op jit(solution)/shard_map/ppermute | solution.py:481
  74.9 3.2 joint_projection.1.q_ref.k_ref.v_ref
  79.3 7.2 %attention_forward.2 = (bf16[1568,128]{1,0:T(8,128)(2,1)S(1)}, f32[8,1568]{1,0:T(8,128)S(1)}) custom-call(bf16[1568,768]{1,0:T(8,128)(2,1)S(1)} %joint_projection.1.q_ref.k_ref.v_ref, bf16[1568,768]{1,0:T(8,128)(2,1)S(1)} %joint_projection.1.q_ref.k_ref.v_ref, bf16[1568,768]{1,0:T(8,128)(2,1)S(1)} %joint_projection.1.q_ref.k_ref.v_ref), custom_call_target="tpu_custom_call" | custom-call | tf_op jit(solution)/shard_map/attention_forward/pallas_call | solution.py:240
  91.8 7.7 %attention_forward.3 = (bf16[1568,128]{1,0:T(8,128)(2,1)S(1)}, f32[8,1568]{1,0:T(8,128)S(1)}) custom-call(bf16[1568,768]{1,0:T(8,128)(2,1)S(1)} %joint_projection.1.q_ref.k_ref.v_ref, bf16[1568,768]{1,0:T(8,128)(2,1)S(1)} %joint_projection.1.q_ref.k_ref.v_ref, bf16[1568,768]{1,0:T(8,128)(2,1)S(1)} %joint_projection.1.q_ref.k_ref.v_ref), custom_call_target="tpu_custom_call" | custom-call | tf_op jit(solution)/shard_map/attention_forward/pallas_call | solution.py:240
  117.0 3.4 convert_reduce_fusion.1
  122.2 6.2 %second_norm.1.refs_1_ = bf16[784,1024]{1,0:T(8,128)(2,1)S(1)} custom-call(bf16[784,1024]{1,0:T(8,128)(2,1)S(1)} %bitcast.92, bf16[784,1024]{1,0:T(8,128)(2,1)} %convolution_convert_fusion.6.one_ref, bf16[784,1024]{1,0:T(8,128)(2,1)} %collective-permute-done.21.two_ref, f32[1,1024]{1,0:T(1,128)S(1)} %bitcast.100, f32[1,1024]{1,0:T(1,128)S(1)} %bitcast.104, ...), custom_call_target="tpu_custom_call" | custom-call | tf_op jit(solution)/shard_map/second_norm/pallas_call | solution.py:104
  131.9 18.7 %feed_forward.1 = (bf16[784,2048]{1,0:T(8,128)(2,1)}, bf16[784,2048]{1,0:T(8,128)(2,1)}, bf16[784,1024]{1,0:T(8,128)(2,1)}, f32[1,2048]{1,0:T(1,128)S(1)}) custom-call(s32[5]{0:T(128)S(1)} %multiply_add_fusion.refs_0_.place_ref, bf16[784,1024]{1,0:T(8,128)(2,1)} %copy-done.19, bf16[784,1024]{1,0:T(8,128)(2,1)} %bitcast.95, f32[1,2048]{1,0:T(1,128)S(1)} %bitcast.106, ...), custom_call_target="tpu_custom_call" | custom-call | tf_op jit(solution)/shard_map/feed_forward/pallas_call | solution.py:415
  150.7 3.3 convolution_convert_fusion.5
  161.4 6.3 %second_norm_back.1 = (bf16[784,1024]{1,0:T(8,128)(2,1)S(1)}, f32[784,1024]{1,0:T(8,128)S(1)}, f32[8,1024]{1,0:T(8,128)S(1)}) custom-call(bf16[784,1024]{1,0:T(8,128)(2,1)S(1)} %bitcast.93, bf16[784,1024]{1,0:T(8,128)(2,1)} %convolution_convert_fusion.6.one_ref, bf16[784,1024]{1,0:T(8,128)(2,1)} %collective-permute-done.21.two_ref, f32[1,1024]{1,0:T(1,128)S(1)} %bitcast.101, ...), custom_call_target="tpu_custom_call" | custom-call | tf_op jit(solution)/shard_map/second_norm_back/pallas_call | solution.py:104
  177.8 5.0 %convolution_convert_fusion = bf16[1024,2048]{1,0:T(8,128)(2,1)S(1)} fusion(bf16[784,1024]{1,0:T(8,128)(2,1)S(1)} %bitcast.97, bf16[784,2048]{1,0:T(8,128)(2,1)S(1)} %copy-done.32), kind=kOutput, calls=%fused_computation.1 | convolution fusion | flops 3290431488 | bytes 9011200 | tf_op jit(solution)/shard_map/dot_general | solution.py:19
  189.1 10.6 %collective-permute-done.30 = bf16[256,2048]{1,0:T(8,128)(2,1)S(1)} collective-permute-done((bf16[256,2048]{1,0:T(8,128)(2,1)S(1)}, bf16[256,2048]{1,0:T(8,128)(2,1)S(1)}, u32[]{:S(2)}, u32[]{:S(2)}) %collective-permute-start.30) | collective-permute-done | bytes 1048608 | tf_op jit(solution)/shard_map/ppermute | solution.py:481
  205.5 15.9 %attention_backward.2 = (bf16[1568,128]{1,0:T(8,128)(2,1)S(1)}, bf16[1568,128]{1,0:T(8,128)(2,1)S(1)}, bf16[1568,128]{1,0:T(8,128)(2,1)S(1)}) custom-call(bf16[1568,768]{1,0:T(8,128)(2,1)S(1)} %joint_projection.1.q_ref.k_ref.v_ref, bf16[1568,768]{1,0:T(8,128)(2,1)S(1)} %joint_projection.1.q_ref.k_ref.v_ref, ...), custom_call_target="tpu_custom_call" | custom-call | tf_op jit(solution)/shard_map/attention_backward/pallas_call | solution.py:313
  230.7 15.7 %attention_backward.3 = (bf16[1568,128]{1,0:T(8,128)(2,1)S(1)}, bf16[1568,128]{1,0:T(8,128)(2,1)S(1)}, bf16[1568,128]{1,0:T(8,128)(2,1)S(1)}) custom-call(bf16[1568,768]{1,0:T(8,128)(2,1)S(1)} %joint_projection.1.q_ref.k_ref.v_ref, bf16[1568,768]{1,0:T(8,128)(2,1)S(1)} %joint_projection.1.q_ref.k_ref.v_ref, ...), custom_call_target="tpu_custom_call" | custom-call | tf_op jit(solution)/shard_map/attention_backward/pallas_call | solution.py:313
  248.9 2.8 convolution_convert_fusion.1
  257.1 2.9 first_slope.1
  261.9 8.7 %collective-permute-done.39 = bf16[128,2560]{1,0:T(8,128)(2,1)S(1)} collective-permute-done((bf16[128,2560]{1,0:T(8,128)(2,1)}, bf16[128,2560]{1,0:T(8,128)(2,1)S(1)}, u32[]{:S(2)}, u32[]{:S(2)}) %collective-permute-start.39) | collective-permute-done | bytes 655392 | tf_op jit(solution)/shard_map/ppermute | solution.py:481
  275.2 3.0 collective-permute-start.44
  278.2 6.0 %joint_grad.1 = bf16[4,256,768]{2,1,0:T(8,128)(2,1)S(1)} custom-call(s32[1]{0:T(128)} %bitcast.21.refs_0_, bf16[1568,512]{1,0:T(8,128)(2,1)S(1)} %copy-done.7, bf16[1568,512]{1,0:T(8,128)(2,1)S(1)} %copy-done.9, bf16[1568,768]{1,0:T(8,128)(2,1)} %copy-done.3), custom_call_target="tpu_custom_call" | custom-call | tf_op jit(solution)/shard_map/joint_grad/pallas_call | solution.py:188
  286.9 7.6 %collective-permute-done.44 = bf16[64,2048]{1,0:T(8,128)(2,1)S(1)} collective-permute-done((bf16[64,2048]{1,0:T(8,128)(2,1)S(1)}, bf16[64,2048]{1,0:T(8,128)(2,1)S(1)}, u32[]{:S(2)}, u32[]{:S(2)}) %collective-permute-start.44) | collective-permute-done | bytes 262176 | tf_op jit(solution)/shard_map/ppermute | solution.py:481
  303.0 7.6 %reduce_output.1 = bf16[784,1024]{1,0:T(8,128)(2,1)S(1)} custom-call(s32[5]{0:T(128)S(1)} %multiply_add_fusion.refs_0_.place_ref, bf16[784,2048]{1,0:T(8,128)(2,1)S(1)} %copy-done.33, bf16[256,2048]{1,0:T(8,128)(2,1)S(1)} %copy-done.29, bf16[256,2048]{1,0:T(8,128)(2,1)S(1)} %copy-done.14, bf16[256,2048]{1,0:T(8,128)(2,1)S(1)} %copy-done.17, ...), custom_call_target="tpu_custom_call" | custom-call | tf_op jit(solution)/shard_map/reduce_output/pallas_call | solution.py:461
  310.5 9.3 %collective-permute-done.46 = bf16[392,256]{1,0:T(8,128)(2,1)S(1)} collective-permute-done((bf16[392,256]{1,0:T(8,128)(2,1)S(1)}, bf16[392,256]{1,0:T(8,128)(2,1)S(1)}, u32[]{:S(2)}, u32[]{:S(2)}) %collective-permute-start.46) | collective-permute-done | bytes 200736 | tf_op jit(solution)/shard_map/ppermute | solution.py:481
  331.1 5.1 %first_norm_back.1 = (f32[784,1024]{1,0:T(8,128)}, f32[8,1024]{1,0:T(8,128)S(1)}) custom-call(bf16[784,1024]{1,0:T(8,128)(2,1)S(1)} %bitcast.94, bf16[784,1024]{1,0:T(8,128)(2,1)S(1)} %pad_maximum_fusion.1.upstream_ref, f32[1,1024]{1,0:T(1,128)S(1)} %bitcast.103, bf16[784,1024]{1,0:T(8,128)(2,1)S(1)} %bitcast.98, f32[784,1024]{1,0:T(8,128)S(1)} %copy-done.31), custom_call_target="tpu_custom_call" | custom-call | tf_op jit(solution)/shard_map/first_norm_back/pallas_call | solution.py:104
  336.2 12.1 %collective-permute-done.63 = bf16[128,2048]{1,0:T(8,128)(2,1)S(1)} collective-permute-done((bf16[128,2048]{1,0:T(8,128)(2,1)S(1)}, bf16[128,2048]{1,0:T(8,128)(2,1)S(1)}, u32[]{:S(2)}, u32[]{:S(2)}) %collective-permute-start.63) | collective-permute-done | bytes 524320 | tf_op jit(solution)/shard_map/ppermute | solution.py:481
  351.9 2.6 collective-permute-start.54
  354.5 3.4 add_add_fusion
  369.3 11.2 %collective-permute-done.61 = bf16[64,2560]{1,0:T(8,128)(2,1)S(1)} collective-permute-done((bf16[64,2560]{1,0:T(8,128)(2,1)S(1)}, bf16[64,2560]{1,0:T(8,128)(2,1)S(1)}, u32[]{:S(2)}, u32[]{:S(2)}) %collective-permute-start.61) | collective-permute-done | bytes 327712 | tf_op jit(solution)/shard_map/ppermute | solution.py:481
  380.6 3.9 collective-permute-start.62
  388.6 7.5 %collective-permute-done.62 = bf16[128,2560]{1,0:T(8,128)(2,1)} collective-permute-done((bf16[128,2560]{1,0:T(8,128)(2,1)S(1)}, bf16[128,2560]{1,0:T(8,128)(2,1)}, u32[]{:S(2)}, u32[]{:S(2)}) %collective-permute-start.62) | collective-permute-done | bytes 655392 | tf_op jit(solution)/shard_map/ppermute | solution.py:481
  (435 shorter events, 156.6 us)
Async XLA Ops:
  8.6 23.5 %collective-permute-start = (bf16[392,512]{1,0:T(8,128)(2,1)}, bf16[392,512]{1,0:T(8,128)(2,1)}, u32[]{:S(2)}, u32[]{:S(2)}) collective-permute-start(bf16[392,512]{1,0:T(8,128)(2,1)} %get-tuple-element.168), channel_id=1, source_target_pairs={{0,2},{2,0},{4,6},{6,4},{1,3},{3,1},{5,7},{7,5},{8,10},{10,8},{12,... | collective-permute-start | bytes 1204232 | tf_op jit(solution)/shard_map/ppermute | solution.py:481
  14.3 17.8 %collective-permute-start.2 = (bf16[392,256]{1,0:T(8,128)(2,1)}, bf16[392,256]{1,0:T(8,128)(2,1)S(1)}, u32[]{:S(2)}, u32[]{:S(2)}) collective-permute-start(bf16[392,256]{1,0:T(8,128)(2,1)} %get-tuple-element.170), channel_id=1, source_target_pairs={{0,6},{2,4},{4,2},{6,0},{1,7},{3,5},{5,3},{7,1},{8,14},{10,12},{12... | collective-permute-start | bytes 602120 | tf_op jit(solution)/shard_map/ppermute | solution.py:481
  14.3 31.5 %collective-permute-start.5 = (bf16[256,2304]{1,0:T(8,128)(2,1)S(1)}, bf16[256,2304]{1,0:T(8,128)(2,1)S(1)}, u32[]{:S(2)}, u32[]{:S(2)}) collective-permute-start(bf16[256,2304]{1,0:T(8,128)(2,1)S(1)} %constant_dynamic-update-slice_fusion.refs_4_), channel_id=1, source_target_pairs={{0,8},{8,0},{16,24},{24,16},{1,9},{9,1},{17,25},{25,17},{2,10},{10... | collective-permute-start | bytes 3538952 | tf_op jit(solution)/shard_map/ppermute | solution.py:481
  16.0 29.8 %collective-permute-start.6 = (bf16[256,2304]{1,0:T(8,128)(2,1)S(1)}, bf16[256,2304]{1,0:T(8,128)(2,1)S(1)}, u32[]{:S(2)}, u32[]{:S(2)}) collective-permute-start(bf16[256,2304]{1,0:T(8,128)(2,1)S(1)} %constant_dynamic-update-slice_fusion.refs_4_), channel_id=1, source_target_pairs={{0,16},{8,24},{16,0},{24,8},{1,17},{9,25},{17,1},{25,9},{2,18},{10... | collective-permute-start | bytes 3538952 | tf_op jit(solution)/shard_map/ppermute | solution.py:481
  45.7 23.0 %collective-permute-start.4 = (bf16[1176,512]{1,0:T(8,128)(2,1)S(1)}, bf16[1176,512]{1,0:T(8,128)(2,1)S(1)}, u32[]{:S(2)}, u32[]{:S(2)}) collective-permute-start(bf16[1176,512]{1,0:T(8,128)(2,1)S(1)} %maximum_maximum_fusion.1), channel_id=1, source_target_pairs={{0,1},{1,0},{2,3},{3,2},{4,5},{5,4},{6,7},{7,6},{8,9},{9,8},{10,11... | collective-permute-start | bytes 3612680 | tf_op jit(solution)/shard_map/ppermute | solution.py:481
  45.8 41.3 %collective-permute-start.9 = (bf16[256,1024]{1,0:T(8,128)(2,1)S(1)}, bf16[256,1024]{1,0:T(8,128)(2,1)S(1)}, u32[]{:S(2)}, u32[]{:S(2)}) collective-permute-start(bf16[256,1024]{1,0:T(8,128)(2,1)S(1)} %copy-done.34), channel_id=1, source_target_pairs={{0,8},{8,0},{16,24},{24,16},{1,9},{9,1},{17,25},{25,17},{2,10},{10... | collective-permute-start | bytes 1572872 | tf_op jit(solution)/shard_map/ppermute | solution.py:481
  47.4 39.8 %collective-permute-start.10 = (bf16[256,1024]{1,0:T(8,128)(2,1)S(1)}, bf16[256,1024]{1,0:T(8,128)(2,1)S(1)}, u32[]{:S(2)}, u32[]{:S(2)}) collective-permute-start(bf16[256,1024]{1,0:T(8,128)(2,1)S(1)} %copy-done.34), channel_id=1, source_target_pairs={{0,16},{8,24},{16,0},{24,8},{1,17},{9,25},{17,1},{25,9},{2,18},{10... | collective-permute-start | bytes 1572872 | tf_op jit(solution)/shard_map/ppermute | solution.py:481
  48.9 18.3 %collective-permute-start.7 = (bf16[128,1280]{1,0:T(8,128)(2,1)S(1)}, bf16[128,1280]{1,0:T(8,128)(2,1)S(1)}, u32[]{:S(2)}, u32[]{:S(2)}) collective-permute-start(bf16[128,1280]{1,0:T(8,128)(2,1)S(1)} %slice.273), channel_id=1, source_target_pairs={{0,8},{8,0},{16,24},{24,16},{1,9},{9,1},{17,25},{25,17},{2,10},{10... | collective-permute-start | bytes 983048 | tf_op jit(solution)/shard_map/ppermute | solution.py:481
  49.6 18.9 %collective-permute-start.8 = (bf16[128,1280]{1,0:T(8,128)(2,1)S(1)}, bf16[128,1280]{1,0:T(8,128)(2,1)S(1)}, u32[]{:S(2)}, u32[]{:S(2)}) collective-permute-start(bf16[128,1280]{1,0:T(8,128)(2,1)S(1)} %slice.274), channel_id=1, source_target_pairs={{0,16},{8,24},{16,0},{24,8},{1,17},{9,25},{17,1},{25,9},{2,18},{10... | collective-permute-start | bytes 983048 | tf_op jit(solution)/shard_map/ppermute | solution.py:481
  70.2 29.3 %collective-permute-start.14 = (bf16[256,2048]{1,0:T(8,128)(2,1)S(1)}, bf16[256,2048]{1,0:T(8,128)(2,1)S(1)}, u32[]{:S(2)}, u32[]{:S(2)}) collective-permute-start(bf16[256,2048]{1,0:T(8,128)(2,1)S(1)} %copy-done.27), channel_id=1, source_target_pairs={{0,8},{8,0},{16,24},{24,16},{1,9},{9,1},{17,25},{25,17},{2,10},{10... | collective-permute-start | bytes 3145736 | tf_op jit(solution)/shard_map/ppermute | solution.py:481
  70.7 28.8 %collective-permute-start.15 = (bf16[256,2048]{1,0:T(8,128)(2,1)S(1)}, bf16[256,2048]{1,0:T(8,128)(2,1)S(1)}, u32[]{:S(2)}, u32[]{:S(2)}) collective-permute-start(bf16[256,2048]{1,0:T(8,128)(2,1)S(1)} %copy-done.27), channel_id=1, source_target_pairs={{0,16},{8,24},{16,0},{24,8},{1,17},{9,25},{17,1},{25,9},{2,18},{10... | collective-permute-start | bytes 3145736 | tf_op jit(solution)/shard_map/ppermute | solution.py:481
  171.7 17.4 %collective-permute-start.28 = (bf16[392,256]{1,0:T(8,128)(2,1)S(1)}, bf16[392,256]{1,0:T(8,128)(2,1)S(1)}, u32[]{:S(2)}, u32[]{:S(2)}) collective-permute-start(bf16[392,256]{1,0:T(8,128)(2,1)S(1)} %get-tuple-element.231), channel_id=1, source_target_pairs={{0,4},{2,6},{4,0},{6,2},{1,5},{3,7},{5,1},{7,3},{8,12},{10,14},{12... | collective-permute-start | bytes 602120 | tf_op jit(solution)/shard_map/ppermute | solution.py:481
  175.6 24.1 %collective-permute-start.30 = (bf16[256,2048]{1,0:T(8,128)(2,1)S(1)}, bf16[256,2048]{1,0:T(8,128)(2,1)S(1)}, u32[]{:S(2)}, u32[]{:S(2)}) collective-permute-start(bf16[256,2048]{1,0:T(8,128)(2,1)S(1)} %pad_maximum_fusion.3), channel_id=1, source_target_pairs={{0,8},{8,0},{16,24},{24,16},{1,9},{9,1},{17,25},{25,17},{2,10},{10... | collective-permute-start | bytes 3145736 | tf_op jit(solution)/shard_map/ppermute | solution.py:481
  176.3 23.9 %collective-permute-start.31 = (bf16[256,2048]{1,0:T(8,128)(2,1)S(1)}, bf16[256,2048]{1,0:T(8,128)(2,1)S(1)}, u32[]{:S(2)}, u32[]{:S(2)}) collective-permute-start(bf16[256,2048]{1,0:T(8,128)(2,1)S(1)} %pad_maximum_fusion.4), channel_id=1, source_target_pairs={{0,16},{8,24},{16,0},{24,8},{1,17},{9,25},{17,1},{25,9},{2,18},{10... | collective-permute-start | bytes 3145736 | tf_op jit(solution)/shard_map/ppermute | solution.py:481
  200.8 20.8 %collective-permute-start.32 = (bf16[128,2560]{1,0:T(8,128)(2,1)S(1)}, bf16[128,2560]{1,0:T(8,128)(2,1)S(1)}, u32[]{:S(2)}, u32[]{:S(2)}) collective-permute-start(bf16[128,2560]{1,0:T(8,128)(2,1)S(1)} %get-tuple-element.251), channel_id=1, source_target_pairs={{0,8},{8,0},{16,24},{24,16},{1,9},{9,1},{17,25},{25,17},{2,10},{10... | collective-permute-start | bytes 1966088 | tf_op jit(solution)/shard_map/ppermute | solution.py:481
  202.2 19.4 %collective-permute-start.33 = (bf16[128,2560]{1,0:T(8,128)(2,1)S(1)}, bf16[128,2560]{1,0:T(8,128)(2,1)S(1)}, u32[]{:S(2)}, u32[]{:S(2)}) collective-permute-start(bf16[128,2560]{1,0:T(8,128)(2,1)S(1)} %get-tuple-element.252), channel_id=1, source_target_pairs={{0,16},{8,24},{16,0},{24,8},{1,17},{9,25},{17,1},{25,9},{2,18},{10... | collective-permute-start | bytes 1966088 | tf_op jit(solution)/shard_map/ppermute | solution.py:481
  225.5 21.0 %collective-permute-start.36 = (bf16[128,2560]{1,0:T(8,128)(2,1)}, bf16[128,2560]{1,0:T(8,128)(2,1)}, u32[]{:S(2)}, u32[]{:S(2)}) collective-permute-start(bf16[128,2560]{1,0:T(8,128)(2,1)} %fusion.5), channel_id=1, source_target_pairs={{0,8},{8,0},{16,24},{24,16},{1,9},{9,1},{17,25},{25,17},{2,10},{10... | collective-permute-start | bytes 1966088 | tf_op jit(solution)/shard_map/ppermute | solution.py:481
  226.2 20.4 %collective-permute-start.37 = (bf16[128,2560]{1,0:T(8,128)(2,1)}, bf16[128,2560]{1,0:T(8,128)(2,1)}, u32[]{:S(2)}, u32[]{:S(2)}) collective-permute-start(bf16[128,2560]{1,0:T(8,128)(2,1)} %fusion.4), channel_id=1, source_target_pairs={{0,16},{8,24},{16,0},{24,8},{1,17},{9,25},{17,1},{25,9},{2,18},{10... | collective-permute-start | bytes 1966088 | tf_op jit(solution)/shard_map/ppermute | solution.py:481
  226.7 19.8 %collective-permute-start.35 = (bf16[64,2048]{1,0:T(8,128)(2,1)}, bf16[64,2048]{1,0:T(8,128)(2,1)S(1)}, u32[]{:S(2)}, u32[]{:S(2)}) collective-permute-start(bf16[64,2048]{1,0:T(8,128)(2,1)} %dynamic-slice_convert_fusion.3), channel_id=1, source_target_pairs={{0,4},{2,6},{4,0},{6,2},{1,5},{3,7},{5,1},{7,3},{8,12},{10,14},{12... | collective-permute-start | bytes 786440 | tf_op jit(solution)/shard_map/ppermute | solution.py:481
  253.1 17.4 %collective-permute-start.39 = (bf16[128,2560]{1,0:T(8,128)(2,1)}, bf16[128,2560]{1,0:T(8,128)(2,1)S(1)}, u32[]{:S(2)}, u32[]{:S(2)}) collective-permute-start(bf16[128,2560]{1,0:T(8,128)(2,1)} %add_convert_fusion.3), channel_id=1, source_target_pairs={{0,8},{8,0},{16,24},{24,16},{1,9},{9,1},{17,25},{25,17},{2,10},{10... | collective-permute-start | bytes 1966088 | tf_op jit(solution)/shard_map/ppermute | solution.py:481
  271.8 24.9 %collective-permute-start.41 = (bf16[392,1024]{1,0:T(8,128)(2,1)S(1)}, bf16[392,1024]{1,0:T(8,128)(2,1)S(1)}, u32[]{:S(2)}, u32[]{:S(2)}) collective-permute-start(bf16[392,1024]{1,0:T(8,128)(2,1)S(1)} %pad_maximum_fusion.7), channel_id=1, source_target_pairs={{0,2},{2,0},{4,6},{6,4},{1,3},{3,1},{5,7},{7,5},{8,10},{10,8},{12,... | collective-permute-start | bytes 2408456 | tf_op jit(solution)/shard_map/ppermute | solution.py:481
  275.2 19.3 %collective-permute-start.44 = (bf16[64,2048]{1,0:T(8,128)(2,1)S(1)}, bf16[64,2048]{1,0:T(8,128)(2,1)S(1)}, u32[]{:S(2)}, u32[]{:S(2)}) collective-permute-start(bf16[64,2048]{1,0:T(8,128)(2,1)S(1)} %add_convert_fusion.9), channel_id=1, source_target_pairs={{0,4},{2,6},{4,0},{6,2},{1,5},{3,7},{5,1},{7,3},{8,12},{10,14},{12... | collective-permute-start | bytes 786440 | tf_op jit(solution)/shard_map/ppermute | solution.py:481
  297.1 23.8 %collective-permute-start.49 = (bf16[128,2560]{1,0:T(8,128)(2,1)S(1)}, bf16[128,2560]{1,0:T(8,128)(2,1)S(1)}, u32[]{:S(2)}, u32[]{:S(2)}) collective-permute-start(bf16[128,2560]{1,0:T(8,128)(2,1)S(1)} %dynamic-slice_convert_fusion), channel_id=1, source_target_pairs={{0,2},{2,0},{4,6},{6,4},{1,3},{3,1},{5,7},{7,5},{8,10},{10,8},{12,... | collective-permute-start | bytes 1966088 | tf_op jit(solution)/shard_map/ppermute | solution.py:481
  298.6 21.6 %collective-permute-start.47 = (bf16[256,768]{1,0:T(8,128)(2,1)S(1)}, bf16[256,768]{1,0:T(8,128)(2,1)S(1)}, u32[]{:S(2)}, u32[]{:S(2)}) collective-permute-start(bf16[256,768]{1,0:T(8,128)(2,1)S(1)} %pad_maximum_fusion.18), channel_id=1, source_target_pairs={{0,8},{8,0},{16,24},{24,16},{1,9},{9,1},{17,25},{25,17},{2,10},{10... | collective-permute-start | bytes 1179656 | tf_op jit(solution)/shard_map/ppermute | solution.py:481
  299.3 20.9 %collective-permute-start.48 = (bf16[256,768]{1,0:T(8,128)(2,1)S(1)}, bf16[256,768]{1,0:T(8,128)(2,1)S(1)}, u32[]{:S(2)}, u32[]{:S(2)}) collective-permute-start(bf16[256,768]{1,0:T(8,128)(2,1)S(1)} %pad_maximum_fusion.19), channel_id=1, source_target_pairs={{0,16},{8,24},{16,0},{24,8},{1,17},{9,25},{17,1},{25,9},{2,18},{10... | collective-permute-start | bytes 1179656 | tf_op jit(solution)/shard_map/ppermute | solution.py:481
  300.8 19.1 %collective-permute-start.46 = (bf16[392,256]{1,0:T(8,128)(2,1)S(1)}, bf16[392,256]{1,0:T(8,128)(2,1)S(1)}, u32[]{:S(2)}, u32[]{:S(2)}) collective-permute-start(bf16[392,256]{1,0:T(8,128)(2,1)S(1)} %get-tuple-element.291), channel_id=1, source_target_pairs={{0,6},{2,4},{4,2},{6,0},{1,7},{3,5},{5,3},{7,1},{8,14},{10,12},{12... | collective-permute-start | bytes 602120 | tf_op jit(solution)/shard_map/ppermute | solution.py:481
  302.2 17.9 %collective-permute-start.45 = (bf16[392,256]{1,0:T(8,128)(2,1)S(1)}, bf16[392,256]{1,0:T(8,128)(2,1)S(1)}, u32[]{:S(2)}, u32[]{:S(2)}) collective-permute-start(bf16[392,256]{1,0:T(8,128)(2,1)S(1)} %get-tuple-element.290), channel_id=1, source_target_pairs={{0,4},{2,6},{4,0},{6,2},{1,5},{3,7},{5,1},{7,3},{8,12},{10,14},{12... | collective-permute-start | bytes 602120 | tf_op jit(solution)/shard_map/ppermute | solution.py:481
  321.1 28.8 %collective-permute-start.51 = (bf16[784,1024]{1,0:T(8,128)(2,1)S(1)}, bf16[784,1024]{1,0:T(8,128)(2,1)S(1)}, u32[]{:S(2)}, u32[]{:S(2)}) collective-permute-start(bf16[784,1024]{1,0:T(8,128)(2,1)S(1)} %reduce_output.1), channel_id=1, source_target_pairs={{0,1},{1,0},{2,3},{3,2},{4,5},{5,4},{6,7},{7,6},{8,9},{9,8},{10,11... | collective-permute-start | bytes 4816904 | tf_op jit(solution)/shard_map/ppermute | solution.py:481
  323.4 24.9 %collective-permute-start.63 = (bf16[128,2048]{1,0:T(8,128)(2,1)S(1)}, bf16[128,2048]{1,0:T(8,128)(2,1)S(1)}, u32[]{:S(2)}, u32[]{:S(2)}) collective-permute-start(bf16[128,2048]{1,0:T(8,128)(2,1)S(1)} %maximum_select_fusion.3), channel_id=1, source_target_pairs={{0,2},{2,0},{4,6},{6,4},{1,3},{3,1},{5,7},{7,5},{8,10},{10,8},{12,... | collective-permute-start | bytes 1572872 | tf_op jit(solution)/shard_map/ppermute | solution.py:481
  325.2 36.7 %collective-permute-start.55 = (bf16[256,768]{1,0:T(8,128)(2,1)S(1)}, bf16[256,768]{1,0:T(8,128)(2,1)S(1)}, u32[]{:S(2)}, u32[]{:S(2)}) collective-permute-start(bf16[256,768]{1,0:T(8,128)(2,1)S(1)} %fusion.2), channel_id=1, source_target_pairs={{0,4},{2,6},{4,0},{6,2},{1,5},{3,7},{5,1},{7,3},{8,12},{10,14},{12... | collective-permute-start | bytes 1179656 | tf_op jit(solution)/shard_map/ppermute | solution.py:481
  326.6 35.3 %collective-permute-start.56 = (bf16[64,2560]{1,0:T(8,128)(2,1)S(1)}, bf16[64,2560]{1,0:T(8,128)(2,1)S(1)}, u32[]{:S(2)}, u32[]{:S(2)}) collective-permute-start(bf16[64,2560]{1,0:T(8,128)(2,1)S(1)} %dynamic-slice_convert_fusion.2), channel_id=1, source_target_pairs={{0,4},{2,6},{4,0},{6,2},{1,5},{3,7},{5,1},{7,3},{8,12},{10,14},{12... | collective-permute-start | bytes 983048 | tf_op jit(solution)/shard_map/ppermute | solution.py:481
  366.0 20.5 %collective-permute-start.60 = (bf16[256,768]{1,0:T(8,128)(2,1)S(1)}, bf16[256,768]{1,0:T(8,128)(2,1)S(1)}, u32[]{:S(2)}, u32[]{:S(2)}) collective-permute-start(bf16[256,768]{1,0:T(8,128)(2,1)S(1)} %add_convert_fusion.7), channel_id=1, source_target_pairs={{0,2},{2,0},{4,6},{6,4},{1,3},{3,1},{5,7},{7,5},{8,10},{10,8},{12,... | collective-permute-start | bytes 1179656 | tf_op jit(solution)/shard_map/ppermute | solution.py:481
  (122 other events, 926.7 us)

commit v6 on v4

--- a/solution.py
+++ b/solution.py
@@ -662,14 +662,13 @@
     far_right = swap(right, "ctx", 3)
     wide_held = gather_near(wide_part)
 
-    near_rows, across_left, far_right, wide_held, expand_rest = fence(
-        near_rows, across_left, far_right, wide_held, expand_weight[:, early:]
-    )
+    near_rows, across_left, far_right = fence(near_rows, across_left, far_right)
     passed = swap(jnp.concatenate([across_left, far_right], axis=1), "ctx", 1)
+    (wide_held,) = fence(wide_held)
     held = gather_far(tuple(piece[:, early:] for piece in wide_held))
+
+    passed, held, expand_rest = fence(passed, held, expand_weight[:, early:])
     rest_held = gather_near(expand_rest)
-
-    passed, held = fence(passed, held)
     cross_rows = jnp.concatenate(
         [
             near_rows,

time: 394 us -> 393 us (level)
    unnamed x208 -> x204, local copies, waits for them, and re-layouts: 25.2 us -> 25.2 us
  transfers between devices with their start and end apart: 64 -> 64, of which waited for: 28 -> 26; matrix products, arithmetic and copies ran while one was open for 12% -> 13% of each run, Pallas kernels for 22% -> 22%
where the time goes in v6:
time: 393 us; the launch traced here: 388 us
  waiting for transfers between devices  111 us (28%)
  Pallas kernels  104 us (26%)
  starting transfers between devices  74.8 us (19%)
  local copies, waits for them, and re-layouts  46 us (12%)
  other arithmetic  29.4 us (7%)
  matrix products  19.5 us (5%)
    ppermute x64, waiting for transfers between devices, swap(): return lax.ppermute(value, axis, [(i, i ^ distance) for i in range(size)])  111 us
    ppermute x64, starting transfers between devices, swap(): return lax.ppermute(value, axis, [(i, i ^ distance) for i in range(size)])  74.8 us
    pallas_call x2, Pallas kernels, attention_backward(): pl.pallas_call(attention_backward_kernel, grid=(1,), in_specs=[pl.BlockSp...  31.6 us
    unnamed x204, local copies, waits for them, and re-layouts  25.2 us
    dot_general x9, matrix products, product(): return lax.dot_general(left, right, dims, preferred_element_type=FULL)  19.5 us
    pallas_call x4, Pallas kernels, by_rows(): pl.pallas_call(kernel, grid=(count // chunk,), in_specs=in_specs, out_spe...  19.5 us
    pallas_call x1, Pallas kernels, feed_forward(): pl.pallas_call(lambda *refs: feed_forward_kernel(expand, reduce, edge, *r...  18.7 us
    pallas_call x2, Pallas kernels, attention_forward(): pl.pallas_call(attention_forward_kernel, grid=(1,), in_specs=[pl.BlockSpe...  14.9 us
  transfers between devices with their start and end apart: 64, of which 26 were waited for; matrix products, arithmetic and copies ran while one was open for 13% of the time, Pallas kernels for 22%

profile of v6, /device:TPU:0, one launch (start us, length us, event | category | flops | bytes accessed | tf_op | source)
XLA Modules:
  0.0 388.0 jit_solution(17028598046463986548)
XLA Ops:
  8.6 3.0 collective-permute-start.4
  17.5 11.6 %collective-permute-done.1 = bf16[392,256]{1,0:T(8,128)(2,1)S(1)} collective-permute-done((bf16[392,256]{1,0:T(8,128)(2,1)}, bf16[392,256]{1,0:T(8,128)(2,1)S(1)}, u32[]{:S(2)}, u32[]{:S(2)}) %collective-permute-start.1) | collective-permute-done | bytes 200736 | tf_op jit(solution)/shard_map/ppermute | solution.py:481
  29.1 5.4 %collective-permute-done.2 = bf16[392,256]{1,0:T(8,128)(2,1)S(1)} collective-permute-done((bf16[392,256]{1,0:T(8,128)(2,1)}, bf16[392,256]{1,0:T(8,128)(2,1)S(1)}, u32[]{:S(2)}, u32[]{:S(2)}) %collective-permute-start.2) | collective-permute-done | bytes 200736 | tf_op jit(solution)/shard_map/ppermute | solution.py:481
  45.2 3.3 collective-permute-done.6
  63.5 3.1 joint_projection.1.q_ref.k_ref.v_ref
  67.8 7.2 %attention_forward.2 = (bf16[1568,128]{1,0:T(8,128)(2,1)S(1)}, f32[8,1568]{1,0:T(8,128)S(1)}) custom-call(bf16[1568,768]{1,0:T(8,128)(2,1)S(1)} %joint_projection.1.q_ref.k_ref.v_ref, bf16[1568,768]{1,0:T(8,128)(2,1)S(1)} %joint_projection.1.q_ref.k_ref.v_ref, bf16[1568,768]{1,0:T(8,128)(2,1)S(1)} %joint_projection.1.q_ref.k_ref.v_ref), custom_call_target="tpu_custom_call" | custom-call | tf_op jit(solution)/shard_map/attention_forward/pallas_call | solution.py:240
  80.3 7.7 %attention_forward.3 = (bf16[1568,128]{1,0:T(8,128)(2,1)S(1)}, f32[8,1568]{1,0:T(8,128)S(1)}) custom-call(bf16[1568,768]{1,0:T(8,128)(2,1)S(1)} %joint_projection.1.q_ref.k_ref.v_ref, bf16[1568,768]{1,0:T(8,128)(2,1)S(1)} %joint_projection.1.q_ref.k_ref.v_ref, bf16[1568,768]{1,0:T(8,128)(2,1)S(1)} %joint_projection.1.q_ref.k_ref.v_ref), custom_call_target="tpu_custom_call" | custom-call | tf_op jit(solution)/shard_map/attention_forward/pallas_call | solution.py:240
  97.3 4.6 %collective-permute-done.17 = bf16[392,128]{1,0:T(8,128)(2,1)S(1)} collective-permute-done((bf16[392,128]{1,0:T(8,128)(2,1)S(1)}, bf16[392,128]{1,0:T(8,128)(2,1)S(1)}, u32[]{:S(2)}, u32[]{:S(2)}) %collective-permute-start.17) | collective-permute-done | bytes 100384 | tf_op jit(solution)/shard_map/ppermute | solution.py:481
  107.6 3.4 convert_reduce_fusion.1
  112.7 6.2 %second_norm.1.refs_1_ = bf16[784,1024]{1,0:T(8,128)(2,1)S(1)} custom-call(bf16[784,1024]{1,0:T(8,128)(2,1)S(1)} %bitcast.92, bf16[784,1024]{1,0:T(8,128)(2,1)} %convolution_convert_fusion.6.one_ref, bf16[784,1024]{1,0:T(8,128)(2,1)} %collective-permute-done.21.two_ref, f32[1,1024]{1,0:T(1,128)S(1)} %bitcast.100, f32[1,1024]{1,0:T(1,128)S(1)} %bitcast.104, ...), custom_call_target="tpu_custom_call" | custom-call | tf_op jit(solution)/shard_map/second_norm/pallas_call | solution.py:104
  121.4 18.7 %feed_forward.1 = (bf16[784,2048]{1,0:T(8,128)(2,1)}, bf16[784,2048]{1,0:T(8,128)(2,1)}, bf16[784,1024]{1,0:T(8,128)(2,1)}, f32[1,2048]{1,0:T(1,128)S(1)}) custom-call(s32[5]{0:T(128)S(1)} %multiply_add_fusion.refs_0_.place_ref, bf16[784,1024]{1,0:T(8,128)(2,1)} %copy-done.19, bf16[784,1024]{1,0:T(8,128)(2,1)} %bitcast.95, f32[1,2048]{1,0:T(1,128)S(1)} %bitcast.106, ...), custom_call_target="tpu_custom_call" | custom-call | tf_op jit(solution)/shard_map/feed_forward/pallas_call | solution.py:415
  140.2 3.3 convolution_convert_fusion.5
  152.0 6.3 %second_norm_back.1 = (bf16[784,1024]{1,0:T(8,128)(2,1)S(1)}, f32[784,1024]{1,0:T(8,128)S(1)}, f32[8,1024]{1,0:T(8,128)S(1)}) custom-call(bf16[784,1024]{1,0:T(8,128)(2,1)S(1)} %bitcast.93, bf16[784,1024]{1,0:T(8,128)(2,1)} %convolution_convert_fusion.6.one_ref, bf16[784,1024]{1,0:T(8,128)(2,1)} %collective-permute-done.21.two_ref, f32[1,1024]{1,0:T(1,128)S(1)} %bitcast.101, ...), custom_call_target="tpu_custom_call" | custom-call | tf_op jit(solution)/shard_map/second_norm_back/pallas_call | solution.py:104
  167.3 5.0 %convolution_convert_fusion = bf16[1024,2048]{1,0:T(8,128)(2,1)S(1)} fusion(bf16[784,1024]{1,0:T(8,128)(2,1)S(1)} %bitcast.97, bf16[784,2048]{1,0:T(8,128)(2,1)S(1)} %copy-done.32), kind=kOutput, calls=%fused_computation.1 | convolution fusion | flops 3290431488 | bytes 9011200 | tf_op jit(solution)/shard_map/dot_general | solution.py:19
  176.1 4.3 %collective-permute-done.28 = bf16[392,256]{1,0:T(8,128)(2,1)S(1)} collective-permute-done((bf16[392,256]{1,0:T(8,128)(2,1)S(1)}, bf16[392,256]{1,0:T(8,128)(2,1)S(1)}, u32[]{:S(2)}, u32[]{:S(2)}) %collective-permute-start.28) | collective-permute-done | bytes 200736 | tf_op jit(solution)/shard_map/ppermute | solution.py:481
  180.4 9.9 %collective-permute-done.30 = bf16[256,2048]{1,0:T(8,128)(2,1)S(1)} collective-permute-done((bf16[256,2048]{1,0:T(8,128)(2,1)S(1)}, bf16[256,2048]{1,0:T(8,128)(2,1)S(1)}, u32[]{:S(2)}, u32[]{:S(2)}) %collective-permute-start.30) | collective-permute-done | bytes 1048608 | tf_op jit(solution)/shard_map/ppermute | solution.py:481
  195.7 15.9 %attention_backward.2 = (bf16[1568,128]{1,0:T(8,128)(2,1)S(1)}, bf16[1568,128]{1,0:T(8,128)(2,1)S(1)}, bf16[1568,128]{1,0:T(8,128)(2,1)S(1)}) custom-call(bf16[1568,768]{1,0:T(8,128)(2,1)S(1)} %joint_projection.1.q_ref.k_ref.v_ref, bf16[1568,768]{1,0:T(8,128)(2,1)S(1)} %joint_projection.1.q_ref.k_ref.v_ref, ...), custom_call_target="tpu_custom_call" | custom-call | tf_op jit(solution)/shard_map/attention_backward/pallas_call | solution.py:313
  217.8 3.5 collective-permute-start.35
  223.4 15.7 %attention_backward.3 = (bf16[1568,128]{1,0:T(8,128)(2,1)S(1)}, bf16[1568,128]{1,0:T(8,128)(2,1)S(1)}, bf16[1568,128]{1,0:T(8,128)(2,1)S(1)}) custom-call(bf16[1568,768]{1,0:T(8,128)(2,1)S(1)} %joint_projection.1.q_ref.k_ref.v_ref, bf16[1568,768]{1,0:T(8,128)(2,1)S(1)} %joint_projection.1.q_ref.k_ref.v_ref, ...), custom_call_target="tpu_custom_call" | custom-call | tf_op jit(solution)/shard_map/attention_backward/pallas_call | solution.py:313
  251.2 8.1 %collective-permute-done.44 = bf16[64,2048]{1,0:T(8,128)(2,1)S(1)} collective-permute-done((bf16[64,2048]{1,0:T(8,128)(2,1)S(1)}, bf16[64,2048]{1,0:T(8,128)(2,1)S(1)}, u32[]{:S(2)}, u32[]{:S(2)}) %collective-permute-start.44) | collective-permute-done | bytes 262176 | tf_op jit(solution)/shard_map/ppermute | solution.py:481
  263.1 6.0 %joint_grad.1 = bf16[4,256,768]{2,1,0:T(8,128)(2,1)S(1)} custom-call(s32[1]{0:T(128)} %bitcast.21.refs_0_, bf16[1568,512]{1,0:T(8,128)(2,1)S(1)} %copy-done.7, bf16[1568,512]{1,0:T(8,128)(2,1)S(1)} %copy-done.9, bf16[1568,768]{1,0:T(8,128)(2,1)} %copy-done.3), custom_call_target="tpu_custom_call" | custom-call | tf_op jit(solution)/shard_map/joint_grad/pallas_call | solution.py:188
  271.6 4.5 %collective-permute-done.40 = bf16[128,768]{1,0:T(8,128)(2,1)S(1)} collective-permute-done((bf16[128,768]{1,0:T(8,128)(2,1)S(1)}, bf16[128,768]{1,0:T(8,128)(2,1)S(1)}, u32[]{:S(2)}, u32[]{:S(2)}) %collective-permute-start.40) | collective-permute-done | bytes 196640 | tf_op jit(solution)/shard_map/ppermute | solution.py:481
  277.2 4.1 %collective-permute-done.39 = bf16[392,1024]{1,0:T(8,128)(2,1)S(1)} collective-permute-done((bf16[392,1024]{1,0:T(8,128)(2,1)S(1)}, bf16[392,1024]{1,0:T(8,128)(2,1)S(1)}, u32[]{:S(2)}, u32[]{:S(2)}) %collective-permute-start.39) | collective-permute-done | bytes 802848 | tf_op jit(solution)/shard_map/ppermute | solution.py:481
  290.4 7.6 %reduce_output.1 = bf16[784,1024]{1,0:T(8,128)(2,1)S(1)} custom-call(s32[5]{0:T(128)S(1)} %multiply_add_fusion.refs_0_.place_ref, bf16[784,2048]{1,0:T(8,128)(2,1)S(1)} %copy-done.33, bf16[256,2048]{1,0:T(8,128)(2,1)S(1)} %copy-done.29, bf16[256,2048]{1,0:T(8,128)(2,1)S(1)} %copy-done.14, bf16[256,2048]{1,0:T(8,128)(2,1)S(1)} %copy-done.17, ...), custom_call_target="tpu_custom_call" | custom-call | tf_op jit(solution)/shard_map/reduce_output/pallas_call | solution.py:461
  298.1 7.9 %collective-permute-done.46 = bf16[392,256]{1,0:T(8,128)(2,1)S(1)} collective-permute-done((bf16[392,256]{1,0:T(8,128)(2,1)S(1)}, bf16[392,256]{1,0:T(8,128)(2,1)S(1)}, u32[]{:S(2)}, u32[]{:S(2)}) %collective-permute-start.46) | collective-permute-done | bytes 200736 | tf_op jit(solution)/shard_map/ppermute | solution.py:481
  318.2 5.1 %first_norm_back.1 = (f32[784,1024]{1,0:T(8,128)}, f32[8,1024]{1,0:T(8,128)S(1)}) custom-call(bf16[784,1024]{1,0:T(8,128)(2,1)S(1)} %bitcast.94, bf16[784,1024]{1,0:T(8,128)(2,1)S(1)} %pad_maximum_fusion.1.upstream_ref, f32[1,1024]{1,0:T(1,128)S(1)} %bitcast.103, bf16[784,1024]{1,0:T(8,128)(2,1)S(1)} %bitcast.98, f32[784,1024]{1,0:T(8,128)S(1)} %copy-done.31), custom_call_target="tpu_custom_call" | custom-call | tf_op jit(solution)/shard_map/first_norm_back/pallas_call | solution.py:104
  323.3 14.0 %collective-permute-done.63 = bf16[128,2048]{1,0:T(8,128)(2,1)S(1)} collective-permute-done((bf16[128,2048]{1,0:T(8,128)(2,1)S(1)}, bf16[128,2048]{1,0:T(8,128)(2,1)S(1)}, u32[]{:S(2)}, u32[]{:S(2)}) %collective-permute-start.63) | collective-permute-done | bytes 524320 | tf_op jit(solution)/shard_map/ppermute | solution.py:481
  339.1 4.3 %collective-permute-start.54 = (f32[72,128]{1,0:T(8,128)S(1)}, f32[72,128]{1,0:T(8,128)S(1)}, u32[]{:S(2)}, u32[]{:S(2)}) collective-permute-start(f32[72,128]{1,0:T(8,128)S(1)} %bitcast.115), channel_id=1, source_target_pairs={{0,6},{2,4},{4,2},{6,0},{1,7},{3,5},{5,3},{7,1},{8,14},{10,12},{12... | collective-permute-start | bytes 110600 | tf_op jit(solution)/shard_map/ppermute | solution.py:481
  343.4 3.4 add_add_fusion
  356.9 11.2 %collective-permute-done.61 = bf16[64,2560]{1,0:T(8,128)(2,1)S(1)} collective-permute-done((bf16[64,2560]{1,0:T(8,128)(2,1)S(1)}, bf16[64,2560]{1,0:T(8,128)(2,1)S(1)}, u32[]{:S(2)}, u32[]{:S(2)}) %collective-permute-start.61) | collective-permute-done | bytes 327712 | tf_op jit(solution)/shard_map/ppermute | solution.py:481
  368.2 3.6 collective-permute-start.62
  375.9 7.8 %collective-permute-done.62 = bf16[128,2560]{1,0:T(8,128)(2,1)} collective-permute-done((bf16[128,2560]{1,0:T(8,128)(2,1)S(1)}, bf16[128,2560]{1,0:T(8,128)(2,1)}, u32[]{:S(2)}, u32[]{:S(2)}) %collective-permute-start.62) | collective-permute-done | bytes 655392 | tf_op jit(solution)/shard_map/ppermute | solution.py:481
  (448 shorter events, 159.3 us)
Async XLA Ops:
  8.6 29.0 %collective-permute-start.4 = (bf16[256,2304]{1,0:T(8,128)(2,1)S(1)}, bf16[256,2304]{1,0:T(8,128)(2,1)S(1)}, u32[]{:S(2)}, u32[]{:S(2)}) collective-permute-start(bf16[256,2304]{1,0:T(8,128)(2,1)S(1)} %constant_dynamic-update-slice_fusion.refs_4_), channel_id=1, source_target_pairs={{0,8},{8,0},{16,24},{24,16},{1,9},{9,1},{17,25},{25,17},{2,10},{10... | collective-permute-start | bytes 3538952 | tf_op jit(solution)/shard_map/ppermute | solution.py:481
  11.6 27.4 %collective-permute-start.5 = (bf16[256,2304]{1,0:T(8,128)(2,1)S(1)}, bf16[256,2304]{1,0:T(8,128)(2,1)S(1)}, u32[]{:S(2)}, u32[]{:S(2)}) collective-permute-start(bf16[256,2304]{1,0:T(8,128)(2,1)S(1)} %constant_dynamic-update-slice_fusion.refs_4_), channel_id=1, source_target_pairs={{0,16},{8,24},{16,0},{24,8},{1,17},{9,25},{17,1},{25,9},{2,18},{10... | collective-permute-start | bytes 3538952 | tf_op jit(solution)/shard_map/ppermute | solution.py:481
  13.1 21.4 %collective-permute-start = (bf16[392,512]{1,0:T(8,128)(2,1)}, bf16[392,512]{1,0:T(8,128)(2,1)}, u32[]{:S(2)}, u32[]{:S(2)}) collective-permute-start(bf16[392,512]{1,0:T(8,128)(2,1)} %get-tuple-element.173), channel_id=1, source_target_pairs={{0,2},{2,0},{4,6},{6,4},{1,3},{3,1},{5,7},{7,5},{8,10},{10,8},{12,... | collective-permute-start | bytes 1204232 | tf_op jit(solution)/shard_map/ppermute | solution.py:481
  17.3 17.3 %collective-permute-start.2 = (bf16[392,256]{1,0:T(8,128)(2,1)}, bf16[392,256]{1,0:T(8,128)(2,1)S(1)}, u32[]{:S(2)}, u32[]{:S(2)}) collective-permute-start(bf16[392,256]{1,0:T(8,128)(2,1)} %get-tuple-element.175), channel_id=1, source_target_pairs={{0,6},{2,4},{4,2},{6,0},{1,7},{3,5},{5,3},{7,1},{8,14},{10,12},{12... | collective-permute-start | bytes 602120 | tf_op jit(solution)/shard_map/ppermute | solution.py:481
  49.7 26.0 %collective-permute-start.9 = (bf16[256,1024]{1,0:T(8,128)(2,1)S(1)}, bf16[256,1024]{1,0:T(8,128)(2,1)S(1)}, u32[]{:S(2)}, u32[]{:S(2)}) collective-permute-start(bf16[256,1024]{1,0:T(8,128)(2,1)S(1)} %copy-done.34), channel_id=1, source_target_pairs={{0,8},{8,0},{16,24},{24,16},{1,9},{9,1},{17,25},{25,17},{2,10},{10... | collective-permute-start | bytes 1572872 | tf_op jit(solution)/shard_map/ppermute | solution.py:481
  51.0 24.7 %collective-permute-start.10 = (bf16[256,1024]{1,0:T(8,128)(2,1)S(1)}, bf16[256,1024]{1,0:T(8,128)(2,1)S(1)}, u32[]{:S(2)}, u32[]{:S(2)}) collective-permute-start(bf16[256,1024]{1,0:T(8,128)(2,1)S(1)} %copy-done.34), channel_id=1, source_target_pairs={{0,16},{8,24},{16,0},{24,8},{1,17},{9,25},{17,1},{25,9},{2,18},{10... | collective-permute-start | bytes 1572872 | tf_op jit(solution)/shard_map/ppermute | solution.py:481
  59.9 28.2 %collective-permute-start.14 = (bf16[256,2048]{1,0:T(8,128)(2,1)S(1)}, bf16[256,2048]{1,0:T(8,128)(2,1)S(1)}, u32[]{:S(2)}, u32[]{:S(2)}) collective-permute-start(bf16[256,2048]{1,0:T(8,128)(2,1)S(1)} %copy-done.27), channel_id=1, source_target_pairs={{0,8},{8,0},{16,24},{24,16},{1,9},{9,1},{17,25},{25,17},{2,10},{10... | collective-permute-start | bytes 3145736 | tf_op jit(solution)/shard_map/ppermute | solution.py:481
  60.5 27.5 %collective-permute-start.15 = (bf16[256,2048]{1,0:T(8,128)(2,1)S(1)}, bf16[256,2048]{1,0:T(8,128)(2,1)S(1)}, u32[]{:S(2)}, u32[]{:S(2)}) collective-permute-start(bf16[256,2048]{1,0:T(8,128)(2,1)S(1)} %copy-done.27), channel_id=1, source_target_pairs={{0,16},{8,24},{16,0},{24,8},{1,17},{9,25},{17,1},{25,9},{2,18},{10... | collective-permute-start | bytes 3145736 | tf_op jit(solution)/shard_map/ppermute | solution.py:481
  145.3 16.1 %collective-permute-start.26 = (bf16[128,2048]{1,0:T(8,128)(2,1)S(1)}, bf16[128,2048]{1,0:T(8,128)(2,1)S(1)}, u32[]{:S(2)}, u32[]{:S(2)}) collective-permute-start(bf16[128,2048]{1,0:T(8,128)(2,1)S(1)} %get-tuple-element.239), channel_id=1, source_target_pairs={{0,8},{8,0},{16,24},{24,16},{1,9},{9,1},{17,25},{25,17},{2,10},{10... | collective-permute-start | bytes 1572872 | tf_op jit(solution)/shard_map/ppermute | solution.py:481
  163.0 17.4 %collective-permute-start.28 = (bf16[392,256]{1,0:T(8,128)(2,1)S(1)}, bf16[392,256]{1,0:T(8,128)(2,1)S(1)}, u32[]{:S(2)}, u32[]{:S(2)}) collective-permute-start(bf16[392,256]{1,0:T(8,128)(2,1)S(1)} %get-tuple-element.242), channel_id=1, source_target_pairs={{0,4},{2,6},{4,0},{6,2},{1,5},{3,7},{5,1},{7,3},{8,12},{10,14},{12... | collective-permute-start | bytes 602120 | tf_op jit(solution)/shard_map/ppermute | solution.py:481
  166.1 24.1 %collective-permute-start.30 = (bf16[256,2048]{1,0:T(8,128)(2,1)S(1)}, bf16[256,2048]{1,0:T(8,128)(2,1)S(1)}, u32[]{:S(2)}, u32[]{:S(2)}) collective-permute-start(bf16[256,2048]{1,0:T(8,128)(2,1)S(1)} %pad_maximum_fusion.3), channel_id=1, source_target_pairs={{0,8},{8,0},{16,24},{24,16},{1,9},{9,1},{17,25},{25,17},{2,10},{10... | collective-permute-start | bytes 3145736 | tf_op jit(solution)/shard_map/ppermute | solution.py:481
  166.8 23.9 %collective-permute-start.31 = (bf16[256,2048]{1,0:T(8,128)(2,1)S(1)}, bf16[256,2048]{1,0:T(8,128)(2,1)S(1)}, u32[]{:S(2)}, u32[]{:S(2)}) collective-permute-start(bf16[256,2048]{1,0:T(8,128)(2,1)S(1)} %pad_maximum_fusion.4), channel_id=1, source_target_pairs={{0,16},{8,24},{16,0},{24,8},{1,17},{9,25},{17,1},{25,9},{2,18},{10... | collective-permute-start | bytes 3145736 | tf_op jit(solution)/shard_map/ppermute | solution.py:481
  191.3 20.4 %collective-permute-start.32 = (bf16[128,2560]{1,0:T(8,128)(2,1)S(1)}, bf16[128,2560]{1,0:T(8,128)(2,1)S(1)}, u32[]{:S(2)}, u32[]{:S(2)}) collective-permute-start(bf16[128,2560]{1,0:T(8,128)(2,1)S(1)} %get-tuple-element.262), channel_id=1, source_target_pairs={{0,8},{8,0},{16,24},{24,16},{1,9},{9,1},{17,25},{25,17},{2,10},{10... | collective-permute-start | bytes 1966088 | tf_op jit(solution)/shard_map/ppermute | solution.py:481
  192.8 19.0 %collective-permute-start.33 = (bf16[128,2560]{1,0:T(8,128)(2,1)S(1)}, bf16[128,2560]{1,0:T(8,128)(2,1)S(1)}, u32[]{:S(2)}, u32[]{:S(2)}) collective-permute-start(bf16[128,2560]{1,0:T(8,128)(2,1)S(1)} %get-tuple-element.263), channel_id=1, source_target_pairs={{0,16},{8,24},{16,0},{24,8},{1,17},{9,25},{17,1},{25,9},{2,18},{10... | collective-permute-start | bytes 1966088 | tf_op jit(solution)/shard_map/ppermute | solution.py:481
  194.2 17.6 %collective-permute-start.34 = (bf16[128,2048]{1,0:T(8,128)(2,1)S(1)}, bf16[128,2048]{1,0:T(8,128)(2,1)S(1)}, u32[]{:S(2)}, u32[]{:S(2)}) collective-permute-start(bf16[128,2048]{1,0:T(8,128)(2,1)S(1)} %dynamic-slice_convert_fusion.1), channel_id=1, source_target_pairs={{0,2},{2,0},{4,6},{6,4},{1,3},{3,1},{5,7},{7,5},{8,10},{10,8},{12,... | collective-permute-start | bytes 1572872 | tf_op jit(solution)/shard_map/ppermute | solution.py:481
  215.7 23.5 %collective-permute-start.36 = (bf16[128,2560]{1,0:T(8,128)(2,1)}, bf16[128,2560]{1,0:T(8,128)(2,1)}, u32[]{:S(2)}, u32[]{:S(2)}) collective-permute-start(bf16[128,2560]{1,0:T(8,128)(2,1)} %fusion.5), channel_id=1, source_target_pairs={{0,8},{8,0},{16,24},{24,16},{1,9},{9,1},{17,25},{25,17},{2,10},{10... | collective-permute-start | bytes 1966088 | tf_op jit(solution)/shard_map/ppermute | solution.py:481
  216.3 22.9 %collective-permute-start.37 = (bf16[128,2560]{1,0:T(8,128)(2,1)}, bf16[128,2560]{1,0:T(8,128)(2,1)}, u32[]{:S(2)}, u32[]{:S(2)}) collective-permute-start(bf16[128,2560]{1,0:T(8,128)(2,1)} %fusion.4), channel_id=1, source_target_pairs={{0,16},{8,24},{16,0},{24,8},{1,17},{9,25},{17,1},{25,9},{2,18},{10... | collective-permute-start | bytes 1966088 | tf_op jit(solution)/shard_map/ppermute | solution.py:481
  217.8 21.4 %collective-permute-start.35 = (bf16[64,2048]{1,0:T(8,128)(2,1)}, bf16[64,2048]{1,0:T(8,128)(2,1)S(1)}, u32[]{:S(2)}, u32[]{:S(2)}) collective-permute-start(bf16[64,2048]{1,0:T(8,128)(2,1)} %dynamic-slice_convert_fusion.3), channel_id=1, source_target_pairs={{0,4},{2,6},{4,0},{6,2},{1,5},{3,7},{5,1},{7,3},{8,12},{10,14},{12... | collective-permute-start | bytes 786440 | tf_op jit(solution)/shard_map/ppermute | solution.py:481
  249.2 22.3 %collective-permute-start.42 = (bf16[128,2560]{1,0:T(8,128)(2,1)S(1)}, bf16[128,2560]{1,0:T(8,128)(2,1)S(1)}, u32[]{:S(2)}, u32[]{:S(2)}) collective-permute-start(bf16[128,2560]{1,0:T(8,128)(2,1)S(1)} %copy-done.81), channel_id=1, source_target_pairs={{0,8},{8,0},{16,24},{24,16},{1,9},{9,1},{17,25},{25,17},{2,10},{10... | collective-permute-start | bytes 1966088 | tf_op jit(solution)/shard_map/ppermute | solution.py:481
  250.7 20.9 %collective-permute-start.43 = (bf16[128,2560]{1,0:T(8,128)(2,1)S(1)}, bf16[128,2560]{1,0:T(8,128)(2,1)S(1)}, u32[]{:S(2)}, u32[]{:S(2)}) collective-permute-start(bf16[128,2560]{1,0:T(8,128)(2,1)S(1)} %copy-done.82), channel_id=1, source_target_pairs={{0,16},{8,24},{16,0},{24,8},{1,17},{9,25},{17,1},{25,9},{2,18},{10... | collective-permute-start | bytes 1966088 | tf_op jit(solution)/shard_map/ppermute | solution.py:481
  261.4 19.9 %collective-permute-start.39 = (bf16[392,1024]{1,0:T(8,128)(2,1)S(1)}, bf16[392,1024]{1,0:T(8,128)(2,1)S(1)}, u32[]{:S(2)}, u32[]{:S(2)}) collective-permute-start(bf16[392,1024]{1,0:T(8,128)(2,1)S(1)} %pad_maximum_fusion.7), channel_id=1, source_target_pairs={{0,2},{2,0},{4,6},{6,4},{1,3},{3,1},{5,7},{7,5},{8,10},{10,8},{12,... | collective-permute-start | bytes 2408456 | tf_op jit(solution)/shard_map/ppermute | solution.py:481
  285.0 24.5 %collective-permute-start.49 = (bf16[128,2560]{1,0:T(8,128)(2,1)S(1)}, bf16[128,2560]{1,0:T(8,128)(2,1)S(1)}, u32[]{:S(2)}, u32[]{:S(2)}) collective-permute-start(bf16[128,2560]{1,0:T(8,128)(2,1)S(1)} %dynamic-slice_convert_fusion), channel_id=1, source_target_pairs={{0,2},{2,0},{4,6},{6,4},{1,3},{3,1},{5,7},{7,5},{8,10},{10,8},{12,... | collective-permute-start | bytes 1966088 | tf_op jit(solution)/shard_map/ppermute | solution.py:481
  285.4 20.7 %collective-permute-start.46 = (bf16[392,256]{1,0:T(8,128)(2,1)S(1)}, bf16[392,256]{1,0:T(8,128)(2,1)S(1)}, u32[]{:S(2)}, u32[]{:S(2)}) collective-permute-start(bf16[392,256]{1,0:T(8,128)(2,1)S(1)} %get-tuple-element.301), channel_id=1, source_target_pairs={{0,6},{2,4},{4,2},{6,0},{1,7},{3,5},{5,3},{7,1},{8,14},{10,12},{12... | collective-permute-start | bytes 602120 | tf_op jit(solution)/shard_map/ppermute | solution.py:481
  286.1 21.6 %collective-permute-start.45 = (bf16[392,256]{1,0:T(8,128)(2,1)S(1)}, bf16[392,256]{1,0:T(8,128)(2,1)S(1)}, u32[]{:S(2)}, u32[]{:S(2)}) collective-permute-start(bf16[392,256]{1,0:T(8,128)(2,1)S(1)} %get-tuple-element.300), channel_id=1, source_target_pairs={{0,4},{2,6},{4,0},{6,2},{1,5},{3,7},{5,1},{7,3},{8,12},{10,14},{12... | collective-permute-start | bytes 602120 | tf_op jit(solution)/shard_map/ppermute | solution.py:481
  288.6 19.1 %collective-permute-start.47 = (bf16[256,768]{1,0:T(8,128)(2,1)S(1)}, bf16[256,768]{1,0:T(8,128)(2,1)S(1)}, u32[]{:S(2)}, u32[]{:S(2)}) collective-permute-start(bf16[256,768]{1,0:T(8,128)(2,1)S(1)} %pad_maximum_fusion.18), channel_id=1, source_target_pairs={{0,8},{8,0},{16,24},{24,16},{1,9},{9,1},{17,25},{25,17},{2,10},{10... | collective-permute-start | bytes 1179656 | tf_op jit(solution)/shard_map/ppermute | solution.py:481
  289.9 17.8 %collective-permute-start.48 = (bf16[256,768]{1,0:T(8,128)(2,1)S(1)}, bf16[256,768]{1,0:T(8,128)(2,1)S(1)}, u32[]{:S(2)}, u32[]{:S(2)}) collective-permute-start(bf16[256,768]{1,0:T(8,128)(2,1)S(1)} %pad_maximum_fusion.19), channel_id=1, source_target_pairs={{0,16},{8,24},{16,0},{24,8},{1,17},{9,25},{17,1},{25,9},{2,18},{10... | collective-permute-start | bytes 1179656 | tf_op jit(solution)/shard_map/ppermute | solution.py:481
  309.8 29.1 %collective-permute-start.51 = (bf16[784,1024]{1,0:T(8,128)(2,1)S(1)}, bf16[784,1024]{1,0:T(8,128)(2,1)S(1)}, u32[]{:S(2)}, u32[]{:S(2)}) collective-permute-start(bf16[784,1024]{1,0:T(8,128)(2,1)S(1)} %reduce_output.1), channel_id=1, source_target_pairs={{0,1},{1,0},{2,3},{3,2},{4,5},{5,4},{6,7},{7,6},{8,9},{9,8},{10,11... | collective-permute-start | bytes 4816904 | tf_op jit(solution)/shard_map/ppermute | solution.py:481
  312.0 25.2 %collective-permute-start.63 = (bf16[128,2048]{1,0:T(8,128)(2,1)S(1)}, bf16[128,2048]{1,0:T(8,128)(2,1)S(1)}, u32[]{:S(2)}, u32[]{:S(2)}) collective-permute-start(bf16[128,2048]{1,0:T(8,128)(2,1)S(1)} %maximum_select_fusion.3), channel_id=1, source_target_pairs={{0,2},{2,0},{4,6},{6,4},{1,3},{3,1},{5,7},{7,5},{8,10},{10,8},{12,... | collective-permute-start | bytes 1572872 | tf_op jit(solution)/shard_map/ppermute | solution.py:481
  312.2 37.0 %collective-permute-start.55 = (bf16[256,768]{1,0:T(8,128)(2,1)S(1)}, bf16[256,768]{1,0:T(8,128)(2,1)S(1)}, u32[]{:S(2)}, u32[]{:S(2)}) collective-permute-start(bf16[256,768]{1,0:T(8,128)(2,1)S(1)} %fusion.2), channel_id=1, source_target_pairs={{0,4},{2,6},{4,0},{6,2},{1,5},{3,7},{5,1},{7,3},{8,12},{10,14},{12... | collective-permute-start | bytes 1179656 | tf_op jit(solution)/shard_map/ppermute | solution.py:481
  313.9 35.3 %collective-permute-start.56 = (bf16[64,2560]{1,0:T(8,128)(2,1)S(1)}, bf16[64,2560]{1,0:T(8,128)(2,1)S(1)}, u32[]{:S(2)}, u32[]{:S(2)}) collective-permute-start(bf16[64,2560]{1,0:T(8,128)(2,1)S(1)} %dynamic-slice_convert_fusion.2), channel_id=1, source_target_pairs={{0,4},{2,6},{4,0},{6,2},{1,5},{3,7},{5,1},{7,3},{8,12},{10,14},{12... | collective-permute-start | bytes 983048 | tf_op jit(solution)/shard_map/ppermute | solution.py:481
  353.3 20.5 %collective-permute-start.60 = (bf16[256,768]{1,0:T(8,128)(2,1)S(1)}, bf16[256,768]{1,0:T(8,128)(2,1)S(1)}, u32[]{:S(2)}, u32[]{:S(2)}) collective-permute-start(bf16[256,768]{1,0:T(8,128)(2,1)S(1)} %add_convert_fusion.7), channel_id=1, source_target_pairs={{0,2},{2,0},{4,6},{6,4},{1,3},{3,1},{5,7},{7,5},{8,10},{10,8},{12,... | collective-permute-start | bytes 1179656 | tf_op jit(solution)/shard_map/ppermute | solution.py:481
  368.2 15.5 %collective-permute-start.62 = (bf16[128,2560]{1,0:T(8,128)(2,1)S(1)}, bf16[128,2560]{1,0:T(8,128)(2,1)}, u32[]{:S(2)}, u32[]{:S(2)}) collective-permute-start(bf16[128,2560]{1,0:T(8,128)(2,1)S(1)} %maximum_select_fusion.2), channel_id=1, source_target_pairs={{0,2},{2,0},{4,6},{6,4},{1,3},{3,1},{5,7},{7,5},{8,10},{10,8},{12,... | collective-permute-start | bytes 1966088 | tf_op jit(solution)/shard_map/ppermute | solution.py:481
  (128 other events, 868.7 us)

commit v7 on v6

--- a/solution.py
+++ b/solution.py
@@ -90,7 +90,7 @@
 
 def by_rows(kernel, name, out_types, sums, *values):
     count, width = values[0].shape
-    chunk = row_chunk(count, 112)
+    chunk = count // 2 if count % 16 == 0 else count
     part = pl.BlockSpec((chunk, width), lambda i: (i, 0))
     in_specs = [
         part if value.shape[0] == count else pl.BlockSpec((1, width), lambda i: (0, 0))
@@ -107,7 +107,7 @@
         in_specs=in_specs,
         out_specs=out_specs,
         out_shape=out_shape,
-        compiler_params=pltpu.CompilerParams(vmem_limit_bytes=16 << 20),
+        compiler_params=pltpu.CompilerParams(vmem_limit_bytes=40 << 20),
         name=name,
     )(*values)
 
@@ -943,9 +943,13 @@
         [piece.reshape(-1, 3, part_width) for piece in joint_parts], axis=2
     ).astype(FULL)
     wide_rows = join_rows(both(wide_rows).astype(LOW), clip_at, 2)
-    wide_rows = join_rows(wide_rows, part_at, 1).astype(FULL)
-    reduce_grad = wide_rows[:, : activated.shape[1]]
-    mixer_grad = wide_rows[:, activated.shape[1] :]
+    wide_other = swap(wide_rows, "ctx", 1)
+    reduce_grad, mixer_grad = (
+        jnp.concatenate(
+            swapped_if(part_at, [wide_rows[:, columns], wide_other[:, columns]]), axis=0
+        ).astype(FULL)
+        for columns in (slice(None, activated.shape[1]), slice(activated.shape[1], None))
+    )
     packed = packed.reshape(-1)
     shares = []
     start = 0

time: 393 us -> 392 us (level)
  Pallas kernels: 104 us -> 97.7 us
  waiting for transfers between devices: 111 us -> 115 us
    pallas_call x4, Pallas kernels: 19.5 us -> 13.2 us  [by_rows(): pl.pallas_call(kernel, grid=(count // chunk,), in_specs=in_specs, out_spe...]
    ppermute x64, waiting for transfers between devices: 111 us -> 115 us  [swap(): return lax.ppermute(value, axis, [(i, i ^ distance) for i in range(size)])]
    unnamed x204 -> x202, local copies, waits for them, and re-layouts: 25.2 us -> 24.2 us
  transfers between devices with their start and end apart: 64 -> 64, of which waited for: 26 -> 29; matrix products, arithmetic and copies ran while one was open for 13% -> 14% of each run, Pallas kernels for 22% -> 20%
where the time goes in v7:
time: 392 us; the launch traced here: 387 us
  waiting for transfers between devices  115 us (29%)
  Pallas kernels  97.7 us (25%)
  starting transfers between devices  75 us (19%)
  local copies, waits for them, and re-layouts  43.5 us (11%)
  other arithmetic  32.1 us (8%)
  matrix products  20.8 us (5%)
    ppermute x64, waiting for transfers between devices, swap(): return lax.ppermute(value, axis, [(i, i ^ distance) for i in range(size)])  115 us
    ppermute x64, starting transfers between devices, swap(): return lax.ppermute(value, axis, [(i, i ^ distance) for i in range(size)])  75 us
    pallas_call x2, Pallas kernels, attention_backward(): pl.pallas_call(attention_backward_kernel, grid=(1,), in_specs=[pl.BlockSp...  31.4 us
    unnamed x202, local copies, waits for them, and re-layouts  24.2 us
    dot_general x9, matrix products, product(): return lax.dot_general(left, right, dims, preferred_element_type=FULL)  20.8 us
    pallas_call x1, Pallas kernels, feed_forward(): pl.pallas_call(lambda *refs: feed_forward_kernel(expand, reduce, edge, *r...  18.8 us
    pallas_call x2, Pallas kernels, attention_forward(): pl.pallas_call(attention_forward_kernel, grid=(1,), in_specs=[pl.BlockSpe...  14.5 us
    pallas_call x4, Pallas kernels, by_rows(): pl.pallas_call(kernel, grid=(count // chunk,), in_specs=in_specs, out_spe...  13.2 us
  transfers between devices with their start and end apart: 64, of which 29 were waited for; matrix products, arithmetic and copies ran while one was open for 14% of the time, Pallas kernels for 20%

profile of v7, /device:TPU:0, one launch (start us, length us, event | category | flops | bytes accessed | tf_op | source)
XLA Modules:
  0.0 387.0 jit_solution(4549532039242792754)
XLA Ops:
  16.9 11.6 %collective-permute-done.1 = bf16[392,256]{1,0:T(8,128)(2,1)S(1)} collective-permute-done((bf16[392,256]{1,0:T(8,128)(2,1)}, bf16[392,256]{1,0:T(8,128)(2,1)S(1)}, u32[]{:S(2)}, u32[]{:S(2)}) %collective-permute-start.1) | collective-permute-done | bytes 200736 | tf_op jit(solution)/shard_map/ppermute | solution.py:481
  28.5 5.4 %collective-permute-done.2 = bf16[392,256]{1,0:T(8,128)(2,1)S(1)} collective-permute-done((bf16[392,256]{1,0:T(8,128)(2,1)}, bf16[392,256]{1,0:T(8,128)(2,1)S(1)}, u32[]{:S(2)}, u32[]{:S(2)}) %collective-permute-start.2) | collective-permute-done | bytes 200736 | tf_op jit(solution)/shard_map/ppermute | solution.py:481
  44.6 3.3 collective-permute-done.6
  62.9 3.4 joint_projection.1.q_ref.k_ref.v_ref
  67.4 7.2 %attention_forward.2 = (bf16[1568,128]{1,0:T(8,128)(2,1)S(1)}, f32[8,1568]{1,0:T(8,128)S(1)}) custom-call(bf16[1568,768]{1,0:T(8,128)(2,1)S(1)} %joint_projection.1.q_ref.k_ref.v_ref, bf16[1568,768]{1,0:T(8,128)(2,1)S(1)} %joint_projection.1.q_ref.k_ref.v_ref, bf16[1568,768]{1,0:T(8,128)(2,1)S(1)} %joint_projection.1.q_ref.k_ref.v_ref), custom_call_target="tpu_custom_call" | custom-call | tf_op jit(solution)/shard_map/attention_forward/pallas_call | solution.py:240
  80.0 7.3 %attention_forward.3 = (bf16[1568,128]{1,0:T(8,128)(2,1)S(1)}, f32[8,1568]{1,0:T(8,128)S(1)}) custom-call(bf16[1568,768]{1,0:T(8,128)(2,1)S(1)} %joint_projection.1.q_ref.k_ref.v_ref, bf16[1568,768]{1,0:T(8,128)(2,1)S(1)} %joint_projection.1.q_ref.k_ref.v_ref, bf16[1568,768]{1,0:T(8,128)(2,1)S(1)} %joint_projection.1.q_ref.k_ref.v_ref), custom_call_target="tpu_custom_call" | custom-call | tf_op jit(solution)/shard_map/attention_forward/pallas_call | solution.py:240
  96.9 4.3 %collective-permute-done.17 = bf16[392,128]{1,0:T(8,128)(2,1)S(1)} collective-permute-done((bf16[392,128]{1,0:T(8,128)(2,1)S(1)}, bf16[392,128]{1,0:T(8,128)(2,1)S(1)}, u32[]{:S(2)}, u32[]{:S(2)}) %collective-permute-start.17) | collective-permute-done | bytes 100384 | tf_op jit(solution)/shard_map/ppermute | solution.py:481
  106.9 3.4 convert_reduce_fusion.1
  112.0 3.1 second_norm.1.refs_1_
  119.7 18.8 %feed_forward.1 = (bf16[784,2048]{1,0:T(8,128)(2,1)}, bf16[784,2048]{1,0:T(8,128)(2,1)}, bf16[784,1024]{1,0:T(8,128)(2,1)}, f32[1,2048]{1,0:T(1,128)S(1)}) custom-call(s32[5]{0:T(128)S(1)} %multiply_add_fusion.refs_0_.place_ref, bf16[784,1024]{1,0:T(8,128)(2,1)} %copy-done.19, bf16[784,1024]{1,0:T(8,128)(2,1)} %bitcast.95, f32[1,2048]{1,0:T(1,128)S(1)} %bitcast.106, ...), custom_call_target="tpu_custom_call" | custom-call | tf_op jit(solution)/shard_map/feed_forward/pallas_call | solution.py:415
  138.6 3.3 convolution_convert_fusion.5
  152.0 4.9 %second_norm_back.1 = (bf16[784,1024]{1,0:T(8,128)(2,1)S(1)}, f32[784,1024]{1,0:T(8,128)S(1)}, f32[8,1024]{1,0:T(8,128)S(1)}) custom-call(bf16[784,1024]{1,0:T(8,128)(2,1)S(1)} %bitcast.93, bf16[784,1024]{1,0:T(8,128)(2,1)} %convolution_convert_fusion.6.one_ref, bf16[784,1024]{1,0:T(8,128)(2,1)} %collective-permute-done.21.two_ref, f32[1,1024]{1,0:T(1,128)S(1)} %bitcast.101, ...), custom_call_target="tpu_custom_call" | custom-call | tf_op jit(solution)/shard_map/second_norm_back/pallas_call | solution.py:104
  166.0 5.2 %convolution_convert_fusion = bf16[1024,2048]{1,0:T(8,128)(2,1)S(1)} fusion(bf16[784,1024]{1,0:T(8,128)(2,1)S(1)} %bitcast.97, bf16[784,2048]{1,0:T(8,128)(2,1)S(1)} %copy-done.32), kind=kOutput, calls=%fused_computation.1 | convolution fusion | flops 3290431488 | bytes 9011200 | tf_op jit(solution)/shard_map/dot_general | solution.py:19
  174.9 4.4 %collective-permute-done.28 = bf16[392,256]{1,0:T(8,128)(2,1)S(1)} collective-permute-done((bf16[392,256]{1,0:T(8,128)(2,1)S(1)}, bf16[392,256]{1,0:T(8,128)(2,1)S(1)}, u32[]{:S(2)}, u32[]{:S(2)}) %collective-permute-start.28) | collective-permute-done | bytes 200736 | tf_op jit(solution)/shard_map/ppermute | solution.py:481
  179.3 9.6 %collective-permute-done.30 = bf16[256,2048]{1,0:T(8,128)(2,1)S(1)} collective-permute-done((bf16[256,2048]{1,0:T(8,128)(2,1)S(1)}, bf16[256,2048]{1,0:T(8,128)(2,1)S(1)}, u32[]{:S(2)}, u32[]{:S(2)}) %collective-permute-start.30) | collective-permute-done | bytes 1048608 | tf_op jit(solution)/shard_map/ppermute | solution.py:481
  194.4 15.7 %attention_backward.2 = (bf16[1568,128]{1,0:T(8,128)(2,1)S(1)}, bf16[1568,128]{1,0:T(8,128)(2,1)S(1)}, bf16[1568,128]{1,0:T(8,128)(2,1)S(1)}) custom-call(bf16[1568,768]{1,0:T(8,128)(2,1)S(1)} %joint_projection.1.q_ref.k_ref.v_ref, bf16[1568,768]{1,0:T(8,128)(2,1)S(1)} %joint_projection.1.q_ref.k_ref.v_ref, ...), custom_call_target="tpu_custom_call" | custom-call | tf_op jit(solution)/shard_map/attention_backward/pallas_call | solution.py:313
  216.3 3.4 collective-permute-start.35
  221.8 15.7 %attention_backward.3 = (bf16[1568,128]{1,0:T(8,128)(2,1)S(1)}, bf16[1568,128]{1,0:T(8,128)(2,1)S(1)}, bf16[1568,128]{1,0:T(8,128)(2,1)S(1)}) custom-call(bf16[1568,768]{1,0:T(8,128)(2,1)S(1)} %joint_projection.1.q_ref.k_ref.v_ref, bf16[1568,768]{1,0:T(8,128)(2,1)S(1)} %joint_projection.1.q_ref.k_ref.v_ref, ...), custom_call_target="tpu_custom_call" | custom-call | tf_op jit(solution)/shard_map/attention_backward/pallas_call | solution.py:313
  240.0 3.0 convolution_convert_fusion.1
  249.8 8.0 %collective-permute-done.44 = bf16[64,2048]{1,0:T(8,128)(2,1)S(1)} collective-permute-done((bf16[64,2048]{1,0:T(8,128)(2,1)S(1)}, bf16[64,2048]{1,0:T(8,128)(2,1)S(1)}, u32[]{:S(2)}, u32[]{:S(2)}) %collective-permute-start.44) | collective-permute-done | bytes 262176 | tf_op jit(solution)/shard_map/ppermute | solution.py:481
  261.7 6.0 %joint_grad.1 = bf16[4,256,768]{2,1,0:T(8,128)(2,1)S(1)} custom-call(s32[1]{0:T(128)} %bitcast.21.refs_0_, bf16[1568,512]{1,0:T(8,128)(2,1)S(1)} %copy-done.7, bf16[1568,512]{1,0:T(8,128)(2,1)S(1)} %copy-done.9, bf16[1568,768]{1,0:T(8,128)(2,1)} %copy-done.3), custom_call_target="tpu_custom_call" | custom-call | tf_op jit(solution)/shard_map/joint_grad/pallas_call | solution.py:188
  270.2 4.5 %collective-permute-done.40 = bf16[128,768]{1,0:T(8,128)(2,1)S(1)} collective-permute-done((bf16[128,768]{1,0:T(8,128)(2,1)S(1)}, bf16[128,768]{1,0:T(8,128)(2,1)S(1)}, u32[]{:S(2)}, u32[]{:S(2)}) %collective-permute-start.40) | collective-permute-done | bytes 196640 | tf_op jit(solution)/shard_map/ppermute | solution.py:481
  275.8 4.1 %collective-permute-done.39 = bf16[392,1024]{1,0:T(8,128)(2,1)S(1)} collective-permute-done((bf16[392,1024]{1,0:T(8,128)(2,1)S(1)}, bf16[392,1024]{1,0:T(8,128)(2,1)S(1)}, u32[]{:S(2)}, u32[]{:S(2)}) %collective-permute-start.39) | collective-permute-done | bytes 802848 | tf_op jit(solution)/shard_map/ppermute | solution.py:481
  289.0 7.6 %reduce_output.1 = bf16[784,1024]{1,0:T(8,128)(2,1)S(1)} custom-call(s32[5]{0:T(128)S(1)} %multiply_add_fusion.refs_0_.place_ref, bf16[784,2048]{1,0:T(8,128)(2,1)S(1)} %copy-done.33, bf16[256,2048]{1,0:T(8,128)(2,1)S(1)} %copy-done.29, bf16[256,2048]{1,0:T(8,128)(2,1)S(1)} %copy-done.14, bf16[256,2048]{1,0:T(8,128)(2,1)S(1)} %copy-done.17, ...), custom_call_target="tpu_custom_call" | custom-call | tf_op jit(solution)/shard_map/reduce_output/pallas_call | solution.py:461
  296.7 7.9 %collective-permute-done.46 = bf16[392,256]{1,0:T(8,128)(2,1)S(1)} collective-permute-done((bf16[392,256]{1,0:T(8,128)(2,1)S(1)}, bf16[392,256]{1,0:T(8,128)(2,1)S(1)}, u32[]{:S(2)}, u32[]{:S(2)}) %collective-permute-start.46) | collective-permute-done | bytes 200736 | tf_op jit(solution)/shard_map/ppermute | solution.py:481
  316.7 3.9 %first_norm_back.1 = (f32[784,1024]{1,0:T(8,128)}, f32[8,1024]{1,0:T(8,128)S(1)}) custom-call(bf16[784,1024]{1,0:T(8,128)(2,1)S(1)} %bitcast.94, bf16[784,1024]{1,0:T(8,128)(2,1)S(1)} %pad_maximum_fusion.1.upstream_ref, f32[1,1024]{1,0:T(1,128)S(1)} %bitcast.103, bf16[784,1024]{1,0:T(8,128)(2,1)S(1)} %bitcast.98, f32[784,1024]{1,0:T(8,128)S(1)} %copy-done.31), custom_call_target="tpu_custom_call" | custom-call | tf_op jit(solution)/shard_map/first_norm_back/pallas_call | solution.py:104
  320.6 15.2 %collective-permute-done.63 = bf16[128,2048]{1,0:T(8,128)(2,1)S(1)} collective-permute-done((bf16[128,2048]{1,0:T(8,128)(2,1)S(1)}, bf16[128,2048]{1,0:T(8,128)(2,1)S(1)}, u32[]{:S(2)}, u32[]{:S(2)}) %collective-permute-start.63) | collective-permute-done | bytes 524320 | tf_op jit(solution)/shard_map/ppermute | solution.py:481
  337.7 4.3 %collective-permute-start.54 = (f32[72,128]{1,0:T(8,128)S(1)}, f32[72,128]{1,0:T(8,128)S(1)}, u32[]{:S(2)}, u32[]{:S(2)}) collective-permute-start(f32[72,128]{1,0:T(8,128)S(1)} %bitcast.115), channel_id=1, source_target_pairs={{0,6},{2,4},{4,2},{6,0},{1,7},{3,5},{5,3},{7,1},{8,14},{10,12},{12... | collective-permute-start | bytes 110600 | tf_op jit(solution)/shard_map/ppermute | solution.py:481
  342.0 3.4 add_add_fusion
  355.4 11.2 %collective-permute-done.61 = bf16[64,2560]{1,0:T(8,128)(2,1)S(1)} collective-permute-done((bf16[64,2560]{1,0:T(8,128)(2,1)S(1)}, bf16[64,2560]{1,0:T(8,128)(2,1)S(1)}, u32[]{:S(2)}, u32[]{:S(2)}) %collective-permute-start.61) | collective-permute-done | bytes 327712 | tf_op jit(solution)/shard_map/ppermute | solution.py:481
  366.8 3.6 collective-permute-start.62
  374.5 7.8 %collective-permute-done.62 = bf16[128,2560]{1,0:T(8,128)(2,1)} collective-permute-done((bf16[128,2560]{1,0:T(8,128)(2,1)S(1)}, bf16[128,2560]{1,0:T(8,128)(2,1)}, u32[]{:S(2)}, u32[]{:S(2)}) %collective-permute-start.62) | collective-permute-done | bytes 655392 | tf_op jit(solution)/shard_map/ppermute | solution.py:481
  (447 shorter events, 163.7 us)
Async XLA Ops:
  8.0 29.0 %collective-permute-start.4 = (bf16[256,2304]{1,0:T(8,128)(2,1)S(1)}, bf16[256,2304]{1,0:T(8,128)(2,1)S(1)}, u32[]{:S(2)}, u32[]{:S(2)}) collective-permute-start(bf16[256,2304]{1,0:T(8,128)(2,1)S(1)} %constant_dynamic-update-slice_fusion.refs_4_), channel_id=1, source_target_pairs={{0,8},{8,0},{16,24},{24,16},{1,9},{9,1},{17,25},{25,17},{2,10},{10... | collective-permute-start | bytes 3538952 | tf_op jit(solution)/shard_map/ppermute | solution.py:481
  11.0 27.4 %collective-permute-start.5 = (bf16[256,2304]{1,0:T(8,128)(2,1)S(1)}, bf16[256,2304]{1,0:T(8,128)(2,1)S(1)}, u32[]{:S(2)}, u32[]{:S(2)}) collective-permute-start(bf16[256,2304]{1,0:T(8,128)(2,1)S(1)} %constant_dynamic-update-slice_fusion.refs_4_), channel_id=1, source_target_pairs={{0,16},{8,24},{16,0},{24,8},{1,17},{9,25},{17,1},{25,9},{2,18},{10... | collective-permute-start | bytes 3538952 | tf_op jit(solution)/shard_map/ppermute | solution.py:481
  12.5 21.4 %collective-permute-start = (bf16[392,512]{1,0:T(8,128)(2,1)}, bf16[392,512]{1,0:T(8,128)(2,1)}, u32[]{:S(2)}, u32[]{:S(2)}) collective-permute-start(bf16[392,512]{1,0:T(8,128)(2,1)} %get-tuple-element.173), channel_id=1, source_target_pairs={{0,2},{2,0},{4,6},{6,4},{1,3},{3,1},{5,7},{7,5},{8,10},{10,8},{12,... | collective-permute-start | bytes 1204232 | tf_op jit(solution)/shard_map/ppermute | solution.py:481
  16.7 17.3 %collective-permute-start.2 = (bf16[392,256]{1,0:T(8,128)(2,1)}, bf16[392,256]{1,0:T(8,128)(2,1)S(1)}, u32[]{:S(2)}, u32[]{:S(2)}) collective-permute-start(bf16[392,256]{1,0:T(8,128)(2,1)} %get-tuple-element.175), channel_id=1, source_target_pairs={{0,6},{2,4},{4,2},{6,0},{1,7},{3,5},{5,3},{7,1},{8,14},{10,12},{12... | collective-permute-start | bytes 602120 | tf_op jit(solution)/shard_map/ppermute | solution.py:481
  49.1 26.2 %collective-permute-start.9 = (bf16[256,1024]{1,0:T(8,128)(2,1)S(1)}, bf16[256,1024]{1,0:T(8,128)(2,1)S(1)}, u32[]{:S(2)}, u32[]{:S(2)}) collective-permute-start(bf16[256,1024]{1,0:T(8,128)(2,1)S(1)} %copy-done.34), channel_id=1, source_target_pairs={{0,8},{8,0},{16,24},{24,16},{1,9},{9,1},{17,25},{25,17},{2,10},{10... | collective-permute-start | bytes 1572872 | tf_op jit(solution)/shard_map/ppermute | solution.py:481
  50.4 25.0 %collective-permute-start.10 = (bf16[256,1024]{1,0:T(8,128)(2,1)S(1)}, bf16[256,1024]{1,0:T(8,128)(2,1)S(1)}, u32[]{:S(2)}, u32[]{:S(2)}) collective-permute-start(bf16[256,1024]{1,0:T(8,128)(2,1)S(1)} %copy-done.34), channel_id=1, source_target_pairs={{0,16},{8,24},{16,0},{24,8},{1,17},{9,25},{17,1},{25,9},{2,18},{10... | collective-permute-start | bytes 1572872 | tf_op jit(solution)/shard_map/ppermute | solution.py:481
  59.3 28.3 %collective-permute-start.14 = (bf16[256,2048]{1,0:T(8,128)(2,1)S(1)}, bf16[256,2048]{1,0:T(8,128)(2,1)S(1)}, u32[]{:S(2)}, u32[]{:S(2)}) collective-permute-start(bf16[256,2048]{1,0:T(8,128)(2,1)S(1)} %copy-done.27), channel_id=1, source_target_pairs={{0,8},{8,0},{16,24},{24,16},{1,9},{9,1},{17,25},{25,17},{2,10},{10... | collective-permute-start | bytes 3145736 | tf_op jit(solution)/shard_map/ppermute | solution.py:481
  59.9 27.7 %collective-permute-start.15 = (bf16[256,2048]{1,0:T(8,128)(2,1)S(1)}, bf16[256,2048]{1,0:T(8,128)(2,1)S(1)}, u32[]{:S(2)}, u32[]{:S(2)}) collective-permute-start(bf16[256,2048]{1,0:T(8,128)(2,1)S(1)} %copy-done.27), channel_id=1, source_target_pairs={{0,16},{8,24},{16,0},{24,8},{1,17},{9,25},{17,1},{25,9},{2,18},{10... | collective-permute-start | bytes 3145736 | tf_op jit(solution)/shard_map/ppermute | solution.py:481
  144.3 15.6 %collective-permute-start.26 = (bf16[128,2048]{1,0:T(8,128)(2,1)}, bf16[128,2048]{1,0:T(8,128)(2,1)S(1)}, u32[]{:S(2)}, u32[]{:S(2)}) collective-permute-start(bf16[128,2048]{1,0:T(8,128)(2,1)} %get-tuple-element.239), channel_id=1, source_target_pairs={{0,8},{8,0},{16,24},{24,16},{1,9},{9,1},{17,25},{25,17},{2,10},{10... | collective-permute-start | bytes 1572872 | tf_op jit(solution)/shard_map/ppermute | solution.py:481
  161.9 17.4 %collective-permute-start.28 = (bf16[392,256]{1,0:T(8,128)(2,1)S(1)}, bf16[392,256]{1,0:T(8,128)(2,1)S(1)}, u32[]{:S(2)}, u32[]{:S(2)}) collective-permute-start(bf16[392,256]{1,0:T(8,128)(2,1)S(1)} %get-tuple-element.242), channel_id=1, source_target_pairs={{0,4},{2,6},{4,0},{6,2},{1,5},{3,7},{5,1},{7,3},{8,12},{10,14},{12... | collective-permute-start | bytes 602120 | tf_op jit(solution)/shard_map/ppermute | solution.py:481
  164.7 24.2 %collective-permute-start.30 = (bf16[256,2048]{1,0:T(8,128)(2,1)S(1)}, bf16[256,2048]{1,0:T(8,128)(2,1)S(1)}, u32[]{:S(2)}, u32[]{:S(2)}) collective-permute-start(bf16[256,2048]{1,0:T(8,128)(2,1)S(1)} %pad_maximum_fusion.3), channel_id=1, source_target_pairs={{0,8},{8,0},{16,24},{24,16},{1,9},{9,1},{17,25},{25,17},{2,10},{10... | collective-permute-start | bytes 3145736 | tf_op jit(solution)/shard_map/ppermute | solution.py:481
  165.4 23.9 %collective-permute-start.31 = (bf16[256,2048]{1,0:T(8,128)(2,1)S(1)}, bf16[256,2048]{1,0:T(8,128)(2,1)S(1)}, u32[]{:S(2)}, u32[]{:S(2)}) collective-permute-start(bf16[256,2048]{1,0:T(8,128)(2,1)S(1)} %pad_maximum_fusion.4), channel_id=1, source_target_pairs={{0,16},{8,24},{16,0},{24,8},{1,17},{9,25},{17,1},{25,9},{2,18},{10... | collective-permute-start | bytes 3145736 | tf_op jit(solution)/shard_map/ppermute | solution.py:481
  190.0 20.3 %collective-permute-start.32 = (bf16[128,2560]{1,0:T(8,128)(2,1)S(1)}, bf16[128,2560]{1,0:T(8,128)(2,1)S(1)}, u32[]{:S(2)}, u32[]{:S(2)}) collective-permute-start(bf16[128,2560]{1,0:T(8,128)(2,1)S(1)} %get-tuple-element.262), channel_id=1, source_target_pairs={{0,8},{8,0},{16,24},{24,16},{1,9},{9,1},{17,25},{25,17},{2,10},{10... | collective-permute-start | bytes 1966088 | tf_op jit(solution)/shard_map/ppermute | solution.py:481
  191.4 18.9 %collective-permute-start.33 = (bf16[128,2560]{1,0:T(8,128)(2,1)S(1)}, bf16[128,2560]{1,0:T(8,128)(2,1)S(1)}, u32[]{:S(2)}, u32[]{:S(2)}) collective-permute-start(bf16[128,2560]{1,0:T(8,128)(2,1)S(1)} %get-tuple-element.263), channel_id=1, source_target_pairs={{0,16},{8,24},{16,0},{24,8},{1,17},{9,25},{17,1},{25,9},{2,18},{10... | collective-permute-start | bytes 1966088 | tf_op jit(solution)/shard_map/ppermute | solution.py:481
  192.8 17.5 %collective-permute-start.34 = (bf16[128,2048]{1,0:T(8,128)(2,1)S(1)}, bf16[128,2048]{1,0:T(8,128)(2,1)S(1)}, u32[]{:S(2)}, u32[]{:S(2)}) collective-permute-start(bf16[128,2048]{1,0:T(8,128)(2,1)S(1)} %dynamic-slice_convert_fusion.1), channel_id=1, source_target_pairs={{0,2},{2,0},{4,6},{6,4},{1,3},{3,1},{5,7},{7,5},{8,10},{10,8},{12,... | collective-permute-start | bytes 1572872 | tf_op jit(solution)/shard_map/ppermute | solution.py:481
  214.2 23.5 %collective-permute-start.36 = (bf16[128,2560]{1,0:T(8,128)(2,1)}, bf16[128,2560]{1,0:T(8,128)(2,1)}, u32[]{:S(2)}, u32[]{:S(2)}) collective-permute-start(bf16[128,2560]{1,0:T(8,128)(2,1)} %fusion.4), channel_id=1, source_target_pairs={{0,8},{8,0},{16,24},{24,16},{1,9},{9,1},{17,25},{25,17},{2,10},{10... | collective-permute-start | bytes 1966088 | tf_op jit(solution)/shard_map/ppermute | solution.py:481
  214.8 22.8 %collective-permute-start.37 = (bf16[128,2560]{1,0:T(8,128)(2,1)}, bf16[128,2560]{1,0:T(8,128)(2,1)}, u32[]{:S(2)}, u32[]{:S(2)}) collective-permute-start(bf16[128,2560]{1,0:T(8,128)(2,1)} %fusion.3), channel_id=1, source_target_pairs={{0,16},{8,24},{16,0},{24,8},{1,17},{9,25},{17,1},{25,9},{2,18},{10... | collective-permute-start | bytes 1966088 | tf_op jit(solution)/shard_map/ppermute | solution.py:481
  216.3 21.3 %collective-permute-start.35 = (bf16[64,2048]{1,0:T(8,128)(2,1)}, bf16[64,2048]{1,0:T(8,128)(2,1)S(1)}, u32[]{:S(2)}, u32[]{:S(2)}) collective-permute-start(bf16[64,2048]{1,0:T(8,128)(2,1)} %dynamic-slice_convert_fusion.3), channel_id=1, source_target_pairs={{0,4},{2,6},{4,0},{6,2},{1,5},{3,7},{5,1},{7,3},{8,12},{10,14},{12... | collective-permute-start | bytes 786440 | tf_op jit(solution)/shard_map/ppermute | solution.py:481
  247.9 22.3 %collective-permute-start.42 = (bf16[128,2560]{1,0:T(8,128)(2,1)S(1)}, bf16[128,2560]{1,0:T(8,128)(2,1)S(1)}, u32[]{:S(2)}, u32[]{:S(2)}) collective-permute-start(bf16[128,2560]{1,0:T(8,128)(2,1)S(1)} %copy-done.82), channel_id=1, source_target_pairs={{0,8},{8,0},{16,24},{24,16},{1,9},{9,1},{17,25},{25,17},{2,10},{10... | collective-permute-start | bytes 1966088 | tf_op jit(solution)/shard_map/ppermute | solution.py:481
  249.3 20.9 %collective-permute-start.43 = (bf16[128,2560]{1,0:T(8,128)(2,1)S(1)}, bf16[128,2560]{1,0:T(8,128)(2,1)S(1)}, u32[]{:S(2)}, u32[]{:S(2)}) collective-permute-start(bf16[128,2560]{1,0:T(8,128)(2,1)S(1)} %copy-done.83), channel_id=1, source_target_pairs={{0,16},{8,24},{16,0},{24,8},{1,17},{9,25},{17,1},{25,9},{2,18},{10... | collective-permute-start | bytes 1966088 | tf_op jit(solution)/shard_map/ppermute | solution.py:481
  260.0 19.9 %collective-permute-start.39 = (bf16[392,1024]{1,0:T(8,128)(2,1)S(1)}, bf16[392,1024]{1,0:T(8,128)(2,1)S(1)}, u32[]{:S(2)}, u32[]{:S(2)}) collective-permute-start(bf16[392,1024]{1,0:T(8,128)(2,1)S(1)} %pad_maximum_fusion.7), channel_id=1, source_target_pairs={{0,2},{2,0},{4,6},{6,4},{1,3},{3,1},{5,7},{7,5},{8,10},{10,8},{12,... | collective-permute-start | bytes 2408456 | tf_op jit(solution)/shard_map/ppermute | solution.py:481
  283.6 24.5 %collective-permute-start.49 = (bf16[128,2560]{1,0:T(8,128)(2,1)S(1)}, bf16[128,2560]{1,0:T(8,128)(2,1)S(1)}, u32[]{:S(2)}, u32[]{:S(2)}) collective-permute-start(bf16[128,2560]{1,0:T(8,128)(2,1)S(1)} %dynamic-slice_convert_fusion), channel_id=1, source_target_pairs={{0,2},{2,0},{4,6},{6,4},{1,3},{3,1},{5,7},{7,5},{8,10},{10,8},{12,... | collective-permute-start | bytes 1966088 | tf_op jit(solution)/shard_map/ppermute | solution.py:481
  283.9 20.7 %collective-permute-start.46 = (bf16[392,256]{1,0:T(8,128)(2,1)S(1)}, bf16[392,256]{1,0:T(8,128)(2,1)S(1)}, u32[]{:S(2)}, u32[]{:S(2)}) collective-permute-start(bf16[392,256]{1,0:T(8,128)(2,1)S(1)} %get-tuple-element.301), channel_id=1, source_target_pairs={{0,6},{2,4},{4,2},{6,0},{1,7},{3,5},{5,3},{7,1},{8,14},{10,12},{12... | collective-permute-start | bytes 602120 | tf_op jit(solution)/shard_map/ppermute | solution.py:481
  284.7 21.6 %collective-permute-start.45 = (bf16[392,256]{1,0:T(8,128)(2,1)S(1)}, bf16[392,256]{1,0:T(8,128)(2,1)S(1)}, u32[]{:S(2)}, u32[]{:S(2)}) collective-permute-start(bf16[392,256]{1,0:T(8,128)(2,1)S(1)} %get-tuple-element.300), channel_id=1, source_target_pairs={{0,4},{2,6},{4,0},{6,2},{1,5},{3,7},{5,1},{7,3},{8,12},{10,14},{12... | collective-permute-start | bytes 602120 | tf_op jit(solution)/shard_map/ppermute | solution.py:481
  287.1 19.1 %collective-permute-start.47 = (bf16[256,768]{1,0:T(8,128)(2,1)S(1)}, bf16[256,768]{1,0:T(8,128)(2,1)S(1)}, u32[]{:S(2)}, u32[]{:S(2)}) collective-permute-start(bf16[256,768]{1,0:T(8,128)(2,1)S(1)} %pad_maximum_fusion.18), channel_id=1, source_target_pairs={{0,8},{8,0},{16,24},{24,16},{1,9},{9,1},{17,25},{25,17},{2,10},{10... | collective-permute-start | bytes 1179656 | tf_op jit(solution)/shard_map/ppermute | solution.py:481
  288.5 17.7 %collective-permute-start.48 = (bf16[256,768]{1,0:T(8,128)(2,1)S(1)}, bf16[256,768]{1,0:T(8,128)(2,1)S(1)}, u32[]{:S(2)}, u32[]{:S(2)}) collective-permute-start(bf16[256,768]{1,0:T(8,128)(2,1)S(1)} %pad_maximum_fusion.19), channel_id=1, source_target_pairs={{0,16},{8,24},{16,0},{24,8},{1,17},{9,25},{17,1},{25,9},{2,18},{10... | collective-permute-start | bytes 1179656 | tf_op jit(solution)/shard_map/ppermute | solution.py:481
  308.3 29.1 %collective-permute-start.51 = (bf16[784,1024]{1,0:T(8,128)(2,1)S(1)}, bf16[784,1024]{1,0:T(8,128)(2,1)S(1)}, u32[]{:S(2)}, u32[]{:S(2)}) collective-permute-start(bf16[784,1024]{1,0:T(8,128)(2,1)S(1)} %reduce_output.1), channel_id=1, source_target_pairs={{0,1},{1,0},{2,3},{3,2},{4,5},{5,4},{6,7},{7,6},{8,9},{9,8},{10,11... | collective-permute-start | bytes 4816904 | tf_op jit(solution)/shard_map/ppermute | solution.py:481
  310.6 25.2 %collective-permute-start.63 = (bf16[128,2048]{1,0:T(8,128)(2,1)S(1)}, bf16[128,2048]{1,0:T(8,128)(2,1)S(1)}, u32[]{:S(2)}, u32[]{:S(2)}) collective-permute-start(bf16[128,2048]{1,0:T(8,128)(2,1)S(1)} %maximum_select_fusion.2), channel_id=1, source_target_pairs={{0,2},{2,0},{4,6},{6,4},{1,3},{3,1},{5,7},{7,5},{8,10},{10,8},{12,... | collective-permute-start | bytes 1572872 | tf_op jit(solution)/shard_map/ppermute | solution.py:481
  310.8 37.0 %collective-permute-start.55 = (bf16[256,768]{1,0:T(8,128)(2,1)S(1)}, bf16[256,768]{1,0:T(8,128)(2,1)S(1)}, u32[]{:S(2)}, u32[]{:S(2)}) collective-permute-start(bf16[256,768]{1,0:T(8,128)(2,1)S(1)} %fusion.1), channel_id=1, source_target_pairs={{0,4},{2,6},{4,0},{6,2},{1,5},{3,7},{5,1},{7,3},{8,12},{10,14},{12... | collective-permute-start | bytes 1179656 | tf_op jit(solution)/shard_map/ppermute | solution.py:481
  312.5 35.3 %collective-permute-start.56 = (bf16[64,2560]{1,0:T(8,128)(2,1)S(1)}, bf16[64,2560]{1,0:T(8,128)(2,1)S(1)}, u32[]{:S(2)}, u32[]{:S(2)}) collective-permute-start(bf16[64,2560]{1,0:T(8,128)(2,1)S(1)} %dynamic-slice_convert_fusion.2), channel_id=1, source_target_pairs={{0,4},{2,6},{4,0},{6,2},{1,5},{3,7},{5,1},{7,3},{8,12},{10,14},{12... | collective-permute-start | bytes 983048 | tf_op jit(solution)/shard_map/ppermute | solution.py:481
  351.9 20.4 %collective-permute-start.60 = (bf16[256,768]{1,0:T(8,128)(2,1)S(1)}, bf16[256,768]{1,0:T(8,128)(2,1)S(1)}, u32[]{:S(2)}, u32[]{:S(2)}) collective-permute-start(bf16[256,768]{1,0:T(8,128)(2,1)S(1)} %add_convert_fusion.7), channel_id=1, source_target_pairs={{0,2},{2,0},{4,6},{6,4},{1,3},{3,1},{5,7},{7,5},{8,10},{10,8},{12,... | collective-permute-start | bytes 1179656 | tf_op jit(solution)/shard_map/ppermute | solution.py:481
  366.8 15.5 %collective-permute-start.62 = (bf16[128,2560]{1,0:T(8,128)(2,1)S(1)}, bf16[128,2560]{1,0:T(8,128)(2,1)}, u32[]{:S(2)}, u32[]{:S(2)}) collective-permute-start(bf16[128,2560]{1,0:T(8,128)(2,1)S(1)} %maximum_select_fusion.1), channel_id=1, source_target_pairs={{0,2},{2,0},{4,6},{6,4},{1,3},{3,1},{5,7},{7,5},{8,10},{10,8},{12,... | collective-permute-start | bytes 1966088 | tf_op jit(solution)/shard_map/ppermute | solution.py:481
  (127 other events, 887.1 us)

commit v8 on v7

--- a/solution.py
+++ b/solution.py
@@ -820,6 +820,16 @@
     grad_first, slope_clip, wide_far, expand_rows = fence(
         grad_first, slope_clip, wide_far, expand_rows
     )
+    expand_keep, expand_send = halves(both(expand_rows), clip_at)
+    expand_send, slope_clip, wide_early = fence(expand_send, slope_clip, wide_early)
+    if four:
+        wide_early = near_rows_out(wide_early)
+    expand_rows = (expand_keep, swap(expand_send, "ctx", 2))
+    grad_second = attention_backward(joint_out, slope_clip, out_second, log_second, 1)
+
+    grad_second, expand_rows, wide_early, wide_far = fence(
+        grad_second, expand_rows, wide_early, wide_far
+    )
     if four:
         wide_late = (
             both((wide_next[half:], wide_far[1])).astype(LOW),
@@ -827,18 +837,6 @@
         )
     else:
         wide_late = ()
-    expand_keep, expand_send = halves(both(expand_rows), clip_at)
-    expand_send, slope_clip, wide_early, wide_late = fence(
-        expand_send, slope_clip, wide_early, wide_late
-    )
-    if four:
-        wide_early = near_rows_out(wide_early)
-    expand_rows = (expand_keep, swap(expand_send, "ctx", 2))
-    grad_second = attention_backward(joint_out, slope_clip, out_second, log_second, 1)
-
-    grad_second, expand_rows, wide_early, wide_late = fence(
-        grad_second, expand_rows, wide_early, wide_late
-    )
     if four:
         wide_late = near_rows_out(wide_late)
     expand_rows = join_rows(both(expand_rows).astype(LOW), clip_at, 2)
@@ -865,10 +863,9 @@
         jnp.zeros((2, features), FULL), bias_sums, (0, part_at * part_width)
     )
 
-    joint_far = far_halves(joint_parts[0]) if four else ()
-    passing, joint_far, wide_late, expand_rows = fence(
-        passing, joint_far, wide_late, expand_rows
-    )
+    joint_leaves, wide_late = fence(joint_parts[0], wide_late)
+    joint_far = far_halves(joint_leaves) if four else ()
+    passing, joint_far, expand_rows = fence(passing, joint_far, expand_rows)
     if four:
         near_sum = [both((wide_early[0], wide_late[1])), both((wide_late[0], wide_early[1]))]
         wide_sum = rows_at(wide, 0).astype(FULL) + jnp.concatenate(near_sum, axis=0)
@@ -944,12 +941,16 @@
     ).astype(FULL)
     wide_rows = join_rows(both(wide_rows).astype(LOW), clip_at, 2)
     wide_other = swap(wide_rows, "ctx", 1)
-    reduce_grad, mixer_grad = (
-        jnp.concatenate(
-            swapped_if(part_at, [wide_rows[:, columns], wide_other[:, columns]]), axis=0
-        ).astype(FULL)
-        for columns in (slice(None, activated.shape[1]), slice(activated.shape[1], None))
-    )
+    rows = wide_rows.shape[0]
+
+    def placed(columns):
+        mine, other = wide_rows[:, columns], wide_other[:, columns]
+        out = jnp.zeros((2 * rows, mine.shape[1]), FULL)
+        out = lax.dynamic_update_slice(out, mine.astype(FULL), (part_at * rows, 0))
+        return lax.dynamic_update_slice(out, other.astype(FULL), ((1 - part_at) * rows, 0))
+
+    reduce_grad = placed(slice(None, activated.shape[1]))
+    mixer_grad = placed(slice(activated.shape[1], None))
     packed = packed.reshape(-1)
     shares = []
     start = 0

time: 392 us -> 399 us (1.018)
  other arithmetic: 32.1 us -> 40.9 us
    unnamed x202 -> x204, local copies, waits for them, and re-layouts: 24.2 us -> 22.5 us
  transfers between devices with their start and end apart: 64 -> 64, of which waited for: 29 -> 28; matrix products, arithmetic and copies ran while one was open for 14% -> 16% of each run, Pallas kernels for 20% -> 20%
where the time goes in v8:
time: 399 us; the launch traced here: 394 us
  waiting for transfers between devices  113 us (28%)
  Pallas kernels  97.4 us (24%)
  starting transfers between devices  74.2 us (19%)
  local copies, waits for them, and re-layouts  45.3 us (11%)
  other arithmetic  40.9 us (10%)
  matrix products  20.8 us (5%)
    ppermute x64, waiting for transfers between devices, swap(): return lax.ppermute(value, axis, [(i, i ^ distance) for i in range(size)])  113 us
    ppermute x64, starting transfers between devices, swap(): return lax.ppermute(value, axis, [(i, i ^ distance) for i in range(size)])  74.2 us
    pallas_call x2, Pallas kernels, attention_backward(): pl.pallas_call(attention_backward_kernel, grid=(1,), in_specs=[pl.BlockSp...  31.4 us
    unnamed x204, local copies, waits for them, and re-layouts  22.5 us
    dot_general x9, matrix products, product(): return lax.dot_general(left, right, dims, preferred_element_type=FULL)  20.8 us
    pallas_call x1, Pallas kernels, feed_forward(): pl.pallas_call(lambda *refs: feed_forward_kernel(expand, reduce, edge, *r...  18.7 us
    pallas_call x2, Pallas kernels, attention_forward(): pl.pallas_call(attention_forward_kernel, grid=(1,), in_specs=[pl.BlockSpe...  14.5 us
    pallas_call x4, Pallas kernels, by_rows(): pl.pallas_call(kernel, grid=(count // chunk,), in_specs=in_specs, out_spe...  13.1 us
  transfers between devices with their start and end apart: 64, of which 28 were waited for; matrix products, arithmetic and copies ran while one was open for 16% of the time, Pallas kernels for 20%

profile of v8, /device:TPU:0, one launch (start us, length us, event | category | flops | bytes accessed | tf_op | source)
XLA Modules:
  0.0 393.9 jit_solution(9719176958785186401)
XLA Ops:
  19.7 11.6 %collective-permute-done.1 = bf16[392,256]{1,0:T(8,128)(2,1)S(1)} collective-permute-done((bf16[392,256]{1,0:T(8,128)(2,1)}, bf16[392,256]{1,0:T(8,128)(2,1)S(1)}, u32[]{:S(2)}, u32[]{:S(2)}) %collective-permute-start.1) | collective-permute-done | bytes 200736 | tf_op jit(solution)/shard_map/ppermute | solution.py:481
  31.3 5.4 %collective-permute-done.2 = bf16[392,256]{1,0:T(8,128)(2,1)S(1)} collective-permute-done((bf16[392,256]{1,0:T(8,128)(2,1)}, bf16[392,256]{1,0:T(8,128)(2,1)S(1)}, u32[]{:S(2)}, u32[]{:S(2)}) %collective-permute-start.2) | collective-permute-done | bytes 200736 | tf_op jit(solution)/shard_map/ppermute | solution.py:481
  47.4 3.5 collective-permute-done.6
  64.8 3.4 joint_projection.1.q_ref.k_ref.v_ref
  69.4 7.2 %attention_forward.2 = (bf16[1568,128]{1,0:T(8,128)(2,1)S(1)}, f32[8,1568]{1,0:T(8,128)S(1)}) custom-call(bf16[1568,768]{1,0:T(8,128)(2,1)S(1)} %joint_projection.1.q_ref.k_ref.v_ref, bf16[1568,768]{1,0:T(8,128)(2,1)S(1)} %joint_projection.1.q_ref.k_ref.v_ref, bf16[1568,768]{1,0:T(8,128)(2,1)S(1)} %joint_projection.1.q_ref.k_ref.v_ref), custom_call_target="tpu_custom_call" | custom-call | tf_op jit(solution)/shard_map/attention_forward/pallas_call | solution.py:240
  81.9 7.4 %attention_forward.3 = (bf16[1568,128]{1,0:T(8,128)(2,1)S(1)}, f32[8,1568]{1,0:T(8,128)S(1)}) custom-call(bf16[1568,768]{1,0:T(8,128)(2,1)S(1)} %joint_projection.1.q_ref.k_ref.v_ref, bf16[1568,768]{1,0:T(8,128)(2,1)S(1)} %joint_projection.1.q_ref.k_ref.v_ref, bf16[1568,768]{1,0:T(8,128)(2,1)S(1)} %joint_projection.1.q_ref.k_ref.v_ref), custom_call_target="tpu_custom_call" | custom-call | tf_op jit(solution)/shard_map/attention_forward/pallas_call | solution.py:240
  98.9 4.3 %collective-permute-done.17 = bf16[392,128]{1,0:T(8,128)(2,1)S(1)} collective-permute-done((bf16[392,128]{1,0:T(8,128)(2,1)S(1)}, bf16[392,128]{1,0:T(8,128)(2,1)S(1)}, u32[]{:S(2)}, u32[]{:S(2)}) %collective-permute-start.17) | collective-permute-done | bytes 100384 | tf_op jit(solution)/shard_map/ppermute | solution.py:481
  108.8 3.4 convert_reduce_fusion.1
  114.0 3.1 second_norm.1.refs_1_
  118.3 2.9 collective-permute-done.22.refs_15_.refs_3_
  121.7 18.7 %feed_forward.1 = (bf16[784,2048]{1,0:T(8,128)(2,1)}, bf16[784,2048]{1,0:T(8,128)(2,1)}, bf16[784,1024]{1,0:T(8,128)(2,1)}, f32[1,2048]{1,0:T(1,128)S(1)}) custom-call(s32[5]{0:T(128)S(1)} %multiply_add_fusion.refs_0_.place_ref, bf16[784,1024]{1,0:T(8,128)(2,1)} %copy-done.14, bf16[784,1024]{1,0:T(8,128)(2,1)} %bitcast.93, f32[1,2048]{1,0:T(1,128)S(1)} %bitcast.104, ...), custom_call_target="tpu_custom_call" | custom-call | tf_op jit(solution)/shard_map/feed_forward/pallas_call | solution.py:415
  140.5 3.3 convolution_convert_fusion.5
  154.6 4.9 %second_norm_back.1 = (bf16[784,1024]{1,0:T(8,128)(2,1)S(1)}, f32[784,1024]{1,0:T(8,128)S(1)}, f32[8,1024]{1,0:T(8,128)S(1)}) custom-call(bf16[784,1024]{1,0:T(8,128)(2,1)S(1)} %bitcast.91, bf16[784,1024]{1,0:T(8,128)(2,1)} %convolution_convert_fusion.6.one_ref, bf16[784,1024]{1,0:T(8,128)(2,1)} %collective-permute-done.21.two_ref, f32[1,1024]{1,0:T(1,128)S(1)} %bitcast.99, ...), custom_call_target="tpu_custom_call" | custom-call | tf_op jit(solution)/shard_map/second_norm_back/pallas_call | solution.py:104
  171.5 5.2 %convolution_convert_fusion = bf16[1024,2048]{1,0:T(8,128)(2,1)S(1)} fusion(bf16[784,1024]{1,0:T(8,128)(2,1)S(1)} %bitcast.95, bf16[784,2048]{1,0:T(8,128)(2,1)S(1)} %copy-done.24), kind=kOutput, calls=%fused_computation.1 | convolution fusion | flops 3290431488 | bytes 9011200 | tf_op jit(solution)/shard_map/dot_general | solution.py:19
  181.5 3.2 collective-permute-done.28
  184.6 9.6 %collective-permute-done.30 = bf16[256,2048]{1,0:T(8,128)(2,1)S(1)} collective-permute-done((bf16[256,2048]{1,0:T(8,128)(2,1)S(1)}, bf16[256,2048]{1,0:T(8,128)(2,1)S(1)}, u32[]{:S(2)}, u32[]{:S(2)}) %collective-permute-start.30) | collective-permute-done | bytes 1048608 | tf_op jit(solution)/shard_map/ppermute | solution.py:481
  200.9 15.7 %attention_backward.2 = (bf16[1568,128]{1,0:T(8,128)(2,1)S(1)}, bf16[1568,128]{1,0:T(8,128)(2,1)S(1)}, bf16[1568,128]{1,0:T(8,128)(2,1)S(1)}) custom-call(bf16[1568,768]{1,0:T(8,128)(2,1)S(1)} %joint_projection.1.q_ref.k_ref.v_ref, bf16[1568,768]{1,0:T(8,128)(2,1)S(1)} %joint_projection.1.q_ref.k_ref.v_ref, ...), custom_call_target="tpu_custom_call" | custom-call | tf_op jit(solution)/shard_map/attention_backward/pallas_call | solution.py:313
  220.9 3.5 collective-permute-start.35
  224.5 15.7 %attention_backward.3 = (bf16[1568,128]{1,0:T(8,128)(2,1)S(1)}, bf16[1568,128]{1,0:T(8,128)(2,1)S(1)}, bf16[1568,128]{1,0:T(8,128)(2,1)S(1)}) custom-call(bf16[1568,768]{1,0:T(8,128)(2,1)S(1)} %joint_projection.1.q_ref.k_ref.v_ref, bf16[1568,768]{1,0:T(8,128)(2,1)S(1)} %joint_projection.1.q_ref.k_ref.v_ref, ...), custom_call_target="tpu_custom_call" | custom-call | tf_op jit(solution)/shard_map/attention_backward/pallas_call | solution.py:313
  241.9 3.0 convolution_convert_fusion.1
  255.0 11.5 %collective-permute-done.44 = bf16[64,2048]{1,0:T(8,128)(2,1)S(1)} collective-permute-done((bf16[64,2048]{1,0:T(8,128)(2,1)S(1)}, bf16[64,2048]{1,0:T(8,128)(2,1)S(1)}, u32[]{:S(2)}, u32[]{:S(2)}) %collective-permute-start.44) | collective-permute-done | bytes 262176 | tf_op jit(solution)/shard_map/ppermute | solution.py:481
  270.1 5.8 %joint_grad.1 = bf16[4,256,768]{2,1,0:T(8,128)(2,1)S(1)} custom-call(s32[1]{0:T(128)} %bitcast.21.refs_0_, bf16[1568,512]{1,0:T(8,128)(2,1)S(1)} %copy-done.5, bf16[1568,512]{1,0:T(8,128)(2,1)S(1)} %copy-done.7, bf16[1568,768]{1,0:T(8,128)(2,1)} %copy-done.2), custom_call_target="tpu_custom_call" | custom-call | tf_op jit(solution)/shard_map/joint_grad/pallas_call | solution.py:188
  283.7 5.4 %collective-permute-done.39 = bf16[392,1024]{1,0:T(8,128)(2,1)} collective-permute-done((bf16[392,1024]{1,0:T(8,128)(2,1)}, bf16[392,1024]{1,0:T(8,128)(2,1)}, u32[]{:S(2)}, u32[]{:S(2)}) %collective-permute-start.39) | collective-permute-done | bytes 802848 | tf_op jit(solution)/shard_map/ppermute | solution.py:481
  296.8 7.6 %reduce_output.1 = bf16[784,1024]{1,0:T(8,128)(2,1)S(1)} custom-call(s32[5]{0:T(128)S(1)} %multiply_add_fusion.refs_0_.place_ref, bf16[784,2048]{1,0:T(8,128)(2,1)S(1)} %copy-done.25, bf16[256,2048]{1,0:T(8,128)(2,1)S(1)} %copy-done.21, bf16[256,2048]{1,0:T(8,128)(2,1)S(1)} %collective-permute-done.14.refs_13_.refs_1_, bf16[256,2048]{1,0:T(8,128)(2,1)S(1)} %copy-done.12, ...), custom_call_target="tpu_custom_call" | custom-call | tf_op jit(solution)/shard_map/reduce_output/pallas_call | solution.py:461
  304.3 8.5 %collective-permute-done.46 = bf16[392,256]{1,0:T(8,128)(2,1)S(1)} collective-permute-done((bf16[392,256]{1,0:T(8,128)(2,1)S(1)}, bf16[392,256]{1,0:T(8,128)(2,1)S(1)}, u32[]{:S(2)}, u32[]{:S(2)}) %collective-permute-start.46) | collective-permute-done | bytes 200736 | tf_op jit(solution)/shard_map/ppermute | solution.py:481
  324.4 3.9 first_norm_back.1
  328.3 15.6 %collective-permute-done.63 = bf16[128,2048]{1,0:T(8,128)(2,1)S(1)} collective-permute-done((bf16[128,2048]{1,0:T(8,128)(2,1)S(1)}, bf16[128,2048]{1,0:T(8,128)(2,1)S(1)}, u32[]{:S(2)}, u32[]{:S(2)}) %collective-permute-start.63) | collective-permute-done | bytes 524320 | tf_op jit(solution)/shard_map/ppermute | solution.py:481
  345.8 4.3 %collective-permute-start.54 = (f32[72,128]{1,0:T(8,128)S(1)}, f32[72,128]{1,0:T(8,128)S(1)}, u32[]{:S(2)}, u32[]{:S(2)}) collective-permute-start(f32[72,128]{1,0:T(8,128)S(1)} %bitcast.113), channel_id=1, source_target_pairs={{0,6},{2,4},{4,2},{6,0},{1,7},{3,5},{5,3},{7,1},{8,14},{10,12},{12... | collective-permute-start | bytes 110600 | tf_op jit(solution)/shard_map/ppermute | solution.py:481
  350.1 3.4 add_add_fusion
  365.6 9.2 %collective-permute-done.61 = bf16[64,2560]{1,0:T(8,128)(2,1)S(1)} collective-permute-done((bf16[64,2560]{1,0:T(8,128)(2,1)S(1)}, bf16[64,2560]{1,0:T(8,128)(2,1)S(1)}, u32[]{:S(2)}, u32[]{:S(2)}) %collective-permute-start.61) | collective-permute-done | bytes 327712 | tf_op jit(solution)/shard_map/ppermute | solution.py:481
  374.9 3.6 collective-permute-start.62
  382.3 8.1 %collective-permute-done.62 = bf16[128,2560]{1,0:T(8,128)(2,1)} collective-permute-done((bf16[128,2560]{1,0:T(8,128)(2,1)S(1)}, bf16[128,2560]{1,0:T(8,128)(2,1)}, u32[]{:S(2)}, u32[]{:S(2)}) %collective-permute-start.62) | collective-permute-done | bytes 655392 | tf_op jit(solution)/shard_map/ppermute | solution.py:481
  (454 shorter events, 169.3 us)
Async XLA Ops:
  10.9 29.1 %collective-permute-start.4 = (bf16[256,2304]{1,0:T(8,128)(2,1)}, bf16[256,2304]{1,0:T(8,128)(2,1)S(1)}, u32[]{:S(2)}, u32[]{:S(2)}) collective-permute-start(bf16[256,2304]{1,0:T(8,128)(2,1)} %constant_dynamic-update-slice_fusion.refs_4_), channel_id=1, source_target_pairs={{0,8},{8,0},{16,24},{24,16},{1,9},{9,1},{17,25},{25,17},{2,10},{10... | collective-permute-start | bytes 3538952 | tf_op jit(solution)/shard_map/ppermute | solution.py:481
  13.8 27.6 %collective-permute-start.5 = (bf16[256,2304]{1,0:T(8,128)(2,1)}, bf16[256,2304]{1,0:T(8,128)(2,1)S(1)}, u32[]{:S(2)}, u32[]{:S(2)}) collective-permute-start(bf16[256,2304]{1,0:T(8,128)(2,1)} %constant_dynamic-update-slice_fusion.refs_4_), channel_id=1, source_target_pairs={{0,16},{8,24},{16,0},{24,8},{1,17},{9,25},{17,1},{25,9},{2,18},{10... | collective-permute-start | bytes 3538952 | tf_op jit(solution)/shard_map/ppermute | solution.py:481
  15.3 21.4 %collective-permute-start = (bf16[392,512]{1,0:T(8,128)(2,1)}, bf16[392,512]{1,0:T(8,128)(2,1)S(1)}, u32[]{:S(2)}, u32[]{:S(2)}) collective-permute-start(bf16[392,512]{1,0:T(8,128)(2,1)} %get-tuple-element.172), channel_id=1, source_target_pairs={{0,2},{2,0},{4,6},{6,4},{1,3},{3,1},{5,7},{7,5},{8,10},{10,8},{12,... | collective-permute-start | bytes 1204232 | tf_op jit(solution)/shard_map/ppermute | solution.py:481
  19.5 17.3 %collective-permute-start.2 = (bf16[392,256]{1,0:T(8,128)(2,1)}, bf16[392,256]{1,0:T(8,128)(2,1)S(1)}, u32[]{:S(2)}, u32[]{:S(2)}) collective-permute-start(bf16[392,256]{1,0:T(8,128)(2,1)} %get-tuple-element.174), channel_id=1, source_target_pairs={{0,6},{2,4},{4,2},{6,0},{1,7},{3,5},{5,3},{7,1},{8,14},{10,12},{12... | collective-permute-start | bytes 602120 | tf_op jit(solution)/shard_map/ppermute | solution.py:481
  52.1 25.2 %collective-permute-start.9 = (bf16[256,1024]{1,0:T(8,128)(2,1)}, bf16[256,1024]{1,0:T(8,128)(2,1)S(1)}, u32[]{:S(2)}, u32[]{:S(2)}) collective-permute-start(bf16[256,1024]{1,0:T(8,128)(2,1)} %get-tuple-element.219.refs_5_), channel_id=1, source_target_pairs={{0,8},{8,0},{16,24},{24,16},{1,9},{9,1},{17,25},{25,17},{2,10},{10... | collective-permute-start | bytes 1572872 | tf_op jit(solution)/shard_map/ppermute | solution.py:481
  53.4 23.9 %collective-permute-start.10 = (bf16[256,1024]{1,0:T(8,128)(2,1)}, bf16[256,1024]{1,0:T(8,128)(2,1)S(1)}, u32[]{:S(2)}, u32[]{:S(2)}) collective-permute-start(bf16[256,1024]{1,0:T(8,128)(2,1)} %get-tuple-element.219.refs_5_), channel_id=1, source_target_pairs={{0,16},{8,24},{16,0},{24,8},{1,17},{9,25},{17,1},{25,9},{2,18},{10... | collective-permute-start | bytes 1572872 | tf_op jit(solution)/shard_map/ppermute | solution.py:481
  61.3 28.3 %collective-permute-start.14 = (bf16[256,2048]{1,0:T(8,128)(2,1)S(1)}, bf16[256,2048]{1,0:T(8,128)(2,1)S(1)}, u32[]{:S(2)}, u32[]{:S(2)}) collective-permute-start(bf16[256,2048]{1,0:T(8,128)(2,1)S(1)} %copy-done.20), channel_id=1, source_target_pairs={{0,8},{8,0},{16,24},{24,16},{1,9},{9,1},{17,25},{25,17},{2,10},{10... | collective-permute-start | bytes 3145736 | tf_op jit(solution)/shard_map/ppermute | solution.py:481
  61.9 27.7 %collective-permute-start.15 = (bf16[256,2048]{1,0:T(8,128)(2,1)S(1)}, bf16[256,2048]{1,0:T(8,128)(2,1)S(1)}, u32[]{:S(2)}, u32[]{:S(2)}) collective-permute-start(bf16[256,2048]{1,0:T(8,128)(2,1)S(1)} %copy-done.20), channel_id=1, source_target_pairs={{0,16},{8,24},{16,0},{24,8},{1,17},{9,25},{17,1},{25,9},{2,18},{10... | collective-permute-start | bytes 3145736 | tf_op jit(solution)/shard_map/ppermute | solution.py:481
  146.4 17.6 %collective-permute-start.26 = (bf16[128,2048]{1,0:T(8,128)(2,1)}, bf16[128,2048]{1,0:T(8,128)(2,1)}, u32[]{:S(2)}, u32[]{:S(2)}) collective-permute-start(bf16[128,2048]{1,0:T(8,128)(2,1)} %get-tuple-element.238), channel_id=1, source_target_pairs={{0,8},{8,0},{16,24},{24,16},{1,9},{9,1},{17,25},{25,17},{2,10},{10... | collective-permute-start | bytes 1572872 | tf_op jit(solution)/shard_map/ppermute | solution.py:481
  167.2 17.4 %collective-permute-start.28 = (bf16[392,256]{1,0:T(8,128)(2,1)S(1)}, bf16[392,256]{1,0:T(8,128)(2,1)S(1)}, u32[]{:S(2)}, u32[]{:S(2)}) collective-permute-start(bf16[392,256]{1,0:T(8,128)(2,1)S(1)} %get-tuple-element.241), channel_id=1, source_target_pairs={{0,4},{2,6},{4,0},{6,2},{1,5},{3,7},{5,1},{7,3},{8,12},{10,14},{12... | collective-permute-start | bytes 602120 | tf_op jit(solution)/shard_map/ppermute | solution.py:481
  170.0 24.1 %collective-permute-start.30 = (bf16[256,2048]{1,0:T(8,128)(2,1)S(1)}, bf16[256,2048]{1,0:T(8,128)(2,1)S(1)}, u32[]{:S(2)}, u32[]{:S(2)}) collective-permute-start(bf16[256,2048]{1,0:T(8,128)(2,1)S(1)} %pad_maximum_fusion.3), channel_id=1, source_target_pairs={{0,8},{8,0},{16,24},{24,16},{1,9},{9,1},{17,25},{25,17},{2,10},{10... | collective-permute-start | bytes 3145736 | tf_op jit(solution)/shard_map/ppermute | solution.py:481
  170.9 23.9 %collective-permute-start.31 = (bf16[256,2048]{1,0:T(8,128)(2,1)S(1)}, bf16[256,2048]{1,0:T(8,128)(2,1)S(1)}, u32[]{:S(2)}, u32[]{:S(2)}) collective-permute-start(bf16[256,2048]{1,0:T(8,128)(2,1)S(1)} %pad_maximum_fusion.4), channel_id=1, source_target_pairs={{0,16},{8,24},{16,0},{24,8},{1,17},{9,25},{17,1},{25,9},{2,18},{10... | collective-permute-start | bytes 3145736 | tf_op jit(solution)/shard_map/ppermute | solution.py:481
  196.4 20.3 %collective-permute-start.32 = (bf16[128,2560]{1,0:T(8,128)(2,1)}, bf16[128,2560]{1,0:T(8,128)(2,1)}, u32[]{:S(2)}, u32[]{:S(2)}) collective-permute-start(bf16[128,2560]{1,0:T(8,128)(2,1)} %get-tuple-element.261), channel_id=1, source_target_pairs={{0,8},{8,0},{16,24},{24,16},{1,9},{9,1},{17,25},{25,17},{2,10},{10... | collective-permute-start | bytes 1966088 | tf_op jit(solution)/shard_map/ppermute | solution.py:481
  197.6 19.1 %collective-permute-start.33 = (bf16[128,2560]{1,0:T(8,128)(2,1)}, bf16[128,2560]{1,0:T(8,128)(2,1)}, u32[]{:S(2)}, u32[]{:S(2)}) collective-permute-start(bf16[128,2560]{1,0:T(8,128)(2,1)} %get-tuple-element.262), channel_id=1, source_target_pairs={{0,16},{8,24},{16,0},{24,8},{1,17},{9,25},{17,1},{25,9},{2,18},{10... | collective-permute-start | bytes 1966088 | tf_op jit(solution)/shard_map/ppermute | solution.py:481
  199.2 17.4 %collective-permute-start.34 = (bf16[128,2048]{1,0:T(8,128)(2,1)}, bf16[128,2048]{1,0:T(8,128)(2,1)}, u32[]{:S(2)}, u32[]{:S(2)}) collective-permute-start(bf16[128,2048]{1,0:T(8,128)(2,1)} %dynamic-slice_convert_fusion.1), channel_id=1, source_target_pairs={{0,2},{2,0},{4,6},{6,4},{1,3},{3,1},{5,7},{7,5},{8,10},{10,8},{12,... | collective-permute-start | bytes 1572872 | tf_op jit(solution)/shard_map/ppermute | solution.py:481
  218.8 22.5 %collective-permute-start.36 = (bf16[128,2560]{1,0:T(8,128)(2,1)}, bf16[128,2560]{1,0:T(8,128)(2,1)}, u32[]{:S(2)}, u32[]{:S(2)}) collective-permute-start(bf16[128,2560]{1,0:T(8,128)(2,1)} %fusion.4), channel_id=1, source_target_pairs={{0,8},{8,0},{16,24},{24,16},{1,9},{9,1},{17,25},{25,17},{2,10},{10... | collective-permute-start | bytes 1966088 | tf_op jit(solution)/shard_map/ppermute | solution.py:481
  219.4 21.9 %collective-permute-start.37 = (bf16[128,2560]{1,0:T(8,128)(2,1)}, bf16[128,2560]{1,0:T(8,128)(2,1)}, u32[]{:S(2)}, u32[]{:S(2)}) collective-permute-start(bf16[128,2560]{1,0:T(8,128)(2,1)} %fusion.3), channel_id=1, source_target_pairs={{0,16},{8,24},{16,0},{24,8},{1,17},{9,25},{17,1},{25,9},{2,18},{10... | collective-permute-start | bytes 1966088 | tf_op jit(solution)/shard_map/ppermute | solution.py:481
  220.9 20.4 %collective-permute-start.35 = (bf16[64,2048]{1,0:T(8,128)(2,1)}, bf16[64,2048]{1,0:T(8,128)(2,1)}, u32[]{:S(2)}, u32[]{:S(2)}) collective-permute-start(bf16[64,2048]{1,0:T(8,128)(2,1)} %dynamic-slice_convert_fusion.3), channel_id=1, source_target_pairs={{0,4},{2,6},{4,0},{6,2},{1,5},{3,7},{5,1},{7,3},{8,12},{10,14},{12... | collective-permute-start | bytes 786440 | tf_op jit(solution)/shard_map/ppermute | solution.py:481
  244.9 22.6 %collective-permute-start.38 = (bf16[1568,512]{1,0:T(8,128)(2,1)}, bf16[1568,512]{1,0:T(8,128)(2,1)S(1)}, u32[]{:S(2)}, u32[]{:S(2)}) collective-permute-start(bf16[1568,512]{1,0:T(8,128)(2,1)} %convolution_convert_fusion.1), channel_id=1, source_target_pairs={{0,1},{1,0},{2,3},{3,2},{4,5},{5,4},{6,7},{7,6},{8,9},{9,8},{10,11... | collective-permute-start | bytes 4816904 | tf_op jit(solution)/shard_map/ppermute | solution.py:481
  249.9 26.1 %collective-permute-start.40 = (bf16[128,2560]{1,0:T(8,128)(2,1)}, bf16[128,2560]{1,0:T(8,128)(2,1)S(1)}, u32[]{:S(2)}, u32[]{:S(2)}) collective-permute-start(bf16[128,2560]{1,0:T(8,128)(2,1)} %add_convert_fusion.3), channel_id=1, source_target_pairs={{0,8},{8,0},{16,24},{24,16},{1,9},{9,1},{17,25},{25,17},{2,10},{10... | collective-permute-start | bytes 1966088 | tf_op jit(solution)/shard_map/ppermute | solution.py:481
  254.3 21.8 %collective-permute-start.41 = (bf16[128,2560]{1,0:T(8,128)(2,1)}, bf16[128,2560]{1,0:T(8,128)(2,1)S(1)}, u32[]{:S(2)}, u32[]{:S(2)}) collective-permute-start(bf16[128,2560]{1,0:T(8,128)(2,1)} %add_convert_fusion.2), channel_id=1, source_target_pairs={{0,16},{8,24},{16,0},{24,8},{1,17},{9,25},{17,1},{25,9},{2,18},{10... | collective-permute-start | bytes 1966088 | tf_op jit(solution)/shard_map/ppermute | solution.py:481
  269.0 20.2 %collective-permute-start.39 = (bf16[392,1024]{1,0:T(8,128)(2,1)}, bf16[392,1024]{1,0:T(8,128)(2,1)}, u32[]{:S(2)}, u32[]{:S(2)}) collective-permute-start(bf16[392,1024]{1,0:T(8,128)(2,1)} %pad_maximum_fusion.7), channel_id=1, source_target_pairs={{0,2},{2,0},{4,6},{6,4},{1,3},{3,1},{5,7},{7,5},{8,10},{10,8},{12,... | collective-permute-start | bytes 2408456 | tf_op jit(solution)/shard_map/ppermute | solution.py:481
  291.8 24.5 %collective-permute-start.49 = (bf16[128,2560]{1,0:T(8,128)(2,1)S(1)}, bf16[128,2560]{1,0:T(8,128)(2,1)S(1)}, u32[]{:S(2)}, u32[]{:S(2)}) collective-permute-start(bf16[128,2560]{1,0:T(8,128)(2,1)S(1)} %dynamic-slice_convert_fusion), channel_id=1, source_target_pairs={{0,2},{2,0},{4,6},{6,4},{1,3},{3,1},{5,7},{7,5},{8,10},{10,8},{12,... | collective-permute-start | bytes 1966088 | tf_op jit(solution)/shard_map/ppermute | solution.py:481
  292.1 22.3 %collective-permute-start.47 = (bf16[256,768]{1,0:T(8,128)(2,1)S(1)}, bf16[256,768]{1,0:T(8,128)(2,1)S(1)}, u32[]{:S(2)}, u32[]{:S(2)}) collective-permute-start(bf16[256,768]{1,0:T(8,128)(2,1)S(1)} %pad_maximum_fusion.18), channel_id=1, source_target_pairs={{0,8},{8,0},{16,24},{24,16},{1,9},{9,1},{17,25},{25,17},{2,10},{10... | collective-permute-start | bytes 1179656 | tf_op jit(solution)/shard_map/ppermute | solution.py:481
  293.0 21.5 %collective-permute-start.48 = (bf16[256,768]{1,0:T(8,128)(2,1)S(1)}, bf16[256,768]{1,0:T(8,128)(2,1)S(1)}, u32[]{:S(2)}, u32[]{:S(2)}) collective-permute-start(bf16[256,768]{1,0:T(8,128)(2,1)S(1)} %pad_maximum_fusion.19), channel_id=1, source_target_pairs={{0,16},{8,24},{16,0},{24,8},{1,17},{9,25},{17,1},{25,9},{2,18},{10... | collective-permute-start | bytes 1179656 | tf_op jit(solution)/shard_map/ppermute | solution.py:481
  293.5 19.3 %collective-permute-start.46 = (bf16[392,256]{1,0:T(8,128)(2,1)S(1)}, bf16[392,256]{1,0:T(8,128)(2,1)S(1)}, u32[]{:S(2)}, u32[]{:S(2)}) collective-permute-start(bf16[392,256]{1,0:T(8,128)(2,1)S(1)} %get-tuple-element.299), channel_id=1, source_target_pairs={{0,6},{2,4},{4,2},{6,0},{1,7},{3,5},{5,3},{7,1},{8,14},{10,12},{12... | collective-permute-start | bytes 602120 | tf_op jit(solution)/shard_map/ppermute | solution.py:481
  294.3 20.1 %collective-permute-start.45 = (bf16[392,256]{1,0:T(8,128)(2,1)S(1)}, bf16[392,256]{1,0:T(8,128)(2,1)S(1)}, u32[]{:S(2)}, u32[]{:S(2)}) collective-permute-start(bf16[392,256]{1,0:T(8,128)(2,1)S(1)} %get-tuple-element.298), channel_id=1, source_target_pairs={{0,4},{2,6},{4,0},{6,2},{1,5},{3,7},{5,1},{7,3},{8,12},{10,14},{12... | collective-permute-start | bytes 602120 | tf_op jit(solution)/shard_map/ppermute | solution.py:481
  316.5 29.1 %collective-permute-start.51 = (bf16[784,1024]{1,0:T(8,128)(2,1)S(1)}, bf16[784,1024]{1,0:T(8,128)(2,1)S(1)}, u32[]{:S(2)}, u32[]{:S(2)}) collective-permute-start(bf16[784,1024]{1,0:T(8,128)(2,1)S(1)} %reduce_output.1), channel_id=1, source_target_pairs={{0,1},{1,0},{2,3},{3,2},{4,5},{5,4},{6,7},{7,6},{8,9},{9,8},{10,11... | collective-permute-start | bytes 4816904 | tf_op jit(solution)/shard_map/ppermute | solution.py:481
  318.8 25.2 %collective-permute-start.63 = (bf16[128,2048]{1,0:T(8,128)(2,1)S(1)}, bf16[128,2048]{1,0:T(8,128)(2,1)S(1)}, u32[]{:S(2)}, u32[]{:S(2)}) collective-permute-start(bf16[128,2048]{1,0:T(8,128)(2,1)S(1)} %copy-done.62), channel_id=1, source_target_pairs={{0,2},{2,0},{4,6},{6,4},{1,3},{3,1},{5,7},{7,5},{8,10},{10,8},{12,... | collective-permute-start | bytes 1572872 | tf_op jit(solution)/shard_map/ppermute | solution.py:481
  318.9 37.0 %collective-permute-start.55 = (bf16[256,768]{1,0:T(8,128)(2,1)S(1)}, bf16[256,768]{1,0:T(8,128)(2,1)S(1)}, u32[]{:S(2)}, u32[]{:S(2)}) collective-permute-start(bf16[256,768]{1,0:T(8,128)(2,1)S(1)} %fusion.1), channel_id=1, source_target_pairs={{0,4},{2,6},{4,0},{6,2},{1,5},{3,7},{5,1},{7,3},{8,12},{10,14},{12... | collective-permute-start | bytes 1179656 | tf_op jit(solution)/shard_map/ppermute | solution.py:481
  320.6 35.3 %collective-permute-start.56 = (bf16[64,2560]{1,0:T(8,128)(2,1)S(1)}, bf16[64,2560]{1,0:T(8,128)(2,1)S(1)}, u32[]{:S(2)}, u32[]{:S(2)}) collective-permute-start(bf16[64,2560]{1,0:T(8,128)(2,1)S(1)} %dynamic-slice_convert_fusion.2), channel_id=1, source_target_pairs={{0,4},{2,6},{4,0},{6,2},{1,5},{3,7},{5,1},{7,3},{8,12},{10,14},{12... | collective-permute-start | bytes 983048 | tf_op jit(solution)/shard_map/ppermute | solution.py:481
  360.0 20.2 %collective-permute-start.60 = (bf16[256,768]{1,0:T(8,128)(2,1)S(1)}, bf16[256,768]{1,0:T(8,128)(2,1)S(1)}, u32[]{:S(2)}, u32[]{:S(2)}) collective-permute-start(bf16[256,768]{1,0:T(8,128)(2,1)S(1)} %add_convert_fusion.7), channel_id=1, source_target_pairs={{0,2},{2,0},{4,6},{6,4},{1,3},{3,1},{5,7},{7,5},{8,10},{10,8},{12,... | collective-permute-start | bytes 1179656 | tf_op jit(solution)/shard_map/ppermute | solution.py:481
  (129 other events, 887.5 us)

commit v9 on v7

--- a/solution.py
+++ b/solution.py
@@ -144,9 +144,8 @@
     out_ref[...] = product(left_ref[...], right_ref[...], ROW_BY_ROW).astype(LOW)
 
 
-def rows_product(left, right, name):
+def rows_product(left, right, columns, name):
     count, depth = left.shape
-    columns = right.shape[0]
     chunk = row_chunk(count, 400)
     return pl.pallas_call(
         rows_kernel,
@@ -364,30 +363,23 @@
     put_together(place_ref, expand_ref, nested(refs[:arrays], expand), edge)
     put_together(place_ref, reduce_ref, nested(refs[arrays:-7], reduce))
     step = pl.program_id(0)
-    count = normed_ref.shape[0]
-    half = count // 2
-    bias_grad = None
-    for rows in (slice(0, half), slice(half, count)):
-        hidden = product(normed_ref[rows], expand_ref[...], PLAIN) + bias_ref[...]
-        upstream = product(slope_ref[rows], reduce_ref[...], PLAIN)
-        share = 0.5 * (1.0 + lax.erf(hidden * (0.5**0.5)))
-        active_ref[rows] = (hidden * share).astype(LOW)
-        density = jnp.exp(-0.5 * hidden * hidden) * 0.3989422804014327
-        slope = (upstream * (share + hidden * density)).astype(LOW)
-        expand_slope_ref[rows] = slope
-        part = jnp.sum(slope.astype(FULL), axis=0, keepdims=True)
-        bias_grad = part if bias_grad is None else bias_grad + part
-        back = product(slope, expand_ref[...], ROW_BY_ROW)
-
-        @pl.when(step == 0)
-        def _():
-            total[rows] = back
-
-        @pl.when(step > 0)
-        def _():
-            total[rows] += back
-
-    bias_grad_ref[...] = bias_grad
+    hidden = product(normed_ref[...], expand_ref[...], PLAIN) + bias_ref[...]
+    upstream = product(slope_ref[...], reduce_ref[...], PLAIN)
+    share = 0.5 * (1.0 + lax.erf(hidden * (0.5**0.5)))
+    active_ref[...] = (hidden * share).astype(LOW)
+    density = jnp.exp(-0.5 * hidden * hidden) * 0.3989422804014327
+    slope = (upstream * (share + hidden * density)).astype(LOW)
+    expand_slope_ref[...] = slope
+    bias_grad_ref[...] = jnp.sum(slope.astype(FULL), axis=0, keepdims=True)
+    back = product(slope, expand_ref[...], ROW_BY_ROW)
+
+    @pl.when(step == 0)
+    def _():
+        total[...] = back
+
+    @pl.when(step > 0)
+    def _():
+        total[...] += back
 
     @pl.when(step == pl.num_programs(0) - 1)
     def _():
@@ -846,7 +838,7 @@
         [grad[kind] for kind in range(3) for grad in (grad_first, grad_second)], axis=1
     )
     first_there = product(joint_slope, joint_full[width_half:], ROW_BY_ROW).astype(LOW)
-    first_here = rows_product(joint_slope, joint_full[:width_half], "first_slope")
+    first_here = rows_product(joint_slope, joint_full, width_half, "first_slope")
     first_half = both((first_here, swap(first_there, "tp", 1))).astype(LOW)
 
     if not four:
@@ -944,12 +936,16 @@
     ).astype(FULL)
     wide_rows = join_rows(both(wide_rows).astype(LOW), clip_at, 2)
     wide_other = swap(wide_rows, "ctx", 1)
-    reduce_grad, mixer_grad = (
-        jnp.concatenate(
-            swapped_if(part_at, [wide_rows[:, columns], wide_other[:, columns]]), axis=0
-        ).astype(FULL)
-        for columns in (slice(None, activated.shape[1]), slice(activated.shape[1], None))
-    )
+    rows = wide_rows.shape[0]
+
+    def placed(columns):
+        mine, other = wide_rows[:, columns], wide_other[:, columns]
+        out = jnp.zeros((2 * rows, mine.shape[1]), FULL)
+        out = lax.dynamic_update_slice(out, mine.astype(FULL), (part_at * rows, 0))
+        return lax.dynamic_update_slice(out, other.astype(FULL), ((1 - part_at) * rows, 0))
+
+    reduce_grad = placed(slice(None, activated.shape[1]))
+    mixer_grad = placed(slice(activated.shape[1], None))
     packed = packed.reshape(-1)
     shares = []
     start = 0

time: 392 us -> 390 us (level)
    unnamed x202 -> x206, local copies, waits for them, and re-layouts: 24.2 us -> 26.7 us
where the time goes in v9:
time: 390 us; the launch traced here: 385 us
  waiting for transfers between devices  114 us (29%)
  Pallas kernels  96.7 us (25%)
  starting transfers between devices  75 us (19%)
  local copies, waits for them, and re-layouts  44.9 us (12%)
  other arithmetic  31.1 us (8%)
  matrix products  20.8 us (5%)
    ppermute x64, waiting for transfers between devices, swap(): return lax.ppermute(value, axis, [(i, i ^ distance) for i in range(size)])  114 us
    ppermute x64, starting transfers between devices, swap(): return lax.ppermute(value, axis, [(i, i ^ distance) for i in range(size)])  75 us
    pallas_call x2, Pallas kernels, attention_backward(): pl.pallas_call(attention_backward_kernel, grid=(1,), in_specs=[pl.BlockSp...  31.4 us
    unnamed x206, local copies, waits for them, and re-layouts  26.7 us
    dot_general x9, matrix products, product(): return lax.dot_general(left, right, dims, preferred_element_type=FULL)  20.8 us
    pallas_call x1, Pallas kernels, feed_forward(): pl.pallas_call(lambda *refs: feed_forward_kernel(expand, reduce, edge, *r...  17.8 us
    pallas_call x2, Pallas kernels, attention_forward(): pl.pallas_call(attention_forward_kernel, grid=(1,), in_specs=[pl.BlockSpe...  14.5 us
    pallas_call x4, Pallas kernels, by_rows(): pl.pallas_call(kernel, grid=(count // chunk,), in_specs=in_specs, out_spe...  13.2 us
  transfers between devices with their start and end apart: 64, of which 29 were waited for; matrix products, arithmetic and copies ran while one was open for 14% of the time, Pallas kernels for 20%

profile of v9, /device:TPU:0, one launch (start us, length us, event | category | flops | bytes accessed | tf_op | source)
XLA Modules:
  0.0 384.9 jit_solution(13941127122735884645)
XLA Ops:
  16.9 11.6 %collective-permute-done.1 = bf16[392,256]{1,0:T(8,128)(2,1)S(1)} collective-permute-done((bf16[392,256]{1,0:T(8,128)(2,1)}, bf16[392,256]{1,0:T(8,128)(2,1)S(1)}, u32[]{:S(2)}, u32[]{:S(2)}) %collective-permute-start.1) | collective-permute-done | bytes 200736 | tf_op jit(solution)/shard_map/ppermute | solution.py:473
  28.5 5.4 %collective-permute-done.2 = bf16[392,256]{1,0:T(8,128)(2,1)S(1)} collective-permute-done((bf16[392,256]{1,0:T(8,128)(2,1)}, bf16[392,256]{1,0:T(8,128)(2,1)S(1)}, u32[]{:S(2)}, u32[]{:S(2)}) %collective-permute-start.2) | collective-permute-done | bytes 200736 | tf_op jit(solution)/shard_map/ppermute | solution.py:473
  44.6 3.3 collective-permute-done.6
  62.9 3.4 joint_projection.1.q_ref.k_ref.v_ref
  67.4 7.2 %attention_forward.2 = (bf16[1568,128]{1,0:T(8,128)(2,1)S(1)}, f32[8,1568]{1,0:T(8,128)S(1)}) custom-call(bf16[1568,768]{1,0:T(8,128)(2,1)S(1)} %joint_projection.1.q_ref.k_ref.v_ref, bf16[1568,768]{1,0:T(8,128)(2,1)S(1)} %joint_projection.1.q_ref.k_ref.v_ref, bf16[1568,768]{1,0:T(8,128)(2,1)S(1)} %joint_projection.1.q_ref.k_ref.v_ref), custom_call_target="tpu_custom_call" | custom-call | tf_op jit(solution)/shard_map/attention_forward/pallas_call | solution.py:239
  80.0 7.3 %attention_forward.3 = (bf16[1568,128]{1,0:T(8,128)(2,1)S(1)}, f32[8,1568]{1,0:T(8,128)S(1)}) custom-call(bf16[1568,768]{1,0:T(8,128)(2,1)S(1)} %joint_projection.1.q_ref.k_ref.v_ref, bf16[1568,768]{1,0:T(8,128)(2,1)S(1)} %joint_projection.1.q_ref.k_ref.v_ref, bf16[1568,768]{1,0:T(8,128)(2,1)S(1)} %joint_projection.1.q_ref.k_ref.v_ref), custom_call_target="tpu_custom_call" | custom-call | tf_op jit(solution)/shard_map/attention_forward/pallas_call | solution.py:239
  96.9 4.3 %collective-permute-done.17 = bf16[392,128]{1,0:T(8,128)(2,1)S(1)} collective-permute-done((bf16[392,128]{1,0:T(8,128)(2,1)S(1)}, bf16[392,128]{1,0:T(8,128)(2,1)S(1)}, u32[]{:S(2)}, u32[]{:S(2)}) %collective-permute-start.17) | collective-permute-done | bytes 100384 | tf_op jit(solution)/shard_map/ppermute | solution.py:473
  106.9 3.4 convert_reduce_fusion.1
  112.0 3.1 second_norm.1.refs_1_
  119.7 17.8 %feed_forward.1 = (bf16[784,2048]{1,0:T(8,128)(2,1)}, bf16[784,2048]{1,0:T(8,128)(2,1)}, bf16[784,1024]{1,0:T(8,128)(2,1)}, f32[1,2048]{1,0:T(1,128)S(1)}) custom-call(s32[5]{0:T(128)S(1)} %multiply_add_fusion.refs_0_.place_ref, bf16[784,1024]{1,0:T(8,128)(2,1)} %copy-done.19, bf16[784,1024]{1,0:T(8,128)(2,1)} %bitcast.95, f32[1,2048]{1,0:T(1,128)S(1)} %bitcast.106, ...), custom_call_target="tpu_custom_call" | custom-call | tf_op jit(solution)/shard_map/feed_forward/pallas_call | solution.py:407
  137.6 3.3 convolution_convert_fusion.5
  151.1 4.9 %second_norm_back.1 = (bf16[784,1024]{1,0:T(8,128)(2,1)S(1)}, f32[784,1024]{1,0:T(8,128)S(1)}, f32[8,1024]{1,0:T(8,128)S(1)}) custom-call(bf16[784,1024]{1,0:T(8,128)(2,1)S(1)} %bitcast.93, bf16[784,1024]{1,0:T(8,128)(2,1)} %convolution_convert_fusion.6.one_ref, bf16[784,1024]{1,0:T(8,128)(2,1)} %collective-permute-done.21.two_ref, f32[1,1024]{1,0:T(1,128)S(1)} %bitcast.101, ...), custom_call_target="tpu_custom_call" | custom-call | tf_op jit(solution)/shard_map/second_norm_back/pallas_call | solution.py:104
  165.1 5.2 %convolution_convert_fusion = bf16[1024,2048]{1,0:T(8,128)(2,1)S(1)} fusion(bf16[784,1024]{1,0:T(8,128)(2,1)S(1)} %bitcast.97, bf16[784,2048]{1,0:T(8,128)(2,1)S(1)} %copy-done.32), kind=kOutput, calls=%fused_computation.1 | convolution fusion | flops 3290431488 | bytes 9011200 | tf_op jit(solution)/shard_map/dot_general | solution.py:19
  174.0 4.4 %collective-permute-done.28 = bf16[392,256]{1,0:T(8,128)(2,1)S(1)} collective-permute-done((bf16[392,256]{1,0:T(8,128)(2,1)S(1)}, bf16[392,256]{1,0:T(8,128)(2,1)S(1)}, u32[]{:S(2)}, u32[]{:S(2)}) %collective-permute-start.28) | collective-permute-done | bytes 200736 | tf_op jit(solution)/shard_map/ppermute | solution.py:473
  178.4 9.6 %collective-permute-done.30 = bf16[256,2048]{1,0:T(8,128)(2,1)S(1)} collective-permute-done((bf16[256,2048]{1,0:T(8,128)(2,1)S(1)}, bf16[256,2048]{1,0:T(8,128)(2,1)S(1)}, u32[]{:S(2)}, u32[]{:S(2)}) %collective-permute-start.30) | collective-permute-done | bytes 1048608 | tf_op jit(solution)/shard_map/ppermute | solution.py:473
  193.5 15.7 %attention_backward.2 = (bf16[1568,128]{1,0:T(8,128)(2,1)S(1)}, bf16[1568,128]{1,0:T(8,128)(2,1)S(1)}, bf16[1568,128]{1,0:T(8,128)(2,1)S(1)}) custom-call(bf16[1568,768]{1,0:T(8,128)(2,1)S(1)} %joint_projection.1.q_ref.k_ref.v_ref, bf16[1568,768]{1,0:T(8,128)(2,1)S(1)} %joint_projection.1.q_ref.k_ref.v_ref, ...), custom_call_target="tpu_custom_call" | custom-call | tf_op jit(solution)/shard_map/attention_backward/pallas_call | solution.py:312
  215.4 3.4 collective-permute-start.35
  220.9 15.7 %attention_backward.3 = (bf16[1568,128]{1,0:T(8,128)(2,1)S(1)}, bf16[1568,128]{1,0:T(8,128)(2,1)S(1)}, bf16[1568,128]{1,0:T(8,128)(2,1)S(1)}) custom-call(bf16[1568,768]{1,0:T(8,128)(2,1)S(1)} %joint_projection.1.q_ref.k_ref.v_ref, bf16[1568,768]{1,0:T(8,128)(2,1)S(1)} %joint_projection.1.q_ref.k_ref.v_ref, ...), custom_call_target="tpu_custom_call" | custom-call | tf_op jit(solution)/shard_map/attention_backward/pallas_call | solution.py:312
  239.1 3.0 convolution_convert_fusion.1
  248.8 8.1 %collective-permute-done.44 = bf16[64,2048]{1,0:T(8,128)(2,1)S(1)} collective-permute-done((bf16[64,2048]{1,0:T(8,128)(2,1)S(1)}, bf16[64,2048]{1,0:T(8,128)(2,1)S(1)}, u32[]{:S(2)}, u32[]{:S(2)}) %collective-permute-start.44) | collective-permute-done | bytes 262176 | tf_op jit(solution)/shard_map/ppermute | solution.py:473
  260.8 6.0 %joint_grad.1 = bf16[4,256,768]{2,1,0:T(8,128)(2,1)S(1)} custom-call(s32[1]{0:T(128)} %bitcast.21.refs_0_, bf16[1568,512]{1,0:T(8,128)(2,1)S(1)} %copy-done.7, bf16[1568,512]{1,0:T(8,128)(2,1)S(1)} %copy-done.9, bf16[1568,768]{1,0:T(8,128)(2,1)} %copy-done.3), custom_call_target="tpu_custom_call" | custom-call | tf_op jit(solution)/shard_map/joint_grad/pallas_call | solution.py:187
  269.3 4.5 %collective-permute-done.40 = bf16[128,768]{1,0:T(8,128)(2,1)S(1)} collective-permute-done((bf16[128,768]{1,0:T(8,128)(2,1)S(1)}, bf16[128,768]{1,0:T(8,128)(2,1)S(1)}, u32[]{:S(2)}, u32[]{:S(2)}) %collective-permute-start.40) | collective-permute-done | bytes 196640 | tf_op jit(solution)/shard_map/ppermute | solution.py:473
  274.9 4.1 %collective-permute-done.39 = bf16[392,1024]{1,0:T(8,128)(2,1)S(1)} collective-permute-done((bf16[392,1024]{1,0:T(8,128)(2,1)S(1)}, bf16[392,1024]{1,0:T(8,128)(2,1)S(1)}, u32[]{:S(2)}, u32[]{:S(2)}) %collective-permute-start.39) | collective-permute-done | bytes 802848 | tf_op jit(solution)/shard_map/ppermute | solution.py:473
  288.1 7.6 %reduce_output.1 = bf16[784,1024]{1,0:T(8,128)(2,1)S(1)} custom-call(s32[5]{0:T(128)S(1)} %multiply_add_fusion.refs_0_.place_ref, bf16[784,2048]{1,0:T(8,128)(2,1)S(1)} %copy-done.33, bf16[256,2048]{1,0:T(8,128)(2,1)S(1)} %copy-done.29, bf16[256,2048]{1,0:T(8,128)(2,1)S(1)} %copy-done.14, bf16[256,2048]{1,0:T(8,128)(2,1)S(1)} %copy-done.17, ...), custom_call_target="tpu_custom_call" | custom-call | tf_op jit(solution)/shard_map/reduce_output/pallas_call | solution.py:453
  295.8 7.9 %collective-permute-done.46 = bf16[392,256]{1,0:T(8,128)(2,1)S(1)} collective-permute-done((bf16[392,256]{1,0:T(8,128)(2,1)S(1)}, bf16[392,256]{1,0:T(8,128)(2,1)S(1)}, u32[]{:S(2)}, u32[]{:S(2)}) %collective-permute-start.46) | collective-permute-done | bytes 200736 | tf_op jit(solution)/shard_map/ppermute | solution.py:473
  315.8 3.9 %first_norm_back.1 = (f32[784,1024]{1,0:T(8,128)}, f32[8,1024]{1,0:T(8,128)S(1)}) custom-call(bf16[784,1024]{1,0:T(8,128)(2,1)S(1)} %bitcast.94, bf16[784,1024]{1,0:T(8,128)(2,1)S(1)} %pad_maximum_fusion.1.upstream_ref, f32[1,1024]{1,0:T(1,128)S(1)} %bitcast.103, bf16[784,1024]{1,0:T(8,128)(2,1)S(1)} %bitcast.98, f32[784,1024]{1,0:T(8,128)S(1)} %copy-done.31), custom_call_target="tpu_custom_call" | custom-call | tf_op jit(solution)/shard_map/first_norm_back/pallas_call | solution.py:104
  319.7 15.2 %collective-permute-done.63 = bf16[128,2048]{1,0:T(8,128)(2,1)S(1)} collective-permute-done((bf16[128,2048]{1,0:T(8,128)(2,1)S(1)}, bf16[128,2048]{1,0:T(8,128)(2,1)S(1)}, u32[]{:S(2)}, u32[]{:S(2)}) %collective-permute-start.63) | collective-permute-done | bytes 524320 | tf_op jit(solution)/shard_map/ppermute | solution.py:473
  336.8 4.3 %collective-permute-start.54 = (f32[72,128]{1,0:T(8,128)S(1)}, f32[72,128]{1,0:T(8,128)S(1)}, u32[]{:S(2)}, u32[]{:S(2)}) collective-permute-start(f32[72,128]{1,0:T(8,128)S(1)} %bitcast.115), channel_id=1, source_target_pairs={{0,6},{2,4},{4,2},{6,0},{1,7},{3,5},{5,3},{7,1},{8,14},{10,12},{12... | collective-permute-start | bytes 110600 | tf_op jit(solution)/shard_map/ppermute | solution.py:473
  341.0 3.4 add_add_fusion
  356.5 9.2 %collective-permute-done.61 = bf16[64,2560]{1,0:T(8,128)(2,1)S(1)} collective-permute-done((bf16[64,2560]{1,0:T(8,128)(2,1)S(1)}, bf16[64,2560]{1,0:T(8,128)(2,1)S(1)}, u32[]{:S(2)}, u32[]{:S(2)}) %collective-permute-start.61) | collective-permute-done | bytes 327712 | tf_op jit(solution)/shard_map/ppermute | solution.py:473
  365.9 3.6 collective-permute-start.62
  373.3 8.1 %collective-permute-done.62 = bf16[128,2560]{1,0:T(8,128)(2,1)} collective-permute-done((bf16[128,2560]{1,0:T(8,128)(2,1)S(1)}, bf16[128,2560]{1,0:T(8,128)(2,1)}, u32[]{:S(2)}, u32[]{:S(2)}) %collective-permute-start.62) | collective-permute-done | bytes 655392 | tf_op jit(solution)/shard_map/ppermute | solution.py:473
  (452 shorter events, 164.1 us)
Async XLA Ops:
  8.0 29.0 %collective-permute-start.4 = (bf16[256,2304]{1,0:T(8,128)(2,1)S(1)}, bf16[256,2304]{1,0:T(8,128)(2,1)S(1)}, u32[]{:S(2)}, u32[]{:S(2)}) collective-permute-start(bf16[256,2304]{1,0:T(8,128)(2,1)S(1)} %constant_dynamic-update-slice_fusion.refs_4_), channel_id=1, source_target_pairs={{0,8},{8,0},{16,24},{24,16},{1,9},{9,1},{17,25},{25,17},{2,10},{10... | collective-permute-start | bytes 3538952 | tf_op jit(solution)/shard_map/ppermute | solution.py:473
  11.0 27.4 %collective-permute-start.5 = (bf16[256,2304]{1,0:T(8,128)(2,1)S(1)}, bf16[256,2304]{1,0:T(8,128)(2,1)S(1)}, u32[]{:S(2)}, u32[]{:S(2)}) collective-permute-start(bf16[256,2304]{1,0:T(8,128)(2,1)S(1)} %constant_dynamic-update-slice_fusion.refs_4_), channel_id=1, source_target_pairs={{0,16},{8,24},{16,0},{24,8},{1,17},{9,25},{17,1},{25,9},{2,18},{10... | collective-permute-start | bytes 3538952 | tf_op jit(solution)/shard_map/ppermute | solution.py:473
  12.5 21.4 %collective-permute-start = (bf16[392,512]{1,0:T(8,128)(2,1)}, bf16[392,512]{1,0:T(8,128)(2,1)}, u32[]{:S(2)}, u32[]{:S(2)}) collective-permute-start(bf16[392,512]{1,0:T(8,128)(2,1)} %get-tuple-element.173), channel_id=1, source_target_pairs={{0,2},{2,0},{4,6},{6,4},{1,3},{3,1},{5,7},{7,5},{8,10},{10,8},{12,... | collective-permute-start | bytes 1204232 | tf_op jit(solution)/shard_map/ppermute | solution.py:473
  16.7 17.3 %collective-permute-start.2 = (bf16[392,256]{1,0:T(8,128)(2,1)}, bf16[392,256]{1,0:T(8,128)(2,1)S(1)}, u32[]{:S(2)}, u32[]{:S(2)}) collective-permute-start(bf16[392,256]{1,0:T(8,128)(2,1)} %get-tuple-element.175), channel_id=1, source_target_pairs={{0,6},{2,4},{4,2},{6,0},{1,7},{3,5},{5,3},{7,1},{8,14},{10,12},{12... | collective-permute-start | bytes 602120 | tf_op jit(solution)/shard_map/ppermute | solution.py:473
  49.1 26.2 %collective-permute-start.9 = (bf16[256,1024]{1,0:T(8,128)(2,1)S(1)}, bf16[256,1024]{1,0:T(8,128)(2,1)S(1)}, u32[]{:S(2)}, u32[]{:S(2)}) collective-permute-start(bf16[256,1024]{1,0:T(8,128)(2,1)S(1)} %copy-done.34), channel_id=1, source_target_pairs={{0,8},{8,0},{16,24},{24,16},{1,9},{9,1},{17,25},{25,17},{2,10},{10... | collective-permute-start | bytes 1572872 | tf_op jit(solution)/shard_map/ppermute | solution.py:473
  50.4 25.0 %collective-permute-start.10 = (bf16[256,1024]{1,0:T(8,128)(2,1)S(1)}, bf16[256,1024]{1,0:T(8,128)(2,1)S(1)}, u32[]{:S(2)}, u32[]{:S(2)}) collective-permute-start(bf16[256,1024]{1,0:T(8,128)(2,1)S(1)} %copy-done.34), channel_id=1, source_target_pairs={{0,16},{8,24},{16,0},{24,8},{1,17},{9,25},{17,1},{25,9},{2,18},{10... | collective-permute-start | bytes 1572872 | tf_op jit(solution)/shard_map/ppermute | solution.py:473
  59.3 28.3 %collective-permute-start.14 = (bf16[256,2048]{1,0:T(8,128)(2,1)S(1)}, bf16[256,2048]{1,0:T(8,128)(2,1)S(1)}, u32[]{:S(2)}, u32[]{:S(2)}) collective-permute-start(bf16[256,2048]{1,0:T(8,128)(2,1)S(1)} %copy-done.27), channel_id=1, source_target_pairs={{0,8},{8,0},{16,24},{24,16},{1,9},{9,1},{17,25},{25,17},{2,10},{10... | collective-permute-start | bytes 3145736 | tf_op jit(solution)/shard_map/ppermute | solution.py:473
  59.9 27.7 %collective-permute-start.15 = (bf16[256,2048]{1,0:T(8,128)(2,1)S(1)}, bf16[256,2048]{1,0:T(8,128)(2,1)S(1)}, u32[]{:S(2)}, u32[]{:S(2)}) collective-permute-start(bf16[256,2048]{1,0:T(8,128)(2,1)S(1)} %copy-done.27), channel_id=1, source_target_pairs={{0,16},{8,24},{16,0},{24,8},{1,17},{9,25},{17,1},{25,9},{2,18},{10... | collective-permute-start | bytes 3145736 | tf_op jit(solution)/shard_map/ppermute | solution.py:473
  143.4 15.7 %collective-permute-start.26 = (bf16[128,2048]{1,0:T(8,128)(2,1)}, bf16[128,2048]{1,0:T(8,128)(2,1)S(1)}, u32[]{:S(2)}, u32[]{:S(2)}) collective-permute-start(bf16[128,2048]{1,0:T(8,128)(2,1)} %get-tuple-element.239), channel_id=1, source_target_pairs={{0,8},{8,0},{16,24},{24,16},{1,9},{9,1},{17,25},{25,17},{2,10},{10... | collective-permute-start | bytes 1572872 | tf_op jit(solution)/shard_map/ppermute | solution.py:473
  161.0 17.4 %collective-permute-start.28 = (bf16[392,256]{1,0:T(8,128)(2,1)S(1)}, bf16[392,256]{1,0:T(8,128)(2,1)S(1)}, u32[]{:S(2)}, u32[]{:S(2)}) collective-permute-start(bf16[392,256]{1,0:T(8,128)(2,1)S(1)} %get-tuple-element.242), channel_id=1, source_target_pairs={{0,4},{2,6},{4,0},{6,2},{1,5},{3,7},{5,1},{7,3},{8,12},{10,14},{12... | collective-permute-start | bytes 602120 | tf_op jit(solution)/shard_map/ppermute | solution.py:473
  163.8 24.1 %collective-permute-start.30 = (bf16[256,2048]{1,0:T(8,128)(2,1)S(1)}, bf16[256,2048]{1,0:T(8,128)(2,1)S(1)}, u32[]{:S(2)}, u32[]{:S(2)}) collective-permute-start(bf16[256,2048]{1,0:T(8,128)(2,1)S(1)} %pad_maximum_fusion.3), channel_id=1, source_target_pairs={{0,8},{8,0},{16,24},{24,16},{1,9},{9,1},{17,25},{25,17},{2,10},{10... | collective-permute-start | bytes 3145736 | tf_op jit(solution)/shard_map/ppermute | solution.py:473
  164.5 23.9 %collective-permute-start.31 = (bf16[256,2048]{1,0:T(8,128)(2,1)S(1)}, bf16[256,2048]{1,0:T(8,128)(2,1)S(1)}, u32[]{:S(2)}, u32[]{:S(2)}) collective-permute-start(bf16[256,2048]{1,0:T(8,128)(2,1)S(1)} %pad_maximum_fusion.4), channel_id=1, source_target_pairs={{0,16},{8,24},{16,0},{24,8},{1,17},{9,25},{17,1},{25,9},{2,18},{10... | collective-permute-start | bytes 3145736 | tf_op jit(solution)/shard_map/ppermute | solution.py:473
  189.0 20.3 %collective-permute-start.32 = (bf16[128,2560]{1,0:T(8,128)(2,1)S(1)}, bf16[128,2560]{1,0:T(8,128)(2,1)S(1)}, u32[]{:S(2)}, u32[]{:S(2)}) collective-permute-start(bf16[128,2560]{1,0:T(8,128)(2,1)S(1)} %get-tuple-element.262), channel_id=1, source_target_pairs={{0,8},{8,0},{16,24},{24,16},{1,9},{9,1},{17,25},{25,17},{2,10},{10... | collective-permute-start | bytes 1966088 | tf_op jit(solution)/shard_map/ppermute | solution.py:473
  190.5 18.9 %collective-permute-start.33 = (bf16[128,2560]{1,0:T(8,128)(2,1)S(1)}, bf16[128,2560]{1,0:T(8,128)(2,1)S(1)}, u32[]{:S(2)}, u32[]{:S(2)}) collective-permute-start(bf16[128,2560]{1,0:T(8,128)(2,1)S(1)} %get-tuple-element.263), channel_id=1, source_target_pairs={{0,16},{8,24},{16,0},{24,8},{1,17},{9,25},{17,1},{25,9},{2,18},{10... | collective-permute-start | bytes 1966088 | tf_op jit(solution)/shard_map/ppermute | solution.py:473
  191.8 17.5 %collective-permute-start.34 = (bf16[128,2048]{1,0:T(8,128)(2,1)S(1)}, bf16[128,2048]{1,0:T(8,128)(2,1)S(1)}, u32[]{:S(2)}, u32[]{:S(2)}) collective-permute-start(bf16[128,2048]{1,0:T(8,128)(2,1)S(1)} %dynamic-slice_convert_fusion.1), channel_id=1, source_target_pairs={{0,2},{2,0},{4,6},{6,4},{1,3},{3,1},{5,7},{7,5},{8,10},{10,8},{12,... | collective-permute-start | bytes 1572872 | tf_op jit(solution)/shard_map/ppermute | solution.py:473
  213.2 23.5 %collective-permute-start.36 = (bf16[128,2560]{1,0:T(8,128)(2,1)}, bf16[128,2560]{1,0:T(8,128)(2,1)}, u32[]{:S(2)}, u32[]{:S(2)}) collective-permute-start(bf16[128,2560]{1,0:T(8,128)(2,1)} %fusion.4), channel_id=1, source_target_pairs={{0,8},{8,0},{16,24},{24,16},{1,9},{9,1},{17,25},{25,17},{2,10},{10... | collective-permute-start | bytes 1966088 | tf_op jit(solution)/shard_map/ppermute | solution.py:473
  213.9 22.8 %collective-permute-start.37 = (bf16[128,2560]{1,0:T(8,128)(2,1)}, bf16[128,2560]{1,0:T(8,128)(2,1)}, u32[]{:S(2)}, u32[]{:S(2)}) collective-permute-start(bf16[128,2560]{1,0:T(8,128)(2,1)} %fusion.3), channel_id=1, source_target_pairs={{0,16},{8,24},{16,0},{24,8},{1,17},{9,25},{17,1},{25,9},{2,18},{10... | collective-permute-start | bytes 1966088 | tf_op jit(solution)/shard_map/ppermute | solution.py:473
  215.4 21.3 %collective-permute-start.35 = (bf16[64,2048]{1,0:T(8,128)(2,1)}, bf16[64,2048]{1,0:T(8,128)(2,1)S(1)}, u32[]{:S(2)}, u32[]{:S(2)}) collective-permute-start(bf16[64,2048]{1,0:T(8,128)(2,1)} %dynamic-slice_convert_fusion.3), channel_id=1, source_target_pairs={{0,4},{2,6},{4,0},{6,2},{1,5},{3,7},{5,1},{7,3},{8,12},{10,14},{12... | collective-permute-start | bytes 786440 | tf_op jit(solution)/shard_map/ppermute | solution.py:473
  246.9 22.4 %collective-permute-start.42 = (bf16[128,2560]{1,0:T(8,128)(2,1)S(1)}, bf16[128,2560]{1,0:T(8,128)(2,1)S(1)}, u32[]{:S(2)}, u32[]{:S(2)}) collective-permute-start(bf16[128,2560]{1,0:T(8,128)(2,1)S(1)} %copy-done.83), channel_id=1, source_target_pairs={{0,8},{8,0},{16,24},{24,16},{1,9},{9,1},{17,25},{25,17},{2,10},{10... | collective-permute-start | bytes 1966088 | tf_op jit(solution)/shard_map/ppermute | solution.py:473
  248.3 20.9 %collective-permute-start.43 = (bf16[128,2560]{1,0:T(8,128)(2,1)S(1)}, bf16[128,2560]{1,0:T(8,128)(2,1)S(1)}, u32[]{:S(2)}, u32[]{:S(2)}) collective-permute-start(bf16[128,2560]{1,0:T(8,128)(2,1)S(1)} %copy-done.84), channel_id=1, source_target_pairs={{0,16},{8,24},{16,0},{24,8},{1,17},{9,25},{17,1},{25,9},{2,18},{10... | collective-permute-start | bytes 1966088 | tf_op jit(solution)/shard_map/ppermute | solution.py:473
  259.1 19.9 %collective-permute-start.39 = (bf16[392,1024]{1,0:T(8,128)(2,1)S(1)}, bf16[392,1024]{1,0:T(8,128)(2,1)S(1)}, u32[]{:S(2)}, u32[]{:S(2)}) collective-permute-start(bf16[392,1024]{1,0:T(8,128)(2,1)S(1)} %pad_maximum_fusion.7), channel_id=1, source_target_pairs={{0,2},{2,0},{4,6},{6,4},{1,3},{3,1},{5,7},{7,5},{8,10},{10,8},{12,... | collective-permute-start | bytes 2408456 | tf_op jit(solution)/shard_map/ppermute | solution.py:473
  282.7 24.5 %collective-permute-start.49 = (bf16[128,2560]{1,0:T(8,128)(2,1)S(1)}, bf16[128,2560]{1,0:T(8,128)(2,1)S(1)}, u32[]{:S(2)}, u32[]{:S(2)}) collective-permute-start(bf16[128,2560]{1,0:T(8,128)(2,1)S(1)} %dynamic-slice_convert_fusion), channel_id=1, source_target_pairs={{0,2},{2,0},{4,6},{6,4},{1,3},{3,1},{5,7},{7,5},{8,10},{10,8},{12,... | collective-permute-start | bytes 1966088 | tf_op jit(solution)/shard_map/ppermute | solution.py:473
  283.0 20.7 %collective-permute-start.46 = (bf16[392,256]{1,0:T(8,128)(2,1)S(1)}, bf16[392,256]{1,0:T(8,128)(2,1)S(1)}, u32[]{:S(2)}, u32[]{:S(2)}) collective-permute-start(bf16[392,256]{1,0:T(8,128)(2,1)S(1)} %get-tuple-element.301), channel_id=1, source_target_pairs={{0,6},{2,4},{4,2},{6,0},{1,7},{3,5},{5,3},{7,1},{8,14},{10,12},{12... | collective-permute-start | bytes 602120 | tf_op jit(solution)/shard_map/ppermute | solution.py:473
  283.8 21.6 %collective-permute-start.45 = (bf16[392,256]{1,0:T(8,128)(2,1)S(1)}, bf16[392,256]{1,0:T(8,128)(2,1)S(1)}, u32[]{:S(2)}, u32[]{:S(2)}) collective-permute-start(bf16[392,256]{1,0:T(8,128)(2,1)S(1)} %get-tuple-element.300), channel_id=1, source_target_pairs={{0,4},{2,6},{4,0},{6,2},{1,5},{3,7},{5,1},{7,3},{8,12},{10,14},{12... | collective-permute-start | bytes 602120 | tf_op jit(solution)/shard_map/ppermute | solution.py:473
  286.2 19.1 %collective-permute-start.47 = (bf16[256,768]{1,0:T(8,128)(2,1)S(1)}, bf16[256,768]{1,0:T(8,128)(2,1)S(1)}, u32[]{:S(2)}, u32[]{:S(2)}) collective-permute-start(bf16[256,768]{1,0:T(8,128)(2,1)S(1)} %pad_maximum_fusion.18), channel_id=1, source_target_pairs={{0,8},{8,0},{16,24},{24,16},{1,9},{9,1},{17,25},{25,17},{2,10},{10... | collective-permute-start | bytes 1179656 | tf_op jit(solution)/shard_map/ppermute | solution.py:473
  287.6 17.8 %collective-permute-start.48 = (bf16[256,768]{1,0:T(8,128)(2,1)S(1)}, bf16[256,768]{1,0:T(8,128)(2,1)S(1)}, u32[]{:S(2)}, u32[]{:S(2)}) collective-permute-start(bf16[256,768]{1,0:T(8,128)(2,1)S(1)} %pad_maximum_fusion.19), channel_id=1, source_target_pairs={{0,16},{8,24},{16,0},{24,8},{1,17},{9,25},{17,1},{25,9},{2,18},{10... | collective-permute-start | bytes 1179656 | tf_op jit(solution)/shard_map/ppermute | solution.py:473
  307.4 29.1 %collective-permute-start.51 = (bf16[784,1024]{1,0:T(8,128)(2,1)S(1)}, bf16[784,1024]{1,0:T(8,128)(2,1)S(1)}, u32[]{:S(2)}, u32[]{:S(2)}) collective-permute-start(bf16[784,1024]{1,0:T(8,128)(2,1)S(1)} %reduce_output.1), channel_id=1, source_target_pairs={{0,1},{1,0},{2,3},{3,2},{4,5},{5,4},{6,7},{7,6},{8,9},{9,8},{10,11... | collective-permute-start | bytes 4816904 | tf_op jit(solution)/shard_map/ppermute | solution.py:473
  309.7 25.2 %collective-permute-start.63 = (bf16[128,2048]{1,0:T(8,128)(2,1)S(1)}, bf16[128,2048]{1,0:T(8,128)(2,1)S(1)}, u32[]{:S(2)}, u32[]{:S(2)}) collective-permute-start(bf16[128,2048]{1,0:T(8,128)(2,1)S(1)} %maximum_select_fusion.2), channel_id=1, source_target_pairs={{0,2},{2,0},{4,6},{6,4},{1,3},{3,1},{5,7},{7,5},{8,10},{10,8},{12,... | collective-permute-start | bytes 1572872 | tf_op jit(solution)/shard_map/ppermute | solution.py:473
  309.9 37.0 %collective-permute-start.55 = (bf16[256,768]{1,0:T(8,128)(2,1)S(1)}, bf16[256,768]{1,0:T(8,128)(2,1)S(1)}, u32[]{:S(2)}, u32[]{:S(2)}) collective-permute-start(bf16[256,768]{1,0:T(8,128)(2,1)S(1)} %fusion.1), channel_id=1, source_target_pairs={{0,4},{2,6},{4,0},{6,2},{1,5},{3,7},{5,1},{7,3},{8,12},{10,14},{12... | collective-permute-start | bytes 1179656 | tf_op jit(solution)/shard_map/ppermute | solution.py:473
  311.5 35.3 %collective-permute-start.56 = (bf16[64,2560]{1,0:T(8,128)(2,1)S(1)}, bf16[64,2560]{1,0:T(8,128)(2,1)S(1)}, u32[]{:S(2)}, u32[]{:S(2)}) collective-permute-start(bf16[64,2560]{1,0:T(8,128)(2,1)S(1)} %dynamic-slice_convert_fusion.2), channel_id=1, source_target_pairs={{0,4},{2,6},{4,0},{6,2},{1,5},{3,7},{5,1},{7,3},{8,12},{10,14},{12... | collective-permute-start | bytes 983048 | tf_op jit(solution)/shard_map/ppermute | solution.py:473
  350.9 20.2 %collective-permute-start.60 = (bf16[256,768]{1,0:T(8,128)(2,1)S(1)}, bf16[256,768]{1,0:T(8,128)(2,1)S(1)}, u32[]{:S(2)}, u32[]{:S(2)}) collective-permute-start(bf16[256,768]{1,0:T(8,128)(2,1)S(1)} %add_convert_fusion.7), channel_id=1, source_target_pairs={{0,2},{2,0},{4,6},{6,4},{1,3},{3,1},{5,7},{7,5},{8,10},{10,8},{12,... | collective-permute-start | bytes 1179656 | tf_op jit(solution)/shard_map/ppermute | solution.py:473
  365.9 15.5 %collective-permute-start.62 = (bf16[128,2560]{1,0:T(8,128)(2,1)S(1)}, bf16[128,2560]{1,0:T(8,128)(2,1)}, u32[]{:S(2)}, u32[]{:S(2)}) collective-permute-start(bf16[128,2560]{1,0:T(8,128)(2,1)S(1)} %maximum_select_fusion.1), channel_id=1, source_target_pairs={{0,2},{2,0},{4,6},{6,4},{1,3},{3,1},{5,7},{7,5},{8,10},{10,8},{12,... | collective-permute-start | bytes 1966088 | tf_op jit(solution)/shard_map/ppermute | solution.py:473
  (129 other events, 889.6 us)

commit v10 on v9

--- a/solution.py
+++ b/solution.py
@@ -579,13 +579,17 @@
     return pair[0].astype(FULL) + pair[1].astype(FULL)
 
 
-def join_rows(value, bit, distance):
-    other = swap(value, "ctx", distance)
+def joined(pair, bit):
+    value, other = pair
     return jnp.where(
         bit == 0,
         jnp.concatenate([value, other], axis=0),
         jnp.concatenate([other, value], axis=0),
     )
+
+
+def join_rows(value, bit, distance):
+    return joined((value, swap(value, "ctx", distance)), bit)
 
 
 def pairwise(pieces):
@@ -833,7 +837,8 @@
     )
     if four:
         wide_late = near_rows_out(wide_late)
-    expand_rows = join_rows(both(expand_rows).astype(LOW), clip_at, 2)
+    expand_rows = both(expand_rows).astype(LOW)
+    expand_rows = (expand_rows, swap(expand_rows, "ctx", 2))
     joint_slope = jnp.concatenate(
         [grad[kind] for kind in range(3) for grad in (grad_first, grad_second)], axis=1
     )
@@ -861,6 +866,7 @@
     passing, joint_far, wide_late, expand_rows = fence(
         passing, joint_far, wide_late, expand_rows
     )
+    expand_rows = joined(expand_rows, clip_at)
     if four:
         near_sum = [both((wide_early[0], wide_late[1])), both((wide_late[0], wide_early[1]))]
         wide_sum = rows_at(wide, 0).astype(FULL) + jnp.concatenate(near_sum, axis=0)

time: 390 us -> 388 us (level)
    unnamed x206 -> x210, local copies, waits for them, and re-layouts: 26.7 us -> 25.9 us
  transfers between devices with their start and end apart: 64 -> 64, of which waited for: 29 -> 31; matrix products, arithmetic and copies ran while one was open for 14% -> 14% of each run, Pallas kernels for 20% -> 20%
where the time goes in v10:
time: 388 us; the launch traced here: 383 us
  waiting for transfers between devices  111 us (29%)
  Pallas kernels  96.7 us (25%)
  starting transfers between devices  76.3 us (20%)
  local copies, waits for them, and re-layouts  44.1 us (11%)
  other arithmetic  30.9 us (8%)
  matrix products  20.9 us (5%)
    ppermute x64, waiting for transfers between devices, swap(): return lax.ppermute(value, axis, [(i, i ^ distance) for i in range(size)])  111 us
    ppermute x64, starting transfers between devices, swap(): return lax.ppermute(value, axis, [(i, i ^ distance) for i in range(size)])  76.3 us
    pallas_call x2, Pallas kernels, attention_backward(): pl.pallas_call(attention_backward_kernel, grid=(1,), in_specs=[pl.BlockSp...  31.4 us
    unnamed x210, local copies, waits for them, and re-layouts  25.9 us
    dot_general x9, matrix products, product(): return lax.dot_general(left, right, dims, preferred_element_type=FULL)  20.9 us
    pallas_call x1, Pallas kernels, feed_forward(): pl.pallas_call(lambda *refs: feed_forward_kernel(expand, reduce, edge, *r...  17.8 us
    pallas_call x2, Pallas kernels, attention_forward(): pl.pallas_call(attention_forward_kernel, grid=(1,), in_specs=[pl.BlockSpe...  14.5 us
    pallas_call x4, Pallas kernels, by_rows(): pl.pallas_call(kernel, grid=(count // chunk,), in_specs=in_specs, out_spe...  13.2 us
  transfers between devices with their start and end apart: 64, of which 31 were waited for; matrix products, arithmetic and copies ran while one was open for 14% of the time, Pallas kernels for 20%

profile of v10, /device:TPU:0, one launch (start us, length us, event | category | flops | bytes accessed | tf_op | source)
XLA Modules:
  0.0 383.1 jit_solution(5851500973664696268)
XLA Ops:
  16.9 11.6 %collective-permute-done.1 = bf16[392,256]{1,0:T(8,128)(2,1)S(1)} collective-permute-done((bf16[392,256]{1,0:T(8,128)(2,1)}, bf16[392,256]{1,0:T(8,128)(2,1)S(1)}, u32[]{:S(2)}, u32[]{:S(2)}) %collective-permute-start.1) | collective-permute-done | bytes 200736 | tf_op jit(solution)/shard_map/ppermute | solution.py:473
  28.5 5.4 %collective-permute-done.2 = bf16[392,256]{1,0:T(8,128)(2,1)S(1)} collective-permute-done((bf16[392,256]{1,0:T(8,128)(2,1)}, bf16[392,256]{1,0:T(8,128)(2,1)S(1)}, u32[]{:S(2)}, u32[]{:S(2)}) %collective-permute-start.2) | collective-permute-done | bytes 200736 | tf_op jit(solution)/shard_map/ppermute | solution.py:473
  44.6 3.3 collective-permute-done.6
  62.8 3.4 joint_projection.1.q_ref.k_ref.v_ref
  67.4 7.2 %attention_forward.2 = (bf16[1568,128]{1,0:T(8,128)(2,1)S(1)}, f32[8,1568]{1,0:T(8,128)S(1)}) custom-call(bf16[1568,768]{1,0:T(8,128)(2,1)S(1)} %joint_projection.1.q_ref.k_ref.v_ref, bf16[1568,768]{1,0:T(8,128)(2,1)S(1)} %joint_projection.1.q_ref.k_ref.v_ref, bf16[1568,768]{1,0:T(8,128)(2,1)S(1)} %joint_projection.1.q_ref.k_ref.v_ref), custom_call_target="tpu_custom_call" | custom-call | tf_op jit(solution)/shard_map/attention_forward/pallas_call | solution.py:239
  79.9 7.4 %attention_forward.3 = (bf16[1568,128]{1,0:T(8,128)(2,1)S(1)}, f32[8,1568]{1,0:T(8,128)S(1)}) custom-call(bf16[1568,768]{1,0:T(8,128)(2,1)S(1)} %joint_projection.1.q_ref.k_ref.v_ref, bf16[1568,768]{1,0:T(8,128)(2,1)S(1)} %joint_projection.1.q_ref.k_ref.v_ref, bf16[1568,768]{1,0:T(8,128)(2,1)S(1)} %joint_projection.1.q_ref.k_ref.v_ref), custom_call_target="tpu_custom_call" | custom-call | tf_op jit(solution)/shard_map/attention_forward/pallas_call | solution.py:239
  96.9 4.3 %collective-permute-done.17 = bf16[392,128]{1,0:T(8,128)(2,1)S(1)} collective-permute-done((bf16[392,128]{1,0:T(8,128)(2,1)S(1)}, bf16[392,128]{1,0:T(8,128)(2,1)S(1)}, u32[]{:S(2)}, u32[]{:S(2)}) %collective-permute-start.17) | collective-permute-done | bytes 100384 | tf_op jit(solution)/shard_map/ppermute | solution.py:473
  106.8 3.4 convert_reduce_fusion.1
  112.0 3.1 second_norm.1.refs_1_
  119.7 17.8 %feed_forward.1 = (bf16[784,2048]{1,0:T(8,128)(2,1)}, bf16[784,2048]{1,0:T(8,128)(2,1)}, bf16[784,1024]{1,0:T(8,128)(2,1)}, f32[1,2048]{1,0:T(1,128)S(1)}) custom-call(s32[5]{0:T(128)S(1)} %multiply_add_fusion.refs_0_.place_ref, bf16[784,1024]{1,0:T(8,128)(2,1)} %copy-done.19, bf16[784,1024]{1,0:T(8,128)(2,1)} %bitcast.95, f32[1,2048]{1,0:T(1,128)S(1)} %bitcast.106, ...), custom_call_target="tpu_custom_call" | custom-call | tf_op jit(solution)/shard_map/feed_forward/pallas_call | solution.py:407
  137.6 3.3 convolution_convert_fusion.5
  151.0 4.9 %second_norm_back.1 = (bf16[784,1024]{1,0:T(8,128)(2,1)S(1)}, f32[784,1024]{1,0:T(8,128)S(1)}, f32[8,1024]{1,0:T(8,128)S(1)}) custom-call(bf16[784,1024]{1,0:T(8,128)(2,1)S(1)} %bitcast.93, bf16[784,1024]{1,0:T(8,128)(2,1)} %convolution_convert_fusion.6.one_ref, bf16[784,1024]{1,0:T(8,128)(2,1)} %collective-permute-done.21.two_ref, f32[1,1024]{1,0:T(1,128)S(1)} %bitcast.101, ...), custom_call_target="tpu_custom_call" | custom-call | tf_op jit(solution)/shard_map/second_norm_back/pallas_call | solution.py:104
  165.1 5.2 %convolution_convert_fusion = bf16[1024,2048]{1,0:T(8,128)(2,1)S(1)} fusion(bf16[784,1024]{1,0:T(8,128)(2,1)S(1)} %bitcast.97, bf16[784,2048]{1,0:T(8,128)(2,1)S(1)} %copy-done.32), kind=kOutput, calls=%fused_computation.1 | convolution fusion | flops 3290431488 | bytes 9011200 | tf_op jit(solution)/shard_map/dot_general | solution.py:19
  174.0 4.4 %collective-permute-done.28 = bf16[392,256]{1,0:T(8,128)(2,1)S(1)} collective-permute-done((bf16[392,256]{1,0:T(8,128)(2,1)S(1)}, bf16[392,256]{1,0:T(8,128)(2,1)S(1)}, u32[]{:S(2)}, u32[]{:S(2)}) %collective-permute-start.28) | collective-permute-done | bytes 200736 | tf_op jit(solution)/shard_map/ppermute | solution.py:473
  178.4 9.6 %collective-permute-done.30 = bf16[256,2048]{1,0:T(8,128)(2,1)S(1)} collective-permute-done((bf16[256,2048]{1,0:T(8,128)(2,1)S(1)}, bf16[256,2048]{1,0:T(8,128)(2,1)S(1)}, u32[]{:S(2)}, u32[]{:S(2)}) %collective-permute-start.30) | collective-permute-done | bytes 1048608 | tf_op jit(solution)/shard_map/ppermute | solution.py:473
  193.4 15.7 %attention_backward.2 = (bf16[1568,128]{1,0:T(8,128)(2,1)S(1)}, bf16[1568,128]{1,0:T(8,128)(2,1)S(1)}, bf16[1568,128]{1,0:T(8,128)(2,1)S(1)}) custom-call(bf16[1568,768]{1,0:T(8,128)(2,1)S(1)} %joint_projection.1.q_ref.k_ref.v_ref, bf16[1568,768]{1,0:T(8,128)(2,1)S(1)} %joint_projection.1.q_ref.k_ref.v_ref, ...), custom_call_target="tpu_custom_call" | custom-call | tf_op jit(solution)/shard_map/attention_backward/pallas_call | solution.py:312
  215.3 3.4 collective-permute-start.35
  220.8 15.7 %attention_backward.3 = (bf16[1568,128]{1,0:T(8,128)(2,1)S(1)}, bf16[1568,128]{1,0:T(8,128)(2,1)S(1)}, bf16[1568,128]{1,0:T(8,128)(2,1)S(1)}) custom-call(bf16[1568,768]{1,0:T(8,128)(2,1)S(1)} %joint_projection.1.q_ref.k_ref.v_ref, bf16[1568,768]{1,0:T(8,128)(2,1)S(1)} %joint_projection.1.q_ref.k_ref.v_ref, ...), custom_call_target="tpu_custom_call" | custom-call | tf_op jit(solution)/shard_map/attention_backward/pallas_call | solution.py:312
  239.1 3.0 convolution_convert_fusion.1
  252.6 6.0 %joint_grad.1 = bf16[4,256,768]{2,1,0:T(8,128)(2,1)S(1)} custom-call(s32[1]{0:T(128)} %bitcast.21.refs_0_, bf16[1568,512]{1,0:T(8,128)(2,1)S(1)} %copy-done.7, bf16[1568,512]{1,0:T(8,128)(2,1)S(1)} %copy-done.9, bf16[1568,768]{1,0:T(8,128)(2,1)} %copy-done.3), custom_call_target="tpu_custom_call" | custom-call | tf_op jit(solution)/shard_map/joint_grad/pallas_call | solution.py:187
  259.8 3.2 collective-permute-done.44
  265.0 3.1 collective-permute-done.40
  269.8 6.4 %collective-permute-done.39 = bf16[392,1024]{1,0:T(8,128)(2,1)S(1)} collective-permute-done((bf16[392,1024]{1,0:T(8,128)(2,1)S(1)}, bf16[392,1024]{1,0:T(8,128)(2,1)S(1)}, u32[]{:S(2)}, u32[]{:S(2)}) %collective-permute-start.39) | collective-permute-done | bytes 802848 | tf_op jit(solution)/shard_map/ppermute | solution.py:473
  285.7 7.6 %reduce_output.1 = bf16[784,1024]{1,0:T(8,128)(2,1)S(1)} custom-call(s32[5]{0:T(128)S(1)} %multiply_add_fusion.refs_0_.place_ref, bf16[784,2048]{1,0:T(8,128)(2,1)S(1)} %copy-done.33, bf16[256,2048]{1,0:T(8,128)(2,1)S(1)} %copy-done.29, bf16[256,2048]{1,0:T(8,128)(2,1)S(1)} %copy-done.14, bf16[256,2048]{1,0:T(8,128)(2,1)S(1)} %copy-done.17, ...), custom_call_target="tpu_custom_call" | custom-call | tf_op jit(solution)/shard_map/reduce_output/pallas_call | solution.py:453
  293.4 10.1 %collective-permute-done.46 = bf16[392,256]{1,0:T(8,128)(2,1)S(1)} collective-permute-done((bf16[392,256]{1,0:T(8,128)(2,1)S(1)}, bf16[392,256]{1,0:T(8,128)(2,1)S(1)}, u32[]{:S(2)}, u32[]{:S(2)}) %collective-permute-start.46) | collective-permute-done | bytes 200736 | tf_op jit(solution)/shard_map/ppermute | solution.py:473
  314.7 3.9 %first_norm_back.1 = (f32[784,1024]{1,0:T(8,128)}, f32[8,1024]{1,0:T(8,128)S(1)}) custom-call(bf16[784,1024]{1,0:T(8,128)(2,1)S(1)} %bitcast.94, bf16[784,1024]{1,0:T(8,128)(2,1)S(1)} %pad_maximum_fusion.1.upstream_ref, f32[1,1024]{1,0:T(1,128)S(1)} %bitcast.103, bf16[784,1024]{1,0:T(8,128)(2,1)S(1)} %bitcast.98, f32[784,1024]{1,0:T(8,128)S(1)} %copy-done.31), custom_call_target="tpu_custom_call" | custom-call | tf_op jit(solution)/shard_map/first_norm_back/pallas_call | solution.py:104
  318.6 14.4 %collective-permute-done.63 = bf16[128,2048]{1,0:T(8,128)(2,1)S(1)} collective-permute-done((bf16[128,2048]{1,0:T(8,128)(2,1)S(1)}, bf16[128,2048]{1,0:T(8,128)(2,1)S(1)}, u32[]{:S(2)}, u32[]{:S(2)}) %collective-permute-start.63) | collective-permute-done | bytes 524320 | tf_op jit(solution)/shard_map/ppermute | solution.py:473
  335.9 3.2 collective-permute-start.54
  339.2 3.4 add_add_fusion
  354.8 9.2 %collective-permute-done.61 = bf16[64,2560]{1,0:T(8,128)(2,1)S(1)} collective-permute-done((bf16[64,2560]{1,0:T(8,128)(2,1)S(1)}, bf16[64,2560]{1,0:T(8,128)(2,1)S(1)}, u32[]{:S(2)}, u32[]{:S(2)}) %collective-permute-start.61) | collective-permute-done | bytes 327712 | tf_op jit(solution)/shard_map/ppermute | solution.py:473
  364.2 3.6 collective-permute-start.62
  371.6 8.0 %collective-permute-done.62 = bf16[128,2560]{1,0:T(8,128)(2,1)} collective-permute-done((bf16[128,2560]{1,0:T(8,128)(2,1)S(1)}, bf16[128,2560]{1,0:T(8,128)(2,1)}, u32[]{:S(2)}, u32[]{:S(2)}) %collective-permute-start.62) | collective-permute-done | bytes 655392 | tf_op jit(solution)/shard_map/ppermute | solution.py:473
  (456 shorter events, 166.0 us)
Async XLA Ops:
  8.0 29.0 %collective-permute-start.4 = (bf16[256,2304]{1,0:T(8,128)(2,1)S(1)}, bf16[256,2304]{1,0:T(8,128)(2,1)S(1)}, u32[]{:S(2)}, u32[]{:S(2)}) collective-permute-start(bf16[256,2304]{1,0:T(8,128)(2,1)S(1)} %constant_dynamic-update-slice_fusion.refs_4_), channel_id=1, source_target_pairs={{0,8},{8,0},{16,24},{24,16},{1,9},{9,1},{17,25},{25,17},{2,10},{10... | collective-permute-start | bytes 3538952 | tf_op jit(solution)/shard_map/ppermute | solution.py:473
  11.0 27.4 %collective-permute-start.5 = (bf16[256,2304]{1,0:T(8,128)(2,1)S(1)}, bf16[256,2304]{1,0:T(8,128)(2,1)S(1)}, u32[]{:S(2)}, u32[]{:S(2)}) collective-permute-start(bf16[256,2304]{1,0:T(8,128)(2,1)S(1)} %constant_dynamic-update-slice_fusion.refs_4_), channel_id=1, source_target_pairs={{0,16},{8,24},{16,0},{24,8},{1,17},{9,25},{17,1},{25,9},{2,18},{10... | collective-permute-start | bytes 3538952 | tf_op jit(solution)/shard_map/ppermute | solution.py:473
  12.5 21.4 %collective-permute-start = (bf16[392,512]{1,0:T(8,128)(2,1)}, bf16[392,512]{1,0:T(8,128)(2,1)}, u32[]{:S(2)}, u32[]{:S(2)}) collective-permute-start(bf16[392,512]{1,0:T(8,128)(2,1)} %get-tuple-element.174), channel_id=1, source_target_pairs={{0,2},{2,0},{4,6},{6,4},{1,3},{3,1},{5,7},{7,5},{8,10},{10,8},{12,... | collective-permute-start | bytes 1204232 | tf_op jit(solution)/shard_map/ppermute | solution.py:473
  16.7 17.3 %collective-permute-start.2 = (bf16[392,256]{1,0:T(8,128)(2,1)}, bf16[392,256]{1,0:T(8,128)(2,1)S(1)}, u32[]{:S(2)}, u32[]{:S(2)}) collective-permute-start(bf16[392,256]{1,0:T(8,128)(2,1)} %get-tuple-element.176), channel_id=1, source_target_pairs={{0,6},{2,4},{4,2},{6,0},{1,7},{3,5},{5,3},{7,1},{8,14},{10,12},{12... | collective-permute-start | bytes 602120 | tf_op jit(solution)/shard_map/ppermute | solution.py:473
  49.1 26.2 %collective-permute-start.9 = (bf16[256,1024]{1,0:T(8,128)(2,1)S(1)}, bf16[256,1024]{1,0:T(8,128)(2,1)S(1)}, u32[]{:S(2)}, u32[]{:S(2)}) collective-permute-start(bf16[256,1024]{1,0:T(8,128)(2,1)S(1)} %copy-done.34), channel_id=1, source_target_pairs={{0,8},{8,0},{16,24},{24,16},{1,9},{9,1},{17,25},{25,17},{2,10},{10... | collective-permute-start | bytes 1572872 | tf_op jit(solution)/shard_map/ppermute | solution.py:473
  50.3 25.0 %collective-permute-start.10 = (bf16[256,1024]{1,0:T(8,128)(2,1)S(1)}, bf16[256,1024]{1,0:T(8,128)(2,1)S(1)}, u32[]{:S(2)}, u32[]{:S(2)}) collective-permute-start(bf16[256,1024]{1,0:T(8,128)(2,1)S(1)} %copy-done.34), channel_id=1, source_target_pairs={{0,16},{8,24},{16,0},{24,8},{1,17},{9,25},{17,1},{25,9},{2,18},{10... | collective-permute-start | bytes 1572872 | tf_op jit(solution)/shard_map/ppermute | solution.py:473
  59.3 28.3 %collective-permute-start.14 = (bf16[256,2048]{1,0:T(8,128)(2,1)S(1)}, bf16[256,2048]{1,0:T(8,128)(2,1)S(1)}, u32[]{:S(2)}, u32[]{:S(2)}) collective-permute-start(bf16[256,2048]{1,0:T(8,128)(2,1)S(1)} %copy-done.27), channel_id=1, source_target_pairs={{0,8},{8,0},{16,24},{24,16},{1,9},{9,1},{17,25},{25,17},{2,10},{10... | collective-permute-start | bytes 3145736 | tf_op jit(solution)/shard_map/ppermute | solution.py:473
  59.9 27.7 %collective-permute-start.15 = (bf16[256,2048]{1,0:T(8,128)(2,1)S(1)}, bf16[256,2048]{1,0:T(8,128)(2,1)S(1)}, u32[]{:S(2)}, u32[]{:S(2)}) collective-permute-start(bf16[256,2048]{1,0:T(8,128)(2,1)S(1)} %copy-done.27), channel_id=1, source_target_pairs={{0,16},{8,24},{16,0},{24,8},{1,17},{9,25},{17,1},{25,9},{2,18},{10... | collective-permute-start | bytes 3145736 | tf_op jit(solution)/shard_map/ppermute | solution.py:473
  143.3 15.7 %collective-permute-start.26 = (bf16[128,2048]{1,0:T(8,128)(2,1)}, bf16[128,2048]{1,0:T(8,128)(2,1)S(1)}, u32[]{:S(2)}, u32[]{:S(2)}) collective-permute-start(bf16[128,2048]{1,0:T(8,128)(2,1)} %get-tuple-element.240), channel_id=1, source_target_pairs={{0,8},{8,0},{16,24},{24,16},{1,9},{9,1},{17,25},{25,17},{2,10},{10... | collective-permute-start | bytes 1572872 | tf_op jit(solution)/shard_map/ppermute | solution.py:473
  161.0 17.4 %collective-permute-start.28 = (bf16[392,256]{1,0:T(8,128)(2,1)S(1)}, bf16[392,256]{1,0:T(8,128)(2,1)S(1)}, u32[]{:S(2)}, u32[]{:S(2)}) collective-permute-start(bf16[392,256]{1,0:T(8,128)(2,1)S(1)} %get-tuple-element.243), channel_id=1, source_target_pairs={{0,4},{2,6},{4,0},{6,2},{1,5},{3,7},{5,1},{7,3},{8,12},{10,14},{12... | collective-permute-start | bytes 602120 | tf_op jit(solution)/shard_map/ppermute | solution.py:473
  163.8 24.1 %collective-permute-start.30 = (bf16[256,2048]{1,0:T(8,128)(2,1)S(1)}, bf16[256,2048]{1,0:T(8,128)(2,1)S(1)}, u32[]{:S(2)}, u32[]{:S(2)}) collective-permute-start(bf16[256,2048]{1,0:T(8,128)(2,1)S(1)} %pad_maximum_fusion.3), channel_id=1, source_target_pairs={{0,8},{8,0},{16,24},{24,16},{1,9},{9,1},{17,25},{25,17},{2,10},{10... | collective-permute-start | bytes 3145736 | tf_op jit(solution)/shard_map/ppermute | solution.py:473
  164.4 23.9 %collective-permute-start.31 = (bf16[256,2048]{1,0:T(8,128)(2,1)S(1)}, bf16[256,2048]{1,0:T(8,128)(2,1)S(1)}, u32[]{:S(2)}, u32[]{:S(2)}) collective-permute-start(bf16[256,2048]{1,0:T(8,128)(2,1)S(1)} %pad_maximum_fusion.4), channel_id=1, source_target_pairs={{0,16},{8,24},{16,0},{24,8},{1,17},{9,25},{17,1},{25,9},{2,18},{10... | collective-permute-start | bytes 3145736 | tf_op jit(solution)/shard_map/ppermute | solution.py:473
  189.0 20.3 %collective-permute-start.32 = (bf16[128,2560]{1,0:T(8,128)(2,1)S(1)}, bf16[128,2560]{1,0:T(8,128)(2,1)S(1)}, u32[]{:S(2)}, u32[]{:S(2)}) collective-permute-start(bf16[128,2560]{1,0:T(8,128)(2,1)S(1)} %get-tuple-element.263), channel_id=1, source_target_pairs={{0,8},{8,0},{16,24},{24,16},{1,9},{9,1},{17,25},{25,17},{2,10},{10... | collective-permute-start | bytes 1966088 | tf_op jit(solution)/shard_map/ppermute | solution.py:473
  190.4 18.9 %collective-permute-start.33 = (bf16[128,2560]{1,0:T(8,128)(2,1)S(1)}, bf16[128,2560]{1,0:T(8,128)(2,1)S(1)}, u32[]{:S(2)}, u32[]{:S(2)}) collective-permute-start(bf16[128,2560]{1,0:T(8,128)(2,1)S(1)} %get-tuple-element.264), channel_id=1, source_target_pairs={{0,16},{8,24},{16,0},{24,8},{1,17},{9,25},{17,1},{25,9},{2,18},{10... | collective-permute-start | bytes 1966088 | tf_op jit(solution)/shard_map/ppermute | solution.py:473
  191.8 17.4 %collective-permute-start.34 = (bf16[128,2048]{1,0:T(8,128)(2,1)S(1)}, bf16[128,2048]{1,0:T(8,128)(2,1)S(1)}, u32[]{:S(2)}, u32[]{:S(2)}) collective-permute-start(bf16[128,2048]{1,0:T(8,128)(2,1)S(1)} %dynamic-slice_convert_fusion.1), channel_id=1, source_target_pairs={{0,2},{2,0},{4,6},{6,4},{1,3},{3,1},{5,7},{7,5},{8,10},{10,8},{12,... | collective-permute-start | bytes 1572872 | tf_op jit(solution)/shard_map/ppermute | solution.py:473
  213.2 23.5 %collective-permute-start.36 = (bf16[128,2560]{1,0:T(8,128)(2,1)}, bf16[128,2560]{1,0:T(8,128)(2,1)}, u32[]{:S(2)}, u32[]{:S(2)}) collective-permute-start(bf16[128,2560]{1,0:T(8,128)(2,1)} %fusion.4), channel_id=1, source_target_pairs={{0,8},{8,0},{16,24},{24,16},{1,9},{9,1},{17,25},{25,17},{2,10},{10... | collective-permute-start | bytes 1966088 | tf_op jit(solution)/shard_map/ppermute | solution.py:473
  213.8 22.8 %collective-permute-start.37 = (bf16[128,2560]{1,0:T(8,128)(2,1)}, bf16[128,2560]{1,0:T(8,128)(2,1)}, u32[]{:S(2)}, u32[]{:S(2)}) collective-permute-start(bf16[128,2560]{1,0:T(8,128)(2,1)} %fusion.3), channel_id=1, source_target_pairs={{0,16},{8,24},{16,0},{24,8},{1,17},{9,25},{17,1},{25,9},{2,18},{10... | collective-permute-start | bytes 1966088 | tf_op jit(solution)/shard_map/ppermute | solution.py:473
  215.3 21.3 %collective-permute-start.35 = (bf16[64,2048]{1,0:T(8,128)(2,1)}, bf16[64,2048]{1,0:T(8,128)(2,1)S(1)}, u32[]{:S(2)}, u32[]{:S(2)}) collective-permute-start(bf16[64,2048]{1,0:T(8,128)(2,1)} %dynamic-slice_convert_fusion.3), channel_id=1, source_target_pairs={{0,4},{2,6},{4,0},{6,2},{1,5},{3,7},{5,1},{7,3},{8,12},{10,14},{12... | collective-permute-start | bytes 786440 | tf_op jit(solution)/shard_map/ppermute | solution.py:473
  246.7 17.8 %collective-permute-start.42 = (bf16[128,2560]{1,0:T(8,128)(2,1)S(1)}, bf16[128,2560]{1,0:T(8,128)(2,1)S(1)}, u32[]{:S(2)}, u32[]{:S(2)}) collective-permute-start(bf16[128,2560]{1,0:T(8,128)(2,1)S(1)} %copy-done.83), channel_id=1, source_target_pairs={{0,8},{8,0},{16,24},{24,16},{1,9},{9,1},{17,25},{25,17},{2,10},{10... | collective-permute-start | bytes 1966088 | tf_op jit(solution)/shard_map/ppermute | solution.py:473
  248.1 16.9 %collective-permute-start.43 = (bf16[128,2560]{1,0:T(8,128)(2,1)S(1)}, bf16[128,2560]{1,0:T(8,128)(2,1)S(1)}, u32[]{:S(2)}, u32[]{:S(2)}) collective-permute-start(bf16[128,2560]{1,0:T(8,128)(2,1)S(1)} %copy-done.84), channel_id=1, source_target_pairs={{0,16},{8,24},{16,0},{24,8},{1,17},{9,25},{17,1},{25,9},{2,18},{10... | collective-permute-start | bytes 1966088 | tf_op jit(solution)/shard_map/ppermute | solution.py:473
  250.9 25.4 %collective-permute-start.39 = (bf16[392,1024]{1,0:T(8,128)(2,1)S(1)}, bf16[392,1024]{1,0:T(8,128)(2,1)S(1)}, u32[]{:S(2)}, u32[]{:S(2)}) collective-permute-start(bf16[392,1024]{1,0:T(8,128)(2,1)S(1)} %pad_maximum_fusion.7), channel_id=1, source_target_pairs={{0,2},{2,0},{4,6},{6,4},{1,3},{3,1},{5,7},{7,5},{8,10},{10,8},{12,... | collective-permute-start | bytes 2408456 | tf_op jit(solution)/shard_map/ppermute | solution.py:473
  279.8 23.8 %collective-permute-start.47 = (bf16[256,768]{1,0:T(8,128)(2,1)S(1)}, bf16[256,768]{1,0:T(8,128)(2,1)S(1)}, u32[]{:S(2)}, u32[]{:S(2)}) collective-permute-start(bf16[256,768]{1,0:T(8,128)(2,1)S(1)} %pad_maximum_fusion.18), channel_id=1, source_target_pairs={{0,8},{8,0},{16,24},{24,16},{1,9},{9,1},{17,25},{25,17},{2,10},{10... | collective-permute-start | bytes 1179656 | tf_op jit(solution)/shard_map/ppermute | solution.py:473
  280.5 23.1 %collective-permute-start.48 = (bf16[256,768]{1,0:T(8,128)(2,1)S(1)}, bf16[256,768]{1,0:T(8,128)(2,1)S(1)}, u32[]{:S(2)}, u32[]{:S(2)}) collective-permute-start(bf16[256,768]{1,0:T(8,128)(2,1)S(1)} %pad_maximum_fusion.19), channel_id=1, source_target_pairs={{0,16},{8,24},{16,0},{24,8},{1,17},{9,25},{17,1},{25,9},{2,18},{10... | collective-permute-start | bytes 1179656 | tf_op jit(solution)/shard_map/ppermute | solution.py:473
  282.0 23.7 %collective-permute-start.49 = (bf16[128,2560]{1,0:T(8,128)(2,1)S(1)}, bf16[128,2560]{1,0:T(8,128)(2,1)S(1)}, u32[]{:S(2)}, u32[]{:S(2)}) collective-permute-start(bf16[128,2560]{1,0:T(8,128)(2,1)S(1)} %dynamic-slice_convert_fusion), channel_id=1, source_target_pairs={{0,2},{2,0},{4,6},{6,4},{1,3},{3,1},{5,7},{7,5},{8,10},{10,8},{12,... | collective-permute-start | bytes 1966088 | tf_op jit(solution)/shard_map/ppermute | solution.py:473
  282.1 21.3 %collective-permute-start.46 = (bf16[392,256]{1,0:T(8,128)(2,1)S(1)}, bf16[392,256]{1,0:T(8,128)(2,1)S(1)}, u32[]{:S(2)}, u32[]{:S(2)}) collective-permute-start(bf16[392,256]{1,0:T(8,128)(2,1)S(1)} %get-tuple-element.302), channel_id=1, source_target_pairs={{0,6},{2,4},{4,2},{6,0},{1,7},{3,5},{5,3},{7,1},{8,14},{10,12},{12... | collective-permute-start | bytes 602120 | tf_op jit(solution)/shard_map/ppermute | solution.py:473
  283.7 19.9 %collective-permute-start.45 = (bf16[392,256]{1,0:T(8,128)(2,1)S(1)}, bf16[392,256]{1,0:T(8,128)(2,1)S(1)}, u32[]{:S(2)}, u32[]{:S(2)}) collective-permute-start(bf16[392,256]{1,0:T(8,128)(2,1)S(1)} %get-tuple-element.301), channel_id=1, source_target_pairs={{0,4},{2,6},{4,0},{6,2},{1,5},{3,7},{5,1},{7,3},{8,12},{10,14},{12... | collective-permute-start | bytes 602120 | tf_op jit(solution)/shard_map/ppermute | solution.py:473
  306.0 28.6 %collective-permute-start.51 = (bf16[784,1024]{1,0:T(8,128)(2,1)S(1)}, bf16[784,1024]{1,0:T(8,128)(2,1)S(1)}, u32[]{:S(2)}, u32[]{:S(2)}) collective-permute-start(bf16[784,1024]{1,0:T(8,128)(2,1)S(1)} %reduce_output.1), channel_id=1, source_target_pairs={{0,1},{1,0},{2,3},{3,2},{4,5},{5,4},{6,7},{7,6},{8,9},{9,8},{10,11... | collective-permute-start | bytes 4816904 | tf_op jit(solution)/shard_map/ppermute | solution.py:473
  308.3 24.7 %collective-permute-start.63 = (bf16[128,2048]{1,0:T(8,128)(2,1)S(1)}, bf16[128,2048]{1,0:T(8,128)(2,1)S(1)}, u32[]{:S(2)}, u32[]{:S(2)}) collective-permute-start(bf16[128,2048]{1,0:T(8,128)(2,1)S(1)} %maximum_select_fusion.2), channel_id=1, source_target_pairs={{0,2},{2,0},{4,6},{6,4},{1,3},{3,1},{5,7},{7,5},{8,10},{10,8},{12,... | collective-permute-start | bytes 1572872 | tf_op jit(solution)/shard_map/ppermute | solution.py:473
  308.8 36.7 %collective-permute-start.55 = (bf16[256,768]{1,0:T(8,128)(2,1)S(1)}, bf16[256,768]{1,0:T(8,128)(2,1)S(1)}, u32[]{:S(2)}, u32[]{:S(2)}) collective-permute-start(bf16[256,768]{1,0:T(8,128)(2,1)S(1)} %fusion.1), channel_id=1, source_target_pairs={{0,4},{2,6},{4,0},{6,2},{1,5},{3,7},{5,1},{7,3},{8,12},{10,14},{12... | collective-permute-start | bytes 1179656 | tf_op jit(solution)/shard_map/ppermute | solution.py:473
  310.5 35.0 %collective-permute-start.56 = (bf16[64,2560]{1,0:T(8,128)(2,1)S(1)}, bf16[64,2560]{1,0:T(8,128)(2,1)S(1)}, u32[]{:S(2)}, u32[]{:S(2)}) collective-permute-start(bf16[64,2560]{1,0:T(8,128)(2,1)S(1)} %dynamic-slice_convert_fusion.2), channel_id=1, source_target_pairs={{0,4},{2,6},{4,0},{6,2},{1,5},{3,7},{5,1},{7,3},{8,12},{10,14},{12... | collective-permute-start | bytes 983048 | tf_op jit(solution)/shard_map/ppermute | solution.py:473
  349.6 19.9 %collective-permute-start.60 = (bf16[256,768]{1,0:T(8,128)(2,1)S(1)}, bf16[256,768]{1,0:T(8,128)(2,1)S(1)}, u32[]{:S(2)}, u32[]{:S(2)}) collective-permute-start(bf16[256,768]{1,0:T(8,128)(2,1)S(1)} %add_convert_fusion.7), channel_id=1, source_target_pairs={{0,2},{2,0},{4,6},{6,4},{1,3},{3,1},{5,7},{7,5},{8,10},{10,8},{12,... | collective-permute-start | bytes 1179656 | tf_op jit(solution)/shard_map/ppermute | solution.py:473
  364.2 15.5 %collective-permute-start.62 = (bf16[128,2560]{1,0:T(8,128)(2,1)S(1)}, bf16[128,2560]{1,0:T(8,128)(2,1)}, u32[]{:S(2)}, u32[]{:S(2)}) collective-permute-start(bf16[128,2560]{1,0:T(8,128)(2,1)S(1)} %maximum_select_fusion.1), channel_id=1, source_target_pairs={{0,2},{2,0},{4,6},{6,4},{1,3},{3,1},{5,7},{7,5},{8,10},{10,8},{12,... | collective-permute-start | bytes 1966088 | tf_op jit(solution)/shard_map/ppermute | solution.py:473
  (131 other events, 886.2 us)
